TPU v7x, 128 devices: a whole 4x4x4 slice. The times are simulated.
128 devices in a mesh: gx: 16 (over z_lo, x, core), gy: 8 (over y, z_hi).
Axes of the slice: x: 4, y: 4, z: 4 (z_hi: 2, z_lo: 2; z = z_hi * 2 + z_lo), core: 2. Of those that a mesh axis runs over, the one named last changes fastest.
Arguments:
- features: bfloat16 [64, 128, 64, 128], P(None, 'gx', 'gy'), may hold values from -6 to 6
- cotangent: bfloat16 [64, 128, 64, 128], P(None, 'gx', 'gy'), may hold values from -6 to 6
- block_mask: int32 [16, 8, 16], P('gx', 'gy'), may hold values from 0 to 1, as said below
- kernel_one: bfloat16 [3, 3, 3, 64, 64], replicated, may hold values from -0.15625 to 0.15625
- kernel_two: bfloat16 [3, 3, 3, 64, 64], replicated, may hold values from -0.15625 to 0.15625
Outputs:
- grad_features: bfloat16 [64, 128, 64, 128], P(None, 'gx', 'gy')
- grad_one: float32 [3, 3, 3, 64, 64], replicated
- grad_two: float32 [3, 3, 3, 64, 64], replicated
Inputs may be any that keep to these rules, and one draw needn't show every extreme that they name: `block_mask`: 1 marks an active block of 8 x 8 x 8 cells, 0 an empty one.
All inputs are finite; a program needn't handle non-finite values.
Results may differ from a plain program's by a relative error of at most 0.0032.
Values may be sent and summed in bfloat16 or wider, within the bound.
No kernel may reach another device: no remote copies, remote signals or barrier semaphores. Data moves between devices by JAX's collectives and lax.ppermute only.
A program may use at most 192 MiB of HBM per device.

v0:
```python
import math

import jax
import jax.numpy as jnp
from jax import lax
from jax.sharding import PartitionSpec as P

BS = 8


def padded_2(cells, sides, width):
    for axis, dim in sides:
        count = lax.axis_size(axis)
        ends = count - 1
        head = lax.slice_in_dim(cells, 0, width, axis=dim)
        tail = lax.slice_in_dim(cells, cells.shape[dim] - width, cells.shape[dim], axis=dim)
        cells = jnp.concatenate(
            [
                lax.ppermute(tail, axis, [(i, (i + 1) % count) for i in range(ends)]),
                cells,
                lax.ppermute(head, axis, [((i + 1) % count, i) for i in range(ends)]),
            ],
            axis=dim,
        )
    return cells


def upsample(block_mask):
    nbx, nby, nbz = block_mask.shape
    wide = jnp.broadcast_to(block_mask[:, None, :, None, :, None], (nbx, BS, nby, BS, nbz, BS))
    return wide.reshape(nbx * BS, nby * BS, nbz * BS)


def flip_kernel(kernel):
    return jnp.transpose(jnp.flip(kernel, (0, 1, 2)), (0, 1, 2, 4, 3))


def silu_slope(value):
    sig = jax.nn.sigmoid(value)
    return sig * (1.0 + value * (1.0 - sig))


def stack_depth(source):
    depth = source.shape[-1]
    padded = jnp.pad(source, ((0, 0), (0, 0), (0, 0), (1, 1)))
    return jnp.concatenate(
        [padded[..., 0:depth], padded[..., 1 : depth + 1], padded[..., 2 : depth + 2]], 0
    )


def stack_reverse(source):
    depth = source.shape[-1]
    padded = jnp.pad(source, ((0, 0), (0, 0), (0, 0), (1, 1)))
    return jnp.concatenate(
        [padded[..., 2 : depth + 2], padded[..., 1 : depth + 1], padded[..., 0:depth]], 0
    )


def conv_pad(source, kernel, size_x, size_y):
    stacked = stack_depth(source)
    folded = kernel.reshape(3, 3, 3 * kernel.shape[3], kernel.shape[4])
    total = None
    for row_off in range(3):
        for col_off in range(3):
            window = stacked[:, row_off : row_off + size_x, col_off : col_off + size_y]
            term = jnp.einsum(
                "co,cxyz->oxyz",
                folded[row_off, col_off],
                window,
                preferred_element_type=jnp.float32,
            )
            total = term if total is None else total + term
    return total


def grad_forward(source, grad, size_x, size_y):
    stacked = stack_depth(source)
    pieces = []
    for row_off in range(3):
        for col_off in range(3):
            window = stacked[:, row_off : row_off + size_x, col_off : col_off + size_y]
            pieces.append(
                jnp.einsum("cxyz,oxyz->co", window, grad, preferred_element_type=jnp.float32)
            )
    return jnp.stack(pieces, 0).reshape(3, 3, 3, source.shape[0], grad.shape[0])


def grad_backward(activ, grad_pad, size_x, size_y):
    stacked = stack_reverse(grad_pad)
    pieces = []
    for row_off in range(3):
        for col_off in range(3):
            start_x = 2 - row_off
            start_y = 2 - col_off
            window = stacked[:, start_x : start_x + size_x, start_y : start_y + size_y]
            block = jnp.einsum("cxyz,kxyz->ck", activ, window, preferred_element_type=jnp.float32)
            block = block.reshape(activ.shape[0], 3, grad_pad.shape[0])
            pieces.append(jnp.transpose(block, (1, 0, 2)))
    return jnp.stack(pieces, 0).reshape(3, 3, 3, activ.shape[0], grad_pad.shape[0])


def shards(features, cotangent, block_mask, kernel_one, kernel_two):
    chans, tile_x, tile_y, tile_z = features.shape
    cell = upsample(block_mask).astype(jnp.bfloat16)[None]
    cell_f = cell.astype(jnp.float32)
    masked_in = features * cell
    masked_grad = cotangent * cell
    flip_one = flip_kernel(kernel_one)
    flip_two = flip_kernel(kernel_two)
    cells_all = tile_x * tile_y * tile_z * lax.axis_size("gx") * lax.axis_size("gy")
    scale = 1.0 / math.sqrt(cells_all)
    in_pad, grad_pad = (
        padded_2(masked_in, (("gx", 1), ("gy", 2)), 1),
        padded_2(masked_grad, (("gx", 1), ("gy", 2)), 1),
    )
    pre_act = conv_pad(in_pad, kernel_one, tile_x, tile_y)
    activ = (cell_f * jax.nn.silu(pre_act)).astype(jnp.bfloat16)
    partial_two = grad_backward(activ, grad_pad, tile_x, tile_y)
    summed_two = partial_two
    act_grad = conv_pad(grad_pad, flip_two, tile_x, tile_y)
    pre_grad = (cell_f * silu_slope(pre_act) * act_grad).astype(jnp.bfloat16)
    hidden_pad = padded_2(pre_grad, (("gx", 1), ("gy", 2)), 1)
    partial_one = grad_forward(in_pad, pre_grad, tile_x, tile_y)
    branch = conv_pad(hidden_pad, flip_one, tile_x, tile_y)
    grad_features = (cell_f * (cotangent.astype(jnp.float32) + branch)).astype(jnp.bfloat16)
    summed_one, summed_two = lax.psum((partial_one, summed_two), ("gx", "gy"))
    return (grad_features, summed_one * scale, summed_two * scale)


def solution(mesh):
    placed = (P(None, "gx", "gy", None), P(None, "gx", "gy", None), P("gx", "gy", None), P(), P())
    return jax.shard_map(
        shards,
        mesh=mesh,
        in_specs=placed,
        out_specs=(P(None, "gx", "gy", None), P(), P()),
        check_vma=False,
    )
```

profile of v0, /device:TPU:1, one launch (start us, length us, event | category | flops | bytes accessed | tf_op | source)
XLA Modules:
  0.0 286.3 jit_solution(6869526273240850333)
XLA Ops:
  8.1 3.3 %copy_multiply_fusion.1 = (bf16[64,8,8,128]{3,0,2,1:T(8,128)(2,1)S(1)}, bf16[64,8,8,128]{3,0,2,1:T(8,128)(2,1)S(1)}) fusion(bf16[64,8,8,128]{3,2,1,0:T(8,128)(2,1)} %param.6, bf16[128]{0:T(256)(128)(2,1)S(1)} %convert_element_type.40, bf16[64,8,8,128]{3,2,1,0:T(8,128)(2,1)} %param.5), kind=kLoop, calls=%fused_computation.141 | loop fusion | flops 1048576 | bytes 4194560 | tf_op jit(solution)/shard_map/mul | solution.py:107
  11.5 4.5 %collective-permute-start = (bf16[64,1,8,128]{3,0,2,1:T(8,128)(2,1)S(1)}, bf16[64,1,8,128]{3,0,2,1:T(8,128)(2,1)S(1)}, u32[]{:S(2)}, u32[]{:S(2)}) collective-permute-start(bf16[64,1,8,128]{3,0,2,1:T(8,128)(2,1)S(1)} %get-tuple-element.29), channel_id=1, source_target_pairs={{0,8},{8,16},{16,24},{24,32},{32,40},{40,48},{48,56},{56,64},{64,7... | collective-permute-start | bytes 393224 | tf_op jit(solution)/shard_map/ppermute | solution.py:19
  16.0 1.9 collective-permute-start.1
  18.6 3.8 %collective-permute-start.4 = (bf16[64,1,8,128]{3,0,2,1:T(8,128)(2,1)}, bf16[64,1,8,128]{3,0,2,1:T(8,128)(2,1)S(1)}, u32[]{:S(2)}, u32[]{:S(2)}) collective-permute-start(bf16[64,1,8,128]{3,0,2,1:T(8,128)(2,1)} %get-tuple-element.27), channel_id=1, source_target_pairs={{0,8},{8,16},{16,24},{24,32},{32,40},{40,48},{48,56},{56,64},{64,7... | collective-permute-start | bytes 393224 | tf_op jit(solution)/shard_map/ppermute | solution.py:19
  22.4 1.9 collective-permute-start.5
  24.4 0.8 pad_maximum_fusion.13
  25.2 6.2 %collective-permute-start.2 = (bf16[64,10,1,128]{3,0,2,1:T(8,128)(2,1)}, bf16[64,10,1,128]{3,0,2,1:T(8,128)(2,1)}, u32[]{:S(2)}, u32[]{:S(2)}) collective-permute-start(bf16[64,10,1,128]{3,0,2,1:T(8,128)(2,1)} %get-tuple-element.23), channel_id=1, source_target_pairs={{0,1},{1,2},{2,3},{3,4},{4,5},{5,6},{6,7},{8,9},{9,10},{10,11},{11... | collective-permute-start | bytes 491528 | tf_op jit(solution)/shard_map/ppermute | solution.py:19
  31.4 1.3 collective-permute-start.3
  33.2 1.0 copy.29
  34.2 1.0 copy.39
  35.1 0.8 pad_maximum_fusion.10
  35.9 5.5 %collective-permute-start.6 = (bf16[64,10,1,128]{3,0,2,1:T(8,128)(2,1)S(1)}, bf16[64,10,1,128]{3,0,2,1:T(8,128)(2,1)S(1)}, u32[]{:S(2)}, u32[]{:S(2)}) collective-permute-start(bf16[64,10,1,128]{3,0,2,1:T(8,128)(2,1)S(1)} %get-tuple-element.21), channel_id=1, source_target_pairs={{0,1},{1,2},{2,3},{3,4},{4,5},{5,6},{6,7},{8,9},{9,10},{10,11},{11... | collective-permute-start | bytes 491528 | tf_op jit(solution)/shard_map/ppermute | solution.py:19
  41.4 1.5 collective-permute-start.7
  42.9 4.0 %fusion.15 = bf16[64,10,10,130]{3,0,2,1:T(8,128)(2,1)S(1)} fusion(bf16[64,10,1,128]{3,0,2,1:T(8,128)(2,1)} %collective-permute-done.3, bf16[64,10,1,128]{3,0,2,1:T(8,128)(2,1)} %collective-permute-done.2, bf16[64,1,8,128]{3,0,2,1:T(8,128)(2,1)} %copy-done.6, bf16[64,8,8,128]{3,0,2,1:T(8,128)(2,1)S(1)} %get-tuple-element.32, bf16[64,1,8,128]{3,0,2,1:T(8,128)(2,1)} %copy-done.4), kind=kLoop, calls=%fused_computation.24 | loop fusion | flops 14976000 | bytes 3302400 | tf_op jit(solution)/shard_map/concatenate | solution.py:17
  47.0 0.9 fusion.124
  47.9 4.9 %pad_maximum_fusion = bf16[192,10,10,128]{3,0,2,1:T(8,128)(2,1)S(1)} fusion(bf16[64,10,10,128]{3,0,2,1:T(8,128)(2,1)S(1)} %get-tuple-element.18, bf16[64,10,1,128]{3,0,2,1:T(8,128)(2,1)} %collective-permute-done.3, bf16[64,1,8,128]{3,0,2,1:T(8,128)(2,1)S(1)} %copy-done.7, bf16[64,8,8,128]{3,0,2,1:T(8,128)(2,1)S(1)} %get-tuple-element.32, ...), kind=kLoop, calls=%fused_computation.3 | loop fusion | flops 34406400 | bytes 9830400 | tf_op jit(solution)/shard_map/concatenate | solution.py:46
  53.6 0.7 fusion.82
  55.1 0.7 fusion.86
  56.5 0.7 fusion.90
  58.0 0.7 fusion.94
  58.8 3.9 %fusion.19 = bf16[64,10,10,130]{3,0,2,1:T(8,128)(2,1)S(1)} fusion(bf16[64,10,1,128]{3,0,2,1:T(8,128)(2,1)S(1)} %collective-permute-done.7, bf16[64,10,1,128]{3,0,2,1:T(8,128)(2,1)S(1)} %collective-permute-done.6, bf16[64,1,8,128]{3,0,2,1:T(8,128)(2,1)} %collective-permute-done.5, bf16[64,8,8,128]{3,0,2,1:T(8,128)(2,1)S(1)} %get-tuple-element.31, ...), kind=kLoop, calls=%fused_computation.28 | loop fusion | flops 14976000 | bytes 3302400 | tf_op jit(solution)/shard_map/concatenate | solution.py:17
  62.7 2.1 fusion.123
  64.8 1.7 fusion.106
  66.6 5.5 %pad_maximum_fusion.4 = (bf16[192,10,10,128]{3,0,2,1:T(8,128)(2,1)S(1)}, bf16[192,10,10,128]{3,0,2,1:T(8,128)(2,1)S(1)}) fusion(bf16[64,10,10,128]{3,0,2,1:T(8,128)(2,1)S(1)} %get-tuple-element.15, bf16[64,10,10,128]{3,0,2,1:T(8,128)(2,1)} %get-tuple-element.16, bf16[64,10,1,128]{3,0,2,1:T(8,128)(2,1)S(1)} %collective-permute-done.7, ...), kind=kLoop, calls=%fused_computation.7 | loop fusion | flops 46694400 | bytes 14745600 | tf_op jit(solution)/shard_map/concatenate | solution.py:54
  72.0 1.0 fusion.24
  73.0 1.0 fusion.26
  74.0 1.0 fusion.28
  74.9 1.0 fusion.30
  75.9 1.0 fusion.32
  76.9 1.0 fusion.34
  77.8 1.0 fusion.36
  78.8 1.0 fusion.38
  79.8 1.6 fusion.40
  82.1 0.7 fusion.64
  82.9 0.7 fusion.66
  83.6 0.7 fusion.68
  84.3 0.7 fusion.70
  85.1 0.7 fusion.72
  85.8 0.7 fusion.74
  86.6 2.1 fusion.76
  88.7 3.5 %fusion.98 = bf16[64,8,8,128]{3,0,2,1:T(8,128)(2,1)S(1)} fusion(f32[8,8,128,64]{2,3,1,0:T(8,128)S(1)} %get-tuple-element.34, f32[8,8,128,64]{2,3,1,0:T(8,128)S(1)} %fusion.62, f32[8,8,128,64]{2,3,1,0:T(8,128)S(1)} %fusion.64, f32[8,8,128,64]{2,3,1,0:T(8,128)S(1)} %fusion.66, f32[8,8,128,64]{2,3,1,0:T(8,128)S(1)} %fusion.68, ...), kind=kOutput, calls=%fused_computation.109 | convolution fusion | flops 210763776 | bytes 23118336 | tf_op jit(solution)/shard_map/co,cxyz->oxyz/dot_general | solution.py:66
  92.3 1.1 fusion.115
  93.4 4.5 %collective-permute-start.8 = (bf16[64,1,8,128]{3,0,2,1:T(8,128)(2,1)S(1)}, bf16[64,1,8,128]{3,0,2,1:T(8,128)(2,1)S(1)}, u32[]{:S(2)}, u32[]{:S(2)}) collective-permute-start(bf16[64,1,8,128]{3,0,2,1:T(8,128)(2,1)S(1)} %get-tuple-element.25), channel_id=1, source_target_pairs={{0,8},{8,16},{16,24},{24,32},{32,40},{40,48},{48,56},{56,64},{64,7... | collective-permute-start | bytes 393224 | tf_op jit(solution)/shard_map/ppermute | solution.py:19
  97.8 1.9 collective-permute-start.9
  99.8 1.1 fusion.114
  100.9 1.1 fusion.113
  102.0 1.1 fusion.112
  103.1 1.1 fusion.111
  104.2 1.1 fusion.110
  105.3 1.1 fusion.109
  106.4 1.1 fusion.108
  107.6 1.1 fusion.107
  108.8 5.8 %collective-permute-start.10 = (bf16[64,10,1,128]{3,0,2,1:T(8,128)(2,1)S(1)}, bf16[64,10,1,128]{3,0,2,1:T(8,128)(2,1)S(1)}, u32[]{:S(2)}, u32[]{:S(2)}) collective-permute-start(bf16[64,10,1,128]{3,0,2,1:T(8,128)(2,1)S(1)} %get-tuple-element.19), channel_id=1, source_target_pairs={{0,1},{1,2},{2,3},{3,4},{4,5},{5,6},{6,7},{8,9},{9,10},{10,11},{11... | collective-permute-start | bytes 491528 | tf_op jit(solution)/shard_map/ppermute | solution.py:19
  114.6 1.5 collective-permute-start.11
  116.2 1.2 copy.59
  117.4 1.2 copy.49
  118.7 3.5 %collective-permute-done.11 = bf16[64,10,1,128]{3,0,2,1:T(8,128)(2,1)S(1)} collective-permute-done((bf16[64,10,1,128]{3,0,2,1:T(8,128)(2,1)S(1)}, bf16[64,10,1,128]{3,0,2,1:T(8,128)(2,1)S(1)}, u32[]{:S(2)}, u32[]{:S(2)}) %collective-permute-start.11) | collective-permute-done | bytes 163872 | tf_op jit(solution)/shard_map/ppermute | solution.py:21
  122.2 3.1 %select_maximum_fusion = bf16[64,10,10,130]{3,0,2,1:T(8,128)(2,1)S(1)} fusion(bf16[64,10,1,128]{3,0,2,1:T(8,128)(2,1)S(1)} %collective-permute-done.11, bf16[64,10,1,128]{3,0,2,1:T(8,128)(2,1)S(1)} %collective-permute-done.10, bf16[64,1,8,128]{3,0,2,1:T(8,128)(2,1)S(1)} %collective-permute-done.9, bf16[64,8,8,128]{3,0,2,1:T(8,128)(2,1)S(1)} %fusion.98, ...), kind=kLoop, calls=%fused_computation.8 | loop fusion | flops 14976000 | bytes 3302400 | tf_op jit(solution)/shard_map/concatenate | solution.py:17
  125.3 0.9 fusion.122
  126.2 4.3 %pad_maximum_fusion.3 = bf16[192,10,10,128]{3,0,2,1:T(8,128)(2,1)S(1)} fusion(bf16[64,10,10,128]{3,0,2,1:T(8,128)(2,1)S(1)} %get-tuple-element.14, bf16[64,10,1,128]{3,0,2,1:T(8,128)(2,1)S(1)} %collective-permute-done.11, bf16[64,1,8,128]{3,0,2,1:T(8,128)(2,1)S(1)} %collective-permute-done.9, bf16[64,8,8,128]{3,0,2,1:T(8,128)(2,1)S(1)} %fusion.98, ...), kind=kLoop, calls=%fused_computation.6 | loop fusion | flops 34406400 | bytes 9830400 | tf_op jit(solution)/shard_map/concatenate | solution.py:46
  136.9 2.2 fusion.97
  139.2 1.6 copy.60
  140.8 135.3 %all-reduce.6.cloned.1.call-done = (f32[3,3,3,64,64]{4,3,2,1,0:T(8,128)}, f32[3,3,3,64,64]{4,3,2,1,0:T(8,128)}) async-done(((f32[3,3,3,64,64]{4,3,2,1,0:T(8,128)}, f32[3,3,3,64,64]{4,3,2,1,0:T(8,128)}), (f32[3,3,3,64,64]{4,3,2,1,0:T(8,128)}, f32[3,3,3,64,64]{4,3,2,1,0:T(8,128)})) %all-reduce.6.cloned.1.call-update) | async-done | bytes 884752 | tf_op jit(solution)/shard_map/psum | solution.py:126
  276.1 2.9 %broadcast_multiply_fusion = (f32[3,3,3,64,64]{4,3,2,1,0:T(8,128)}, f32[3,3,3,64,64]{4,3,2,1,0:T(8,128)}) fusion(f32[3,3,3,64,64]{4,3,2,1,0:T(8,128)} %get-tuple-element.10, f32[3,3,3,64,64]{4,3,2,1,0:T(8,128)} %get-tuple-element.9), kind=kLoop, calls=%fused_computation.142 | loop fusion | flops 221184 | bytes 1769472 | tf_op jit(solution)/shard_map/mul | solution.py:127
  (71 shorter events, 12.6 us)
Async XLA Ops:
  7.2 17.2 %copy-start.8 = (bf16[3,3,3,64,64]{4,3,2,1,0:T(8,128)(2,1)S(1)}, bf16[3,3,3,64,64]{4,3,2,1,0:T(8,128)(2,1)}, u32[]{:S(2)}) copy-start(bf16[3,3,3,64,64]{4,3,2,1,0:T(8,128)(2,1)} %param.9) | copy-start | bytes 663556
  7.2 268.9 %all-reduce.6.cloned.1.call-start = ((), (), s32[]{:S(2)}) async-start(), calls=%async_computation | async-start | bytes 3538944 | tf_op jit(solution)/shard_map/psum | solution.py:126
  8.1 10.5 %copy-start.11 = (bf16[128]{0:T(256)(128)(2,1)}, bf16[128]{0:T(256)(128)(2,1)S(1)}, u32[]{:S(2)}) copy-start(bf16[128]{0:T(256)(128)(2,1)S(1)} %convert_element_type.40) | copy-start | bytes 772
  8.1 24.5 %copy-start.1 = (bf16[3,3,3,64,64]{4,3,2,1,0:T(8,128)(2,1)S(1)}, bf16[3,3,3,64,64]{4,3,2,1,0:T(8,128)(2,1)}, u32[]{:S(2)}) copy-start(bf16[3,3,3,64,64]{4,3,2,1,0:T(8,128)(2,1)} %param.8) | copy-start | bytes 663556
  11.5 12.9 %collective-permute-start = (bf16[64,1,8,128]{3,0,2,1:T(8,128)(2,1)S(1)}, bf16[64,1,8,128]{3,0,2,1:T(8,128)(2,1)S(1)}, u32[]{:S(2)}, u32[]{:S(2)}) collective-permute-start(bf16[64,1,8,128]{3,0,2,1:T(8,128)(2,1)S(1)} %get-tuple-element.29), channel_id=1, source_target_pairs={{0,8},{8,16},{16,24},{24,32},{32,40},{40,48},{48,56},{56,64},{64,7... | collective-permute-start | bytes 393224 | tf_op jit(solution)/shard_map/ppermute | solution.py:19
  16.0 8.4 %collective-permute-start.1 = (bf16[64,1,8,128]{3,0,2,1:T(8,128)(2,1)S(1)}, bf16[64,1,8,128]{3,0,2,1:T(8,128)(2,1)S(1)}, u32[]{:S(2)}, u32[]{:S(2)}) collective-permute-start(bf16[64,1,8,128]{3,0,2,1:T(8,128)(2,1)S(1)} %get-tuple-element.30), channel_id=1, source_target_pairs={{8,0},{16,8},{24,16},{32,24},{40,32},{48,40},{56,48},{64,56},{72,6... | collective-permute-start | bytes 393224 | tf_op jit(solution)/shard_map/ppermute | solution.py:21
  18.6 14.1 %copy-start.12 = (bf16[128]{0:T(256)(128)(2,1)S(1)}, bf16[128]{0:T(256)(128)(2,1)}, u32[]{:S(2)}) copy-start(bf16[128]{0:T(256)(128)(2,1)} %copy-done.11) | copy-start | bytes 772
  18.6 16.5 %collective-permute-start.4 = (bf16[64,1,8,128]{3,0,2,1:T(8,128)(2,1)}, bf16[64,1,8,128]{3,0,2,1:T(8,128)(2,1)S(1)}, u32[]{:S(2)}, u32[]{:S(2)}) collective-permute-start(bf16[64,1,8,128]{3,0,2,1:T(8,128)(2,1)} %get-tuple-element.27), channel_id=1, source_target_pairs={{0,8},{8,16},{16,24},{24,32},{32,40},{40,48},{48,56},{56,64},{64,7... | collective-permute-start | bytes 393224 | tf_op jit(solution)/shard_map/ppermute | solution.py:19
  22.4 12.7 %collective-permute-start.5 = (bf16[64,1,8,128]{3,0,2,1:T(8,128)(2,1)}, bf16[64,1,8,128]{3,0,2,1:T(8,128)(2,1)}, u32[]{:S(2)}, u32[]{:S(2)}) collective-permute-start(bf16[64,1,8,128]{3,0,2,1:T(8,128)(2,1)} %get-tuple-element.28), channel_id=1, source_target_pairs={{8,0},{16,8},{24,16},{32,24},{40,32},{48,40},{56,48},{64,56},{72,6... | collective-permute-start | bytes 393224 | tf_op jit(solution)/shard_map/ppermute | solution.py:21
  24.4 7.0 %copy-start.4 = (bf16[64,1,8,128]{3,0,2,1:T(8,128)(2,1)}, bf16[64,1,8,128]{3,0,2,1:T(8,128)(2,1)S(1)}, u32[]{:S(2)}) copy-start(bf16[64,1,8,128]{3,0,2,1:T(8,128)(2,1)S(1)} %collective-permute-done) | copy-start | bytes 393220
  24.4 8.2 %copy-start.6 = (bf16[64,1,8,128]{3,0,2,1:T(8,128)(2,1)}, bf16[64,1,8,128]{3,0,2,1:T(8,128)(2,1)S(1)}, u32[]{:S(2)}) copy-start(bf16[64,1,8,128]{3,0,2,1:T(8,128)(2,1)S(1)} %collective-permute-done.1) | copy-start | bytes 393220
  25.2 17.7 %collective-permute-start.2 = (bf16[64,10,1,128]{3,0,2,1:T(8,128)(2,1)}, bf16[64,10,1,128]{3,0,2,1:T(8,128)(2,1)}, u32[]{:S(2)}, u32[]{:S(2)}) collective-permute-start(bf16[64,10,1,128]{3,0,2,1:T(8,128)(2,1)} %get-tuple-element.23), channel_id=1, source_target_pairs={{0,1},{1,2},{2,3},{3,4},{4,5},{5,6},{6,7},{8,9},{9,10},{10,11},{11... | collective-permute-start | bytes 491528 | tf_op jit(solution)/shard_map/ppermute | solution.py:19
  31.4 11.6 %collective-permute-start.3 = (bf16[64,10,1,128]{3,0,2,1:T(8,128)(2,1)}, bf16[64,10,1,128]{3,0,2,1:T(8,128)(2,1)}, u32[]{:S(2)}, u32[]{:S(2)}) collective-permute-start(bf16[64,10,1,128]{3,0,2,1:T(8,128)(2,1)} %get-tuple-element.24), channel_id=1, source_target_pairs={{1,0},{2,1},{3,2},{4,3},{5,4},{6,5},{7,6},{9,8},{10,9},{11,10},{12... | collective-permute-start | bytes 491528 | tf_op jit(solution)/shard_map/ppermute | solution.py:21
  35.9 22.8 %collective-permute-start.6 = (bf16[64,10,1,128]{3,0,2,1:T(8,128)(2,1)S(1)}, bf16[64,10,1,128]{3,0,2,1:T(8,128)(2,1)S(1)}, u32[]{:S(2)}, u32[]{:S(2)}) collective-permute-start(bf16[64,10,1,128]{3,0,2,1:T(8,128)(2,1)S(1)} %get-tuple-element.21), channel_id=1, source_target_pairs={{0,1},{1,2},{2,3},{3,4},{4,5},{5,6},{6,7},{8,9},{9,10},{10,11},{11... | collective-permute-start | bytes 491528 | tf_op jit(solution)/shard_map/ppermute | solution.py:19
  41.4 17.3 %collective-permute-start.7 = (bf16[64,10,1,128]{3,0,2,1:T(8,128)(2,1)S(1)}, bf16[64,10,1,128]{3,0,2,1:T(8,128)(2,1)S(1)}, u32[]{:S(2)}, u32[]{:S(2)}) collective-permute-start(bf16[64,10,1,128]{3,0,2,1:T(8,128)(2,1)S(1)} %get-tuple-element.22), channel_id=1, source_target_pairs={{1,0},{2,1},{3,2},{4,3},{5,4},{6,5},{7,6},{9,8},{10,9},{11,10},{12... | collective-permute-start | bytes 491528 | tf_op jit(solution)/shard_map/ppermute | solution.py:21
  46.9 0.9 copy-start.5
  47.0 1.0 copy-start.7
  62.7 2.1 copy-start.10
  79.8 1.6 copy-start.3
  92.2 1.2 copy-start.9
  93.4 15.4 %collective-permute-start.8 = (bf16[64,1,8,128]{3,0,2,1:T(8,128)(2,1)S(1)}, bf16[64,1,8,128]{3,0,2,1:T(8,128)(2,1)S(1)}, u32[]{:S(2)}, u32[]{:S(2)}) collective-permute-start(bf16[64,1,8,128]{3,0,2,1:T(8,128)(2,1)S(1)} %get-tuple-element.25), channel_id=1, source_target_pairs={{0,8},{8,16},{16,24},{24,32},{32,40},{40,48},{48,56},{56,64},{64,7... | collective-permute-start | bytes 393224 | tf_op jit(solution)/shard_map/ppermute | solution.py:19
  97.8 10.9 %collective-permute-start.9 = (bf16[64,1,8,128]{3,0,2,1:T(8,128)(2,1)S(1)}, bf16[64,1,8,128]{3,0,2,1:T(8,128)(2,1)S(1)}, u32[]{:S(2)}, u32[]{:S(2)}) collective-permute-start(bf16[64,1,8,128]{3,0,2,1:T(8,128)(2,1)S(1)} %get-tuple-element.26), channel_id=1, source_target_pairs={{8,0},{16,8},{24,16},{32,24},{40,32},{48,40},{56,48},{64,56},{72,6... | collective-permute-start | bytes 393224 | tf_op jit(solution)/shard_map/ppermute | solution.py:21
  108.8 9.8 %collective-permute-start.10 = (bf16[64,10,1,128]{3,0,2,1:T(8,128)(2,1)S(1)}, bf16[64,10,1,128]{3,0,2,1:T(8,128)(2,1)S(1)}, u32[]{:S(2)}, u32[]{:S(2)}) collective-permute-start(bf16[64,10,1,128]{3,0,2,1:T(8,128)(2,1)S(1)} %get-tuple-element.19), channel_id=1, source_target_pairs={{0,1},{1,2},{2,3},{3,4},{4,5},{5,6},{6,7},{8,9},{9,10},{10,11},{11... | collective-permute-start | bytes 491528 | tf_op jit(solution)/shard_map/ppermute | solution.py:19
  114.6 7.6 %collective-permute-start.11 = (bf16[64,10,1,128]{3,0,2,1:T(8,128)(2,1)S(1)}, bf16[64,10,1,128]{3,0,2,1:T(8,128)(2,1)S(1)}, u32[]{:S(2)}, u32[]{:S(2)}) collective-permute-start(bf16[64,10,1,128]{3,0,2,1:T(8,128)(2,1)S(1)} %get-tuple-element.20), channel_id=1, source_target_pairs={{1,0},{2,1},{3,2},{4,3},{5,4},{6,5},{7,6},{9,8},{10,9},{11,10},{12... | collective-permute-start | bytes 491528 | tf_op jit(solution)/shard_map/ppermute | solution.py:21
  126.2 4.4 %copy-start.2 = (bf16[3,3,3,64,64]{4,3,2,1,0:T(8,128)(2,1)S(1)}, bf16[3,3,3,64,64]{4,3,2,1,0:T(8,128)(2,1)}, u32[]{:S(2)}) copy-start(bf16[3,3,3,64,64]{4,3,2,1,0:T(8,128)(2,1)} %copy.39) | copy-start | bytes 663556
  135.7 1.2 copy-start
Sparse Core Ops, SparseCore 0:
  118.8 157.2 all-reduce.5
where the time goes:
time: 290 us; the launch traced here: 286 us
  waiting for transfers between devices  139 us (48%)
  matrix products  45.8 us (16%)
  starting transfers between devices  40.2 us (14%)
  other arithmetic  34.7 us (12%)
  between operations  15.1 us (5%)
  local copies, waits for them, and re-layouts  11.6 us (4%)
    psum x1, waiting for transfers between devices, shards(): summed_one, summed_two = lax.psum((partial_one, summed_two), ('gx', 'gy'))  135 us
    ppermute x6, starting transfers between devices, padded_2(): lax.ppermute(tail, axis, [(i, (i + 1) % count) for i in range(ends)])  30.2 us
    dot_general x27, matrix products, conv_pad(): jnp.einsum('co,cxyz->oxyz', folded[row_off, col_off], window, preferred_e...  26.6 us
    concatenate x3, other arithmetic, padded_2(): jnp.concatenate([lax.ppermute(tail, axis, [(i, (i + 1) % count) for i in...  11 us
    ppermute x6, starting transfers between devices, padded_2(): lax.ppermute(head, axis, [((i + 1) % count, i) for i in range(ends)])  10.1 us
    dot_general x9, matrix products, grad_forward(): jnp.einsum('cxyz,oxyz->co', window, grad, preferred_element_type=jnp.floa...  10 us
    dot_general x9, matrix products, grad_backward(): jnp.einsum('cxyz,kxyz->ck', activ, window, preferred_element_type=jnp.flo...  9.26 us
    concatenate x2, other arithmetic, stack_depth(): jnp.concatenate([padded[..., 0:depth], padded[..., 1:depth + 1], padded[....  9.24 us
  transfers between devices with their start and end apart: 13, of which 2 were waited for; matrix products, arithmetic and copies ran while one was open for 17% of the time, Pallas kernels for 0%

commit v1 on v0

v1 whole, which is shorter than its diff:
```python
import math

import jax
import jax.numpy as jnp
from jax import lax
from jax.experimental import pallas as pl
from jax.experimental.pallas import tpu as pltpu
from jax.sharding import PartitionSpec as P

F32 = jnp.float32
BF16 = jnp.bfloat16
AXES = ("gx", "gy")
PAIRS = 4


def shift_perm(count, step):
    return [(i, i + step) for i in range(count) if 0 <= i + step < count]


def xor_permute(value, mask):
    total = lax.axis_size("gx") * lax.axis_size("gy")
    return lax.ppermute(value, AXES, [(i, i ^ mask) for i in range(total)])


def stack_row(stack, at_x, first_y, row):
    count, chans, depth = row.shape
    lane = lax.broadcasted_iota(jnp.int32, row.shape, 2)
    zero = jnp.zeros_like(row)
    below = jnp.where(lane == 0, zero, pltpu.roll(row, 1, 2))
    above = jnp.where(lane == depth - 1, zero, pltpu.roll(row, depth - 1, 2))
    ys = pl.ds(first_y, count)
    stack[at_x, ys, 0:chans, :] = below
    stack[at_x, ys, chans : 2 * chans, :] = row
    stack[at_x, ys, 2 * chans : 3 * chans, :] = above


def stack_padded(stack, tile, x_lo, x_hi, y_lo, y_hi, c_lo, c_hi):
    size_x, size_y = tile.shape[0], tile.shape[1]
    stack_row(stack, 0, 1, x_lo[...])
    stack_row(stack, size_x + 1, 1, x_hi[...])
    for edge in range(2):
        at_x = edge * (size_x + 1)
        stack_row(stack, at_x, 0, c_lo[pl.ds(edge, 1)])
        stack_row(stack, at_x, size_y + 1, c_hi[pl.ds(edge, 1)])

    def body(i, carry):
        stack_row(stack, i + 1, 1, tile[i])
        stack_row(stack, i + 1, 0, y_lo[pl.ds(i, 1)])
        stack_row(stack, i + 1, size_y + 1, y_hi[pl.ds(i, 1)])
        return carry

    lax.fori_loop(0, size_x, body, 0)


def conv_stack(stack, weights, acc):
    wide, tall, deep, depth = stack.shape
    chans = deep // 3
    acc[0:2] = jnp.zeros((2,) + acc.shape[1:], F32)

    def body(i, carry):
        for pair in range((tall - 2) // 2):
            y = 2 * pair
            left = stack[i, y : y + 3].reshape(3 * deep, depth)
            right = stack[i, y + 1 : y + 4].reshape(3 * deep, depth)
            both = jnp.concatenate([left, right], axis=1)
            out = jnp.dot(weights[...], both, preferred_element_type=F32)
            for side in range(2):
                part = out[:, side * depth : (side + 1) * depth]
                acc[i + 2, y + side] = part[0:chans]
                acc[i + 1, y + side] += part[chans : 2 * chans]
                acc[i, y + side] += part[2 * chans : 3 * chans]
        return carry

    lax.fori_loop(0, wide, body, 0)


def forward_kernel(mask, weights, tile, x_lo, x_hi, y_lo, y_hi, c_lo, c_hi, activ, slope, padded, stack, acc):
    stack_padded(stack, tile, x_lo, x_hi, y_lo, y_hi, c_lo, c_hi)
    chans = tile.shape[2]
    padded[...] = stack[:, :, chans : 2 * chans, :]
    conv_stack(stack, weights, acc)

    def body(i, carry):
        value = acc[i + 2]
        sig = jax.nn.sigmoid(value)
        activ[i] = (mask[...] * (value * sig)).astype(BF16)
        slope[i] = mask[...] * (sig * (1.0 + value * (1.0 - sig)))
        return carry

    lax.fori_loop(0, tile.shape[0], body, 0)


def backward_kernel(
    weights, slope, tile, x_lo, x_hi, y_lo, y_hi, c_lo, c_hi, pre_grad, p_ylo, p_yhi, padded, stack, acc
):
    stack_padded(stack, tile, x_lo, x_hi, y_lo, y_hi, c_lo, c_hi)
    size_x, size_y, chans = tile.shape[0:3]
    padded[...] = stack[:, :, chans : 2 * chans, :]
    conv_stack(stack, weights, acc)

    def body(i, carry):
        value = (slope[i] * acc[i + 2]).astype(BF16)
        pre_grad[i] = value
        p_ylo[i] = value[0]
        p_yhi[i] = value[size_y - 1]
        return carry

    lax.fori_loop(0, size_x, body, 0)


def branch_kernel(mask, weights, base, tile, x_lo, x_hi, y_lo, y_hi, c_lo, c_hi, result, stack, acc):
    stack_padded(stack, tile, x_lo, x_hi, y_lo, y_hi, c_lo, c_hi)
    conv_stack(stack, weights, acc)

    def body(i, carry):
        result[i] = (base[i].astype(F32) + mask[...] * acc[i + 2]).astype(BF16)
        return carry

    lax.fori_loop(0, tile.shape[0], body, 0)


def grad_accumulate(padded, stack, acc, turned):
    size_x, size_y, deep, depth = stack.shape
    chans = deep // 3
    acc[...] = jnp.zeros_like(acc)

    def body(i, carry):
        right = jnp.concatenate([stack[i, y] for y in range(size_y)], axis=1)
        left = []
        for a in range(3):
            rows = [padded[i + a, y] for y in range(size_y + 2)]
            for b in range(3):
                left.append(jnp.concatenate(rows[b : b + size_y], axis=1))
        left = jnp.concatenate(left, axis=0)
        acc[...] += lax.dot_general(left, right, (((1,), (1,)), ((), ())), preferred_element_type=F32)
        return carry

    lax.fori_loop(0, size_x, body, 0)


def pack_grad(dest, acc, chans):
    rows = acc.shape[0]
    half = rows // 2
    dest[0:rows] = acc[:, 0 : 2 * chans]
    low = acc[0:half, 2 * chans : 3 * chans]
    high = acc[half:rows, 2 * chans : 3 * chans]
    dest[rows : rows + half] = jnp.concatenate([low, high], axis=1)


def grads_kernel(core, in_pad, pre_grad, grad_pad, activ, keep, send, stack, acc_one, acc_two):
    size_x, size_y, chans = activ.shape[0:3]

    def stack_all(source):
        def body(i, carry):
            stack_row(stack, i, 0, source[i])
            return carry

        lax.fori_loop(0, size_x, body, 0)

    stack_all(activ)
    grad_accumulate(grad_pad, stack, acc_two, True)
    stack_all(pre_grad)
    grad_accumulate(in_pad, stack, acc_one, False)

    @pl.when(core[0] == 0)
    def _():
        pack_grad(keep, acc_one, chans)
        pack_grad(send, acc_two, chans)

    @pl.when(core[0] != 0)
    def _():
        pack_grad(keep, acc_two, chans)
        pack_grad(send, acc_one, chans)


def split_kernel(spot, keep, recv, *outs):
    rows = outs[0].shape[0]
    for dist, out in enumerate(outs):
        start = pl.multiple_of((spot[0] ^ dist) * rows, 8)
        out[...] = keep[pl.ds(start, rows)] + recv[pl.ds(start, rows)]


def join_kernel(spot, *refs):
    out = refs[-1]
    rows = refs[0].shape[0]
    for dist, part in enumerate(refs[:-1]):
        start = pl.multiple_of((spot[0] ^ dist) * rows, 8)
        out[pl.ds(start, rows)] = part[...]


def unpack_kernel(core, scale, own, other, grad_one, grad_two):
    chans = grad_one.shape[-1]
    rows = 9 * chans
    half = rows // 2

    def block(source, a, b, j):
        start = (3 * a + b) * chans
        if j < 2:
            return source[start : start + chans, j * chans : (j + 1) * chans]
        pieces = []
        step = chans // 2
        for first in (start, start + step):
            if first < half:
                pieces.append(source[rows + first : rows + first + step, 0:chans])
            else:
                pieces.append(source[rows + first - half : rows + first - half + step, chans : 2 * chans])
        return jnp.concatenate(pieces, axis=0)

    def write(one, two):
        for a in range(3):
            for b in range(3):
                for j in range(3):
                    grad_one[a, b, 2 - j] = block(one, a, b, j) * scale
                    grad_two[2 - a, 2 - b, j] = block(two, a, b, j).T * scale

    @pl.when(core[0] == 0)
    def _():
        write(own, other)

    @pl.when(core[0] != 0)
    def _():
        write(other, own)


def call(kernel, outs, scratch=(), scalars=0, flops=0, name=None):
    def run(*operands):
        specs = [pl.BlockSpec(memory_space=pltpu.SMEM)] * scalars
        specs += [pl.BlockSpec(memory_space=pltpu.VMEM)] * (len(operands) - scalars)
        moved = sum(o.size * o.dtype.itemsize for o in operands)
        moved += sum(math.prod(o.shape) * o.dtype.itemsize for o in outs)
        return pl.pallas_call(
            kernel,
            out_shape=tuple(outs),
            in_specs=specs,
            out_specs=tuple(pl.BlockSpec(memory_space=pltpu.VMEM) for _ in outs),
            scratch_shapes=list(scratch),
            cost_estimate=pl.CostEstimate(flops=flops, bytes_accessed=moved, transcendentals=0),
            compiler_params=pltpu.CompilerParams(vmem_limit_bytes=40 * 1024 * 1024),
            name=name,
        )(*operands)

    return run


def halo(x_lo, x_hi, y_lo, y_hi):
    nx, ny = lax.axis_size("gx"), lax.axis_size("gy")
    got_ylo = lax.ppermute(y_hi, "gy", shift_perm(ny, 1))
    got_yhi = lax.ppermute(y_lo, "gy", shift_perm(ny, -1))
    got_xlo = lax.ppermute(x_hi, "gx", shift_perm(nx, 1))
    got_xhi = lax.ppermute(x_lo, "gx", shift_perm(nx, -1))
    first = jnp.stack([got_xlo[0], got_xhi[0]])
    last = jnp.stack([got_xlo[-1], got_xhi[-1]])
    got_clo = lax.ppermute(last, "gy", shift_perm(ny, 1))
    got_chi = lax.ppermute(first, "gy", shift_perm(ny, -1))
    return got_xlo, got_xhi, got_ylo, got_yhi, got_clo, got_chi


def shards(features, cotangent, block_mask, kernel_one, kernel_two):
    chans, tile_x, tile_y, tile_z = features.shape
    blocks = block_mask.shape[2]
    cells_all = tile_x * tile_y * tile_z * lax.axis_size("gx") * lax.axis_size("gy")
    scale = 1.0 / math.sqrt(cells_all)
    place_x, place_y = lax.axis_index("gx"), lax.axis_index("gy")
    core = (place_x & 1).astype(jnp.int32).reshape(1)
    spot = ((place_x >> 1) & 3).astype(jnp.int32).reshape(1)

    mask = jnp.broadcast_to(block_mask.reshape(blocks, 1), (blocks, tile_z // blocks)).reshape(1, tile_z)
    mask_f = mask.astype(F32)
    mask_b = mask.astype(BF16).reshape(1, 1, 1, tile_z)
    masked_in = jnp.transpose(features * mask_b, (1, 2, 0, 3))
    masked_grad = jnp.transpose(cotangent * mask_b, (1, 2, 0, 3))

    def edges(tile):
        return tile[0], tile[-1], tile[:, 0], tile[:, -1]

    in_halo = halo(*edges(masked_in))
    grad_halo = halo(*edges(masked_grad))

    w_pre = jnp.transpose(kernel_one, (0, 4, 1, 2, 3)).reshape(3 * chans, 9 * chans)
    flat = lambda w: jnp.transpose(w[::-1, ::-1, ::-1], (0, 3, 1, 2, 4)).reshape(3 * chans, 9 * chans)
    w_act = flat(kernel_two)
    w_branch = flat(kernel_one)

    tile_shape = (tile_x, tile_y, chans, tile_z)
    pad_shape = (tile_x + 2, tile_y + 2, chans, tile_z)
    scratch = [
        pltpu.VMEM((tile_x + 2, tile_y + 2, 3 * chans, tile_z), BF16),
        pltpu.VMEM((tile_x + 4, tile_y, chans, tile_z), F32),
    ]
    tile_b = jax.ShapeDtypeStruct(tile_shape, BF16)
    edge_b = jax.ShapeDtypeStruct((tile_x, chans, tile_z), BF16)
    pad_b = jax.ShapeDtypeStruct(pad_shape, BF16)
    flops = 2 * 27 * chans * chans * tile_x * tile_y * tile_z

    activ, slope, in_pad = call(
        forward_kernel,
        [tile_b, jax.ShapeDtypeStruct(tile_shape, F32), pad_b],
        scratch,
        flops=flops,
        name="pre_act",
    )(mask_f, w_pre, masked_in, *in_halo)
    pre_grad, p_ylo, p_yhi, grad_pad = call(
        backward_kernel, [tile_b, edge_b, edge_b, pad_b], scratch, flops=flops, name="act_grad"
    )(w_act, slope, masked_grad, *grad_halo)
    pre_halo = halo(pre_grad[0], pre_grad[-1], p_ylo, p_yhi)

    packed = 27 * chans * chans // (2 * chans)
    half = jax.ShapeDtypeStruct((packed, 2 * chans), F32)
    keep, send = call(
        grads_kernel,
        [half, half],
        [
            pltpu.VMEM((tile_x, tile_y, 3 * chans, tile_z), BF16),
            pltpu.VMEM((9 * chans, 3 * chans), F32),
            pltpu.VMEM((9 * chans, 3 * chans), F32),
        ],
        scalars=1,
        flops=2 * flops,
        name="grads",
    )(core, in_pad, pre_grad, grad_pad, activ)

    recv = xor_permute(send, 8)
    chunk = jax.ShapeDtypeStruct((packed // 4, 2 * chans), F32)
    parts = call(split_kernel, [chunk] * 4, scalars=1, name="split")(spot, keep, recv)
    parts = [parts[0]] + [xor_permute(parts[d], 16 * d) for d in range(1, 4)]
    part = (parts[0] + parts[1]) + (parts[2] + parts[3])
    for masks in ((2, 4, 6), (1, 64, 65)):
        near, mid, far = [xor_permute(part, m) for m in masks]
        part = (part + near) + (mid + far)
    pieces = [part] + [xor_permute(part, 16 * d) for d in range(1, 4)]
    (own,) = call(join_kernel, [half], scalars=1, name="join")(spot, *pieces)
    other = xor_permute(own, 8)
    grad_shape = jax.ShapeDtypeStruct((3, 3, 3, chans, chans), F32)

    def unpack(core_ref, own_ref, other_ref, one_ref, two_ref):
        unpack_kernel(core_ref, scale, own_ref, other_ref, one_ref, two_ref)

    grad_one, grad_two = call(unpack, [grad_shape, grad_shape], scalars=1, name="unpack")(core, own, other)

    (branch,) = call(branch_kernel, [tile_b], scratch, flops=flops, name="branch")(
        mask_f, w_branch, masked_grad, pre_grad, *pre_halo
    )
    grad_features = jnp.transpose(branch, (2, 0, 1, 3))
    return grad_features, grad_one, grad_two


def solution(mesh):
    placed = (P(None, "gx", "gy", None), P(None, "gx", "gy", None), P("gx", "gy", None), P(), P())
    return jax.shard_map(
        shards,
        mesh=mesh,
        in_specs=placed,
        out_specs=(P(None, "gx", "gy", None), P(), P()),
        check_vma=False,
    )
```

time: 290 us -> 159 us (0.55)
  waiting for transfers between devices: 139 us -> 17.6 us
  matrix products: 45.8 us -> 0 us
  starting transfers between devices: 40.2 us -> 84.8 us
  Pallas kernels: 0 us -> 35.3 us
  other arithmetic: 34.7 us -> 5.33 us
  between operations: 15.1 us -> 1.11 us
    psum x1 -> x0, waiting for transfers between devices: 135 us -> none  [shards(): summed_one, summed_two = lax.psum((partial_one, summed_two), ('gx', 'gy'))]
    dot_general x45 -> x0, matrix products: 45.8 us -> none  [the longest x27 26.6 us: conv_pad(): jnp.einsum('co,cxyz->oxyz', folded[row_off, col_off], window, preferred_e...]
    ppermute x12 -> x32, starting transfers between devices: 40.2 us -> 84.8 us  [the longest x14 29.4 us: xor_permute(): return lax.ppermute(value, AXES, [(i, i ^ mask) for i in range(total)])]
    pallas_call x0 -> x7, Pallas kernels: none -> 35.3 us  [run(): pl.pallas_call(kernel, out_shape=tuple(outs), in_specs=specs, out_specs=t...]
    concatenate x6 -> x0, other arithmetic: 25.7 us -> none  [the longest x3 11 us: padded_2(): jnp.concatenate([lax.ppermute(tail, axis, [(i, (i + 1) % count) for i in...]
    ppermute x12 -> x32, waiting for transfers between devices: 3.54 us -> 17.6 us  [the longest x14 17.5 us: xor_permute(): return lax.ppermute(value, AXES, [(i, i ^ mask) for i in range(total)])]
    mul x2 -> x0, other arithmetic: 6.2 us -> none  [the longest x1 3.33 us: shards(): masked_grad = cotangent * cell]
    slice x6, local copies, waits for them, and re-layouts: 4.68 us -> 0.03 us  [halo(): first = jnp.stack([got_xlo[0], got_xhi[0]])]
  transfers between devices with their start and end apart: 13 -> 32, of which waited for: 2 -> 7; matrix products, arithmetic and copies ran while one was open for 17% -> 8% of each run, Pallas kernels for 0% -> 10%
where the time goes in v1:
time: 159 us; the launch traced here: 157 us
  starting transfers between devices  84.8 us (53%)
  Pallas kernels  35.3 us (22%)
  waiting for transfers between devices  17.6 us (11%)
  local copies, waits for them, and re-layouts  12.7 us (8%)
  other arithmetic  5.33 us (3%)
    pallas_call x7, Pallas kernels, run(): pl.pallas_call(kernel, out_shape=tuple(outs), in_specs=specs, out_specs=t...  35.3 us
    ppermute x14, starting transfers between devices, xor_permute(): return lax.ppermute(value, AXES, [(i, i ^ mask) for i in range(total)])  29.4 us
    ppermute x14, waiting for transfers between devices, xor_permute(): return lax.ppermute(value, AXES, [(i, i ^ mask) for i in range(total)])  17.5 us
    ppermute x3, starting transfers between devices, halo(): got_ylo = lax.ppermute(y_hi, 'gy', shift_perm(ny, 1))  15.6 us
    ppermute x3, starting transfers between devices, halo(): got_clo = lax.ppermute(last, 'gy', shift_perm(ny, 1))  15.4 us
    ppermute x3, starting transfers between devices, halo(): got_xlo = lax.ppermute(x_hi, 'gx', shift_perm(nx, 1))  10.3 us
    ppermute x3, starting transfers between devices, halo(): got_xhi = lax.ppermute(x_lo, 'gx', shift_perm(nx, -1))  6.32 us
    ppermute x3, starting transfers between devices, halo(): got_yhi = lax.ppermute(y_lo, 'gy', shift_perm(ny, -1))  3.86 us
  transfers between devices with their start and end apart: 32, of which 7 were waited for; matrix products, arithmetic and copies ran while one was open for 8% of the time, Pallas kernels for 10%

profile of v1, /device:TPU:1, one launch (start us, length us, event | category | flops | bytes accessed | tf_op | source)
XLA Modules:
  0.0 156.8 jit_solution(10234669830580738007)
XLA Ops:
  0.6 0.7 convert_bitcast_fusion
  1.4 0.1 broadcast_in_dim.8
  1.4 0.1 convert_element_type.28
  1.5 3.3 %fusion = (bf16[8,8,64,128]{3,2,1,0:T(8,128)(2,1)S(1)}, bf16[8,8,64,128]{3,2,1,0:T(8,128)(2,1)S(1)}) fusion(bf16[64,8,8,128]{3,2,1,0:T(8,128)(2,1)} %param.5, bf16[128]{0:T(256)(128)(2,1)S(1)} %convert_element_type.28, bf16[64,8,8,128]{3,2,1,0:T(8,128)(2,1)} %param.6), kind=kLoop, calls=%fused_computation.1 | loop fusion | flops 1048576 | bytes 4194560 | tf_op jit(solution)/shard_map/transpose | solution.py:270
  4.8 0.0 copy-start
  4.8 0.7 slice_bitcast_fusion.6
  5.5 4.5 %collective-permute-start = (bf16[8,64,128]{2,1,0:T(8,128)(2,1)}, bf16[8,64,128]{2,1,0:T(8,128)(2,1)S(1)}, u32[]{:S(2)}, u32[]{:S(2)}) collective-permute-start(bf16[8,64,128]{2,1,0:T(8,128)(2,1)} %get-tuple-element.48), channel_id=1, source_target_pairs={{0,8},{8,16},{16,24},{24,32},{32,40},{40,48},{48,56},{56,64},{64,7... | collective-permute-start | bytes 393224 | tf_op jit(solution)/shard_map/ppermute | solution.py:249
  10.0 1.9 %collective-permute-start.1 = (bf16[8,64,128]{2,1,0:T(8,128)(2,1)}, bf16[8,64,128]{2,1,0:T(8,128)(2,1)S(1)}, u32[]{:S(2)}, u32[]{:S(2)}) collective-permute-start(bf16[8,64,128]{2,1,0:T(8,128)(2,1)} %get-tuple-element.47), channel_id=1, source_target_pairs={{8,0},{16,8},{24,16},{32,24},{40,32},{48,40},{56,48},{64,56},{72,6... | collective-permute-start | bytes 393224 | tf_op jit(solution)/shard_map/ppermute | solution.py:250
  12.0 5.5 %collective-permute-start.2 = (bf16[8,64,128]{2,1,0:T(8,128)(2,1)S(1)}, bf16[8,64,128]{2,1,0:T(8,128)(2,1)S(1)}, u32[]{:S(2)}, u32[]{:S(2)}) collective-permute-start(bf16[8,64,128]{2,1,0:T(8,128)(2,1)S(1)} %get-tuple-element.46), channel_id=1, source_target_pairs={{0,1},{1,2},{2,3},{3,4},{4,5},{5,6},{6,7},{8,9},{9,10},{10,11},{11... | collective-permute-start | bytes 393224 | tf_op jit(solution)/shard_map/ppermute | solution.py:247
  17.5 1.3 collective-permute-start.3
  18.8 0.7 slice_bitcast_fusion.2
  19.5 3.9 %collective-permute-start.6 = (bf16[8,64,128]{2,1,0:T(8,128)(2,1)}, bf16[8,64,128]{2,1,0:T(8,128)(2,1)S(1)}, u32[]{:S(2)}, u32[]{:S(2)}) collective-permute-start(bf16[8,64,128]{2,1,0:T(8,128)(2,1)} %get-tuple-element.44), channel_id=1, source_target_pairs={{0,8},{8,16},{16,24},{24,32},{32,40},{40,48},{48,56},{56,64},{64,7... | collective-permute-start | bytes 393224 | tf_op jit(solution)/shard_map/ppermute | solution.py:249
  23.4 0.1 broadcast_in_dim.7
  23.5 0.1 convert_element_type.25.mask
  23.6 1.3 copy.17
  25.0 1.5 reshape.51.weights
  26.4 1.0 reverse_bitcast_fusion
  27.5 1.2 copy.16
  28.7 1.5 reshape.50.weights
  30.2 0.0 collective-permute-done.x_lo
  30.2 1.9 %collective-permute-start.7 = (bf16[8,64,128]{2,1,0:T(8,128)(2,1)}, bf16[8,64,128]{2,1,0:T(8,128)(2,1)S(1)}, u32[]{:S(2)}, u32[]{:S(2)}) collective-permute-start(bf16[8,64,128]{2,1,0:T(8,128)(2,1)} %get-tuple-element.43), channel_id=1, source_target_pairs={{8,0},{16,8},{24,16},{32,24},{40,32},{48,40},{56,48},{64,56},{72,6... | collective-permute-start | bytes 393224 | tf_op jit(solution)/shard_map/ppermute | solution.py:250
  32.1 0.0 collective-permute-done.1.x_hi
  32.2 5.8 %collective-permute-start.8 = (bf16[8,64,128]{2,1,0:T(8,128)(2,1)S(1)}, bf16[8,64,128]{2,1,0:T(8,128)(2,1)S(1)}, u32[]{:S(2)}, u32[]{:S(2)}) collective-permute-start(bf16[8,64,128]{2,1,0:T(8,128)(2,1)S(1)} %get-tuple-element.42), channel_id=1, source_target_pairs={{0,1},{1,2},{2,3},{3,4},{4,5},{5,6},{6,7},{8,9},{9,10},{10,11},{11... | collective-permute-start | bytes 393224 | tf_op jit(solution)/shard_map/ppermute | solution.py:247
  38.0 3.2 %collective-permute-start.4 = (bf16[2,64,128]{2,1,0:T(8,128)(2,1)S(1)}, bf16[2,64,128]{2,1,0:T(8,128)(2,1)S(1)}, u32[]{:S(2)}, u32[]{:S(2)}) collective-permute-start(bf16[2,64,128]{2,1,0:T(8,128)(2,1)S(1)} %pad_maximum_fusion), channel_id=1, source_target_pairs={{0,1},{1,2},{2,3},{3,4},{4,5},{5,6},{6,7},{8,9},{9,10},{10,11},{11... | collective-permute-start | bytes 98312 | tf_op jit(solution)/shard_map/ppermute | solution.py:253
  41.2 1.3 collective-permute-start.5
  42.6 1.3 collective-permute-start.9
  43.9 0.0 collective-permute-done.3.y_hi
  43.9 6.1 %collective-permute-start.10 = (bf16[2,64,128]{2,1,0:T(8,128)(2,1)S(1)}, bf16[2,64,128]{2,1,0:T(8,128)(2,1)S(1)}, u32[]{:S(2)}, u32[]{:S(2)}) collective-permute-start(bf16[2,64,128]{2,1,0:T(8,128)(2,1)S(1)} %pad_maximum_fusion.2), channel_id=1, source_target_pairs={{0,1},{1,2},{2,3},{3,4},{4,5},{5,6},{6,7},{8,9},{9,10},{10,11},{11... | collective-permute-start | bytes 98312 | tf_op jit(solution)/shard_map/ppermute | solution.py:253
  50.0 1.3 collective-permute-start.11
  51.3 7.4 %pre_act.1 = (bf16[8,8,64,128]{3,2,1,0:T(8,128)(2,1)S(1)}, f32[8,8,64,128]{3,2,1,0:T(8,128)S(1)}, bf16[10,10,64,128]{3,2,1,0:T(8,128)(2,1)S(1)}) custom-call(f32[1,128]{1,0:T(1,128)S(1)} %convert_element_type.25.mask, bf16[192,576]{1,0:T(8,128)(2,1)S(1)} %reshape.51.weights, bf16[8,8,64,128]{3,2,1,0:T(8,128)(2,1)S(1)} %get-tuple-element.61.tile, ...), custom_call_target="tpu_custom_call" | custom-call | flops 1811939328 | bytes 6644224 | tf_op jit(solution)/shard_map/pre_act/pallas_call | solution.py:231
  58.7 0.0 collective-permute-done.9.y_hi
  58.7 7.4 %act_grad.1 = (bf16[8,8,64,128]{3,2,1,0:T(8,128)(2,1)S(1)}, bf16[8,64,128]{2,1,0:T(8,128)(2,1)}, bf16[8,64,128]{2,1,0:T(8,128)(2,1)}, bf16[10,10,64,128]{3,2,1,0:T(8,128)(2,1)S(1)}) custom-call(bf16[192,576]{1,0:T(8,128)(2,1)S(1)} %reshape.50.weights, f32[8,8,64,128]{3,2,1,0:T(8,128)S(1)} %get-tuple-element.18.slope, ...), custom_call_target="tpu_custom_call" | custom-call | flops 1811939328 | bytes 6905856 | tf_op jit(solution)/shard_map/act_grad/pallas_call | solution.py:231
  66.2 11.0 %grads.1 = (f32[864,128]{1,0:T(8,128)S(1)}, f32[864,128]{1,0:T(8,128)}) custom-call(s32[1]{0:T(128)} %bitcast.18.core.core_ref, bf16[10,10,64,128]{3,2,1,0:T(8,128)(2,1)S(1)} %get-tuple-element.22.in_pad, bf16[8,8,64,128]{3,2,1,0:T(8,128)(2,1)S(1)} %get-tuple-element.19.tile.pre_grad, bf16[10,10,64,128]{3,2,1,0:T(8,128)(2,1)S(1)} %get-tuple-element.23.grad_pad, ...), custom_call_target="tpu_custom_call" | custom-call | flops 3623878656 | bytes 6258692 | tf_op jit(solution)/shard_map/grads/pallas_call | solution.py:231
  77.2 2.0 %collective-permute-done.18.recv = f32[864,128]{1,0:T(8,128)S(1)} collective-permute-done((f32[864,128]{1,0:T(8,128)}, f32[864,128]{1,0:T(8,128)S(1)}, u32[]{:S(2)}, u32[]{:S(2)}) %collective-permute-start.18) | collective-permute-done | bytes 442400 | tf_op jit(solution)/shard_map/ppermute | solution.py:22
  79.2 2.7 %collective-permute-start.19 = (f32[216,128]{1,0:T(8,128)S(1)}, f32[216,128]{1,0:T(8,128)S(1)}, u32[]{:S(2)}, u32[]{:S(2)}) collective-permute-start(f32[216,128]{1,0:T(8,128)S(1)} %get-tuple-element.28), channel_id=1, source_target_pairs={{0,16},{1,17},{2,18},{3,19},{4,20},{5,21},{6,22},{7,23},{8,24},{9,... | collective-permute-start | bytes 331784 | tf_op jit(solution)/shard_map/ppermute | solution.py:22
  81.9 3.5 %collective-permute-start.20 = (f32[216,128]{1,0:T(8,128)S(1)}, f32[216,128]{1,0:T(8,128)S(1)}, u32[]{:S(2)}, u32[]{:S(2)}) collective-permute-start(f32[216,128]{1,0:T(8,128)S(1)} %get-tuple-element.29), channel_id=1, source_target_pairs={{0,32},{1,33},{2,34},{3,35},{4,36},{5,37},{6,38},{7,39},{8,40},{9,... | collective-permute-start | bytes 331784 | tf_op jit(solution)/shard_map/ppermute | solution.py:22
  85.4 0.0 collective-permute-start.21
  85.4 5.4 %collective-permute-done.20 = f32[216,128]{1,0:T(8,128)S(1)} collective-permute-done((f32[216,128]{1,0:T(8,128)S(1)}, f32[216,128]{1,0:T(8,128)S(1)}, u32[]{:S(2)}, u32[]{:S(2)}) %collective-permute-start.20) | collective-permute-done | bytes 110624 | tf_op jit(solution)/shard_map/ppermute | solution.py:22
  90.8 2.5 %collective-permute-done.21 = f32[216,128]{1,0:T(8,128)S(1)} collective-permute-done((f32[216,128]{1,0:T(8,128)S(1)}, f32[216,128]{1,0:T(8,128)S(1)}, u32[]{:S(2)}, u32[]{:S(2)}) %collective-permute-start.21) | collective-permute-done | bytes 110624 | tf_op jit(solution)/shard_map/ppermute | solution.py:22
  93.4 5.7 %collective-permute-start.22 = (f32[216,128]{1,0:T(8,128)S(1)}, f32[216,128]{1,0:T(8,128)S(1)}, u32[]{:S(2)}, u32[]{:S(2)}) collective-permute-start(f32[216,128]{1,0:T(8,128)S(1)} %add_add_fusion.2), channel_id=1, source_target_pairs={{0,2},{1,3},{2,0},{3,1},{4,6},{5,7},{6,4},{7,5},{8,10},{9,11},{10,... | collective-permute-start | bytes 331784 | tf_op jit(solution)/shard_map/ppermute | solution.py:22
  99.2 2.6 %collective-permute-start.23 = (f32[216,128]{1,0:T(8,128)S(1)}, f32[216,128]{1,0:T(8,128)S(1)}, u32[]{:S(2)}, u32[]{:S(2)}) collective-permute-start(f32[216,128]{1,0:T(8,128)S(1)} %add_add_fusion.2), channel_id=1, source_target_pairs={{0,4},{1,5},{2,6},{3,7},{4,0},{5,1},{6,2},{7,3},{8,12},{9,13},{10,... | collective-permute-start | bytes 331784 | tf_op jit(solution)/shard_map/ppermute | solution.py:22
  101.8 1.9 %collective-permute-start.12 = (bf16[8,64,128]{2,1,0:T(8,128)(2,1)S(1)}, bf16[8,64,128]{2,1,0:T(8,128)(2,1)S(1)}, u32[]{:S(2)}, u32[]{:S(2)}) collective-permute-start(bf16[8,64,128]{2,1,0:T(8,128)(2,1)S(1)} %get-tuple-element.40), channel_id=1, source_target_pairs={{0,8},{8,16},{16,24},{24,32},{32,40},{40,48},{48,56},{56,64},{64,7... | collective-permute-start | bytes 393224 | tf_op jit(solution)/shard_map/ppermute | solution.py:249
  103.7 2.5 %collective-permute-start.13 = (bf16[8,64,128]{2,1,0:T(8,128)(2,1)S(1)}, bf16[8,64,128]{2,1,0:T(8,128)(2,1)S(1)}, u32[]{:S(2)}, u32[]{:S(2)}) collective-permute-start(bf16[8,64,128]{2,1,0:T(8,128)(2,1)S(1)} %get-tuple-element.39), channel_id=1, source_target_pairs={{8,0},{16,8},{24,16},{32,24},{40,32},{48,40},{56,48},{64,56},{72,6... | collective-permute-start | bytes 393224 | tf_op jit(solution)/shard_map/ppermute | solution.py:250
  106.2 4.3 %collective-permute-start.14 = (bf16[8,64,128]{2,1,0:T(8,128)(2,1)}, bf16[8,64,128]{2,1,0:T(8,128)(2,1)}, u32[]{:S(2)}, u32[]{:S(2)}) collective-permute-start(bf16[8,64,128]{2,1,0:T(8,128)(2,1)} %get-tuple-element.20), channel_id=1, source_target_pairs={{0,1},{1,2},{2,3},{3,4},{4,5},{5,6},{6,7},{8,9},{9,10},{10,11},{11... | collective-permute-start | bytes 393224 | tf_op jit(solution)/shard_map/ppermute | solution.py:247
  110.6 0.7 collective-permute-start.25
  111.3 3.1 %collective-permute-start.26 = (f32[216,128]{1,0:T(8,128)S(1)}, f32[216,128]{1,0:T(8,128)S(1)}, u32[]{:S(2)}, u32[]{:S(2)}) collective-permute-start(f32[216,128]{1,0:T(8,128)S(1)} %add_add_fusion.1), channel_id=1, source_target_pairs={{0,64},{1,65},{2,66},{3,67},{4,68},{5,69},{6,70},{7,71},{8,72},{9,... | collective-permute-start | bytes 331784 | tf_op jit(solution)/shard_map/ppermute | solution.py:22
  114.4 0.9 collective-permute-start.27
  115.4 1.8 %collective-permute-done.25 = f32[216,128]{1,0:T(8,128)S(1)} collective-permute-done((f32[216,128]{1,0:T(8,128)S(1)}, f32[216,128]{1,0:T(8,128)S(1)}, u32[]{:S(2)}, u32[]{:S(2)}) %collective-permute-start.25) | collective-permute-done | bytes 110624 | tf_op jit(solution)/shard_map/ppermute | solution.py:22
  117.1 1.3 collective-permute-start.15
  118.4 0.8 collective-permute-done.27
  119.3 2.3 %collective-permute-start.28 = (f32[216,128]{1,0:T(8,128)S(1)}, f32[216,128]{1,0:T(8,128)S(1)}, u32[]{:S(2)}, u32[]{:S(2)}) collective-permute-start(f32[216,128]{1,0:T(8,128)S(1)} %add_add_fusion.refs_0_), channel_id=1, source_target_pairs={{0,16},{1,17},{2,18},{3,19},{4,20},{5,21},{6,22},{7,23},{8,24},{9,... | collective-permute-start | bytes 331784 | tf_op jit(solution)/shard_map/ppermute | solution.py:22
  121.5 4.5 %collective-permute-start.29 = (f32[216,128]{1,0:T(8,128)S(1)}, f32[216,128]{1,0:T(8,128)S(1)}, u32[]{:S(2)}, u32[]{:S(2)}) collective-permute-start(f32[216,128]{1,0:T(8,128)S(1)} %add_add_fusion.refs_0_), channel_id=1, source_target_pairs={{0,32},{1,33},{2,34},{3,35},{4,36},{5,37},{6,38},{7,39},{8,40},{9,... | collective-permute-start | bytes 331784 | tf_op jit(solution)/shard_map/ppermute | solution.py:22
  126.0 4.0 %collective-permute-done.29.refs_2_ = f32[216,128]{1,0:T(8,128)S(1)} collective-permute-done((f32[216,128]{1,0:T(8,128)S(1)}, f32[216,128]{1,0:T(8,128)S(1)}, u32[]{:S(2)}, u32[]{:S(2)}) %collective-permute-start.29) | collective-permute-done | bytes 110624 | tf_op jit(solution)/shard_map/ppermute | solution.py:22
  130.1 1.0 collective-permute-done.30.refs_3_
  131.1 3.3 %collective-permute-start.31 = (f32[864,128]{1,0:T(8,128)S(1)}, f32[864,128]{1,0:T(8,128)S(1)}, u32[]{:S(2)}, u32[]{:S(2)}) collective-permute-start(f32[864,128]{1,0:T(8,128)S(1)} %join.1.own_ref), channel_id=1, source_target_pairs={{0,8},{1,9},{2,10},{3,11},{4,12},{5,13},{6,14},{7,15},{8,0},{9,1},... | collective-permute-start | bytes 1327112 | tf_op jit(solution)/shard_map/ppermute | solution.py:22
  134.4 0.6 pad_maximum_fusion.5
  135.0 1.3 collective-permute-start.17
  136.3 0.6 pad_maximum_fusion.4
  136.9 6.1 %collective-permute-start.16 = (bf16[2,64,128]{2,1,0:T(8,128)(2,1)}, bf16[2,64,128]{2,1,0:T(8,128)(2,1)}, u32[]{:S(2)}, u32[]{:S(2)}) collective-permute-start(bf16[2,64,128]{2,1,0:T(8,128)(2,1)} %pad_maximum_fusion.4), channel_id=1, source_target_pairs={{0,1},{1,2},{2,3},{3,4},{4,5},{5,6},{6,7},{8,9},{9,10},{10,11},{11... | collective-permute-start | bytes 98312 | tf_op jit(solution)/shard_map/ppermute | solution.py:253
  143.0 1.2 copy.14
  144.2 1.5 reshape.49.weights
  145.7 7.7 %branch.1 = bf16[8,8,64,128]{3,2,1,0:T(8,128)(2,1)S(1)} custom-call(f32[1,128]{1,0:T(1,128)S(1)} %convert_element_type.25.mask, bf16[192,576]{1,0:T(8,128)(2,1)S(1)} %reshape.49.weights, bf16[8,8,64,128]{3,2,1,0:T(8,128)(2,1)S(1)} %get-tuple-element.62.tile.base, bf16[8,8,64,128]{3,2,1,0:T(8,128)(2,1)S(1)} %get-tuple-element.19.tile.pre_grad, ...), custom_call_target="tpu_custom_call" | custom-call | flops 1811939328 | bytes 3957248 | tf_op jit(solution)/shard_map/branch/pallas_call | solution.py:231
  153.4 1.6 %copy.19 = bf16[64,8,8,128]{3,2,1,0:T(8,128)(2,1)} copy(bf16[64,8,8,128]{3,0,2,1:T(8,128)(2,1)S(1)} %bitcast.36) | data formatting | bytes 2097152
  155.1 1.8 %unpack.1 = (f32[3,3,3,64,64]{4,3,2,1,0:T(8,128)}, f32[3,3,3,64,64]{4,3,2,1,0:T(8,128)}) custom-call(s32[1]{0:T(128)} %bitcast.18.core.core_ref, f32[864,128]{1,0:T(8,128)S(1)} %join.1.own_ref, f32[864,128]{1,0:T(8,128)S(1)} %collective-permute-done.31.other_ref), custom_call_target="tpu_custom_call" | custom-call | bytes 1769476 | tf_op jit(solution)/shard_map/unpack/pallas_call | solution.py:231
  (46 shorter events, 0.4 us)
Async XLA Ops:
  4.8 18.8 %copy-start = (bf16[3,3,3,64,64]{4,3,2,1,0:T(8,128)(2,1)S(1)}, bf16[3,3,3,64,64]{4,3,2,1,0:T(8,128)(2,1)}, u32[]{:S(2)}) copy-start(bf16[3,3,3,64,64]{4,3,2,1,0:T(8,128)(2,1)} %param.8) | copy-start | bytes 663556
  5.5 24.7 %collective-permute-start = (bf16[8,64,128]{2,1,0:T(8,128)(2,1)}, bf16[8,64,128]{2,1,0:T(8,128)(2,1)S(1)}, u32[]{:S(2)}, u32[]{:S(2)}) collective-permute-start(bf16[8,64,128]{2,1,0:T(8,128)(2,1)} %get-tuple-element.48), channel_id=1, source_target_pairs={{0,8},{8,16},{16,24},{24,32},{32,40},{40,48},{48,56},{56,64},{64,7... | collective-permute-start | bytes 393224 | tf_op jit(solution)/shard_map/ppermute | solution.py:249
  10.0 22.1 %collective-permute-start.1 = (bf16[8,64,128]{2,1,0:T(8,128)(2,1)}, bf16[8,64,128]{2,1,0:T(8,128)(2,1)S(1)}, u32[]{:S(2)}, u32[]{:S(2)}) collective-permute-start(bf16[8,64,128]{2,1,0:T(8,128)(2,1)} %get-tuple-element.47), channel_id=1, source_target_pairs={{8,0},{16,8},{24,16},{32,24},{40,32},{48,40},{56,48},{64,56},{72,6... | collective-permute-start | bytes 393224 | tf_op jit(solution)/shard_map/ppermute | solution.py:250
  12.0 30.6 %collective-permute-start.2 = (bf16[8,64,128]{2,1,0:T(8,128)(2,1)S(1)}, bf16[8,64,128]{2,1,0:T(8,128)(2,1)S(1)}, u32[]{:S(2)}, u32[]{:S(2)}) collective-permute-start(bf16[8,64,128]{2,1,0:T(8,128)(2,1)S(1)} %get-tuple-element.46), channel_id=1, source_target_pairs={{0,1},{1,2},{2,3},{3,4},{4,5},{5,6},{6,7},{8,9},{9,10},{10,11},{11... | collective-permute-start | bytes 393224 | tf_op jit(solution)/shard_map/ppermute | solution.py:247
  17.5 26.4 %collective-permute-start.3 = (bf16[8,64,128]{2,1,0:T(8,128)(2,1)S(1)}, bf16[8,64,128]{2,1,0:T(8,128)(2,1)S(1)}, u32[]{:S(2)}, u32[]{:S(2)}) collective-permute-start(bf16[8,64,128]{2,1,0:T(8,128)(2,1)S(1)} %get-tuple-element.45), channel_id=1, source_target_pairs={{1,0},{2,1},{3,2},{4,3},{5,4},{6,5},{7,6},{9,8},{10,9},{11,10},{12... | collective-permute-start | bytes 393224 | tf_op jit(solution)/shard_map/ppermute | solution.py:248
  19.5 18.5 %collective-permute-start.6 = (bf16[8,64,128]{2,1,0:T(8,128)(2,1)}, bf16[8,64,128]{2,1,0:T(8,128)(2,1)S(1)}, u32[]{:S(2)}, u32[]{:S(2)}) collective-permute-start(bf16[8,64,128]{2,1,0:T(8,128)(2,1)} %get-tuple-element.44), channel_id=1, source_target_pairs={{0,8},{8,16},{16,24},{24,32},{32,40},{40,48},{48,56},{56,64},{64,7... | collective-permute-start | bytes 393224 | tf_op jit(solution)/shard_map/ppermute | solution.py:249
  30.2 11.0 %collective-permute-start.7 = (bf16[8,64,128]{2,1,0:T(8,128)(2,1)}, bf16[8,64,128]{2,1,0:T(8,128)(2,1)S(1)}, u32[]{:S(2)}, u32[]{:S(2)}) collective-permute-start(bf16[8,64,128]{2,1,0:T(8,128)(2,1)} %get-tuple-element.43), channel_id=1, source_target_pairs={{8,0},{16,8},{24,16},{32,24},{40,32},{48,40},{56,48},{64,56},{72,6... | collective-permute-start | bytes 393224 | tf_op jit(solution)/shard_map/ppermute | solution.py:250
  32.2 26.5 %collective-permute-start.8 = (bf16[8,64,128]{2,1,0:T(8,128)(2,1)S(1)}, bf16[8,64,128]{2,1,0:T(8,128)(2,1)S(1)}, u32[]{:S(2)}, u32[]{:S(2)}) collective-permute-start(bf16[8,64,128]{2,1,0:T(8,128)(2,1)S(1)} %get-tuple-element.42), channel_id=1, source_target_pairs={{0,1},{1,2},{2,3},{3,4},{4,5},{5,6},{6,7},{8,9},{9,10},{10,11},{11... | collective-permute-start | bytes 393224 | tf_op jit(solution)/shard_map/ppermute | solution.py:247
  38.0 12.0 %collective-permute-start.4 = (bf16[2,64,128]{2,1,0:T(8,128)(2,1)S(1)}, bf16[2,64,128]{2,1,0:T(8,128)(2,1)S(1)}, u32[]{:S(2)}, u32[]{:S(2)}) collective-permute-start(bf16[2,64,128]{2,1,0:T(8,128)(2,1)S(1)} %pad_maximum_fusion), channel_id=1, source_target_pairs={{0,1},{1,2},{2,3},{3,4},{4,5},{5,6},{6,7},{8,9},{9,10},{10,11},{11... | collective-permute-start | bytes 98312 | tf_op jit(solution)/shard_map/ppermute | solution.py:253
  41.2 10.1 %collective-permute-start.5 = (bf16[2,64,128]{2,1,0:T(8,128)(2,1)S(1)}, bf16[2,64,128]{2,1,0:T(8,128)(2,1)S(1)}, u32[]{:S(2)}, u32[]{:S(2)}) collective-permute-start(bf16[2,64,128]{2,1,0:T(8,128)(2,1)S(1)} %pad_maximum_fusion.1), channel_id=1, source_target_pairs={{1,0},{2,1},{3,2},{4,3},{5,4},{6,5},{7,6},{9,8},{10,9},{11,10},{12... | collective-permute-start | bytes 98312 | tf_op jit(solution)/shard_map/ppermute | solution.py:254
  42.6 16.2 %collective-permute-start.9 = (bf16[8,64,128]{2,1,0:T(8,128)(2,1)S(1)}, bf16[8,64,128]{2,1,0:T(8,128)(2,1)S(1)}, u32[]{:S(2)}, u32[]{:S(2)}) collective-permute-start(bf16[8,64,128]{2,1,0:T(8,128)(2,1)S(1)} %get-tuple-element.41), channel_id=1, source_target_pairs={{1,0},{2,1},{3,2},{4,3},{5,4},{6,5},{7,6},{9,8},{10,9},{11,10},{12... | collective-permute-start | bytes 393224 | tf_op jit(solution)/shard_map/ppermute | solution.py:248
  43.9 14.9 %collective-permute-start.10 = (bf16[2,64,128]{2,1,0:T(8,128)(2,1)S(1)}, bf16[2,64,128]{2,1,0:T(8,128)(2,1)S(1)}, u32[]{:S(2)}, u32[]{:S(2)}) collective-permute-start(bf16[2,64,128]{2,1,0:T(8,128)(2,1)S(1)} %pad_maximum_fusion.2), channel_id=1, source_target_pairs={{0,1},{1,2},{2,3},{3,4},{4,5},{5,6},{6,7},{8,9},{9,10},{10,11},{11... | collective-permute-start | bytes 98312 | tf_op jit(solution)/shard_map/ppermute | solution.py:253
  50.0 8.7 %collective-permute-start.11 = (bf16[2,64,128]{2,1,0:T(8,128)(2,1)S(1)}, bf16[2,64,128]{2,1,0:T(8,128)(2,1)S(1)}, u32[]{:S(2)}, u32[]{:S(2)}) collective-permute-start(bf16[2,64,128]{2,1,0:T(8,128)(2,1)S(1)} %pad_maximum_fusion.3), channel_id=1, source_target_pairs={{1,0},{2,1},{3,2},{4,3},{5,4},{6,5},{7,6},{9,8},{10,9},{11,10},{12... | collective-permute-start | bytes 98312 | tf_op jit(solution)/shard_map/ppermute | solution.py:254
  77.2 2.0 %collective-permute-start.18 = (f32[864,128]{1,0:T(8,128)}, f32[864,128]{1,0:T(8,128)S(1)}, u32[]{:S(2)}, u32[]{:S(2)}) collective-permute-start(f32[864,128]{1,0:T(8,128)} %get-tuple-element.26), channel_id=1, source_target_pairs={{0,8},{1,9},{2,10},{3,11},{4,12},{5,13},{6,14},{7,15},{8,0},{9,1},... | collective-permute-start | bytes 1327112 | tf_op jit(solution)/shard_map/ppermute | solution.py:22
  79.2 6.2 %collective-permute-start.19 = (f32[216,128]{1,0:T(8,128)S(1)}, f32[216,128]{1,0:T(8,128)S(1)}, u32[]{:S(2)}, u32[]{:S(2)}) collective-permute-start(f32[216,128]{1,0:T(8,128)S(1)} %get-tuple-element.28), channel_id=1, source_target_pairs={{0,16},{1,17},{2,18},{3,19},{4,20},{5,21},{6,22},{7,23},{8,24},{9,... | collective-permute-start | bytes 331784 | tf_op jit(solution)/shard_map/ppermute | solution.py:22
  81.9 9.0 %collective-permute-start.20 = (f32[216,128]{1,0:T(8,128)S(1)}, f32[216,128]{1,0:T(8,128)S(1)}, u32[]{:S(2)}, u32[]{:S(2)}) collective-permute-start(f32[216,128]{1,0:T(8,128)S(1)} %get-tuple-element.29), channel_id=1, source_target_pairs={{0,32},{1,33},{2,34},{3,35},{4,36},{5,37},{6,38},{7,39},{8,40},{9,... | collective-permute-start | bytes 331784 | tf_op jit(solution)/shard_map/ppermute | solution.py:22
  85.4 8.0 %collective-permute-start.21 = (f32[216,128]{1,0:T(8,128)S(1)}, f32[216,128]{1,0:T(8,128)S(1)}, u32[]{:S(2)}, u32[]{:S(2)}) collective-permute-start(f32[216,128]{1,0:T(8,128)S(1)} %get-tuple-element.30), channel_id=1, source_target_pairs={{0,48},{1,49},{2,50},{3,51},{4,52},{5,53},{6,54},{7,55},{8,56},{9,... | collective-permute-start | bytes 331784 | tf_op jit(solution)/shard_map/ppermute | solution.py:22
  93.4 49.6 %copy-start.1 = (bf16[3,3,3,64,64]{4,3,2,1,0:T(8,128)(2,1)S(1)}, bf16[3,3,3,64,64]{4,3,2,1,0:T(8,128)(2,1)}, u32[]{:S(2)}) copy-start(bf16[3,3,3,64,64]{4,3,2,1,0:T(8,128)(2,1)} %param.8) | copy-start | bytes 663556
  93.4 12.8 %collective-permute-start.22 = (f32[216,128]{1,0:T(8,128)S(1)}, f32[216,128]{1,0:T(8,128)S(1)}, u32[]{:S(2)}, u32[]{:S(2)}) collective-permute-start(f32[216,128]{1,0:T(8,128)S(1)} %add_add_fusion.2), channel_id=1, source_target_pairs={{0,2},{1,3},{2,0},{3,1},{4,6},{5,7},{6,4},{7,5},{8,10},{9,11},{10,... | collective-permute-start | bytes 331784 | tf_op jit(solution)/shard_map/ppermute | solution.py:22
  99.2 11.4 %collective-permute-start.23 = (f32[216,128]{1,0:T(8,128)S(1)}, f32[216,128]{1,0:T(8,128)S(1)}, u32[]{:S(2)}, u32[]{:S(2)}) collective-permute-start(f32[216,128]{1,0:T(8,128)S(1)} %add_add_fusion.2), channel_id=1, source_target_pairs={{0,4},{1,5},{2,6},{3,7},{4,0},{5,1},{6,2},{7,3},{8,12},{9,13},{10,... | collective-permute-start | bytes 331784 | tf_op jit(solution)/shard_map/ppermute | solution.py:22
  101.8 8.8 %collective-permute-start.24 = (f32[216,128]{1,0:T(8,128)S(1)}, f32[216,128]{1,0:T(8,128)S(1)}, u32[]{:S(2)}, u32[]{:S(2)}) collective-permute-start(f32[216,128]{1,0:T(8,128)S(1)} %add_add_fusion.2), channel_id=1, source_target_pairs={{0,6},{1,7},{2,4},{3,5},{4,2},{5,3},{6,0},{7,1},{8,14},{9,15},{10,... | collective-permute-start | bytes 331784 | tf_op jit(solution)/shard_map/ppermute | solution.py:22
  101.8 12.6 %collective-permute-start.12 = (bf16[8,64,128]{2,1,0:T(8,128)(2,1)S(1)}, bf16[8,64,128]{2,1,0:T(8,128)(2,1)S(1)}, u32[]{:S(2)}, u32[]{:S(2)}) collective-permute-start(bf16[8,64,128]{2,1,0:T(8,128)(2,1)S(1)} %get-tuple-element.40), channel_id=1, source_target_pairs={{0,8},{8,16},{16,24},{24,32},{32,40},{40,48},{48,56},{56,64},{64,7... | collective-permute-start | bytes 393224 | tf_op jit(solution)/shard_map/ppermute | solution.py:249
  103.7 22.3 %collective-permute-start.13 = (bf16[8,64,128]{2,1,0:T(8,128)(2,1)S(1)}, bf16[8,64,128]{2,1,0:T(8,128)(2,1)S(1)}, u32[]{:S(2)}, u32[]{:S(2)}) collective-permute-start(bf16[8,64,128]{2,1,0:T(8,128)(2,1)S(1)} %get-tuple-element.39), channel_id=1, source_target_pairs={{8,0},{16,8},{24,16},{32,24},{40,32},{48,40},{56,48},{64,56},{72,6... | collective-permute-start | bytes 393224 | tf_op jit(solution)/shard_map/ppermute | solution.py:250
  106.2 39.5 %collective-permute-start.14 = (bf16[8,64,128]{2,1,0:T(8,128)(2,1)}, bf16[8,64,128]{2,1,0:T(8,128)(2,1)}, u32[]{:S(2)}, u32[]{:S(2)}) collective-permute-start(bf16[8,64,128]{2,1,0:T(8,128)(2,1)} %get-tuple-element.20), channel_id=1, source_target_pairs={{0,1},{1,2},{2,3},{3,4},{4,5},{5,6},{6,7},{8,9},{9,10},{10,11},{11... | collective-permute-start | bytes 393224 | tf_op jit(solution)/shard_map/ppermute | solution.py:247
  110.6 6.5 %collective-permute-start.25 = (f32[216,128]{1,0:T(8,128)S(1)}, f32[216,128]{1,0:T(8,128)S(1)}, u32[]{:S(2)}, u32[]{:S(2)}) collective-permute-start(f32[216,128]{1,0:T(8,128)S(1)} %add_add_fusion.1), channel_id=1, source_target_pairs={{0,1},{1,0},{2,3},{3,2},{4,5},{5,4},{6,7},{7,6},{8,9},{9,8},{10,11... | collective-permute-start | bytes 331784 | tf_op jit(solution)/shard_map/ppermute | solution.py:22
  111.3 7.1 %collective-permute-start.26 = (f32[216,128]{1,0:T(8,128)S(1)}, f32[216,128]{1,0:T(8,128)S(1)}, u32[]{:S(2)}, u32[]{:S(2)}) collective-permute-start(f32[216,128]{1,0:T(8,128)S(1)} %add_add_fusion.1), channel_id=1, source_target_pairs={{0,64},{1,65},{2,66},{3,67},{4,68},{5,69},{6,70},{7,71},{8,72},{9,... | collective-permute-start | bytes 331784 | tf_op jit(solution)/shard_map/ppermute | solution.py:22
  114.4 4.8 %collective-permute-start.27 = (f32[216,128]{1,0:T(8,128)S(1)}, f32[216,128]{1,0:T(8,128)S(1)}, u32[]{:S(2)}, u32[]{:S(2)}) collective-permute-start(f32[216,128]{1,0:T(8,128)S(1)} %add_add_fusion.1), channel_id=1, source_target_pairs={{0,65},{1,64},{2,67},{3,66},{4,69},{5,68},{6,71},{7,70},{8,73},{9,... | collective-permute-start | bytes 331784 | tf_op jit(solution)/shard_map/ppermute | solution.py:22
  117.1 28.6 %collective-permute-start.15 = (bf16[8,64,128]{2,1,0:T(8,128)(2,1)}, bf16[8,64,128]{2,1,0:T(8,128)(2,1)}, u32[]{:S(2)}, u32[]{:S(2)}) collective-permute-start(bf16[8,64,128]{2,1,0:T(8,128)(2,1)} %get-tuple-element.21), channel_id=1, source_target_pairs={{1,0},{2,1},{3,2},{4,3},{5,4},{6,5},{7,6},{9,8},{10,9},{11,10},{12... | collective-permute-start | bytes 393224 | tf_op jit(solution)/shard_map/ppermute | solution.py:248
  119.3 6.8 %collective-permute-start.28 = (f32[216,128]{1,0:T(8,128)S(1)}, f32[216,128]{1,0:T(8,128)S(1)}, u32[]{:S(2)}, u32[]{:S(2)}) collective-permute-start(f32[216,128]{1,0:T(8,128)S(1)} %add_add_fusion.refs_0_), channel_id=1, source_target_pairs={{0,16},{1,17},{2,18},{3,19},{4,20},{5,21},{6,22},{7,23},{8,24},{9,... | collective-permute-start | bytes 331784 | tf_op jit(solution)/shard_map/ppermute | solution.py:22
  121.5 8.5 %collective-permute-start.29 = (f32[216,128]{1,0:T(8,128)S(1)}, f32[216,128]{1,0:T(8,128)S(1)}, u32[]{:S(2)}, u32[]{:S(2)}) collective-permute-start(f32[216,128]{1,0:T(8,128)S(1)} %add_add_fusion.refs_0_), channel_id=1, source_target_pairs={{0,32},{1,33},{2,34},{3,35},{4,36},{5,37},{6,38},{7,39},{8,40},{9,... | collective-permute-start | bytes 331784 | tf_op jit(solution)/shard_map/ppermute | solution.py:22
  126.0 5.0 %collective-permute-start.30 = (f32[216,128]{1,0:T(8,128)S(1)}, f32[216,128]{1,0:T(8,128)S(1)}, u32[]{:S(2)}, u32[]{:S(2)}) collective-permute-start(f32[216,128]{1,0:T(8,128)S(1)} %add_add_fusion.refs_0_), channel_id=1, source_target_pairs={{0,48},{1,49},{2,50},{3,51},{4,52},{5,53},{6,54},{7,55},{8,56},{9,... | collective-permute-start | bytes 331784 | tf_op jit(solution)/shard_map/ppermute | solution.py:22
  131.1 24.0 %collective-permute-start.31 = (f32[864,128]{1,0:T(8,128)S(1)}, f32[864,128]{1,0:T(8,128)S(1)}, u32[]{:S(2)}, u32[]{:S(2)}) collective-permute-start(f32[864,128]{1,0:T(8,128)S(1)} %join.1.own_ref), channel_id=1, source_target_pairs={{0,8},{1,9},{2,10},{3,11},{4,12},{5,13},{6,14},{7,15},{8,0},{9,1},... | collective-permute-start | bytes 1327112 | tf_op jit(solution)/shard_map/ppermute | solution.py:22
  135.0 10.7 %collective-permute-start.17 = (bf16[2,64,128]{2,1,0:T(8,128)(2,1)}, bf16[2,64,128]{2,1,0:T(8,128)(2,1)S(1)}, u32[]{:S(2)}, u32[]{:S(2)}) collective-permute-start(bf16[2,64,128]{2,1,0:T(8,128)(2,1)} %pad_maximum_fusion.5), channel_id=1, source_target_pairs={{1,0},{2,1},{3,2},{4,3},{5,4},{6,5},{7,6},{9,8},{10,9},{11,10},{12... | collective-permute-start | bytes 98312 | tf_op jit(solution)/shard_map/ppermute | solution.py:254
  136.9 8.8 %collective-permute-start.16 = (bf16[2,64,128]{2,1,0:T(8,128)(2,1)}, bf16[2,64,128]{2,1,0:T(8,128)(2,1)}, u32[]{:S(2)}, u32[]{:S(2)}) collective-permute-start(bf16[2,64,128]{2,1,0:T(8,128)(2,1)} %pad_maximum_fusion.4), channel_id=1, source_target_pairs={{0,1},{1,2},{2,3},{3,4},{4,5},{5,6},{6,7},{8,9},{9,10},{10,11},{11... | collective-permute-start | bytes 98312 | tf_op jit(solution)/shard_map/ppermute | solution.py:253

commit v2 on v1

v2 whole, which is shorter than its diff:
```python
import functools
import math

import jax
import jax.numpy as jnp
from jax import lax
from jax.experimental import pallas as pl
from jax.experimental.pallas import tpu as pltpu
from jax.sharding import PartitionSpec as P


F32 = jnp.float32
BF16 = jnp.bfloat16
AXES = ("gx", "gy")


def swap_perms(count):
    even = [(i, i ^ 1) for i in range(count)]
    odd = [(i, i + 1 if i % 2 else i - 1) for i in range(1, count - 1)]
    return even, odd


def xor_permute(value, mask):
    total = lax.axis_size("gx") * lax.axis_size("gy")
    return lax.ppermute(value, AXES, [(i, i ^ mask) for i in range(total)])


def swap(value_even, value_odd, axis):
    even, odd = swap_perms(lax.axis_size(axis))
    return lax.ppermute(value_even, axis, even), lax.ppermute(value_odd, axis, odd)


def stack_row(stack, at_x, first_y, row):
    count, chans, depth = row.shape
    lane = lax.broadcasted_iota(jnp.int32, row.shape, 2)
    zero = jnp.zeros_like(row)
    below = jnp.where(lane == 0, zero, pltpu.roll(row, 1, 2))
    above = jnp.where(lane == depth - 1, zero, pltpu.roll(row, depth - 1, 2))
    ys = pl.ds(first_y, count)
    stack[at_x, ys, 0:chans, :] = below
    stack[at_x, ys, chans : 2 * chans, :] = row
    stack[at_x, ys, 2 * chans : 3 * chans, :] = above


def sides(parity, size):
    even = (1 - parity) * (size + 1)
    return even, size + 1 - even


def stack_padded(stack, place, tile, xr_even, xr_odd, yr_even, yr_odd, which):
    size_x, size_y = tile.shape[0], tile.shape[1]
    x_even, x_odd = sides(place[0], size_x)
    y_even, y_odd = sides(place[1], size_y)
    stack_row(stack, x_even, 1, xr_even[which])
    stack_row(stack, x_odd, 1, xr_odd[which])

    def column(i, carry):
        stack_row(stack, i, y_even, yr_even[pl.ds(i, 1)])
        stack_row(stack, i, y_odd, yr_odd[pl.ds(i, 1)])
        return carry

    lax.fori_loop(0, size_x + 2, column, 0)

    def body(i, carry):
        stack_row(stack, i + 1, 1, tile[i])
        return carry

    lax.fori_loop(0, size_x, body, 0)


def ypack_kernel(place, tile, xr_even, xr_odd, ys_even, ys_odd, *, which):
    size_x, size_y = tile.shape[0], tile.shape[1]
    x_even, x_odd = sides(place[0], size_x)
    for out, edge in ((ys_even, (1 - place[1]) * (size_y - 1)), (ys_odd, place[1] * (size_y - 1))):
        out[x_even] = xr_even[which, edge]
        out[x_odd] = xr_odd[which, edge]
        for i in range(size_x):
            out[i + 1] = tile[i, edge]


def conv_stack(stack, weights, acc, first=0):
    wide, _, deep, depth = stack.shape
    tall = acc.shape[1]
    chans = deep // 3
    acc[0:2] = jnp.zeros((2,) + acc.shape[1:], F32)

    def body(i, carry):
        for y in range(0, tall, 2):
            at = first + y
            left = stack[i, at : at + 3].reshape(3 * deep, depth)
            right = stack[i, at + 1 : at + 4].reshape(3 * deep, depth)
            both = jnp.concatenate([left, right], axis=1)
            out = jnp.dot(weights[...], both, preferred_element_type=F32)
            for side in range(2):
                part = out[:, side * depth : (side + 1) * depth]
                acc[i + 2, y + side] = part[0:chans]
                acc[i + 1, y + side] += part[chans : 2 * chans]
                acc[i, y + side] += part[2 * chans : 3 * chans]
        return carry

    lax.fori_loop(0, wide, body, 0)


def forward_kernel(place, mask, weights, tile, xr_even, xr_odd, yr_even, yr_odd, activ, slope, padded, stack, acc):
    stack_padded(stack, place, tile, xr_even, xr_odd, yr_even, yr_odd, 0)
    chans = tile.shape[2]
    padded[...] = stack[:, :, chans : 2 * chans, :]
    conv_stack(stack, weights, acc)

    def body(i, carry):
        value = acc[i + 2]
        sig = jax.nn.sigmoid(value)
        activ[i] = (mask[...] * (value * sig)).astype(BF16)
        slope[i] = mask[...] * (sig * (1.0 + value * (1.0 - sig)))
        return carry

    lax.fori_loop(0, tile.shape[0], body, 0)


def backward_kernel(
    place, weights, slope, tile, xr_even, xr_odd, yr_even, yr_odd, pre_grad, xs_even, xs_odd, padded, stack, acc
):
    stack_padded(stack, place, tile, xr_even, xr_odd, yr_even, yr_odd, 1)
    size_x, _, chans = tile.shape[0:3]
    padded[...] = stack[:, :, chans : 2 * chans, :]
    conv_stack(stack, weights, acc)

    def body(i, carry):
        pre_grad[i] = (slope[i] * acc[i + 2]).astype(BF16)
        return carry

    lax.fori_loop(0, size_x, body, 0)
    xs_even[0] = pre_grad[(1 - place[0]) * (size_x - 1)]
    xs_odd[0] = pre_grad[place[0] * (size_x - 1)]


def branch_finish(mask, base, result, acc, first):
    tall = acc.shape[1]

    def body(i, carry):
        result[i] = (base[i, first : first + tall].astype(F32) + mask[...] * acc[i + 2]).astype(BF16)
        return carry

    lax.fori_loop(0, base.shape[0], body, 0)


def branch_low_kernel(place, mask, weights, base, tile, xr_even, xr_odd, yr_even, yr_odd, result, stack, acc):
    stack_padded(stack, place, tile, xr_even, xr_odd, yr_even, yr_odd, 0)
    conv_stack(stack, weights, acc, 0)
    branch_finish(mask, base, result, acc, 0)


def branch_high_kernel(mask, weights, base, stack, result, acc):
    first = base.shape[1] // 2
    conv_stack(stack, weights, acc, first)
    branch_finish(mask, base, result, acc, first)


def grad_accumulate(padded, stack, acc):
    size_x, size_y, _, _ = stack.shape
    acc[...] = jnp.zeros_like(acc)

    def body(i, carry):
        right = jnp.concatenate([stack[i, y] for y in range(size_y)], axis=1)
        left = []
        for a in range(3):
            rows = [padded[i + a, y] for y in range(size_y + 2)]
            for b in range(3):
                left.append(jnp.concatenate(rows[b : b + size_y], axis=1))
        left = jnp.concatenate(left, axis=0)
        acc[...] += lax.dot_general(left, right, (((1,), (1,)), ((), ())), preferred_element_type=F32)
        return carry

    lax.fori_loop(0, size_x, body, 0)


def pack_grad(dest, acc, chans):
    rows = acc.shape[0]
    half = rows // 2
    dest[0:rows] = acc[:, 0 : 2 * chans]
    low = acc[0:half, 2 * chans : 3 * chans]
    high = acc[half:rows, 2 * chans : 3 * chans]
    dest[rows : rows + half] = jnp.concatenate([low, high], axis=1)


def stack_tile(stack, source):
    def body(i, carry):
        stack_row(stack, i, 0, source[i])
        return carry

    lax.fori_loop(0, source.shape[0], body, 0)


def grad_two_kernel(grad_pad, activ, packed, stack, acc):
    stack_tile(stack, activ)
    grad_accumulate(grad_pad, stack, acc)
    pack_grad(packed, acc, activ.shape[2])


def grad_one_kernel(place, in_pad, pre_grad, packed_two, keep, send, stack, acc):
    stack_tile(stack, pre_grad)
    grad_accumulate(in_pad, stack, acc)

    @pl.when(place[0] == 0)
    def _():
        pack_grad(keep, acc, pre_grad.shape[2])
        send[...] = packed_two[...]

    @pl.when(place[0] != 0)
    def _():
        pack_grad(send, acc, pre_grad.shape[2])
        keep[...] = packed_two[...]


def split_kernel(place, keep, recv, *outs):
    rows = outs[0].shape[0]
    for dist, out in enumerate(outs):
        start = pl.multiple_of((place[2] ^ dist) * rows, 8)
        out[...] = keep[pl.ds(start, rows)] + recv[pl.ds(start, rows)]


def join_kernel(place, *refs):
    out = refs[-1]
    rows = refs[0].shape[0]
    for dist, part in enumerate(refs[:-1]):
        start = pl.multiple_of((place[2] ^ dist) * rows, 8)
        out[pl.ds(start, rows)] = part[...]


def unpack_kernel(place, scale, own, other, grad_one, grad_two):
    chans = grad_one.shape[-1]
    rows = 9 * chans
    half = rows // 2

    def block(source, a, b, j):
        start = (3 * a + b) * chans
        if j < 2:
            return source[start : start + chans, j * chans : (j + 1) * chans]
        pieces = []
        step = chans // 2
        for first in (start, start + step):
            if first < half:
                pieces.append(source[rows + first : rows + first + step, 0:chans])
            else:
                pieces.append(source[rows + first - half : rows + first - half + step, chans : 2 * chans])
        return jnp.concatenate(pieces, axis=0)

    def write(one, two):
        for a in range(3):
            for b in range(3):
                for j in range(3):
                    grad_one[a, b, 2 - j] = block(one, a, b, j) * scale
                    grad_two[2 - a, 2 - b, j] = block(two, a, b, j).T * scale

    @pl.when(place[0] == 0)
    def _():
        write(own, other)

    @pl.when(place[0] != 0)
    def _():
        write(other, own)


def call(kernel, outs, scratch=(), scalars=0, flops=0):
    def run(*operands):
        specs = [pl.BlockSpec(memory_space=pltpu.SMEM)] * scalars
        specs += [pl.BlockSpec(memory_space=pltpu.VMEM)] * (len(operands) - scalars)
        moved = sum(o.size * o.dtype.itemsize for o in operands)
        moved += sum(math.prod(o.shape) * o.dtype.itemsize for o in outs)
        return pl.pallas_call(
            kernel,
            out_shape=tuple(outs),
            in_specs=specs,
            out_specs=tuple(pl.BlockSpec(memory_space=pltpu.VMEM) for _ in outs),
            scratch_shapes=list(scratch),
            cost_estimate=pl.CostEstimate(flops=flops, bytes_accessed=moved, transcendentals=0),
            compiler_params=pltpu.CompilerParams(vmem_limit_bytes=40 * 1024 * 1024),
        )(*operands)

    return run


def body(features, cotangent, block_mask, kernel_one, kernel_two):
    chans, tile_x, tile_y, tile_z = features.shape
    blocks = block_mask.shape[2]
    cells_all = tile_x * tile_y * tile_z * lax.axis_size("gx") * lax.axis_size("gy")
    scale = 1.0 / math.sqrt(cells_all)
    place_x, place_y = lax.axis_index("gx"), lax.axis_index("gy")
    x_odd, y_odd = place_x & 1, place_y & 1
    place = jnp.stack([x_odd, y_odd, (place_x >> 1) & 3]).astype(jnp.int32)

    mask = jnp.broadcast_to(block_mask.reshape(blocks, 1), (blocks, tile_z // blocks)).reshape(1, tile_z)
    mask_f = mask.astype(F32)
    mask_b = mask.astype(BF16).reshape(1, 1, tile_z)

    def x_edges(at):
        both = [lax.dynamic_index_in_dim(a, at, 1, keepdims=False) * mask_b for a in (features, cotangent)]
        return jnp.stack([jnp.transpose(a, (1, 0, 2)) for a in both])

    xr = swap(x_edges((1 - x_odd) * (tile_x - 1)), x_edges(x_odd * (tile_x - 1)), "gx")
    masked_in = jnp.transpose(features * mask_b[:, None], (1, 2, 0, 3))
    masked_grad = jnp.transpose(cotangent * mask_b[:, None], (1, 2, 0, 3))

    tile_shape = (tile_x, tile_y, chans, tile_z)
    tile_b = jax.ShapeDtypeStruct(tile_shape, BF16)
    column_b = jax.ShapeDtypeStruct((tile_x + 2, chans, tile_z), BF16)
    edge_b = jax.ShapeDtypeStruct((1, tile_y, chans, tile_z), BF16)
    pad_b = jax.ShapeDtypeStruct((tile_x + 2, tile_y + 2, chans, tile_z), BF16)
    flops = 2 * 27 * chans * chans * tile_x * tile_y * tile_z

    def y_sends(tile, halo_x, which):
        kernel = functools.partial(ypack_kernel, which=which)
        return call(kernel, [column_b] * 2, scalars=1)(place, tile, *halo_x)

    in_sends = y_sends(masked_in, xr, 0)
    grad_sends = y_sends(masked_grad, xr, 1)
    in_y = swap(*in_sends, "gy")
    grad_y = swap(*grad_sends, "gy")

    w_pre = jnp.transpose(kernel_one, (0, 4, 1, 2, 3)).reshape(3 * chans, 9 * chans)
    flat = lambda w: jnp.transpose(w[::-1, ::-1, ::-1], (0, 3, 1, 2, 4)).reshape(3 * chans, 9 * chans)
    w_pre, w_act, w_branch = lax.optimization_barrier((w_pre, flat(kernel_two), flat(kernel_one)))

    stack_s = pltpu.VMEM((tile_x + 2, tile_y + 2, 3 * chans, tile_z), BF16)
    stack_o = jax.ShapeDtypeStruct((tile_x + 2, tile_y + 2, 3 * chans, tile_z), BF16)
    acc_s = pltpu.VMEM((tile_x + 4, tile_y, chans, tile_z), F32)
    acc_h = pltpu.VMEM((tile_x + 4, tile_y // 2, chans, tile_z), F32)
    tile_s = pltpu.VMEM((tile_x, tile_y, 3 * chans, tile_z), BF16)
    grad_s = pltpu.VMEM((9 * chans, 3 * chans), F32)

    activ, slope, in_pad = call(
        forward_kernel, [tile_b, jax.ShapeDtypeStruct(tile_shape, F32), pad_b], [stack_s, acc_s], scalars=1, flops=flops
    )(place, mask_f, w_pre, masked_in, *xr, *in_y)
    pre_grad, xs_even, xs_odd, grad_pad = call(
        backward_kernel, [tile_b, edge_b, edge_b, pad_b], [stack_s, acc_s], scalars=1, flops=flops
    )(place, w_act, slope, masked_grad, *xr, *grad_y)

    packed = 27 * chans * chans // (2 * chans)
    half = jax.ShapeDtypeStruct((packed, 2 * chans), F32)
    pre_xr = swap(xs_even, xs_odd, "gx")
    (packed_two,) = call(grad_two_kernel, [half], [tile_s, grad_s], flops=flops)(grad_pad, activ)
    pre_sends = y_sends(pre_grad, pre_xr, 0)
    pre_yr = swap(*pre_sends, "gy")
    keep, send = call(grad_one_kernel, [half, half], [tile_s, grad_s], scalars=1, flops=flops)(
        place, in_pad, pre_grad, packed_two
    )

    recv = xor_permute(send, 8)
    chunk = jax.ShapeDtypeStruct((packed // 4, 2 * chans), F32)
    parts = call(split_kernel, [chunk] * 4, scalars=1)(place, keep, recv)
    parts = [parts[0]] + [xor_permute(parts[d], 16 * d) for d in range(1, 4)]
    part = (parts[0] + parts[1]) + (parts[2] + parts[3])
    for masks in ((2, 4, 6), (1, 64, 65)):
        near, mid, far = [xor_permute(part, m) for m in masks]
        part = (part + near) + (mid + far)
    pieces = [part] + [xor_permute(part, 16 * d) for d in range(1, 4)]
    (own,) = call(join_kernel, [half], scalars=1)(place, *pieces)
    other = xor_permute(own, 8)
    grad_shape = jax.ShapeDtypeStruct((3, 3, 3, chans, chans), F32)

    def unpack(place_ref, own_ref, other_ref, one_ref, two_ref):
        unpack_kernel(place_ref, scale, own_ref, other_ref, one_ref, two_ref)

    grad_one, grad_two = call(unpack, [grad_shape, grad_shape], scalars=1)(place, own, other)

    half_b = jax.ShapeDtypeStruct((tile_x, tile_y // 2, chans, tile_z), BF16)
    low, stacked = call(
        branch_low_kernel, [half_b, stack_o], [acc_h], scalars=1, flops=flops // 2
    )(place, mask_f, w_branch, masked_grad, pre_grad, *pre_xr, *pre_yr)
    (high,) = call(branch_high_kernel, [half_b], [acc_h], flops=flops // 2)(mask_f, w_branch, masked_grad, stacked)
    grad_features = jnp.transpose(jnp.concatenate([low, high], axis=1), (2, 0, 1, 3))
    return grad_features, grad_one, grad_two


def solution(mesh):
    placed = (P(None, "gx", "gy", None), P(None, "gx", "gy", None), P("gx", "gy", None), P(), P())
    return jax.shard_map(
        body,
        mesh=mesh,
        in_specs=placed,
        out_specs=(P(None, "gx", "gy", None), P(), P()),
        check_vma=False,
    )
```

time: 159 us -> 128 us (0.81)
  the two profiles are of different devices: /device:TPU:1 before, /device:TPU:15 now
where the time goes in v2:
time: 128 us
  starting transfers between devices  43.2 us (34%)
  Pallas kernels  43.1 us (34%)
  waiting for transfers between devices  23.3 us (18%)
  local copies, waits for them, and re-layouts  13.1 us (10%)
  other arithmetic  4.46 us (3%)
    pallas_call x12, Pallas kernels, run(): pl.pallas_call(kernel, out_shape=tuple(outs), in_specs=specs, out_specs=t...  43.1 us
    ppermute x14, starting transfers between devices, xor_permute(): return lax.ppermute(value, AXES, [(i, i ^ mask) for i in range(total)])  16.5 us
    ppermute x5, starting transfers between devices, swap(): lax.ppermute(value_odd, axis, odd)  13.7 us
    ppermute x5, starting transfers between devices, swap(): lax.ppermute(value_even, axis, even)  13 us
    ppermute x14, waiting for transfers between devices, xor_permute(): return lax.ppermute(value, AXES, [(i, i ^ mask) for i in range(total)])  11.8 us
    ppermute x5, waiting for transfers between devices, swap(): lax.ppermute(value_odd, axis, odd)  11 us
    transpose x4, local copies, waits for them, and re-layouts, body(): jnp.transpose(w[::-1, ::-1, ::-1], (0, 3, 1, 2, 4))  3.47 us
    transpose x1, other arithmetic, body(): masked_in = jnp.transpose(features * mask_b[:, None], (1, 2, 0, 3))  3.33 us
  transfers between devices with their start and end apart: 24, of which 11 were waited for; matrix products, arithmetic and copies ran while one was open for 12% of the time, Pallas kernels for 16%

profile of v2, /device:TPU:15, one launch (start us, length us, event | category | flops | bytes accessed | tf_op | source)
XLA Modules:
  0.0 128.1 jit_solution(12786671037220213554)
XLA Ops:
  0.6 0.7 convert_bitcast_fusion
  1.4 0.1 broadcast_in_dim.8
  1.4 0.1 convert_element_type.32
  1.5 1.2 constant_dynamic-slice_fusion
  2.7 0.1 fusion.3
  2.8 0.8 collective-permute-start
  3.6 3.4 %collective-permute-start.1 = (bf16[2,8,64,128]{3,2,1,0:T(8,128)(2,1)S(1)}, bf16[2,8,64,128]{3,2,1,0:T(8,128)(2,1)S(1)}, u32[]{:S(2)}, u32[]{:S(2)}) collective-permute-start(bf16[2,8,64,128]{3,2,1,0:T(8,128)(2,1)S(1)} %pad_maximum_fusion.1), channel_id=1, source_target_pairs={{8,16},{16,8},{24,32},{32,24},{40,48},{48,40},{56,64},{64,56},{72,... | collective-permute-start | bytes 786440 | tf_op jit(solution)/shard_map/ppermute | solution.py:30
  7.0 0.1 pad_add_fusion.place.place_ref
  7.1 3.3 %fusion = (bf16[8,8,64,128]{3,2,1,0:T(8,128)(2,1)S(1)}, bf16[8,8,64,128]{3,2,1,0:T(8,128)(2,1)S(1)}) fusion(bf16[64,8,8,128]{3,2,1,0:T(8,128)(2,1)} %param.5, bf16[128]{0:T(256)(128)(2,1)S(1)} %convert_element_type.32, bf16[64,8,8,128]{3,2,1,0:T(8,128)(2,1)} %param.6), kind=kLoop, calls=%fused_computation.2 | loop fusion | flops 1048576 | bytes 4194560 | tf_op jit(solution)/shard_map/transpose | solution.py:301
  10.4 3.0 %collective-permute-done.1.xr_odd = bf16[2,8,64,128]{3,2,1,0:T(8,128)(2,1)S(1)} collective-permute-done((bf16[2,8,64,128]{3,2,1,0:T(8,128)(2,1)S(1)}, bf16[2,8,64,128]{3,2,1,0:T(8,128)(2,1)S(1)}, u32[]{:S(2)}, u32[]{:S(2)}) %collective-permute-start.1) | collective-permute-done | bytes 262176 | tf_op jit(solution)/shard_map/ppermute | solution.py:30
  13.4 1.3 %shard_map.76 = (bf16[10,64,128]{2,1,0:T(8,128)(2,1)}, bf16[10,64,128]{2,1,0:T(8,128)(2,1)}) custom-call(s32[3]{0:T(128)S(1)} %pad_add_fusion.place.place_ref, bf16[8,8,64,128]{3,2,1,0:T(8,128)(2,1)S(1)} %get-tuple-element.69.tile, bf16[2,8,64,128]{3,2,1,0:T(8,128)(2,1)S(1)} %collective-permute-done.xr_even, ...), custom_call_target="tpu_custom_call" | custom-call | bytes 1900556 | tf_op jit(solution)/shard_map/pallas_call | solution.py:270
  14.7 3.7 %collective-permute-start.2 = (bf16[10,64,128]{2,1,0:T(8,128)(2,1)}, bf16[10,64,128]{2,1,0:T(8,128)(2,1)S(1)}, u32[]{:S(2)}, u32[]{:S(2)}) collective-permute-start(bf16[10,64,128]{2,1,0:T(8,128)(2,1)} %get-tuple-element.32), channel_id=1, source_target_pairs={{0,1},{1,0},{2,3},{3,2},{4,5},{5,4},{6,7},{7,6},{8,9},{9,8},{10,11... | collective-permute-start | bytes 491528 | tf_op jit(solution)/shard_map/ppermute | solution.py:30
  18.4 1.9 %collective-permute-start.3 = (bf16[10,64,128]{2,1,0:T(8,128)(2,1)}, bf16[10,64,128]{2,1,0:T(8,128)(2,1)}, u32[]{:S(2)}, u32[]{:S(2)}) collective-permute-start(bf16[10,64,128]{2,1,0:T(8,128)(2,1)} %get-tuple-element.33), channel_id=1, source_target_pairs={{1,2},{2,1},{3,4},{4,3},{5,6},{6,5},{9,10},{10,9},{11,12},{12,11},... | collective-permute-start | bytes 491528 | tf_op jit(solution)/shard_map/ppermute | solution.py:30
  20.4 0.1 broadcast_in_dim.7
  20.4 0.1 convert_element_type.29.mask
  20.5 1.2 copy.19
  21.7 1.5 %reshape.49.weights = bf16[192,576]{1,0:T(8,128)(2,1)S(1)} reshape(bf16[3,64,3,3,64]{4,3,2,1,0:T(4,128)(2,1)} %copy.19) | data formatting | bytes 442368 | tf_op jit(solution)/shard_map/reshape | solution.py:321
  23.2 1.0 reverse_bitcast_fusion
  24.2 1.2 copy.20
  25.4 1.5 %reshape.50.weights = bf16[192,576]{1,0:T(8,128)(2,1)S(1)} reshape(bf16[3,64,3,3,64]{4,3,2,1,0:T(4,128)(2,1)} %copy.20) | data formatting | bytes 442368 | tf_op jit(solution)/shard_map/reshape | solution.py:321
  26.9 2.1 %copy.18 = bf16[3,64,3,3,64]{4,3,2,1,0:T(4,128)(2,1)} copy(bf16[3,64,3,3,64]{1,4,3,2,0:T(8,128)(2,1)} %bitcast.50) | data formatting | bytes 442368 | tf_op jit(solution)/shard_map/transpose | solution.py:320
  29.0 1.5 %reshape.48.weights = bf16[192,576]{1,0:T(8,128)(2,1)S(1)} reshape(bf16[3,64,3,3,64]{4,3,2,1,0:T(4,128)(2,1)} %copy.18) | data formatting | bytes 442368 | tf_op jit(solution)/shard_map/reshape | solution.py:320
  30.5 0.6 shard_map.78
  31.0 4.0 %collective-permute-start.4 = (bf16[10,64,128]{2,1,0:T(8,128)(2,1)S(1)}, bf16[10,64,128]{2,1,0:T(8,128)(2,1)S(1)}, u32[]{:S(2)}, u32[]{:S(2)}) collective-permute-start(bf16[10,64,128]{2,1,0:T(8,128)(2,1)S(1)} %get-tuple-element.35), channel_id=1, source_target_pairs={{0,1},{1,0},{2,3},{3,2},{4,5},{5,4},{6,7},{7,6},{8,9},{9,8},{10,11... | collective-permute-start | bytes 491528 | tf_op jit(solution)/shard_map/ppermute | solution.py:30
  35.1 1.9 %collective-permute-start.5 = (bf16[10,64,128]{2,1,0:T(8,128)(2,1)S(1)}, bf16[10,64,128]{2,1,0:T(8,128)(2,1)S(1)}, u32[]{:S(2)}, u32[]{:S(2)}) collective-permute-start(bf16[10,64,128]{2,1,0:T(8,128)(2,1)S(1)} %get-tuple-element.36), channel_id=1, source_target_pairs={{1,2},{2,1},{3,4},{4,3},{5,6},{6,5},{9,10},{10,9},{11,12},{12,11},... | collective-permute-start | bytes 491528 | tf_op jit(solution)/shard_map/ppermute | solution.py:30
  37.0 8.9 %shard_map.77 = (bf16[8,8,64,128]{3,2,1,0:T(8,128)(2,1)S(1)}, f32[8,8,64,128]{3,2,1,0:T(8,128)S(1)}, bf16[10,10,64,128]{3,2,1,0:T(8,128)(2,1)S(1)}) custom-call(s32[3]{0:T(128)S(1)} %pad_add_fusion.place.place_ref, f32[1,128]{1,0:T(1,128)S(1)} %convert_element_type.29.mask, bf16[192,576]{1,0:T(8,128)(2,1)S(1)} %reshape.48.weights, ...), custom_call_target="tpu_custom_call" | custom-call | flops 1811939328 | bytes 6906380 | tf_op jit(solution)/shard_map/pallas_call | solution.py:270
  46.0 7.9 %shard_map.79 = (bf16[8,8,64,128]{3,2,1,0:T(8,128)(2,1)S(1)}, bf16[1,8,64,128]{3,2,1,0:T(8,128)(2,1)S(1)}, bf16[1,8,64,128]{3,2,1,0:T(8,128)(2,1)S(1)}, bf16[10,10,64,128]{3,2,1,0:T(8,128)(2,1)S(1)}) custom-call(s32[3]{0:T(128)S(1)} %pad_add_fusion.place.place_ref, bf16[192,576]{1,0:T(8,128)(2,1)S(1)} %reshape.49.weights, ...), custom_call_target="tpu_custom_call" | custom-call | flops 1811939328 | bytes 7168012 | tf_op jit(solution)/shard_map/pallas_call | solution.py:270
  53.9 5.1 %shard_map.83.packed_two = f32[864,128]{1,0:T(8,128)S(1)} custom-call(bf16[10,10,64,128]{3,2,1,0:T(8,128)(2,1)S(1)} %get-tuple-element.45.grad_pad, bf16[8,8,64,128]{3,2,1,0:T(8,128)(2,1)S(1)} %get-tuple-element.46.activ), custom_call_target="tpu_custom_call" | custom-call | flops 1811939328 | bytes 3129344 | tf_op jit(solution)/shard_map/pallas_call | solution.py:270
  59.0 5.7 %shard_map.84 = (f32[864,128]{1,0:T(8,128)S(1)}, f32[864,128]{1,0:T(8,128)S(1)}) custom-call(s32[3]{0:T(128)S(1)} %pad_add_fusion.place.place_ref, bf16[10,10,64,128]{3,2,1,0:T(8,128)(2,1)S(1)} %get-tuple-element.44.in_pad, bf16[8,8,64,128]{3,2,1,0:T(8,128)(2,1)S(1)} %get-tuple-element.37.tile.pre_grad, f32[864,128]{1,0:T(8,128)S(1)} %shard_map.83.packed_two), custom_call_target="tpu_custom_call" | custom-call | flops 1811939328 | bytes 4014092 | tf_op jit(solution)/shard_map/pallas_call | solution.py:270
  64.7 0.1 collective-permute-start.10
  64.8 1.8 %collective-permute-done.10.recv = f32[864,128]{1,0:T(8,128)S(1)} collective-permute-done((f32[864,128]{1,0:T(8,128)S(1)}, f32[864,128]{1,0:T(8,128)S(1)}, u32[]{:S(2)}, u32[]{:S(2)}) %collective-permute-start.10) | collective-permute-done | bytes 442400 | tf_op jit(solution)/shard_map/ppermute | solution.py:25
  66.6 0.6 shard_map.85
  67.2 0.1 collective-permute-start.11
  67.3 0.1 collective-permute-start.12
  67.3 3.8 %collective-permute-start.13 = (f32[216,128]{1,0:T(8,128)S(1)}, f32[216,128]{1,0:T(8,128)S(1)}, u32[]{:S(2)}, u32[]{:S(2)}) collective-permute-start(f32[216,128]{1,0:T(8,128)S(1)} %get-tuple-element.52), channel_id=1, source_target_pairs={{0,48},{1,49},{2,50},{3,51},{4,52},{5,53},{6,54},{7,55},{8,56},{9,... | collective-permute-start | bytes 331784 | tf_op jit(solution)/shard_map/ppermute | solution.py:25
  71.1 0.6 collective-permute-done.11
  71.7 1.6 %collective-permute-done.12 = f32[216,128]{1,0:T(8,128)S(1)} collective-permute-done((f32[216,128]{1,0:T(8,128)S(1)}, f32[216,128]{1,0:T(8,128)S(1)}, u32[]{:S(2)}, u32[]{:S(2)}) %collective-permute-start.12) | collective-permute-done | bytes 110624 | tf_op jit(solution)/shard_map/ppermute | solution.py:25
  73.3 2.9 %collective-permute-done.13 = f32[216,128]{1,0:T(8,128)S(1)} collective-permute-done((f32[216,128]{1,0:T(8,128)S(1)}, f32[216,128]{1,0:T(8,128)S(1)}, u32[]{:S(2)}, u32[]{:S(2)}) %collective-permute-start.13) | collective-permute-done | bytes 110624 | tf_op jit(solution)/shard_map/ppermute | solution.py:25
  76.2 1.3 collective-permute-start.16
  77.5 0.8 collective-permute-start.15
  78.3 1.2 collective-permute-start.14
  79.6 0.9 collective-permute-done.16
  80.5 2.2 %collective-permute-done.15 = f32[216,128]{1,0:T(8,128)S(1)} collective-permute-done((f32[216,128]{1,0:T(8,128)S(1)}, f32[216,128]{1,0:T(8,128)S(1)}, u32[]{:S(2)}, u32[]{:S(2)}) %collective-permute-start.15) | collective-permute-done | bytes 110624 | tf_op jit(solution)/shard_map/ppermute | solution.py:25
  82.6 1.8 %collective-permute-done.14 = f32[216,128]{1,0:T(8,128)S(1)} collective-permute-done((f32[216,128]{1,0:T(8,128)S(1)}, f32[216,128]{1,0:T(8,128)S(1)}, u32[]{:S(2)}, u32[]{:S(2)}) %collective-permute-start.14) | collective-permute-done | bytes 110624 | tf_op jit(solution)/shard_map/ppermute | solution.py:25
  84.5 4.5 %collective-permute-start.19 = (f32[216,128]{1,0:T(8,128)S(1)}, f32[216,128]{1,0:T(8,128)S(1)}, u32[]{:S(2)}, u32[]{:S(2)}) collective-permute-start(f32[216,128]{1,0:T(8,128)S(1)} %add_add_fusion.1), channel_id=1, source_target_pairs={{0,65},{1,64},{2,67},{3,66},{4,69},{5,68},{6,71},{7,70},{8,73},{9,... | collective-permute-start | bytes 331784 | tf_op jit(solution)/shard_map/ppermute | solution.py:25
  88.9 1.3 collective-permute-start.17
  90.2 2.5 %collective-permute-start.6 = (bf16[1,8,64,128]{3,2,1,0:T(8,128)(2,1)S(1)}, bf16[1,8,64,128]{3,2,1,0:T(8,128)(2,1)S(1)}, u32[]{:S(2)}, u32[]{:S(2)}) collective-permute-start(bf16[1,8,64,128]{3,2,1,0:T(8,128)(2,1)S(1)} %get-tuple-element.38), channel_id=1, source_target_pairs={{0,8},{8,0},{16,24},{24,16},{32,40},{40,32},{48,56},{56,48},{64,72... | collective-permute-start | bytes 393224 | tf_op jit(solution)/shard_map/ppermute | solution.py:30
  92.6 3.0 %collective-permute-start.7 = (bf16[1,8,64,128]{3,2,1,0:T(8,128)(2,1)S(1)}, bf16[1,8,64,128]{3,2,1,0:T(8,128)(2,1)S(1)}, u32[]{:S(2)}, u32[]{:S(2)}) collective-permute-start(bf16[1,8,64,128]{3,2,1,0:T(8,128)(2,1)S(1)} %get-tuple-element.39), channel_id=1, source_target_pairs={{8,16},{16,8},{24,32},{32,24},{40,48},{48,40},{56,64},{64,56},{72,... | collective-permute-start | bytes 393224 | tf_op jit(solution)/shard_map/ppermute | solution.py:30
  95.7 0.9 collective-permute-start.22
  96.6 1.2 collective-permute-start.21
  97.8 1.2 collective-permute-start.20
  99.0 3.7 %collective-permute-done.7.xr_odd = bf16[1,8,64,128]{3,2,1,0:T(8,128)(2,1)S(1)} collective-permute-done((bf16[1,8,64,128]{3,2,1,0:T(8,128)(2,1)S(1)}, bf16[1,8,64,128]{3,2,1,0:T(8,128)(2,1)S(1)}, u32[]{:S(2)}, u32[]{:S(2)}) %collective-permute-start.7) | collective-permute-done | bytes 131104 | tf_op jit(solution)/shard_map/ppermute | solution.py:30
  102.7 0.6 shard_map.80
  103.3 2.0 %collective-permute-start.8 = (bf16[10,64,128]{2,1,0:T(8,128)(2,1)S(1)}, bf16[10,64,128]{2,1,0:T(8,128)(2,1)S(1)}, u32[]{:S(2)}, u32[]{:S(2)}) collective-permute-start(bf16[10,64,128]{2,1,0:T(8,128)(2,1)S(1)} %get-tuple-element.40), channel_id=1, source_target_pairs={{0,1},{1,0},{2,3},{3,2},{4,5},{5,4},{6,7},{7,6},{8,9},{9,8},{10,11... | collective-permute-start | bytes 491528 | tf_op jit(solution)/shard_map/ppermute | solution.py:30
  105.3 3.5 %collective-permute-start.9 = (bf16[10,64,128]{2,1,0:T(8,128)(2,1)S(1)}, bf16[10,64,128]{2,1,0:T(8,128)(2,1)S(1)}, u32[]{:S(2)}, u32[]{:S(2)}) collective-permute-start(bf16[10,64,128]{2,1,0:T(8,128)(2,1)S(1)} %get-tuple-element.41), channel_id=1, source_target_pairs={{1,2},{2,1},{3,4},{4,3},{5,6},{6,5},{9,10},{10,9},{11,12},{12,11},... | collective-permute-start | bytes 491528 | tf_op jit(solution)/shard_map/ppermute | solution.py:30
  108.9 0.6 shard_map.86.own_ref
  109.5 0.1 collective-permute-start.23
  109.6 0.5 collective-permute-done.8.yr_even
  110.1 4.3 %collective-permute-done.9.yr_odd = bf16[10,64,128]{2,1,0:T(8,128)(2,1)S(1)} collective-permute-done((bf16[10,64,128]{2,1,0:T(8,128)(2,1)S(1)}, bf16[10,64,128]{2,1,0:T(8,128)(2,1)S(1)}, u32[]{:S(2)}, u32[]{:S(2)}) %collective-permute-start.9) | collective-permute-done | bytes 163872 | tf_op jit(solution)/shard_map/ppermute | solution.py:30
  114.4 6.1 %shard_map.81 = (bf16[8,4,64,128]{3,2,1,0:T(8,128)(2,1)S(1)}, bf16[10,10,192,128]{3,2,1,0:T(8,128)(2,1)S(1)}) custom-call(s32[3]{0:T(128)S(1)} %pad_add_fusion.place.place_ref, f32[1,128]{1,0:T(1,128)S(1)} %convert_element_type.29.mask, bf16[192,576]{1,0:T(8,128)(2,1)S(1)} %reshape.50.weights, bf16[8,8,64,128]{3,2,1,0:T(8,128)(2,1)S(1)} %get-tuple-element.70.tile.base, ...), custom_call_target="tpu_custom_call" | custom-call | flops 905969664 | bytes 8348172 | tf_op jit(solution)/shard_map/pallas_call | solution.py:270
  120.6 3.4 %shard_map.82 = bf16[8,4,64,128]{3,2,1,0:T(8,128)(2,1)S(1)} custom-call(f32[1,128]{1,0:T(1,128)S(1)} %convert_element_type.29.mask, bf16[192,576]{1,0:T(8,128)(2,1)S(1)} %reshape.50.weights, bf16[8,8,64,128]{3,2,1,0:T(8,128)(2,1)S(1)} %get-tuple-element.70.tile.base, bf16[10,10,192,128]{3,2,1,0:T(8,128)(2,1)S(1)} %get-tuple-element.43.stack), custom_call_target="tpu_custom_call" | custom-call | flops 905969664 | bytes 6709760 | tf_op jit(solution)/shard_map/pallas_call | solution.py:270
  124.0 0.1 maximum_bitcast_fusion
  124.1 1.6 %copy.27 = bf16[64,8,8,128]{3,2,1,0:T(8,128)(2,1)} copy(bf16[64,8,8,128]{3,0,2,1:T(8,128)(2,1)S(1)} %maximum_bitcast_fusion) | data formatting | bytes 2097152
  125.7 2.3 %shard_map.87 = (f32[3,3,3,64,64]{4,3,2,1,0:T(8,128)}, f32[3,3,3,64,64]{4,3,2,1,0:T(8,128)}) custom-call(s32[3]{0:T(128)S(1)} %pad_add_fusion.place.place_ref, f32[864,128]{1,0:T(8,128)S(1)} %shard_map.86.own_ref, f32[864,128]{1,0:T(8,128)S(1)} %collective-permute-done.23.other_ref), custom_call_target="tpu_custom_call" | custom-call | bytes 1769484 | tf_op jit(solution)/shard_map/pallas_call | solution.py:270
  (22 shorter events, 0.2 us)
Async XLA Ops:
  2.8 7.6 %collective-permute-start = (bf16[2,8,64,128]{3,2,1,0:T(8,128)(2,1)S(1)}, bf16[2,8,64,128]{3,2,1,0:T(8,128)(2,1)S(1)}, u32[]{:S(2)}, u32[]{:S(2)}) collective-permute-start(bf16[2,8,64,128]{3,2,1,0:T(8,128)(2,1)S(1)} %pad_maximum_fusion), channel_id=1, source_target_pairs={{0,8},{8,0},{16,24},{24,16},{32,40},{40,32},{48,56},{56,48},{64,72... | collective-permute-start | bytes 786440 | tf_op jit(solution)/shard_map/ppermute | solution.py:30
  3.6 9.8 %collective-permute-start.1 = (bf16[2,8,64,128]{3,2,1,0:T(8,128)(2,1)S(1)}, bf16[2,8,64,128]{3,2,1,0:T(8,128)(2,1)S(1)}, u32[]{:S(2)}, u32[]{:S(2)}) collective-permute-start(bf16[2,8,64,128]{3,2,1,0:T(8,128)(2,1)S(1)} %pad_maximum_fusion.1), channel_id=1, source_target_pairs={{8,16},{16,8},{24,32},{32,24},{40,48},{48,40},{56,64},{64,56},{72,... | collective-permute-start | bytes 786440 | tf_op jit(solution)/shard_map/ppermute | solution.py:30
  7.1 13.2 %copy-start = (bf16[3,3,3,64,64]{4,3,2,1,0:T(8,128)(2,1)S(1)}, bf16[3,3,3,64,64]{4,3,2,1,0:T(8,128)(2,1)}, u32[]{:S(2)}) copy-start(bf16[3,3,3,64,64]{4,3,2,1,0:T(8,128)(2,1)} %param.9) | copy-start | bytes 663556
  14.7 22.3 %collective-permute-start.2 = (bf16[10,64,128]{2,1,0:T(8,128)(2,1)}, bf16[10,64,128]{2,1,0:T(8,128)(2,1)S(1)}, u32[]{:S(2)}, u32[]{:S(2)}) collective-permute-start(bf16[10,64,128]{2,1,0:T(8,128)(2,1)} %get-tuple-element.32), channel_id=1, source_target_pairs={{0,1},{1,0},{2,3},{3,2},{4,5},{5,4},{6,7},{7,6},{8,9},{9,8},{10,11... | collective-permute-start | bytes 491528 | tf_op jit(solution)/shard_map/ppermute | solution.py:30
  18.4 18.6 %collective-permute-start.3 = (bf16[10,64,128]{2,1,0:T(8,128)(2,1)}, bf16[10,64,128]{2,1,0:T(8,128)(2,1)}, u32[]{:S(2)}, u32[]{:S(2)}) collective-permute-start(bf16[10,64,128]{2,1,0:T(8,128)(2,1)} %get-tuple-element.33), channel_id=1, source_target_pairs={{1,2},{2,1},{3,4},{4,3},{5,6},{6,5},{9,10},{10,9},{11,12},{12,11},... | collective-permute-start | bytes 491528 | tf_op jit(solution)/shard_map/ppermute | solution.py:30
  31.0 14.9 %collective-permute-start.4 = (bf16[10,64,128]{2,1,0:T(8,128)(2,1)S(1)}, bf16[10,64,128]{2,1,0:T(8,128)(2,1)S(1)}, u32[]{:S(2)}, u32[]{:S(2)}) collective-permute-start(bf16[10,64,128]{2,1,0:T(8,128)(2,1)S(1)} %get-tuple-element.35), channel_id=1, source_target_pairs={{0,1},{1,0},{2,3},{3,2},{4,5},{5,4},{6,7},{7,6},{8,9},{9,8},{10,11... | collective-permute-start | bytes 491528 | tf_op jit(solution)/shard_map/ppermute | solution.py:30
  35.1 10.9 %collective-permute-start.5 = (bf16[10,64,128]{2,1,0:T(8,128)(2,1)S(1)}, bf16[10,64,128]{2,1,0:T(8,128)(2,1)S(1)}, u32[]{:S(2)}, u32[]{:S(2)}) collective-permute-start(bf16[10,64,128]{2,1,0:T(8,128)(2,1)S(1)} %get-tuple-element.36), channel_id=1, source_target_pairs={{1,2},{2,1},{3,4},{4,3},{5,6},{6,5},{9,10},{10,9},{11,12},{12,11},... | collective-permute-start | bytes 491528 | tf_op jit(solution)/shard_map/ppermute | solution.py:30
  64.7 1.9 %collective-permute-start.10 = (f32[864,128]{1,0:T(8,128)S(1)}, f32[864,128]{1,0:T(8,128)S(1)}, u32[]{:S(2)}, u32[]{:S(2)}) collective-permute-start(f32[864,128]{1,0:T(8,128)S(1)} %get-tuple-element.48), channel_id=1, source_target_pairs={{0,8},{1,9},{2,10},{3,11},{4,12},{5,13},{6,14},{7,15},{8,0},{9,1},... | collective-permute-start | bytes 1327112 | tf_op jit(solution)/shard_map/ppermute | solution.py:25
  67.2 4.6 %collective-permute-start.11 = (f32[216,128]{1,0:T(8,128)S(1)}, f32[216,128]{1,0:T(8,128)S(1)}, u32[]{:S(2)}, u32[]{:S(2)}) collective-permute-start(f32[216,128]{1,0:T(8,128)S(1)} %get-tuple-element.50), channel_id=1, source_target_pairs={{0,16},{1,17},{2,18},{3,19},{4,20},{5,21},{6,22},{7,23},{8,24},{9,... | collective-permute-start | bytes 331784 | tf_op jit(solution)/shard_map/ppermute | solution.py:25
  67.3 6.1 %collective-permute-start.12 = (f32[216,128]{1,0:T(8,128)S(1)}, f32[216,128]{1,0:T(8,128)S(1)}, u32[]{:S(2)}, u32[]{:S(2)}) collective-permute-start(f32[216,128]{1,0:T(8,128)S(1)} %get-tuple-element.51), channel_id=1, source_target_pairs={{0,32},{1,33},{2,34},{3,35},{4,36},{5,37},{6,38},{7,39},{8,40},{9,... | collective-permute-start | bytes 331784 | tf_op jit(solution)/shard_map/ppermute | solution.py:25
  67.3 8.9 %collective-permute-start.13 = (f32[216,128]{1,0:T(8,128)S(1)}, f32[216,128]{1,0:T(8,128)S(1)}, u32[]{:S(2)}, u32[]{:S(2)}) collective-permute-start(f32[216,128]{1,0:T(8,128)S(1)} %get-tuple-element.52), channel_id=1, source_target_pairs={{0,48},{1,49},{2,50},{3,51},{4,52},{5,53},{6,54},{7,55},{8,56},{9,... | collective-permute-start | bytes 331784 | tf_op jit(solution)/shard_map/ppermute | solution.py:25
  76.2 4.2 %collective-permute-start.16 = (f32[216,128]{1,0:T(8,128)S(1)}, f32[216,128]{1,0:T(8,128)S(1)}, u32[]{:S(2)}, u32[]{:S(2)}) collective-permute-start(f32[216,128]{1,0:T(8,128)S(1)} %add_add_fusion.2), channel_id=1, source_target_pairs={{0,6},{1,7},{2,4},{3,5},{4,2},{5,3},{6,0},{7,1},{8,14},{9,15},{10,... | collective-permute-start | bytes 331784 | tf_op jit(solution)/shard_map/ppermute | solution.py:25
  77.5 5.1 %collective-permute-start.15 = (f32[216,128]{1,0:T(8,128)S(1)}, f32[216,128]{1,0:T(8,128)S(1)}, u32[]{:S(2)}, u32[]{:S(2)}) collective-permute-start(f32[216,128]{1,0:T(8,128)S(1)} %add_add_fusion.2), channel_id=1, source_target_pairs={{0,4},{1,5},{2,6},{3,7},{4,0},{5,1},{6,2},{7,3},{8,12},{9,13},{10,... | collective-permute-start | bytes 331784 | tf_op jit(solution)/shard_map/ppermute | solution.py:25
  78.3 6.1 %collective-permute-start.14 = (f32[216,128]{1,0:T(8,128)S(1)}, f32[216,128]{1,0:T(8,128)S(1)}, u32[]{:S(2)}, u32[]{:S(2)}) collective-permute-start(f32[216,128]{1,0:T(8,128)S(1)} %add_add_fusion.2), channel_id=1, source_target_pairs={{0,2},{1,3},{2,0},{3,1},{4,6},{5,7},{6,4},{7,5},{8,10},{9,11},{10,... | collective-permute-start | bytes 331784 | tf_op jit(solution)/shard_map/ppermute | solution.py:25
  84.5 11.2 %collective-permute-start.19 = (f32[216,128]{1,0:T(8,128)S(1)}, f32[216,128]{1,0:T(8,128)S(1)}, u32[]{:S(2)}, u32[]{:S(2)}) collective-permute-start(f32[216,128]{1,0:T(8,128)S(1)} %add_add_fusion.1), channel_id=1, source_target_pairs={{0,65},{1,64},{2,67},{3,66},{4,69},{5,68},{6,71},{7,70},{8,73},{9,... | collective-permute-start | bytes 331784 | tf_op jit(solution)/shard_map/ppermute | solution.py:25
  88.9 6.7 %collective-permute-start.18 = (f32[216,128]{1,0:T(8,128)S(1)}, f32[216,128]{1,0:T(8,128)S(1)}, u32[]{:S(2)}, u32[]{:S(2)}) collective-permute-start(f32[216,128]{1,0:T(8,128)S(1)} %add_add_fusion.1), channel_id=1, source_target_pairs={{0,64},{1,65},{2,66},{3,67},{4,68},{5,69},{6,70},{7,71},{8,72},{9,... | collective-permute-start | bytes 331784 | tf_op jit(solution)/shard_map/ppermute | solution.py:25
  88.9 6.7 %collective-permute-start.17 = (f32[216,128]{1,0:T(8,128)S(1)}, f32[216,128]{1,0:T(8,128)S(1)}, u32[]{:S(2)}, u32[]{:S(2)}) collective-permute-start(f32[216,128]{1,0:T(8,128)S(1)} %add_add_fusion.1), channel_id=1, source_target_pairs={{0,1},{1,0},{2,3},{3,2},{4,5},{5,4},{6,7},{7,6},{8,9},{9,8},{10,11... | collective-permute-start | bytes 331784 | tf_op jit(solution)/shard_map/ppermute | solution.py:25
  90.2 8.8 %collective-permute-start.6 = (bf16[1,8,64,128]{3,2,1,0:T(8,128)(2,1)S(1)}, bf16[1,8,64,128]{3,2,1,0:T(8,128)(2,1)S(1)}, u32[]{:S(2)}, u32[]{:S(2)}) collective-permute-start(bf16[1,8,64,128]{3,2,1,0:T(8,128)(2,1)S(1)} %get-tuple-element.38), channel_id=1, source_target_pairs={{0,8},{8,0},{16,24},{24,16},{32,40},{40,32},{48,56},{56,48},{64,72... | collective-permute-start | bytes 393224 | tf_op jit(solution)/shard_map/ppermute | solution.py:30
  92.6 10.1 %collective-permute-start.7 = (bf16[1,8,64,128]{3,2,1,0:T(8,128)(2,1)S(1)}, bf16[1,8,64,128]{3,2,1,0:T(8,128)(2,1)S(1)}, u32[]{:S(2)}, u32[]{:S(2)}) collective-permute-start(bf16[1,8,64,128]{3,2,1,0:T(8,128)(2,1)S(1)} %get-tuple-element.39), channel_id=1, source_target_pairs={{8,16},{16,8},{24,32},{32,24},{40,48},{48,40},{56,64},{64,56},{72,... | collective-permute-start | bytes 393224 | tf_op jit(solution)/shard_map/ppermute | solution.py:30
  95.7 13.2 %collective-permute-start.22 = (f32[216,128]{1,0:T(8,128)S(1)}, f32[216,128]{1,0:T(8,128)S(1)}, u32[]{:S(2)}, u32[]{:S(2)}) collective-permute-start(f32[216,128]{1,0:T(8,128)S(1)} %add_add_fusion.refs_0_), channel_id=1, source_target_pairs={{0,48},{1,49},{2,50},{3,51},{4,52},{5,53},{6,54},{7,55},{8,56},{9,... | collective-permute-start | bytes 331784 | tf_op jit(solution)/shard_map/ppermute | solution.py:25
  96.6 12.3 %collective-permute-start.21 = (f32[216,128]{1,0:T(8,128)S(1)}, f32[216,128]{1,0:T(8,128)S(1)}, u32[]{:S(2)}, u32[]{:S(2)}) collective-permute-start(f32[216,128]{1,0:T(8,128)S(1)} %add_add_fusion.refs_0_), channel_id=1, source_target_pairs={{0,32},{1,33},{2,34},{3,35},{4,36},{5,37},{6,38},{7,39},{8,40},{9,... | collective-permute-start | bytes 331784 | tf_op jit(solution)/shard_map/ppermute | solution.py:25
  97.8 11.1 %collective-permute-start.20 = (f32[216,128]{1,0:T(8,128)S(1)}, f32[216,128]{1,0:T(8,128)S(1)}, u32[]{:S(2)}, u32[]{:S(2)}) collective-permute-start(f32[216,128]{1,0:T(8,128)S(1)} %add_add_fusion.refs_0_), channel_id=1, source_target_pairs={{0,16},{1,17},{2,18},{3,19},{4,20},{5,21},{6,22},{7,23},{8,24},{9,... | collective-permute-start | bytes 331784 | tf_op jit(solution)/shard_map/ppermute | solution.py:25
  103.3 6.8 %collective-permute-start.8 = (bf16[10,64,128]{2,1,0:T(8,128)(2,1)S(1)}, bf16[10,64,128]{2,1,0:T(8,128)(2,1)S(1)}, u32[]{:S(2)}, u32[]{:S(2)}) collective-permute-start(bf16[10,64,128]{2,1,0:T(8,128)(2,1)S(1)} %get-tuple-element.40), channel_id=1, source_target_pairs={{0,1},{1,0},{2,3},{3,2},{4,5},{5,4},{6,7},{7,6},{8,9},{9,8},{10,11... | collective-permute-start | bytes 491528 | tf_op jit(solution)/shard_map/ppermute | solution.py:30
  105.3 9.1 %collective-permute-start.9 = (bf16[10,64,128]{2,1,0:T(8,128)(2,1)S(1)}, bf16[10,64,128]{2,1,0:T(8,128)(2,1)S(1)}, u32[]{:S(2)}, u32[]{:S(2)}) collective-permute-start(bf16[10,64,128]{2,1,0:T(8,128)(2,1)S(1)} %get-tuple-element.41), channel_id=1, source_target_pairs={{1,2},{2,1},{3,4},{4,3},{5,6},{6,5},{9,10},{10,9},{11,12},{12,11},... | collective-permute-start | bytes 491528 | tf_op jit(solution)/shard_map/ppermute | solution.py:30
  109.5 16.2 %collective-permute-start.23 = (f32[864,128]{1,0:T(8,128)S(1)}, f32[864,128]{1,0:T(8,128)S(1)}, u32[]{:S(2)}, u32[]{:S(2)}) collective-permute-start(f32[864,128]{1,0:T(8,128)S(1)} %shard_map.86.own_ref), channel_id=1, source_target_pairs={{0,8},{1,9},{2,10},{3,11},{4,12},{5,13},{6,14},{7,15},{8,0},{9,1},... | collective-permute-start | bytes 1327112 | tf_op jit(solution)/shard_map/ppermute | solution.py:25

commit v3 on v2

--- a/solution.py
+++ b/solution.py
@@ -47,22 +47,18 @@
     return even, size + 1 - even
 
 
-def stack_padded(stack, place, tile, xr_even, xr_odd, yr_even, yr_odd, which):
+def pad_tile(padded, place, tile, xr_even, xr_odd, yr_even, yr_odd, which):
     size_x, size_y = tile.shape[0], tile.shape[1]
     x_even, x_odd = sides(place[0], size_x)
     y_even, y_odd = sides(place[1], size_y)
-    stack_row(stack, x_even, 1, xr_even[which])
-    stack_row(stack, x_odd, 1, xr_odd[which])
-
-    def column(i, carry):
-        stack_row(stack, i, y_even, yr_even[pl.ds(i, 1)])
-        stack_row(stack, i, y_odd, yr_odd[pl.ds(i, 1)])
-        return carry
-
-    lax.fori_loop(0, size_x + 2, column, 0)
+    padded[x_even, 1 : size_y + 1] = xr_even[which]
+    padded[x_odd, 1 : size_y + 1] = xr_odd[which]
+    for i in range(size_x + 2):
+        padded[i, y_even] = yr_even[i]
+        padded[i, y_odd] = yr_odd[i]
 
     def body(i, carry):
-        stack_row(stack, i + 1, 1, tile[i])
+        padded[i + 1, 1 : size_y + 1] = tile[i]
         return carry
 
     lax.fori_loop(0, size_x, body, 0)
@@ -78,82 +74,79 @@
             out[i + 1] = tile[i, edge]
 
 
-def conv_stack(stack, weights, acc, first=0):
-    wide, _, deep, depth = stack.shape
-    tall = acc.shape[1]
-    chans = deep // 3
-    acc[0:2] = jnp.zeros((2,) + acc.shape[1:], F32)
-
-    def body(i, carry):
-        for y in range(0, tall, 2):
-            at = first + y
-            left = stack[i, at : at + 3].reshape(3 * deep, depth)
-            right = stack[i, at + 1 : at + 4].reshape(3 * deep, depth)
-            both = jnp.concatenate([left, right], axis=1)
-            out = jnp.dot(weights[...], both, preferred_element_type=F32)
+def conv_padded(padded, weights, first, count, emit):
+    wide, _, chans, depth = padded.shape
+
+    def body(x, carry):
+        lane = lax.broadcasted_iota(jnp.int32, (chans, depth), 1)
+        for y in range(first, first + count, 2):
+            halves = []
+            for side in range(2):
+                at = y + side
+                rows = [padded[x + a, at : at + 3].reshape(3 * chans, depth) for a in range(3)]
+                halves.append(jnp.concatenate(rows, axis=0))
+            out = jnp.dot(weights[...], jnp.concatenate(halves, axis=1), preferred_element_type=F32)
             for side in range(2):
                 part = out[:, side * depth : (side + 1) * depth]
-                acc[i + 2, y + side] = part[0:chans]
-                acc[i + 1, y + side] += part[chans : 2 * chans]
-                acc[i, y + side] += part[2 * chans : 3 * chans]
+                below = jnp.where(lane == 0, 0.0, pltpu.roll(part[0:chans], 1, 1))
+                above = jnp.where(lane == depth - 1, 0.0, pltpu.roll(part[2 * chans :], depth - 1, 1))
+                emit(x, y + side, below + part[chans : 2 * chans] + above)
         return carry
 
-    lax.fori_loop(0, wide, body, 0)
-
-
-def forward_kernel(place, mask, weights, tile, xr_even, xr_odd, yr_even, yr_odd, activ, slope, padded, stack, acc):
-    stack_padded(stack, place, tile, xr_even, xr_odd, yr_even, yr_odd, 0)
-    chans = tile.shape[2]
-    padded[...] = stack[:, :, chans : 2 * chans, :]
-    conv_stack(stack, weights, acc)
-
-    def body(i, carry):
-        value = acc[i + 2]
+    lax.fori_loop(0, wide - 2, body, 0)
+
+
+def weights_kernel(one, two, w_pre, w_act, w_branch):
+    chans = one.shape[-1]
+    for kz in range(3):
+        rows = slice(kz * chans, (kz + 1) * chans)
+        taps = jnp.concatenate([one[a, b, kz] for a in range(3) for b in range(3)], axis=0)
+        w_pre[rows] = taps.T
+        for source, dest in ((two, w_act), (one, w_branch)):
+            dest[rows] = jnp.concatenate(
+                [source[2 - a, 2 - b, 2 - kz] for a in range(3) for b in range(3)], axis=1
+            )
+
+
+def forward_kernel(place, mask, weights, tile, xr_even, xr_odd, yr_even, yr_odd, activ, slope, padded):
+    pad_tile(padded, place, tile, xr_even, xr_odd, yr_even, yr_odd, 0)
+
+    def emit(x, y, value):
         sig = jax.nn.sigmoid(value)
-        activ[i] = (mask[...] * (value * sig)).astype(BF16)
-        slope[i] = mask[...] * (sig * (1.0 + value * (1.0 - sig)))
-        return carry
-
-    lax.fori_loop(0, tile.shape[0], body, 0)
+        activ[x, y] = (mask[...] * (value * sig)).astype(BF16)
+        slope[x, y] = mask[...] * (sig * (1.0 + value * (1.0 - sig)))
+
+    conv_padded(padded, weights, 0, tile.shape[1], emit)
 
 
 def backward_kernel(
-    place, weights, slope, tile, xr_even, xr_odd, yr_even, yr_odd, pre_grad, xs_even, xs_odd, padded, stack, acc
+    place, weights, slope, tile, xr_even, xr_odd, yr_even, yr_odd, pre_grad, xs_even, xs_odd, padded
 ):
-    stack_padded(stack, place, tile, xr_even, xr_odd, yr_even, yr_odd, 1)
-    size_x, _, chans = tile.shape[0:3]
-    padded[...] = stack[:, :, chans : 2 * chans, :]
-    conv_stack(stack, weights, acc)
-
-    def body(i, carry):
-        pre_grad[i] = (slope[i] * acc[i + 2]).astype(BF16)
-        return carry
-
-    lax.fori_loop(0, size_x, body, 0)
+    pad_tile(padded, place, tile, xr_even, xr_odd, yr_even, yr_odd, 1)
+    size_x = tile.shape[0]
+
+    def emit(x, y, value):
+        pre_grad[x, y] = (slope[x, y] * value).astype(BF16)
+
+    conv_padded(padded, weights, 0, tile.shape[1], emit)
     xs_even[0] = pre_grad[(1 - place[0]) * (size_x - 1)]
     xs_odd[0] = pre_grad[place[0] * (size_x - 1)]
 
 
-def branch_finish(mask, base, result, acc, first):
-    tall = acc.shape[1]
-
-    def body(i, carry):
-        result[i] = (base[i, first : first + tall].astype(F32) + mask[...] * acc[i + 2]).astype(BF16)
-        return carry
-
-    lax.fori_loop(0, base.shape[0], body, 0)
-
-
-def branch_low_kernel(place, mask, weights, base, tile, xr_even, xr_odd, yr_even, yr_odd, result, stack, acc):
-    stack_padded(stack, place, tile, xr_even, xr_odd, yr_even, yr_odd, 0)
-    conv_stack(stack, weights, acc, 0)
-    branch_finish(mask, base, result, acc, 0)
-
-
-def branch_high_kernel(mask, weights, base, stack, result, acc):
-    first = base.shape[1] // 2
-    conv_stack(stack, weights, acc, first)
-    branch_finish(mask, base, result, acc, first)
+def branch_part(mask, weights, base, padded, result, first):
+    def emit(x, y, value):
+        result[x, y - first] = (base[x, y].astype(F32) + mask[...] * value).astype(BF16)
+
+    conv_padded(padded, weights, first, result.shape[1], emit)
+
+
+def branch_low_kernel(place, mask, weights, base, tile, xr_even, xr_odd, yr_even, yr_odd, result, padded):
+    pad_tile(padded, place, tile, xr_even, xr_odd, yr_even, yr_odd, 0)
+    branch_part(mask, weights, base, padded, result, 0)
+
+
+def branch_high_kernel(mask, weights, base, padded, result):
+    branch_part(mask, weights, base, padded, result, base.shape[1] // 2)
 
 
 def grad_accumulate(padded, stack, acc):
@@ -314,25 +307,23 @@
 
     in_sends = y_sends(masked_in, xr, 0)
     grad_sends = y_sends(masked_grad, xr, 1)
-    in_y = swap(*in_sends, "gy")
+    matrix = jax.ShapeDtypeStruct((3 * chans, 9 * chans), BF16)
+    even, odd = swap_perms(lax.axis_size("gy"))
+    in_even = lax.ppermute(in_sends[0], "gy", even)
+    w_pre, w_act, w_branch = call(weights_kernel, [matrix] * 3)(kernel_one, kernel_two)
+    in_next, w_pre = lax.optimization_barrier((in_sends[1], w_pre))
+    in_odd = lax.ppermute(in_next, "gy", odd)
+    in_y = (in_even, in_odd)
     grad_y = swap(*grad_sends, "gy")
 
-    w_pre = jnp.transpose(kernel_one, (0, 4, 1, 2, 3)).reshape(3 * chans, 9 * chans)
-    flat = lambda w: jnp.transpose(w[::-1, ::-1, ::-1], (0, 3, 1, 2, 4)).reshape(3 * chans, 9 * chans)
-    w_pre, w_act, w_branch = lax.optimization_barrier((w_pre, flat(kernel_two), flat(kernel_one)))
-
-    stack_s = pltpu.VMEM((tile_x + 2, tile_y + 2, 3 * chans, tile_z), BF16)
-    stack_o = jax.ShapeDtypeStruct((tile_x + 2, tile_y + 2, 3 * chans, tile_z), BF16)
-    acc_s = pltpu.VMEM((tile_x + 4, tile_y, chans, tile_z), F32)
-    acc_h = pltpu.VMEM((tile_x + 4, tile_y // 2, chans, tile_z), F32)
     tile_s = pltpu.VMEM((tile_x, tile_y, 3 * chans, tile_z), BF16)
     grad_s = pltpu.VMEM((9 * chans, 3 * chans), F32)
 
     activ, slope, in_pad = call(
-        forward_kernel, [tile_b, jax.ShapeDtypeStruct(tile_shape, F32), pad_b], [stack_s, acc_s], scalars=1, flops=flops
+        forward_kernel, [tile_b, jax.ShapeDtypeStruct(tile_shape, F32), pad_b], scalars=1, flops=flops
     )(place, mask_f, w_pre, masked_in, *xr, *in_y)
     pre_grad, xs_even, xs_odd, grad_pad = call(
-        backward_kernel, [tile_b, edge_b, edge_b, pad_b], [stack_s, acc_s], scalars=1, flops=flops
+        backward_kernel, [tile_b, edge_b, edge_b, pad_b], scalars=1, flops=flops
     )(place, w_act, slope, masked_grad, *xr, *grad_y)
 
     packed = 27 * chans * chans // (2 * chans)
@@ -364,10 +355,10 @@
     grad_one, grad_two = call(unpack, [grad_shape, grad_shape], scalars=1)(place, own, other)
 
     half_b = jax.ShapeDtypeStruct((tile_x, tile_y // 2, chans, tile_z), BF16)
-    low, stacked = call(
-        branch_low_kernel, [half_b, stack_o], [acc_h], scalars=1, flops=flops // 2
+    low, pre_pad = call(
+        branch_low_kernel, [half_b, pad_b], scalars=1, flops=flops // 2
     )(place, mask_f, w_branch, masked_grad, pre_grad, *pre_xr, *pre_yr)
-    (high,) = call(branch_high_kernel, [half_b], [acc_h], flops=flops // 2)(mask_f, w_branch, masked_grad, stacked)
+    (high,) = call(branch_high_kernel, [half_b], flops=flops // 2)(mask_f, w_branch, masked_grad, pre_pad)
     grad_features = jnp.transpose(jnp.concatenate([low, high], axis=1), (2, 0, 1, 3))
     return grad_features, grad_one, grad_two
 

time: 128 us -> 115 us (0.90)
  the two profiles are of different devices: /device:TPU:15 before, /device:TPU:8 now
where the time goes in v3:
time: 115 us
  starting transfers between devices  42.8 us (37%)
  Pallas kernels  35.4 us (31%)
  waiting for transfers between devices  26.9 us (23%)
  other arithmetic  5.82 us (5%)
  local copies, waits for them, and re-layouts  3.14 us (3%)
    pallas_call x13, Pallas kernels, run(): pl.pallas_call(kernel, out_shape=tuple(outs), in_specs=specs, out_specs=t...  35.4 us
    ppermute x14, starting transfers between devices, xor_permute(): return lax.ppermute(value, AXES, [(i, i ^ mask) for i in range(total)])  24.1 us
    ppermute x14, waiting for transfers between devices, xor_permute(): return lax.ppermute(value, AXES, [(i, i ^ mask) for i in range(total)])  18.4 us
    ppermute x4, starting transfers between devices, swap(): lax.ppermute(value_odd, axis, odd)  8.08 us
    ppermute x1, starting transfers between devices, body(): in_odd = lax.ppermute(in_next, 'gy', odd)  5.66 us
    ppermute x4, starting transfers between devices, swap(): lax.ppermute(value_even, axis, even)  4.1 us
    ppermute x4, waiting for transfers between devices, swap(): lax.ppermute(value_even, axis, even)  3.6 us
    transpose x1, other arithmetic, body(): masked_in = jnp.transpose(features * mask_b[:, None], (1, 2, 0, 3))  3.27 us
  transfers between devices with their start and end apart: 24, of which 14 were waited for; matrix products, arithmetic and copies ran while one was open for 5% of the time, Pallas kernels for 13%

profile of v3, /device:TPU:8, one launch (start us, length us, event | category | flops | bytes accessed | tf_op | source)
XLA Modules:
  0.0 114.9 jit_solution(16119060666362350823)
XLA Ops:
  0.7 0.8 convert_bitcast_fusion
  1.4 0.1 broadcast_in_dim.8
  1.5 0.1 convert_element_type.32
  1.6 1.2 %constant_dynamic-slice_fusion = (bf16[64,1,8,128]{3,2,1,0:T(8,128)(2,1)S(1)}, bf16[64,1,8,128]{3,2,1,0:T(8,128)(2,1)S(1)}, bf16[64,1,8,128]{3,2,1,0:T(8,128)(2,1)S(1)}, bf16[64,1,8,128]{3,2,1,0:T(8,128)(2,1)S(1)}) fusion(bf16[64,8,8,128]{3,2,1,0:T(8,128)(2,1)} %param.6, s32[]{:T(128)S(6)} %select_n.10, s32[]{:T(128)S(6)} %select_n.9, ...), kind=kLoop, calls=%fused_computation.18 | loop fusion | bytes 1048584 | tf_op jit(solution)/shard_map/jit(dynamic_index_in_dim)/dynamic_slice | solution.py:290
  2.7 0.1 fusion.3
  2.8 0.7 pad_maximum_fusion
  3.6 0.0 collective-permute-start
  3.6 0.7 pad_maximum_fusion.1
  4.3 0.7 collective-permute-start.1
  5.0 0.3 shard_map.76
  5.3 0.1 pad_add_fusion.place.place_ref
  5.4 3.3 %fusion = (bf16[8,8,64,128]{3,2,1,0:T(8,128)(2,1)S(1)}, bf16[8,8,64,128]{3,2,1,0:T(8,128)(2,1)S(1)}) fusion(bf16[64,8,8,128]{3,2,1,0:T(8,128)(2,1)} %param.5, bf16[128]{0:T(256)(128)(2,1)S(1)} %convert_element_type.32, bf16[64,8,8,128]{3,2,1,0:T(8,128)(2,1)} %param.6), kind=kLoop, calls=%fused_computation.2 | loop fusion | flops 1048576 | bytes 4194560 | tf_op jit(solution)/shard_map/transpose | solution.py:294
  8.6 0.0 collective-permute-done.xr_even
  8.7 1.3 %shard_map.77 = (bf16[10,64,128]{2,1,0:T(8,128)(2,1)}, bf16[10,64,128]{2,1,0:T(8,128)(2,1)}) custom-call(s32[3]{0:T(128)S(1)} %pad_add_fusion.place.place_ref, bf16[8,8,64,128]{3,2,1,0:T(8,128)(2,1)S(1)} %get-tuple-element.73.tile, bf16[2,8,64,128]{3,2,1,0:T(8,128)(2,1)S(1)} %collective-permute-done.xr_even, ...), custom_call_target="tpu_custom_call" | custom-call | bytes 1900556 | tf_op jit(solution)/shard_map/pallas_call | solution.py:263
  9.9 5.7 %collective-permute-start.3 = (bf16[10,64,128]{2,1,0:T(8,128)(2,1)}, bf16[10,64,128]{2,1,0:T(8,128)(2,1)S(1)}, u32[]{:S(2)}, u32[]{:S(2)}) collective-permute-start(bf16[10,64,128]{2,1,0:T(8,128)(2,1)} %get-tuple-element.37), channel_id=1, source_target_pairs={{1,2},{2,1},{3,4},{4,3},{5,6},{6,5},{9,10},{10,9},{11,12},{12,11},... | collective-permute-start | bytes 491528 | tf_op jit(solution)/shard_map/ppermute | solution.py:315
  15.6 0.9 collective-permute-start.2
  16.5 0.1 broadcast_in_dim.7
  16.5 0.1 convert_element_type.29.mask
  16.6 0.6 shard_map.79
  17.2 2.8 %collective-permute-start.4 = (bf16[10,64,128]{2,1,0:T(8,128)(2,1)S(1)}, bf16[10,64,128]{2,1,0:T(8,128)(2,1)S(1)}, u32[]{:S(2)}, u32[]{:S(2)}) collective-permute-start(bf16[10,64,128]{2,1,0:T(8,128)(2,1)S(1)} %get-tuple-element.39), channel_id=1, source_target_pairs={{0,1},{1,0},{2,3},{3,2},{4,5},{5,4},{6,7},{7,6},{8,9},{9,8},{10,11... | collective-permute-start | bytes 491528 | tf_op jit(solution)/shard_map/ppermute | solution.py:30
  20.0 2.6 %collective-permute-start.5 = (bf16[10,64,128]{2,1,0:T(8,128)(2,1)S(1)}, bf16[10,64,128]{2,1,0:T(8,128)(2,1)S(1)}, u32[]{:S(2)}, u32[]{:S(2)}) collective-permute-start(bf16[10,64,128]{2,1,0:T(8,128)(2,1)S(1)} %get-tuple-element.40), channel_id=1, source_target_pairs={{1,2},{2,1},{3,4},{4,3},{5,6},{6,5},{9,10},{10,9},{11,12},{12,11},... | collective-permute-start | bytes 491528 | tf_op jit(solution)/shard_map/ppermute | solution.py:30
  22.6 0.0 collective-permute-done.3.yr_odd
  22.6 2.7 %collective-permute-done.2.yr_even = bf16[10,64,128]{2,1,0:T(8,128)(2,1)} collective-permute-done((bf16[10,64,128]{2,1,0:T(8,128)(2,1)}, bf16[10,64,128]{2,1,0:T(8,128)(2,1)}, u32[]{:S(2)}, u32[]{:S(2)}) %collective-permute-start.2) | collective-permute-done | bytes 163872 | tf_op jit(solution)/shard_map/ppermute | solution.py:312
  25.3 5.8 %shard_map.78 = (bf16[8,8,64,128]{3,2,1,0:T(8,128)(2,1)S(1)}, f32[8,8,64,128]{3,2,1,0:T(8,128)S(1)}, bf16[10,10,64,128]{3,2,1,0:T(8,128)(2,1)S(1)}) custom-call(s32[3]{0:T(128)S(1)} %pad_add_fusion.place.place_ref, f32[1,128]{1,0:T(1,128)S(1)} %convert_element_type.29.mask, bf16[192,576]{1,0:T(8,128)(2,1)S(1)} %get-tuple-element.35.weights, ...), custom_call_target="tpu_custom_call" | custom-call | flops 1811939328 | bytes 6906380 | tf_op jit(solution)/shard_map/pallas_call | solution.py:263
  31.1 1.1 collective-permute-done.4.yr_even
  32.2 5.2 %shard_map.80 = (bf16[8,8,64,128]{3,2,1,0:T(8,128)(2,1)S(1)}, bf16[1,8,64,128]{3,2,1,0:T(8,128)(2,1)S(1)}, bf16[1,8,64,128]{3,2,1,0:T(8,128)(2,1)S(1)}, bf16[10,10,64,128]{3,2,1,0:T(8,128)(2,1)S(1)}) custom-call(s32[3]{0:T(128)S(1)} %pad_add_fusion.place.place_ref, bf16[192,576]{1,0:T(8,128)(2,1)S(1)} %get-tuple-element.32.weights, ...), custom_call_target="tpu_custom_call" | custom-call | flops 1811939328 | bytes 7168012 | tf_op jit(solution)/shard_map/pallas_call | solution.py:263
  37.5 5.1 %shard_map.84.packed_two = f32[864,128]{1,0:T(8,128)S(1)} custom-call(bf16[10,10,64,128]{3,2,1,0:T(8,128)(2,1)S(1)} %get-tuple-element.49.grad_pad, bf16[8,8,64,128]{3,2,1,0:T(8,128)(2,1)S(1)} %get-tuple-element.50.activ), custom_call_target="tpu_custom_call" | custom-call | flops 1811939328 | bytes 3129344 | tf_op jit(solution)/shard_map/pallas_call | solution.py:263
  42.6 5.7 %shard_map.85 = (f32[864,128]{1,0:T(8,128)S(1)}, f32[864,128]{1,0:T(8,128)S(1)}) custom-call(s32[3]{0:T(128)S(1)} %pad_add_fusion.place.place_ref, bf16[10,10,64,128]{3,2,1,0:T(8,128)(2,1)S(1)} %get-tuple-element.48.in_pad, bf16[8,8,64,128]{3,2,1,0:T(8,128)(2,1)S(1)} %get-tuple-element.41.tile.pre_grad, f32[864,128]{1,0:T(8,128)S(1)} %shard_map.84.packed_two), custom_call_target="tpu_custom_call" | custom-call | flops 1811939328 | bytes 4014092 | tf_op jit(solution)/shard_map/pallas_call | solution.py:263
  48.3 3.1 %collective-permute-start.10 = (f32[864,128]{1,0:T(8,128)S(1)}, f32[864,128]{1,0:T(8,128)S(1)}, u32[]{:S(2)}, u32[]{:S(2)}) collective-permute-start(f32[864,128]{1,0:T(8,128)S(1)} %get-tuple-element.52), channel_id=1, source_target_pairs={{0,8},{1,9},{2,10},{3,11},{4,12},{5,13},{6,14},{7,15},{8,0},{9,1},... | collective-permute-start | bytes 1327112 | tf_op jit(solution)/shard_map/ppermute | solution.py:25
  51.4 1.4 %collective-permute-done.10.recv = f32[864,128]{1,0:T(8,128)S(1)} collective-permute-done((f32[864,128]{1,0:T(8,128)S(1)}, f32[864,128]{1,0:T(8,128)S(1)}, u32[]{:S(2)}, u32[]{:S(2)}) %collective-permute-start.10) | collective-permute-done | bytes 442400 | tf_op jit(solution)/shard_map/ppermute | solution.py:25
  52.8 0.6 shard_map.86
  53.4 4.2 %collective-permute-start.11 = (f32[216,128]{1,0:T(8,128)S(1)}, f32[216,128]{1,0:T(8,128)S(1)}, u32[]{:S(2)}, u32[]{:S(2)}) collective-permute-start(f32[216,128]{1,0:T(8,128)S(1)} %get-tuple-element.54), channel_id=1, source_target_pairs={{0,16},{1,17},{2,18},{3,19},{4,20},{5,21},{6,22},{7,23},{8,24},{9,... | collective-permute-start | bytes 331784 | tf_op jit(solution)/shard_map/ppermute | solution.py:25
  57.6 1.6 %collective-permute-start.12 = (f32[216,128]{1,0:T(8,128)S(1)}, f32[216,128]{1,0:T(8,128)S(1)}, u32[]{:S(2)}, u32[]{:S(2)}) collective-permute-start(f32[216,128]{1,0:T(8,128)S(1)} %get-tuple-element.55), channel_id=1, source_target_pairs={{0,32},{1,33},{2,34},{3,35},{4,36},{5,37},{6,38},{7,39},{8,40},{9,... | collective-permute-start | bytes 331784 | tf_op jit(solution)/shard_map/ppermute | solution.py:25
  59.3 1.2 %collective-permute-start.13 = (f32[216,128]{1,0:T(8,128)S(1)}, f32[216,128]{1,0:T(8,128)S(1)}, u32[]{:S(2)}, u32[]{:S(2)}) collective-permute-start(f32[216,128]{1,0:T(8,128)S(1)} %get-tuple-element.56), channel_id=1, source_target_pairs={{0,48},{1,49},{2,50},{3,51},{4,52},{5,53},{6,54},{7,55},{8,56},{9,... | collective-permute-start | bytes 331784 | tf_op jit(solution)/shard_map/ppermute | solution.py:25
  60.4 0.6 collective-permute-done.11
  61.0 4.0 %collective-permute-done.12 = f32[216,128]{1,0:T(8,128)S(1)} collective-permute-done((f32[216,128]{1,0:T(8,128)S(1)}, f32[216,128]{1,0:T(8,128)S(1)}, u32[]{:S(2)}, u32[]{:S(2)}) %collective-permute-start.12) | collective-permute-done | bytes 110624 | tf_op jit(solution)/shard_map/ppermute | solution.py:25
  65.0 2.2 %collective-permute-done.13 = f32[216,128]{1,0:T(8,128)S(1)} collective-permute-done((f32[216,128]{1,0:T(8,128)S(1)}, f32[216,128]{1,0:T(8,128)S(1)}, u32[]{:S(2)}, u32[]{:S(2)}) %collective-permute-start.13) | collective-permute-done | bytes 110624 | tf_op jit(solution)/shard_map/ppermute | solution.py:25
  67.2 2.8 %collective-permute-start.16 = (f32[216,128]{1,0:T(8,128)S(1)}, f32[216,128]{1,0:T(8,128)S(1)}, u32[]{:S(2)}, u32[]{:S(2)}) collective-permute-start(f32[216,128]{1,0:T(8,128)S(1)} %add_add_fusion.2), channel_id=1, source_target_pairs={{0,6},{1,7},{2,4},{3,5},{4,2},{5,3},{6,0},{7,1},{8,14},{9,15},{10,... | collective-permute-start | bytes 331784 | tf_op jit(solution)/shard_map/ppermute | solution.py:25
  70.0 2.2 %collective-permute-start.14 = (f32[216,128]{1,0:T(8,128)S(1)}, f32[216,128]{1,0:T(8,128)S(1)}, u32[]{:S(2)}, u32[]{:S(2)}) collective-permute-start(f32[216,128]{1,0:T(8,128)S(1)} %add_add_fusion.2), channel_id=1, source_target_pairs={{0,2},{1,3},{2,0},{3,1},{4,6},{5,7},{6,4},{7,5},{8,10},{9,11},{10,... | collective-permute-start | bytes 331784 | tf_op jit(solution)/shard_map/ppermute | solution.py:25
  72.2 2.1 %collective-permute-done.16 = f32[216,128]{1,0:T(8,128)S(1)} collective-permute-done((f32[216,128]{1,0:T(8,128)S(1)}, f32[216,128]{1,0:T(8,128)S(1)}, u32[]{:S(2)}, u32[]{:S(2)}) %collective-permute-start.16) | collective-permute-done | bytes 110624 | tf_op jit(solution)/shard_map/ppermute | solution.py:25
  74.3 3.0 %collective-permute-done.15 = f32[216,128]{1,0:T(8,128)S(1)} collective-permute-done((f32[216,128]{1,0:T(8,128)S(1)}, f32[216,128]{1,0:T(8,128)S(1)}, u32[]{:S(2)}, u32[]{:S(2)}) %collective-permute-start.15) | collective-permute-done | bytes 110624 | tf_op jit(solution)/shard_map/ppermute | solution.py:25
  77.3 0.1 collective-permute-done.14
  77.4 3.2 %collective-permute-start.19 = (f32[216,128]{1,0:T(8,128)S(1)}, f32[216,128]{1,0:T(8,128)S(1)}, u32[]{:S(2)}, u32[]{:S(2)}) collective-permute-start(f32[216,128]{1,0:T(8,128)S(1)} %add_add_fusion.1), channel_id=1, source_target_pairs={{0,65},{1,64},{2,67},{3,66},{4,69},{5,68},{6,71},{7,70},{8,73},{9,... | collective-permute-start | bytes 331784 | tf_op jit(solution)/shard_map/ppermute | solution.py:25
  80.6 1.0 collective-permute-start.18
  81.6 0.6 collective-permute-start.17
  82.2 0.7 collective-permute-start.7
  82.9 1.2 %collective-permute-done.19 = f32[216,128]{1,0:T(8,128)S(1)} collective-permute-done((f32[216,128]{1,0:T(8,128)S(1)}, f32[216,128]{1,0:T(8,128)S(1)}, u32[]{:S(2)}, u32[]{:S(2)}) %collective-permute-start.19) | collective-permute-done | bytes 110624 | tf_op jit(solution)/shard_map/ppermute | solution.py:25
  84.1 1.3 %collective-permute-done.18 = f32[216,128]{1,0:T(8,128)S(1)} collective-permute-done((f32[216,128]{1,0:T(8,128)S(1)}, f32[216,128]{1,0:T(8,128)S(1)}, u32[]{:S(2)}, u32[]{:S(2)}) %collective-permute-start.18) | collective-permute-done | bytes 110624 | tf_op jit(solution)/shard_map/ppermute | solution.py:25
  85.4 2.5 %collective-permute-done.17 = f32[216,128]{1,0:T(8,128)S(1)} collective-permute-done((f32[216,128]{1,0:T(8,128)S(1)}, f32[216,128]{1,0:T(8,128)S(1)}, u32[]{:S(2)}, u32[]{:S(2)}) %collective-permute-start.17) | collective-permute-done | bytes 110624 | tf_op jit(solution)/shard_map/ppermute | solution.py:25
  87.9 0.5 collective-permute-start.22
  88.4 0.5 collective-permute-start.21
  88.8 3.2 %collective-permute-start.20 = (f32[216,128]{1,0:T(8,128)S(1)}, f32[216,128]{1,0:T(8,128)S(1)}, u32[]{:S(2)}, u32[]{:S(2)}) collective-permute-start(f32[216,128]{1,0:T(8,128)S(1)} %add_add_fusion.refs_0_), channel_id=1, source_target_pairs={{0,16},{1,17},{2,18},{3,19},{4,20},{5,21},{6,22},{7,23},{8,24},{9,... | collective-permute-start | bytes 331784 | tf_op jit(solution)/shard_map/ppermute | solution.py:25
  92.0 0.6 shard_map.81
  92.6 1.3 %collective-permute-start.8 = (bf16[10,64,128]{2,1,0:T(8,128)(2,1)S(1)}, bf16[10,64,128]{2,1,0:T(8,128)(2,1)S(1)}, u32[]{:S(2)}, u32[]{:S(2)}) collective-permute-start(bf16[10,64,128]{2,1,0:T(8,128)(2,1)S(1)} %get-tuple-element.44), channel_id=1, source_target_pairs={{0,1},{1,0},{2,3},{3,2},{4,5},{5,4},{6,7},{7,6},{8,9},{9,8},{10,11... | collective-permute-start | bytes 491528 | tf_op jit(solution)/shard_map/ppermute | solution.py:30
  93.9 4.2 %collective-permute-start.9 = (bf16[10,64,128]{2,1,0:T(8,128)(2,1)S(1)}, bf16[10,64,128]{2,1,0:T(8,128)(2,1)S(1)}, u32[]{:S(2)}, u32[]{:S(2)}) collective-permute-start(bf16[10,64,128]{2,1,0:T(8,128)(2,1)S(1)} %get-tuple-element.45), channel_id=1, source_target_pairs={{1,2},{2,1},{3,4},{4,3},{5,6},{6,5},{9,10},{10,9},{11,12},{12,11},... | collective-permute-start | bytes 491528 | tf_op jit(solution)/shard_map/ppermute | solution.py:30
  98.1 0.6 shard_map.87.own_ref
  98.7 0.1 collective-permute-start.23
  98.8 2.5 %collective-permute-done.8.yr_even = bf16[10,64,128]{2,1,0:T(8,128)(2,1)S(1)} collective-permute-done((bf16[10,64,128]{2,1,0:T(8,128)(2,1)S(1)}, bf16[10,64,128]{2,1,0:T(8,128)(2,1)S(1)}, u32[]{:S(2)}, u32[]{:S(2)}) %collective-permute-start.8) | collective-permute-done | bytes 163872 | tf_op jit(solution)/shard_map/ppermute | solution.py:30
  101.3 2.2 %collective-permute-done.9.yr_odd = bf16[10,64,128]{2,1,0:T(8,128)(2,1)S(1)} collective-permute-done((bf16[10,64,128]{2,1,0:T(8,128)(2,1)S(1)}, bf16[10,64,128]{2,1,0:T(8,128)(2,1)S(1)}, u32[]{:S(2)}, u32[]{:S(2)}) %collective-permute-start.9) | collective-permute-done | bytes 163872 | tf_op jit(solution)/shard_map/ppermute | solution.py:30
  103.5 4.0 %shard_map.82 = (bf16[8,4,64,128]{3,2,1,0:T(8,128)(2,1)S(1)}, bf16[10,10,64,128]{3,2,1,0:T(8,128)(2,1)S(1)}) custom-call(s32[3]{0:T(128)S(1)} %pad_add_fusion.place.place_ref, f32[1,128]{1,0:T(1,128)S(1)} %convert_element_type.29.mask, bf16[192,576]{1,0:T(8,128)(2,1)S(1)} %get-tuple-element.31.weights, ...), custom_call_target="tpu_custom_call" | custom-call | flops 905969664 | bytes 5071372 | tf_op jit(solution)/shard_map/pallas_call | solution.py:263
  107.5 3.3 %shard_map.83 = bf16[8,4,64,128]{3,2,1,0:T(8,128)(2,1)S(1)} custom-call(f32[1,128]{1,0:T(1,128)S(1)} %convert_element_type.29.mask, bf16[192,576]{1,0:T(8,128)(2,1)S(1)} %get-tuple-element.31.weights, bf16[8,8,64,128]{3,2,1,0:T(8,128)(2,1)S(1)} %get-tuple-element.74.tile.base, bf16[10,10,64,128]{3,2,1,0:T(8,128)(2,1)S(1)} %get-tuple-element.47.padded), custom_call_target="tpu_custom_call" | custom-call | flops 905969664 | bytes 3432960 | tf_op jit(solution)/shard_map/pallas_call | solution.py:263
  110.8 0.1 maximum_bitcast_fusion
  110.9 1.6 %copy.21 = bf16[64,8,8,128]{3,2,1,0:T(8,128)(2,1)} copy(bf16[64,8,8,128]{3,0,2,1:T(8,128)(2,1)S(1)} %maximum_bitcast_fusion) | data formatting | bytes 2097152
  112.6 2.3 %shard_map.88 = (f32[3,3,3,64,64]{4,3,2,1,0:T(8,128)}, f32[3,3,3,64,64]{4,3,2,1,0:T(8,128)}) custom-call(s32[3]{0:T(128)S(1)} %pad_add_fusion.place.place_ref, f32[864,128]{1,0:T(8,128)S(1)} %shard_map.87.own_ref, f32[864,128]{1,0:T(8,128)S(1)} %collective-permute-done.23.other_ref), custom_call_target="tpu_custom_call" | custom-call | bytes 1769484 | tf_op jit(solution)/shard_map/pallas_call | solution.py:263
  (17 shorter events, 0.1 us)
Async XLA Ops:
  0.6 4.3 %copy-start.1 = (bf16[3,3,3,64,64]{4,3,2,1,0:T(8,128)(2,1)S(1)}, bf16[3,3,3,64,64]{4,3,2,1,0:T(8,128)(2,1)}, u32[]{:S(2)}) copy-start(bf16[3,3,3,64,64]{4,3,2,1,0:T(8,128)(2,1)} %two.1) | copy-start | bytes 663556
  0.6 4.3 %copy-start = (bf16[3,3,3,64,64]{4,3,2,1,0:T(8,128)(2,1)S(1)}, bf16[3,3,3,64,64]{4,3,2,1,0:T(8,128)(2,1)}, u32[]{:S(2)}) copy-start(bf16[3,3,3,64,64]{4,3,2,1,0:T(8,128)(2,1)} %one.1) | copy-start | bytes 663556
  3.6 5.1 %collective-permute-start = (bf16[2,8,64,128]{3,2,1,0:T(8,128)(2,1)}, bf16[2,8,64,128]{3,2,1,0:T(8,128)(2,1)S(1)}, u32[]{:S(2)}, u32[]{:S(2)}) collective-permute-start(bf16[2,8,64,128]{3,2,1,0:T(8,128)(2,1)} %pad_maximum_fusion), channel_id=1, source_target_pairs={{0,8},{8,0},{16,24},{24,16},{32,40},{40,32},{48,56},{56,48},{64,72... | collective-permute-start | bytes 786440 | tf_op jit(solution)/shard_map/ppermute | solution.py:30
  4.3 4.4 %collective-permute-start.1 = (bf16[2,8,64,128]{3,2,1,0:T(8,128)(2,1)}, bf16[2,8,64,128]{3,2,1,0:T(8,128)(2,1)S(1)}, u32[]{:S(2)}, u32[]{:S(2)}) collective-permute-start(bf16[2,8,64,128]{3,2,1,0:T(8,128)(2,1)} %pad_maximum_fusion.1), channel_id=1, source_target_pairs={{8,16},{16,8},{24,32},{32,24},{40,48},{48,40},{56,64},{64,56},{72,... | collective-permute-start | bytes 786440 | tf_op jit(solution)/shard_map/ppermute | solution.py:30
  9.9 12.7 %collective-permute-start.3 = (bf16[10,64,128]{2,1,0:T(8,128)(2,1)}, bf16[10,64,128]{2,1,0:T(8,128)(2,1)S(1)}, u32[]{:S(2)}, u32[]{:S(2)}) collective-permute-start(bf16[10,64,128]{2,1,0:T(8,128)(2,1)} %get-tuple-element.37), channel_id=1, source_target_pairs={{1,2},{2,1},{3,4},{4,3},{5,6},{6,5},{9,10},{10,9},{11,12},{12,11},... | collective-permute-start | bytes 491528 | tf_op jit(solution)/shard_map/ppermute | solution.py:315
  15.6 9.7 %collective-permute-start.2 = (bf16[10,64,128]{2,1,0:T(8,128)(2,1)}, bf16[10,64,128]{2,1,0:T(8,128)(2,1)}, u32[]{:S(2)}, u32[]{:S(2)}) collective-permute-start(bf16[10,64,128]{2,1,0:T(8,128)(2,1)} %get-tuple-element.36), channel_id=1, source_target_pairs={{0,1},{1,0},{2,3},{3,2},{4,5},{5,4},{6,7},{7,6},{8,9},{9,8},{10,11... | collective-permute-start | bytes 491528 | tf_op jit(solution)/shard_map/ppermute | solution.py:312
  17.2 15.0 %collective-permute-start.4 = (bf16[10,64,128]{2,1,0:T(8,128)(2,1)S(1)}, bf16[10,64,128]{2,1,0:T(8,128)(2,1)S(1)}, u32[]{:S(2)}, u32[]{:S(2)}) collective-permute-start(bf16[10,64,128]{2,1,0:T(8,128)(2,1)S(1)} %get-tuple-element.39), channel_id=1, source_target_pairs={{0,1},{1,0},{2,3},{3,2},{4,5},{5,4},{6,7},{7,6},{8,9},{9,8},{10,11... | collective-permute-start | bytes 491528 | tf_op jit(solution)/shard_map/ppermute | solution.py:30
  20.0 12.2 %collective-permute-start.5 = (bf16[10,64,128]{2,1,0:T(8,128)(2,1)S(1)}, bf16[10,64,128]{2,1,0:T(8,128)(2,1)S(1)}, u32[]{:S(2)}, u32[]{:S(2)}) collective-permute-start(bf16[10,64,128]{2,1,0:T(8,128)(2,1)S(1)} %get-tuple-element.40), channel_id=1, source_target_pairs={{1,2},{2,1},{3,4},{4,3},{5,6},{6,5},{9,10},{10,9},{11,12},{12,11},... | collective-permute-start | bytes 491528 | tf_op jit(solution)/shard_map/ppermute | solution.py:30
  48.3 4.5 %collective-permute-start.10 = (f32[864,128]{1,0:T(8,128)S(1)}, f32[864,128]{1,0:T(8,128)S(1)}, u32[]{:S(2)}, u32[]{:S(2)}) collective-permute-start(f32[864,128]{1,0:T(8,128)S(1)} %get-tuple-element.52), channel_id=1, source_target_pairs={{0,8},{1,9},{2,10},{3,11},{4,12},{5,13},{6,14},{7,15},{8,0},{9,1},... | collective-permute-start | bytes 1327112 | tf_op jit(solution)/shard_map/ppermute | solution.py:25
  53.4 7.6 %collective-permute-start.11 = (f32[216,128]{1,0:T(8,128)S(1)}, f32[216,128]{1,0:T(8,128)S(1)}, u32[]{:S(2)}, u32[]{:S(2)}) collective-permute-start(f32[216,128]{1,0:T(8,128)S(1)} %get-tuple-element.54), channel_id=1, source_target_pairs={{0,16},{1,17},{2,18},{3,19},{4,20},{5,21},{6,22},{7,23},{8,24},{9,... | collective-permute-start | bytes 331784 | tf_op jit(solution)/shard_map/ppermute | solution.py:25
  57.6 7.4 %collective-permute-start.12 = (f32[216,128]{1,0:T(8,128)S(1)}, f32[216,128]{1,0:T(8,128)S(1)}, u32[]{:S(2)}, u32[]{:S(2)}) collective-permute-start(f32[216,128]{1,0:T(8,128)S(1)} %get-tuple-element.55), channel_id=1, source_target_pairs={{0,32},{1,33},{2,34},{3,35},{4,36},{5,37},{6,38},{7,39},{8,40},{9,... | collective-permute-start | bytes 331784 | tf_op jit(solution)/shard_map/ppermute | solution.py:25
  59.3 7.9 %collective-permute-start.13 = (f32[216,128]{1,0:T(8,128)S(1)}, f32[216,128]{1,0:T(8,128)S(1)}, u32[]{:S(2)}, u32[]{:S(2)}) collective-permute-start(f32[216,128]{1,0:T(8,128)S(1)} %get-tuple-element.56), channel_id=1, source_target_pairs={{0,48},{1,49},{2,50},{3,51},{4,52},{5,53},{6,54},{7,55},{8,56},{9,... | collective-permute-start | bytes 331784 | tf_op jit(solution)/shard_map/ppermute | solution.py:25
  67.2 7.1 %collective-permute-start.16 = (f32[216,128]{1,0:T(8,128)S(1)}, f32[216,128]{1,0:T(8,128)S(1)}, u32[]{:S(2)}, u32[]{:S(2)}) collective-permute-start(f32[216,128]{1,0:T(8,128)S(1)} %add_add_fusion.2), channel_id=1, source_target_pairs={{0,6},{1,7},{2,4},{3,5},{4,2},{5,3},{6,0},{7,1},{8,14},{9,15},{10,... | collective-permute-start | bytes 331784 | tf_op jit(solution)/shard_map/ppermute | solution.py:25
  70.0 7.2 %collective-permute-start.15 = (f32[216,128]{1,0:T(8,128)S(1)}, f32[216,128]{1,0:T(8,128)S(1)}, u32[]{:S(2)}, u32[]{:S(2)}) collective-permute-start(f32[216,128]{1,0:T(8,128)S(1)} %add_add_fusion.2), channel_id=1, source_target_pairs={{0,4},{1,5},{2,6},{3,7},{4,0},{5,1},{6,2},{7,3},{8,12},{9,13},{10,... | collective-permute-start | bytes 331784 | tf_op jit(solution)/shard_map/ppermute | solution.py:25
  70.0 7.4 %collective-permute-start.14 = (f32[216,128]{1,0:T(8,128)S(1)}, f32[216,128]{1,0:T(8,128)S(1)}, u32[]{:S(2)}, u32[]{:S(2)}) collective-permute-start(f32[216,128]{1,0:T(8,128)S(1)} %add_add_fusion.2), channel_id=1, source_target_pairs={{0,2},{1,3},{2,0},{3,1},{4,6},{5,7},{6,4},{7,5},{8,10},{9,11},{10,... | collective-permute-start | bytes 331784 | tf_op jit(solution)/shard_map/ppermute | solution.py:25
  77.4 6.7 %collective-permute-start.19 = (f32[216,128]{1,0:T(8,128)S(1)}, f32[216,128]{1,0:T(8,128)S(1)}, u32[]{:S(2)}, u32[]{:S(2)}) collective-permute-start(f32[216,128]{1,0:T(8,128)S(1)} %add_add_fusion.1), channel_id=1, source_target_pairs={{0,65},{1,64},{2,67},{3,66},{4,69},{5,68},{6,71},{7,70},{8,73},{9,... | collective-permute-start | bytes 331784 | tf_op jit(solution)/shard_map/ppermute | solution.py:25
  80.6 4.8 %collective-permute-start.18 = (f32[216,128]{1,0:T(8,128)S(1)}, f32[216,128]{1,0:T(8,128)S(1)}, u32[]{:S(2)}, u32[]{:S(2)}) collective-permute-start(f32[216,128]{1,0:T(8,128)S(1)} %add_add_fusion.1), channel_id=1, source_target_pairs={{0,64},{1,65},{2,66},{3,67},{4,68},{5,69},{6,70},{7,71},{8,72},{9,... | collective-permute-start | bytes 331784 | tf_op jit(solution)/shard_map/ppermute | solution.py:25
  81.6 6.3 %collective-permute-start.17 = (f32[216,128]{1,0:T(8,128)S(1)}, f32[216,128]{1,0:T(8,128)S(1)}, u32[]{:S(2)}, u32[]{:S(2)}) collective-permute-start(f32[216,128]{1,0:T(8,128)S(1)} %add_add_fusion.1), channel_id=1, source_target_pairs={{0,1},{1,0},{2,3},{3,2},{4,5},{5,4},{6,7},{7,6},{8,9},{9,8},{10,11... | collective-permute-start | bytes 331784 | tf_op jit(solution)/shard_map/ppermute | solution.py:25
  82.2 9.8 %collective-permute-start.6 = (bf16[1,8,64,128]{3,2,1,0:T(8,128)(2,1)S(1)}, bf16[1,8,64,128]{3,2,1,0:T(8,128)(2,1)S(1)}, u32[]{:S(2)}, u32[]{:S(2)}) collective-permute-start(bf16[1,8,64,128]{3,2,1,0:T(8,128)(2,1)S(1)} %get-tuple-element.42), channel_id=1, source_target_pairs={{0,8},{8,0},{16,24},{24,16},{32,40},{40,32},{48,56},{56,48},{64,72... | collective-permute-start | bytes 393224 | tf_op jit(solution)/shard_map/ppermute | solution.py:30
  82.2 9.8 %collective-permute-start.7 = (bf16[1,8,64,128]{3,2,1,0:T(8,128)(2,1)S(1)}, bf16[1,8,64,128]{3,2,1,0:T(8,128)(2,1)S(1)}, u32[]{:S(2)}, u32[]{:S(2)}) collective-permute-start(bf16[1,8,64,128]{3,2,1,0:T(8,128)(2,1)S(1)} %get-tuple-element.43), channel_id=1, source_target_pairs={{8,16},{16,8},{24,32},{32,24},{40,48},{48,40},{56,64},{64,56},{72,... | collective-permute-start | bytes 393224 | tf_op jit(solution)/shard_map/ppermute | solution.py:30
  87.9 10.2 %collective-permute-start.22 = (f32[216,128]{1,0:T(8,128)S(1)}, f32[216,128]{1,0:T(8,128)S(1)}, u32[]{:S(2)}, u32[]{:S(2)}) collective-permute-start(f32[216,128]{1,0:T(8,128)S(1)} %add_add_fusion.refs_0_), channel_id=1, source_target_pairs={{0,48},{1,49},{2,50},{3,51},{4,52},{5,53},{6,54},{7,55},{8,56},{9,... | collective-permute-start | bytes 331784 | tf_op jit(solution)/shard_map/ppermute | solution.py:25
  88.4 9.7 %collective-permute-start.21 = (f32[216,128]{1,0:T(8,128)S(1)}, f32[216,128]{1,0:T(8,128)S(1)}, u32[]{:S(2)}, u32[]{:S(2)}) collective-permute-start(f32[216,128]{1,0:T(8,128)S(1)} %add_add_fusion.refs_0_), channel_id=1, source_target_pairs={{0,32},{1,33},{2,34},{3,35},{4,36},{5,37},{6,38},{7,39},{8,40},{9,... | collective-permute-start | bytes 331784 | tf_op jit(solution)/shard_map/ppermute | solution.py:25
  88.8 9.3 %collective-permute-start.20 = (f32[216,128]{1,0:T(8,128)S(1)}, f32[216,128]{1,0:T(8,128)S(1)}, u32[]{:S(2)}, u32[]{:S(2)}) collective-permute-start(f32[216,128]{1,0:T(8,128)S(1)} %add_add_fusion.refs_0_), channel_id=1, source_target_pairs={{0,16},{1,17},{2,18},{3,19},{4,20},{5,21},{6,22},{7,23},{8,24},{9,... | collective-permute-start | bytes 331784 | tf_op jit(solution)/shard_map/ppermute | solution.py:25
  92.6 8.7 %collective-permute-start.8 = (bf16[10,64,128]{2,1,0:T(8,128)(2,1)S(1)}, bf16[10,64,128]{2,1,0:T(8,128)(2,1)S(1)}, u32[]{:S(2)}, u32[]{:S(2)}) collective-permute-start(bf16[10,64,128]{2,1,0:T(8,128)(2,1)S(1)} %get-tuple-element.44), channel_id=1, source_target_pairs={{0,1},{1,0},{2,3},{3,2},{4,5},{5,4},{6,7},{7,6},{8,9},{9,8},{10,11... | collective-permute-start | bytes 491528 | tf_op jit(solution)/shard_map/ppermute | solution.py:30
  93.9 9.6 %collective-permute-start.9 = (bf16[10,64,128]{2,1,0:T(8,128)(2,1)S(1)}, bf16[10,64,128]{2,1,0:T(8,128)(2,1)S(1)}, u32[]{:S(2)}, u32[]{:S(2)}) collective-permute-start(bf16[10,64,128]{2,1,0:T(8,128)(2,1)S(1)} %get-tuple-element.45), channel_id=1, source_target_pairs={{1,2},{2,1},{3,4},{4,3},{5,6},{6,5},{9,10},{10,9},{11,12},{12,11},... | collective-permute-start | bytes 491528 | tf_op jit(solution)/shard_map/ppermute | solution.py:30
  98.7 13.9 %collective-permute-start.23 = (f32[864,128]{1,0:T(8,128)S(1)}, f32[864,128]{1,0:T(8,128)S(1)}, u32[]{:S(2)}, u32[]{:S(2)}) collective-permute-start(f32[864,128]{1,0:T(8,128)S(1)} %shard_map.87.own_ref), channel_id=1, source_target_pairs={{0,8},{1,9},{2,10},{3,11},{4,12},{5,13},{6,14},{7,15},{8,0},{9,1},... | collective-permute-start | bytes 1327112 | tf_op jit(solution)/shard_map/ppermute | solution.py:25

commit v4 on v3

--- a/solution.py
+++ b/solution.py
@@ -1,4 +1,3 @@
-import functools
 import math
 
 import jax
@@ -30,16 +29,14 @@
     return lax.ppermute(value_even, axis, even), lax.ppermute(value_odd, axis, odd)
 
 
-def stack_row(stack, at_x, first_y, row):
-    count, chans, depth = row.shape
-    lane = lax.broadcasted_iota(jnp.int32, row.shape, 2)
-    zero = jnp.zeros_like(row)
-    below = jnp.where(lane == 0, zero, pltpu.roll(row, 1, 2))
-    above = jnp.where(lane == depth - 1, zero, pltpu.roll(row, depth - 1, 2))
-    ys = pl.ds(first_y, count)
-    stack[at_x, ys, 0:chans, :] = below
-    stack[at_x, ys, chans : 2 * chans, :] = row
-    stack[at_x, ys, 2 * chans : 3 * chans, :] = above
+def store_shifted(stack, x, y, value):
+    chans, depth = value.shape
+    lane = lax.broadcasted_iota(jnp.int32, value.shape, 1)
+    below = jnp.where(lane == 0, 0.0, pltpu.roll(value, 1, 1))
+    above = jnp.where(lane == depth - 1, 0.0, pltpu.roll(value, depth - 1, 1))
+    stack[x, y, 0:chans] = below.astype(BF16)
+    stack[x, y, chans : 2 * chans] = value.astype(BF16)
+    stack[x, y, 2 * chans : 3 * chans] = above.astype(BF16)
 
 
 def sides(parity, size):
@@ -54,8 +51,8 @@
     padded[x_even, 1 : size_y + 1] = xr_even[which]
     padded[x_odd, 1 : size_y + 1] = xr_odd[which]
     for i in range(size_x + 2):
-        padded[i, y_even] = yr_even[i]
-        padded[i, y_odd] = yr_odd[i]
+        padded[i, y_even] = yr_even[which, i]
+        padded[i, y_odd] = yr_odd[which, i]
 
     def body(i, carry):
         padded[i + 1, 1 : size_y + 1] = tile[i]
@@ -64,14 +61,17 @@
     lax.fori_loop(0, size_x, body, 0)
 
 
-def ypack_kernel(place, tile, xr_even, xr_odd, ys_even, ys_odd, *, which):
-    size_x, size_y = tile.shape[0], tile.shape[1]
+def ypack_kernel(place, ye_even, ye_odd, xr_even, xr_odd, ys_even, ys_odd):
+    count, size_x = ye_even.shape[0:2]
+    size_y = xr_even.shape[1]
     x_even, x_odd = sides(place[0], size_x)
-    for out, edge in ((ys_even, (1 - place[1]) * (size_y - 1)), (ys_odd, place[1] * (size_y - 1))):
-        out[x_even] = xr_even[which, edge]
-        out[x_odd] = xr_odd[which, edge]
-        for i in range(size_x):
-            out[i + 1] = tile[i, edge]
+    at_even, at_odd = (1 - place[1]) * (size_y - 1), place[1] * (size_y - 1)
+    for out, edge, at in ((ys_even, ye_even, at_even), (ys_odd, ye_odd, at_odd)):
+        for k in range(count):
+            out[k, x_even] = xr_even[k, at]
+            out[k, x_odd] = xr_odd[k, at]
+            for i in range(size_x):
+                out[k, i + 1] = edge[k, i]
 
 
 def conv_padded(padded, weights, first, count, emit):
@@ -113,24 +113,31 @@
 
     def emit(x, y, value):
         sig = jax.nn.sigmoid(value)
-        activ[x, y] = (mask[...] * (value * sig)).astype(BF16)
+        store_shifted(activ, x, y, mask[...] * (value * sig))
         slope[x, y] = mask[...] * (sig * (1.0 + value * (1.0 - sig)))
 
     conv_padded(padded, weights, 0, tile.shape[1], emit)
 
 
 def backward_kernel(
-    place, weights, slope, tile, xr_even, xr_odd, yr_even, yr_odd, pre_grad, xs_even, xs_odd, padded
+    place, weights, slope, tile, xr_even, xr_odd, yr_even, yr_odd,
+    pre_grad, shifted, xs_even, xs_odd, ye_even, ye_odd, padded,
 ):
     pad_tile(padded, place, tile, xr_even, xr_odd, yr_even, yr_odd, 1)
     size_x = tile.shape[0]
 
     def emit(x, y, value):
-        pre_grad[x, y] = (slope[x, y] * value).astype(BF16)
+        value = slope[x, y] * value
+        pre_grad[x, y] = value.astype(BF16)
+        store_shifted(shifted, x, y, value)
 
     conv_padded(padded, weights, 0, tile.shape[1], emit)
+    last_y = tile.shape[1] - 1
     xs_even[0] = pre_grad[(1 - place[0]) * (size_x - 1)]
     xs_odd[0] = pre_grad[place[0] * (size_x - 1)]
+    for i in range(size_x):
+        ye_even[0, i] = pre_grad[i, (1 - place[1]) * last_y]
+        ye_odd[0, i] = pre_grad[i, place[1] * last_y]
 
 
 def branch_part(mask, weights, base, padded, result, first):
@@ -176,32 +183,22 @@
     dest[rows : rows + half] = jnp.concatenate([low, high], axis=1)
 
 
-def stack_tile(stack, source):
-    def body(i, carry):
-        stack_row(stack, i, 0, source[i])
-        return carry
-
-    lax.fori_loop(0, source.shape[0], body, 0)
-
-
-def grad_two_kernel(grad_pad, activ, packed, stack, acc):
-    stack_tile(stack, activ)
-    grad_accumulate(grad_pad, stack, acc)
-    pack_grad(packed, acc, activ.shape[2])
-
-
-def grad_one_kernel(place, in_pad, pre_grad, packed_two, keep, send, stack, acc):
-    stack_tile(stack, pre_grad)
-    grad_accumulate(in_pad, stack, acc)
+def grad_two_kernel(grad_pad, activ, packed, acc):
+    grad_accumulate(grad_pad, activ, acc)
+    pack_grad(packed, acc, grad_pad.shape[2])
+
+
+def grad_one_kernel(place, in_pad, shifted, packed_two, keep, send, acc):
+    grad_accumulate(in_pad, shifted, acc)
 
     @pl.when(place[0] == 0)
     def _():
-        pack_grad(keep, acc, pre_grad.shape[2])
+        pack_grad(keep, acc, in_pad.shape[2])
         send[...] = packed_two[...]
 
     @pl.when(place[0] != 0)
     def _():
-        pack_grad(send, acc, pre_grad.shape[2])
+        pack_grad(send, acc, in_pad.shape[2])
         keep[...] = packed_two[...]
 
 
@@ -290,51 +287,54 @@
         both = [lax.dynamic_index_in_dim(a, at, 1, keepdims=False) * mask_b for a in (features, cotangent)]
         return jnp.stack([jnp.transpose(a, (1, 0, 2)) for a in both])
 
-    xr = swap(x_edges((1 - x_odd) * (tile_x - 1)), x_edges(x_odd * (tile_x - 1)), "gx")
+    def y_edges(at):
+        both = [lax.dynamic_index_in_dim(a, at, 2, keepdims=False) * mask_b for a in (features, cotangent)]
+        return jnp.stack([jnp.transpose(a, (1, 0, 2)) for a in both])
+
+    ends = ((1 - x_odd) * (tile_x - 1), x_odd * (tile_x - 1)), ((1 - y_odd) * (tile_y - 1), y_odd * (tile_y - 1))
+    xr = swap(x_edges(ends[0][0]), x_edges(ends[0][1]), "gx")
+    even, odd = swap_perms(lax.axis_size("gy"))
+
+    def columns(count):
+        return [jax.ShapeDtypeStruct((count, tile_x + 2, chans, tile_z), BF16)] * 2
+
+    sends = call(ypack_kernel, columns(2), scalars=1)(place, y_edges(ends[1][0]), y_edges(ends[1][1]), *xr)
+    yr_even = lax.ppermute(sends[0], "gy", even)
     masked_in = jnp.transpose(features * mask_b[:, None], (1, 2, 0, 3))
     masked_grad = jnp.transpose(cotangent * mask_b[:, None], (1, 2, 0, 3))
+    odd_send, masked_in, masked_grad = lax.optimization_barrier((sends[1], masked_in, masked_grad))
+    yr_odd = lax.ppermute(odd_send, "gy", odd)
 
     tile_shape = (tile_x, tile_y, chans, tile_z)
     tile_b = jax.ShapeDtypeStruct(tile_shape, BF16)
-    column_b = jax.ShapeDtypeStruct((tile_x + 2, chans, tile_z), BF16)
-    edge_b = jax.ShapeDtypeStruct((1, tile_y, chans, tile_z), BF16)
+    shifted_b = jax.ShapeDtypeStruct((tile_x, tile_y, 3 * chans, tile_z), BF16)
+    edge_x = jax.ShapeDtypeStruct((1, tile_y, chans, tile_z), BF16)
+    edge_y = jax.ShapeDtypeStruct((1, tile_x, chans, tile_z), BF16)
     pad_b = jax.ShapeDtypeStruct((tile_x + 2, tile_y + 2, chans, tile_z), BF16)
+    matrix = jax.ShapeDtypeStruct((3 * chans, 9 * chans), BF16)
+    grad_s = pltpu.VMEM((9 * chans, 3 * chans), F32)
     flops = 2 * 27 * chans * chans * tile_x * tile_y * tile_z
 
-    def y_sends(tile, halo_x, which):
-        kernel = functools.partial(ypack_kernel, which=which)
-        return call(kernel, [column_b] * 2, scalars=1)(place, tile, *halo_x)
-
-    in_sends = y_sends(masked_in, xr, 0)
-    grad_sends = y_sends(masked_grad, xr, 1)
-    matrix = jax.ShapeDtypeStruct((3 * chans, 9 * chans), BF16)
-    even, odd = swap_perms(lax.axis_size("gy"))
-    in_even = lax.ppermute(in_sends[0], "gy", even)
     w_pre, w_act, w_branch = call(weights_kernel, [matrix] * 3)(kernel_one, kernel_two)
-    in_next, w_pre = lax.optimization_barrier((in_sends[1], w_pre))
-    in_odd = lax.ppermute(in_next, "gy", odd)
-    in_y = (in_even, in_odd)
-    grad_y = swap(*grad_sends, "gy")
-
-    tile_s = pltpu.VMEM((tile_x, tile_y, 3 * chans, tile_z), BF16)
-    grad_s = pltpu.VMEM((9 * chans, 3 * chans), F32)
-
     activ, slope, in_pad = call(
-        forward_kernel, [tile_b, jax.ShapeDtypeStruct(tile_shape, F32), pad_b], scalars=1, flops=flops
-    )(place, mask_f, w_pre, masked_in, *xr, *in_y)
-    pre_grad, xs_even, xs_odd, grad_pad = call(
-        backward_kernel, [tile_b, edge_b, edge_b, pad_b], scalars=1, flops=flops
-    )(place, w_act, slope, masked_grad, *xr, *grad_y)
+        forward_kernel, [shifted_b, jax.ShapeDtypeStruct(tile_shape, F32), pad_b], scalars=1, flops=flops
+    )(place, mask_f, w_pre, masked_in, *xr, yr_even, yr_odd)
+    pre_grad, shifted, xs_even, xs_odd, ye_even, ye_odd, grad_pad = call(
+        backward_kernel, [tile_b, shifted_b, edge_x, edge_x, edge_y, edge_y, pad_b], scalars=1, flops=flops
+    )(place, w_act, slope, masked_grad, *xr, yr_even, yr_odd)
 
     packed = 27 * chans * chans // (2 * chans)
     half = jax.ShapeDtypeStruct((packed, 2 * chans), F32)
     pre_xr = swap(xs_even, xs_odd, "gx")
-    (packed_two,) = call(grad_two_kernel, [half], [tile_s, grad_s], flops=flops)(grad_pad, activ)
-    pre_sends = y_sends(pre_grad, pre_xr, 0)
-    pre_yr = swap(*pre_sends, "gy")
-    keep, send = call(grad_one_kernel, [half, half], [tile_s, grad_s], scalars=1, flops=flops)(
-        place, in_pad, pre_grad, packed_two
+    (packed_two,) = call(grad_two_kernel, [half], [grad_s], flops=flops)(grad_pad, activ)
+    pre_sends = call(ypack_kernel, columns(1), scalars=1)(place, ye_even, ye_odd, *pre_xr)
+    pre_even = lax.ppermute(pre_sends[0], "gy", even)
+    keep, send = call(grad_one_kernel, [half, half], [grad_s], scalars=1, flops=flops)(
+        place, in_pad, shifted, packed_two
     )
+    pre_send, send = lax.optimization_barrier((pre_sends[1], send))
+    pre_odd = lax.ppermute(pre_send, "gy", odd)
+    pre_yr = (pre_even, pre_odd)
 
     recv = xor_permute(send, 8)
     chunk = jax.ShapeDtypeStruct((packed // 4, 2 * chans), F32)

time: 115 us -> 123 us (1.070)
  waiting for transfers between devices: 26.9 us -> 37.5 us
  starting transfers between devices: 42.8 us -> 37.2 us
  local copies, waits for them, and re-layouts: 3.14 us -> 6.57 us
    ppermute x2 -> x4, waiting for transfers between devices: 2.69 us -> 18.6 us  [the longest x1 14.5 us: body(): yr_even = lax.ppermute(sends[0], 'gy', even)]
    ppermute x4 -> x2, starting transfers between devices: 8.08 us -> 1.32 us  [swap(): lax.ppermute(value_odd, axis, odd)]
    ppermute x2 -> x4, starting transfers between devices: 6.52 us -> 12.3 us  [the longest x1 4.17 us: body(): pre_odd = lax.ppermute(pre_send, 'gy', odd)]
    ppermute x4 -> x2, waiting for transfers between devices: 3.6 us -> 0.01 us  [swap(): lax.ppermute(value_even, axis, even)]
    dynamic_slice x0 -> x1, local copies, waits for them, and re-layouts: none -> 3.43 us  [y_edges(): lax.dynamic_index_in_dim(a, at, 2, keepdims=False) * mask_b]
    ppermute x4 -> x2, starting transfers between devices: 4.1 us -> 1.18 us  [swap(): lax.ppermute(value_even, axis, even)]
    ppermute x4 -> x2, waiting for transfers between devices: 2.22 us -> 0.01 us  [swap(): lax.ppermute(value_odd, axis, odd)]
    ppermute x14, starting transfers between devices: 24.1 us -> 22.4 us  [xor_permute(): return lax.ppermute(value, AXES, [(i, i ^ mask) for i in range(total)])]
  transfers between devices with their start and end apart: 24 -> 22, of which waited for: 14 -> 13; matrix products, arithmetic and copies ran while one was open for 5% -> 5% of each run, Pallas kernels for 13% -> 14%
where the time goes in v4:
time: 123 us
  waiting for transfers between devices  37.5 us (30%)
  starting transfers between devices  37.2 us (30%)
  Pallas kernels  34.9 us (28%)
  local copies, waits for them, and re-layouts  6.57 us (5%)
  other arithmetic  6.11 us (5%)
    pallas_call x12, Pallas kernels, run(): pl.pallas_call(kernel, out_shape=tuple(outs), in_specs=specs, out_specs=t...  34.9 us
    ppermute x14, starting transfers between devices, xor_permute(): return lax.ppermute(value, AXES, [(i, i ^ mask) for i in range(total)])  22.4 us
    ppermute x14, waiting for transfers between devices, xor_permute(): return lax.ppermute(value, AXES, [(i, i ^ mask) for i in range(total)])  18.9 us
    ppermute x1, waiting for transfers between devices, body(): yr_even = lax.ppermute(sends[0], 'gy', even)  14.5 us
    ppermute x1, starting transfers between devices, body(): pre_odd = lax.ppermute(pre_send, 'gy', odd)  4.17 us
    ppermute x1, starting transfers between devices, body(): yr_even = lax.ppermute(sends[0], 'gy', even)  3.88 us
    dynamic_slice x1, local copies, waits for them, and re-layouts, y_edges(): lax.dynamic_index_in_dim(a, at, 2, keepdims=False) * mask_b  3.43 us
    transpose x1, other arithmetic, body(): masked_grad = jnp.transpose(cotangent * mask_b[:, None], (1, 2, 0, 3))  3.35 us
  transfers between devices with their start and end apart: 22, of which 13 were waited for; matrix products, arithmetic and copies ran while one was open for 5% of the time, Pallas kernels for 14%

profile of v4, /device:TPU:8, one launch (start us, length us, event | category | flops | bytes accessed | tf_op | source)
XLA Modules:
  0.0 123.2 jit_solution(8321893856687492070)
XLA Ops:
  0.6 0.7 convert_bitcast_fusion
  1.4 0.1 broadcast_in_dim.8
  1.5 0.1 convert_element_type.32
  1.5 1.2 constant_dynamic-slice_fusion
  2.7 3.4 %constant_dynamic-slice_fusion.4 = (bf16[64,8,1,128]{3,2,1,0:T(2,128)(2,1)S(1)}, bf16[64,8,1,128]{3,2,1,0:T(2,128)(2,1)S(1)}, bf16[64,8,1,128]{3,2,1,0:T(2,128)(2,1)S(1)}, bf16[64,8,1,128]{3,2,1,0:T(2,128)(2,1)S(1)}) fusion(bf16[64,8,8,128]{3,2,1,0:T(8,128)(2,1)} %param.6, s32[]{:T(128)S(6)} %select_n.19, s32[]{:T(128)S(6)} %select_n.18, ...), kind=kLoop, calls=%fused_computation.32 | loop fusion | bytes 1048584 | tf_op jit(solution)/shard_map/jit(dynamic_index_in_dim)/dynamic_slice | solution.py:291
  6.1 0.3 fusion.3
  6.4 0.7 pad_maximum_fusion.2
  7.1 0.7 pad_maximum_fusion.3
  7.9 0.7 collective-permute-start.1
  8.6 0.1 pad_add_fusion.place.place_ref
  8.7 3.4 %fusion = (bf16[8,8,64,128]{3,2,1,0:T(8,128)(2,1)S(1)}, bf16[8,8,64,128]{3,2,1,0:T(8,128)(2,1)S(1)}) fusion(bf16[64,8,8,128]{3,2,1,0:T(8,128)(2,1)} %param.6, bf16[128]{0:T(256)(128)(2,1)S(1)} %convert_element_type.32, bf16[64,8,8,128]{3,2,1,0:T(8,128)(2,1)} %param.5), kind=kLoop, calls=%fused_computation.2 | loop fusion | flops 1048576 | bytes 4194560 | tf_op jit(solution)/shard_map/transpose | solution.py:304
  12.1 0.0 collective-permute-done.xr_even
  12.1 1.4 %shard_map.77 = (bf16[2,10,64,128]{3,2,1,0:T(8,128)(2,1)}, bf16[2,10,64,128]{3,2,1,0:T(8,128)(2,1)}) custom-call(s32[3]{0:T(128)S(1)} %pad_add_fusion.place.place_ref, bf16[2,8,64,128]{3,2,1,0:T(8,128)(2,1)S(1)} %pad_maximum_fusion.ye_even, bf16[2,8,64,128]{3,2,1,0:T(8,128)(2,1)S(1)} %pad_maximum_fusion.1.ye_odd, ...), custom_call_target="tpu_custom_call" | custom-call | bytes 1703948 | tf_op jit(solution)/shard_map/pallas_call | solution.py:260
  13.5 3.9 %collective-permute-start.2 = (bf16[2,10,64,128]{3,2,1,0:T(8,128)(2,1)}, bf16[2,10,64,128]{3,2,1,0:T(8,128)(2,1)}, u32[]{:S(2)}, u32[]{:S(2)}) collective-permute-start(bf16[2,10,64,128]{3,2,1,0:T(8,128)(2,1)} %get-tuple-element.41), channel_id=1, source_target_pairs={{0,1},{1,0},{2,3},{3,2},{4,5},{5,4},{6,7},{7,6},{8,9},{9,8},{10,11... | collective-permute-start | bytes 983048 | tf_op jit(solution)/shard_map/ppermute | solution.py:302
  17.4 1.9 %collective-permute-start.3 = (bf16[2,10,64,128]{3,2,1,0:T(8,128)(2,1)}, bf16[2,10,64,128]{3,2,1,0:T(8,128)(2,1)}, u32[]{:S(2)}, u32[]{:S(2)}) collective-permute-start(bf16[2,10,64,128]{3,2,1,0:T(8,128)(2,1)} %get-tuple-element.42), channel_id=1, source_target_pairs={{1,2},{2,1},{3,4},{4,3},{5,6},{6,5},{9,10},{10,9},{11,12},{12,11},... | collective-permute-start | bytes 983048 | tf_op jit(solution)/shard_map/ppermute | solution.py:306
  19.3 0.1 broadcast_in_dim.7
  19.4 0.1 convert_element_type.29.mask
  19.5 0.3 shard_map.76
  19.8 14.5 %collective-permute-done.2.yr_even = bf16[2,10,64,128]{3,2,1,0:T(8,128)(2,1)} collective-permute-done((bf16[2,10,64,128]{3,2,1,0:T(8,128)(2,1)}, bf16[2,10,64,128]{3,2,1,0:T(8,128)(2,1)}, u32[]{:S(2)}, u32[]{:S(2)}) %collective-permute-start.2) | collective-permute-done | bytes 327712 | tf_op jit(solution)/shard_map/ppermute | solution.py:302
  34.2 0.0 collective-permute-done.3.yr_odd
  34.2 6.7 %shard_map.78 = (bf16[8,8,192,128]{3,2,1,0:T(8,128)(2,1)S(1)}, f32[8,8,64,128]{3,2,1,0:T(8,128)S(1)}, bf16[10,10,64,128]{3,2,1,0:T(8,128)(2,1)S(1)}) custom-call(s32[3]{0:T(128)S(1)} %pad_add_fusion.place.place_ref, f32[1,128]{1,0:T(1,128)S(1)} %convert_element_type.29.mask, bf16[192,576]{1,0:T(8,128)(2,1)S(1)} %get-tuple-element.39.weights, ...), custom_call_target="tpu_custom_call" | custom-call | flops 1811939328 | bytes 9331212 | tf_op jit(solution)/shard_map/pallas_call | solution.py:260
  40.9 6.5 %shard_map.79 = (bf16[8,8,64,128]{3,2,1,0:T(8,128)(2,1)S(1)}, bf16[8,8,192,128]{3,2,1,0:T(8,128)(2,1)S(1)}, bf16[1,8,64,128]{3,2,1,0:T(8,128)(2,1)S(1)}, bf16[1,...) custom-call(s32[3]{0:T(128)S(1)} %pad_add_fusion.place.place_ref, ...), custom_call_target="tpu_custom_call" | custom-call | flops 1811939328 | bytes 10903564 | tf_op jit(solution)/shard_map/pallas_call | solution.py:260
  47.4 1.2 collective-permute-start.4
  48.6 0.7 collective-permute-start.5
  49.3 4.0 %shard_map.81.packed_two = f32[864,128]{1,0:T(8,128)S(1)} custom-call(bf16[10,10,64,128]{3,2,1,0:T(8,128)(2,1)S(1)} %get-tuple-element.53.grad_pad, bf16[8,8,192,128]{3,2,1,0:T(8,128)(2,1)S(1)} %get-tuple-element.54.activ), custom_call_target="tpu_custom_call" | custom-call | flops 1811939328 | bytes 5226496 | tf_op jit(solution)/shard_map/pallas_call | solution.py:260
  53.3 4.6 %shard_map.82 = (f32[864,128]{1,0:T(8,128)S(1)}, f32[864,128]{1,0:T(8,128)S(1)}) custom-call(s32[3]{0:T(128)S(1)} %pad_add_fusion.place.place_ref, bf16[10,10,64,128]{3,2,1,0:T(8,128)(2,1)S(1)} %get-tuple-element.51.in_pad, bf16[8,8,192,128]{3,2,1,0:T(8,128)(2,1)S(1)} %get-tuple-element.52.shifted, f32[864,128]{1,0:T(8,128)S(1)} %shard_map.81.packed_two), custom_call_target="tpu_custom_call" | custom-call | flops 1811939328 | bytes 6111244 | tf_op jit(solution)/shard_map/pallas_call | solution.py:260
  57.9 0.0 collective-permute-done.4.xr_even
  57.9 0.0 collective-permute-done.5.xr_odd
  57.9 0.6 shard_map.80
  58.5 4.4 %collective-permute-start.8 = (f32[864,128]{1,0:T(8,128)S(1)}, f32[864,128]{1,0:T(8,128)S(1)}, u32[]{:S(2)}, u32[]{:S(2)}) collective-permute-start(f32[864,128]{1,0:T(8,128)S(1)} %get-tuple-element.60), channel_id=1, source_target_pairs={{0,8},{1,9},{2,10},{3,11},{4,12},{5,13},{6,14},{7,15},{8,0},{9,1},... | collective-permute-start | bytes 1327112 | tf_op jit(solution)/shard_map/ppermute | solution.py:24
  62.9 1.4 %collective-permute-done.8.recv = f32[864,128]{1,0:T(8,128)S(1)} collective-permute-done((f32[864,128]{1,0:T(8,128)S(1)}, f32[864,128]{1,0:T(8,128)S(1)}, u32[]{:S(2)}, u32[]{:S(2)}) %collective-permute-start.8) | collective-permute-done | bytes 442400 | tf_op jit(solution)/shard_map/ppermute | solution.py:24
  64.3 0.6 shard_map.85
  64.9 1.6 %collective-permute-start.9 = (f32[216,128]{1,0:T(8,128)S(1)}, f32[216,128]{1,0:T(8,128)S(1)}, u32[]{:S(2)}, u32[]{:S(2)}) collective-permute-start(f32[216,128]{1,0:T(8,128)S(1)} %get-tuple-element.62), channel_id=1, source_target_pairs={{0,16},{1,17},{2,18},{3,19},{4,20},{5,21},{6,22},{7,23},{8,24},{9,... | collective-permute-start | bytes 331784 | tf_op jit(solution)/shard_map/ppermute | solution.py:24
  66.5 2.7 %collective-permute-start.10 = (f32[216,128]{1,0:T(8,128)S(1)}, f32[216,128]{1,0:T(8,128)S(1)}, u32[]{:S(2)}, u32[]{:S(2)}) collective-permute-start(f32[216,128]{1,0:T(8,128)S(1)} %get-tuple-element.63), channel_id=1, source_target_pairs={{0,32},{1,33},{2,34},{3,35},{4,36},{5,37},{6,38},{7,39},{8,40},{9,... | collective-permute-start | bytes 331784 | tf_op jit(solution)/shard_map/ppermute | solution.py:24
  69.2 0.5 collective-permute-start.11
  69.7 1.2 collective-permute-done.9
  70.9 4.1 %collective-permute-done.10 = f32[216,128]{1,0:T(8,128)S(1)} collective-permute-done((f32[216,128]{1,0:T(8,128)S(1)}, f32[216,128]{1,0:T(8,128)S(1)}, u32[]{:S(2)}, u32[]{:S(2)}) %collective-permute-start.10) | collective-permute-done | bytes 110624 | tf_op jit(solution)/shard_map/ppermute | solution.py:24
  75.0 2.1 %collective-permute-done.11 = f32[216,128]{1,0:T(8,128)S(1)} collective-permute-done((f32[216,128]{1,0:T(8,128)S(1)}, f32[216,128]{1,0:T(8,128)S(1)}, u32[]{:S(2)}, u32[]{:S(2)}) %collective-permute-start.11) | collective-permute-done | bytes 110624 | tf_op jit(solution)/shard_map/ppermute | solution.py:24
  77.2 1.7 %collective-permute-start.14 = (f32[216,128]{1,0:T(8,128)S(1)}, f32[216,128]{1,0:T(8,128)S(1)}, u32[]{:S(2)}, u32[]{:S(2)}) collective-permute-start(f32[216,128]{1,0:T(8,128)S(1)} %add_add_fusion.2), channel_id=1, source_target_pairs={{0,6},{1,7},{2,4},{3,5},{4,2},{5,3},{6,0},{7,1},{8,14},{9,15},{10,... | collective-permute-start | bytes 331784 | tf_op jit(solution)/shard_map/ppermute | solution.py:24
  78.8 0.8 collective-permute-start.13
  79.6 1.7 %collective-permute-start.12 = (f32[216,128]{1,0:T(8,128)S(1)}, f32[216,128]{1,0:T(8,128)S(1)}, u32[]{:S(2)}, u32[]{:S(2)}) collective-permute-start(f32[216,128]{1,0:T(8,128)S(1)} %add_add_fusion.2), channel_id=1, source_target_pairs={{0,2},{1,3},{2,0},{3,1},{4,6},{5,7},{6,4},{7,5},{8,10},{9,11},{10,... | collective-permute-start | bytes 331784 | tf_op jit(solution)/shard_map/ppermute | solution.py:24
  81.3 1.4 %collective-permute-done.14 = f32[216,128]{1,0:T(8,128)S(1)} collective-permute-done((f32[216,128]{1,0:T(8,128)S(1)}, f32[216,128]{1,0:T(8,128)S(1)}, u32[]{:S(2)}, u32[]{:S(2)}) %collective-permute-start.14) | collective-permute-done | bytes 110624 | tf_op jit(solution)/shard_map/ppermute | solution.py:24
  82.7 3.3 %collective-permute-done.13 = f32[216,128]{1,0:T(8,128)S(1)} collective-permute-done((f32[216,128]{1,0:T(8,128)S(1)}, f32[216,128]{1,0:T(8,128)S(1)}, u32[]{:S(2)}, u32[]{:S(2)}) %collective-permute-start.13) | collective-permute-done | bytes 110624 | tf_op jit(solution)/shard_map/ppermute | solution.py:24
  86.1 0.2 collective-permute-done.12
  86.3 2.7 %collective-permute-start.17 = (f32[216,128]{1,0:T(8,128)S(1)}, f32[216,128]{1,0:T(8,128)S(1)}, u32[]{:S(2)}, u32[]{:S(2)}) collective-permute-start(f32[216,128]{1,0:T(8,128)S(1)} %add_add_fusion.1), channel_id=1, source_target_pairs={{0,65},{1,64},{2,67},{3,66},{4,69},{5,68},{6,71},{7,70},{8,73},{9,... | collective-permute-start | bytes 331784 | tf_op jit(solution)/shard_map/ppermute | solution.py:24
  89.0 0.9 collective-permute-start.16
  89.9 1.2 collective-permute-start.15
  91.1 1.7 %collective-permute-done.17 = f32[216,128]{1,0:T(8,128)S(1)} collective-permute-done((f32[216,128]{1,0:T(8,128)S(1)}, f32[216,128]{1,0:T(8,128)S(1)}, u32[]{:S(2)}, u32[]{:S(2)}) %collective-permute-start.17) | collective-permute-done | bytes 110624 | tf_op jit(solution)/shard_map/ppermute | solution.py:24
  92.8 0.9 collective-permute-done.16
  93.8 2.4 %collective-permute-done.15 = f32[216,128]{1,0:T(8,128)S(1)} collective-permute-done((f32[216,128]{1,0:T(8,128)S(1)}, f32[216,128]{1,0:T(8,128)S(1)}, u32[]{:S(2)}, u32[]{:S(2)}) %collective-permute-start.15) | collective-permute-done | bytes 110624 | tf_op jit(solution)/shard_map/ppermute | solution.py:24
  96.2 1.2 collective-permute-start.20
  97.4 3.0 %collective-permute-start.18 = (f32[216,128]{1,0:T(8,128)S(1)}, f32[216,128]{1,0:T(8,128)S(1)}, u32[]{:S(2)}, u32[]{:S(2)}) collective-permute-start(f32[216,128]{1,0:T(8,128)S(1)} %add_add_fusion.refs_0_), channel_id=1, source_target_pairs={{0,16},{1,17},{2,18},{3,19},{4,20},{5,21},{6,22},{7,23},{8,24},{9,... | collective-permute-start | bytes 331784 | tf_op jit(solution)/shard_map/ppermute | solution.py:24
  100.4 4.2 %collective-permute-start.7 = (bf16[1,10,64,128]{3,2,1,0:T(8,128)(2,1)S(1)}, bf16[1,10,64,128]{3,2,1,0:T(8,128)(2,1)S(1)}, u32[]{:S(2)}, u32[]{:S(2)}) collective-permute-start(bf16[1,10,64,128]{3,2,1,0:T(8,128)(2,1)S(1)} %get-tuple-element.56), channel_id=1, source_target_pairs={{1,2},{2,1},{3,4},{4,3},{5,6},{6,5},{9,10},{10,9},{11,12},{12,11},... | collective-permute-start | bytes 491528 | tf_op jit(solution)/shard_map/ppermute | solution.py:336
  104.6 2.3 %collective-permute-start.6 = (bf16[1,10,64,128]{3,2,1,0:T(8,128)(2,1)S(1)}, bf16[1,10,64,128]{3,2,1,0:T(8,128)(2,1)S(1)}, u32[]{:S(2)}, u32[]{:S(2)}) collective-permute-start(bf16[1,10,64,128]{3,2,1,0:T(8,128)(2,1)S(1)} %get-tuple-element.49), channel_id=1, source_target_pairs={{0,1},{1,0},{2,3},{3,2},{4,5},{5,4},{6,7},{7,6},{8,9},{9,8},{10,11... | collective-permute-start | bytes 491528 | tf_op jit(solution)/shard_map/ppermute | solution.py:331
  106.9 0.0 collective-permute-done.18.refs_1_
  106.9 0.6 shard_map.86.own_ref
  107.5 0.1 collective-permute-start.21
  107.6 2.5 %collective-permute-done.7.yr_odd = bf16[1,10,64,128]{3,2,1,0:T(8,128)(2,1)S(1)} collective-permute-done((bf16[1,10,64,128]{3,2,1,0:T(8,128)(2,1)S(1)}, bf16[1,10,64,128]{3,2,1,0:T(8,128)(2,1)S(1)}, u32[]{:S(2)}, u32[]{:S(2)}) %collective-permute-start.7) | collective-permute-done | bytes 163872 | tf_op jit(solution)/shard_map/ppermute | solution.py:336
  110.0 1.7 %collective-permute-done.6.yr_even = bf16[1,10,64,128]{3,2,1,0:T(8,128)(2,1)S(1)} collective-permute-done((bf16[1,10,64,128]{3,2,1,0:T(8,128)(2,1)S(1)}, bf16[1,10,64,128]{3,2,1,0:T(8,128)(2,1)S(1)}, u32[]{:S(2)}, u32[]{:S(2)}) %collective-permute-start.6) | collective-permute-done | bytes 163872 | tf_op jit(solution)/shard_map/ppermute | solution.py:331
  111.8 4.0 %shard_map.83 = (bf16[8,4,64,128]{3,2,1,0:T(8,128)(2,1)S(1)}, bf16[10,10,64,128]{3,2,1,0:T(8,128)(2,1)S(1)}) custom-call(s32[3]{0:T(128)S(1)} %pad_add_fusion.place.place_ref, f32[1,128]{1,0:T(1,128)S(1)} %convert_element_type.29.mask, bf16[192,576]{1,0:T(8,128)(2,1)S(1)} %get-tuple-element.35.weights, ...), custom_call_target="tpu_custom_call" | custom-call | flops 905969664 | bytes 5071372 | tf_op jit(solution)/shard_map/pallas_call | solution.py:260
  115.8 3.3 %shard_map.84 = bf16[8,4,64,128]{3,2,1,0:T(8,128)(2,1)S(1)} custom-call(f32[1,128]{1,0:T(1,128)S(1)} %convert_element_type.29.mask, bf16[192,576]{1,0:T(8,128)(2,1)S(1)} %get-tuple-element.35.weights, bf16[8,8,64,128]{3,2,1,0:T(8,128)(2,1)S(1)} %get-tuple-element.37.tile.base, bf16[10,10,64,128]{3,2,1,0:T(8,128)(2,1)S(1)} %get-tuple-element.58.padded), custom_call_target="tpu_custom_call" | custom-call | flops 905969664 | bytes 3432960 | tf_op jit(solution)/shard_map/pallas_call | solution.py:260
  119.1 0.1 maximum_bitcast_fusion
  119.2 1.6 %copy.29 = bf16[64,8,8,128]{3,2,1,0:T(8,128)(2,1)} copy(bf16[64,8,8,128]{3,0,2,1:T(8,128)(2,1)S(1)} %maximum_bitcast_fusion) | data formatting | bytes 2097152
  120.9 2.3 %shard_map.87 = (f32[3,3,3,64,64]{4,3,2,1,0:T(8,128)}, f32[3,3,3,64,64]{4,3,2,1,0:T(8,128)}) custom-call(s32[3]{0:T(128)S(1)} %pad_add_fusion.place.place_ref, f32[864,128]{1,0:T(8,128)S(1)} %shard_map.86.own_ref, f32[864,128]{1,0:T(8,128)S(1)} %collective-permute-done.21.other_ref), custom_call_target="tpu_custom_call" | custom-call | bytes 1769484 | tf_op jit(solution)/shard_map/pallas_call | solution.py:260
  (15 shorter events, 0.2 us)
Async XLA Ops:
  7.1 4.9 %collective-permute-start = (bf16[2,8,64,128]{3,2,1,0:T(8,128)(2,1)}, bf16[2,8,64,128]{3,2,1,0:T(8,128)(2,1)S(1)}, u32[]{:S(2)}, u32[]{:S(2)}) collective-permute-start(bf16[2,8,64,128]{3,2,1,0:T(8,128)(2,1)} %pad_maximum_fusion.2), channel_id=1, source_target_pairs={{0,8},{8,0},{16,24},{24,16},{32,40},{40,32},{48,56},{56,48},{64,72... | collective-permute-start | bytes 786440 | tf_op jit(solution)/shard_map/ppermute | solution.py:29
  7.9 4.2 %collective-permute-start.1 = (bf16[2,8,64,128]{3,2,1,0:T(8,128)(2,1)}, bf16[2,8,64,128]{3,2,1,0:T(8,128)(2,1)S(1)}, u32[]{:S(2)}, u32[]{:S(2)}) collective-permute-start(bf16[2,8,64,128]{3,2,1,0:T(8,128)(2,1)} %pad_maximum_fusion.3), channel_id=1, source_target_pairs={{8,16},{16,8},{24,32},{32,24},{40,48},{48,40},{56,64},{64,56},{72,... | collective-permute-start | bytes 786440 | tf_op jit(solution)/shard_map/ppermute | solution.py:29
  8.7 10.8 %copy-start = (bf16[3,3,3,64,64]{4,3,2,1,0:T(8,128)(2,1)S(1)}, bf16[3,3,3,64,64]{4,3,2,1,0:T(8,128)(2,1)}, u32[]{:S(2)}) copy-start(bf16[3,3,3,64,64]{4,3,2,1,0:T(8,128)(2,1)} %one.1) | copy-start | bytes 663556
  8.7 10.8 %copy-start.1 = (bf16[3,3,3,64,64]{4,3,2,1,0:T(8,128)(2,1)S(1)}, bf16[3,3,3,64,64]{4,3,2,1,0:T(8,128)(2,1)}, u32[]{:S(2)}) copy-start(bf16[3,3,3,64,64]{4,3,2,1,0:T(8,128)(2,1)} %two.1) | copy-start | bytes 663556
  13.5 20.7 %collective-permute-start.2 = (bf16[2,10,64,128]{3,2,1,0:T(8,128)(2,1)}, bf16[2,10,64,128]{3,2,1,0:T(8,128)(2,1)}, u32[]{:S(2)}, u32[]{:S(2)}) collective-permute-start(bf16[2,10,64,128]{3,2,1,0:T(8,128)(2,1)} %get-tuple-element.41), channel_id=1, source_target_pairs={{0,1},{1,0},{2,3},{3,2},{4,5},{5,4},{6,7},{7,6},{8,9},{9,8},{10,11... | collective-permute-start | bytes 983048 | tf_op jit(solution)/shard_map/ppermute | solution.py:302
  17.4 16.8 %collective-permute-start.3 = (bf16[2,10,64,128]{3,2,1,0:T(8,128)(2,1)}, bf16[2,10,64,128]{3,2,1,0:T(8,128)(2,1)}, u32[]{:S(2)}, u32[]{:S(2)}) collective-permute-start(bf16[2,10,64,128]{3,2,1,0:T(8,128)(2,1)} %get-tuple-element.42), channel_id=1, source_target_pairs={{1,2},{2,1},{3,4},{4,3},{5,6},{6,5},{9,10},{10,9},{11,12},{12,11},... | collective-permute-start | bytes 983048 | tf_op jit(solution)/shard_map/ppermute | solution.py:306
  47.4 10.5 %collective-permute-start.4 = (bf16[1,8,64,128]{3,2,1,0:T(8,128)(2,1)S(1)}, bf16[1,8,64,128]{3,2,1,0:T(8,128)(2,1)S(1)}, u32[]{:S(2)}, u32[]{:S(2)}) collective-permute-start(bf16[1,8,64,128]{3,2,1,0:T(8,128)(2,1)S(1)} %get-tuple-element.45), channel_id=1, source_target_pairs={{0,8},{8,0},{16,24},{24,16},{32,40},{40,32},{48,56},{56,48},{64,72... | collective-permute-start | bytes 393224 | tf_op jit(solution)/shard_map/ppermute | solution.py:29
  48.6 9.3 %collective-permute-start.5 = (bf16[1,8,64,128]{3,2,1,0:T(8,128)(2,1)S(1)}, bf16[1,8,64,128]{3,2,1,0:T(8,128)(2,1)S(1)}, u32[]{:S(2)}, u32[]{:S(2)}) collective-permute-start(bf16[1,8,64,128]{3,2,1,0:T(8,128)(2,1)S(1)} %get-tuple-element.46), channel_id=1, source_target_pairs={{8,16},{16,8},{24,32},{32,24},{40,48},{48,40},{56,64},{64,56},{72,... | collective-permute-start | bytes 393224 | tf_op jit(solution)/shard_map/ppermute | solution.py:29
  58.5 5.8 %collective-permute-start.8 = (f32[864,128]{1,0:T(8,128)S(1)}, f32[864,128]{1,0:T(8,128)S(1)}, u32[]{:S(2)}, u32[]{:S(2)}) collective-permute-start(f32[864,128]{1,0:T(8,128)S(1)} %get-tuple-element.60), channel_id=1, source_target_pairs={{0,8},{1,9},{2,10},{3,11},{4,12},{5,13},{6,14},{7,15},{8,0},{9,1},... | collective-permute-start | bytes 1327112 | tf_op jit(solution)/shard_map/ppermute | solution.py:24
  64.9 6.0 %collective-permute-start.9 = (f32[216,128]{1,0:T(8,128)S(1)}, f32[216,128]{1,0:T(8,128)S(1)}, u32[]{:S(2)}, u32[]{:S(2)}) collective-permute-start(f32[216,128]{1,0:T(8,128)S(1)} %get-tuple-element.62), channel_id=1, source_target_pairs={{0,16},{1,17},{2,18},{3,19},{4,20},{5,21},{6,22},{7,23},{8,24},{9,... | collective-permute-start | bytes 331784 | tf_op jit(solution)/shard_map/ppermute | solution.py:24
  66.5 8.5 %collective-permute-start.10 = (f32[216,128]{1,0:T(8,128)S(1)}, f32[216,128]{1,0:T(8,128)S(1)}, u32[]{:S(2)}, u32[]{:S(2)}) collective-permute-start(f32[216,128]{1,0:T(8,128)S(1)} %get-tuple-element.63), channel_id=1, source_target_pairs={{0,32},{1,33},{2,34},{3,35},{4,36},{5,37},{6,38},{7,39},{8,40},{9,... | collective-permute-start | bytes 331784 | tf_op jit(solution)/shard_map/ppermute | solution.py:24
  69.2 7.9 %collective-permute-start.11 = (f32[216,128]{1,0:T(8,128)S(1)}, f32[216,128]{1,0:T(8,128)S(1)}, u32[]{:S(2)}, u32[]{:S(2)}) collective-permute-start(f32[216,128]{1,0:T(8,128)S(1)} %get-tuple-element.64), channel_id=1, source_target_pairs={{0,48},{1,49},{2,50},{3,51},{4,52},{5,53},{6,54},{7,55},{8,56},{9,... | collective-permute-start | bytes 331784 | tf_op jit(solution)/shard_map/ppermute | solution.py:24
  77.2 5.5 %collective-permute-start.14 = (f32[216,128]{1,0:T(8,128)S(1)}, f32[216,128]{1,0:T(8,128)S(1)}, u32[]{:S(2)}, u32[]{:S(2)}) collective-permute-start(f32[216,128]{1,0:T(8,128)S(1)} %add_add_fusion.2), channel_id=1, source_target_pairs={{0,6},{1,7},{2,4},{3,5},{4,2},{5,3},{6,0},{7,1},{8,14},{9,15},{10,... | collective-permute-start | bytes 331784 | tf_op jit(solution)/shard_map/ppermute | solution.py:24
  78.8 7.2 %collective-permute-start.13 = (f32[216,128]{1,0:T(8,128)S(1)}, f32[216,128]{1,0:T(8,128)S(1)}, u32[]{:S(2)}, u32[]{:S(2)}) collective-permute-start(f32[216,128]{1,0:T(8,128)S(1)} %add_add_fusion.2), channel_id=1, source_target_pairs={{0,4},{1,5},{2,6},{3,7},{4,0},{5,1},{6,2},{7,3},{8,12},{9,13},{10,... | collective-permute-start | bytes 331784 | tf_op jit(solution)/shard_map/ppermute | solution.py:24
  79.6 6.7 %collective-permute-start.12 = (f32[216,128]{1,0:T(8,128)S(1)}, f32[216,128]{1,0:T(8,128)S(1)}, u32[]{:S(2)}, u32[]{:S(2)}) collective-permute-start(f32[216,128]{1,0:T(8,128)S(1)} %add_add_fusion.2), channel_id=1, source_target_pairs={{0,2},{1,3},{2,0},{3,1},{4,6},{5,7},{6,4},{7,5},{8,10},{9,11},{10,... | collective-permute-start | bytes 331784 | tf_op jit(solution)/shard_map/ppermute | solution.py:24
  86.3 6.5 %collective-permute-start.17 = (f32[216,128]{1,0:T(8,128)S(1)}, f32[216,128]{1,0:T(8,128)S(1)}, u32[]{:S(2)}, u32[]{:S(2)}) collective-permute-start(f32[216,128]{1,0:T(8,128)S(1)} %add_add_fusion.1), channel_id=1, source_target_pairs={{0,65},{1,64},{2,67},{3,66},{4,69},{5,68},{6,71},{7,70},{8,73},{9,... | collective-permute-start | bytes 331784 | tf_op jit(solution)/shard_map/ppermute | solution.py:24
  89.0 4.7 %collective-permute-start.16 = (f32[216,128]{1,0:T(8,128)S(1)}, f32[216,128]{1,0:T(8,128)S(1)}, u32[]{:S(2)}, u32[]{:S(2)}) collective-permute-start(f32[216,128]{1,0:T(8,128)S(1)} %add_add_fusion.1), channel_id=1, source_target_pairs={{0,64},{1,65},{2,66},{3,67},{4,68},{5,69},{6,70},{7,71},{8,72},{9,... | collective-permute-start | bytes 331784 | tf_op jit(solution)/shard_map/ppermute | solution.py:24
  89.9 6.3 %collective-permute-start.15 = (f32[216,128]{1,0:T(8,128)S(1)}, f32[216,128]{1,0:T(8,128)S(1)}, u32[]{:S(2)}, u32[]{:S(2)}) collective-permute-start(f32[216,128]{1,0:T(8,128)S(1)} %add_add_fusion.1), channel_id=1, source_target_pairs={{0,1},{1,0},{2,3},{3,2},{4,5},{5,4},{6,7},{7,6},{8,9},{9,8},{10,11... | collective-permute-start | bytes 331784 | tf_op jit(solution)/shard_map/ppermute | solution.py:24
  96.2 10.7 %collective-permute-start.20 = (f32[216,128]{1,0:T(8,128)S(1)}, f32[216,128]{1,0:T(8,128)S(1)}, u32[]{:S(2)}, u32[]{:S(2)}) collective-permute-start(f32[216,128]{1,0:T(8,128)S(1)} %add_add_fusion.refs_0_), channel_id=1, source_target_pairs={{0,48},{1,49},{2,50},{3,51},{4,52},{5,53},{6,54},{7,55},{8,56},{9,... | collective-permute-start | bytes 331784 | tf_op jit(solution)/shard_map/ppermute | solution.py:24
  97.4 9.5 %collective-permute-start.19 = (f32[216,128]{1,0:T(8,128)S(1)}, f32[216,128]{1,0:T(8,128)S(1)}, u32[]{:S(2)}, u32[]{:S(2)}) collective-permute-start(f32[216,128]{1,0:T(8,128)S(1)} %add_add_fusion.refs_0_), channel_id=1, source_target_pairs={{0,32},{1,33},{2,34},{3,35},{4,36},{5,37},{6,38},{7,39},{8,40},{9,... | collective-permute-start | bytes 331784 | tf_op jit(solution)/shard_map/ppermute | solution.py:24
  97.4 9.5 %collective-permute-start.18 = (f32[216,128]{1,0:T(8,128)S(1)}, f32[216,128]{1,0:T(8,128)S(1)}, u32[]{:S(2)}, u32[]{:S(2)}) collective-permute-start(f32[216,128]{1,0:T(8,128)S(1)} %add_add_fusion.refs_0_), channel_id=1, source_target_pairs={{0,16},{1,17},{2,18},{3,19},{4,20},{5,21},{6,22},{7,23},{8,24},{9,... | collective-permute-start | bytes 331784 | tf_op jit(solution)/shard_map/ppermute | solution.py:24
  100.4 9.6 %collective-permute-start.7 = (bf16[1,10,64,128]{3,2,1,0:T(8,128)(2,1)S(1)}, bf16[1,10,64,128]{3,2,1,0:T(8,128)(2,1)S(1)}, u32[]{:S(2)}, u32[]{:S(2)}) collective-permute-start(bf16[1,10,64,128]{3,2,1,0:T(8,128)(2,1)S(1)} %get-tuple-element.56), channel_id=1, source_target_pairs={{1,2},{2,1},{3,4},{4,3},{5,6},{6,5},{9,10},{10,9},{11,12},{12,11},... | collective-permute-start | bytes 491528 | tf_op jit(solution)/shard_map/ppermute | solution.py:336
  104.6 7.2 %collective-permute-start.6 = (bf16[1,10,64,128]{3,2,1,0:T(8,128)(2,1)S(1)}, bf16[1,10,64,128]{3,2,1,0:T(8,128)(2,1)S(1)}, u32[]{:S(2)}, u32[]{:S(2)}) collective-permute-start(bf16[1,10,64,128]{3,2,1,0:T(8,128)(2,1)S(1)} %get-tuple-element.49), channel_id=1, source_target_pairs={{0,1},{1,0},{2,3},{3,2},{4,5},{5,4},{6,7},{7,6},{8,9},{9,8},{10,11... | collective-permute-start | bytes 491528 | tf_op jit(solution)/shard_map/ppermute | solution.py:331
  107.5 13.4 %collective-permute-start.21 = (f32[864,128]{1,0:T(8,128)S(1)}, f32[864,128]{1,0:T(8,128)S(1)}, u32[]{:S(2)}, u32[]{:S(2)}) collective-permute-start(f32[864,128]{1,0:T(8,128)S(1)} %shard_map.86.own_ref), channel_id=1, source_target_pairs={{0,8},{1,9},{2,10},{3,11},{4,12},{5,13},{6,14},{7,15},{8,0},{9,1},... | collective-permute-start | bytes 1327112 | tf_op jit(solution)/shard_map/ppermute | solution.py:24

commit v5 on v3

--- a/solution.py
+++ b/solution.py
@@ -1,4 +1,3 @@
-import functools
 import math
 
 import jax
@@ -64,14 +63,18 @@
     lax.fori_loop(0, size_x, body, 0)
 
 
-def ypack_kernel(place, tile, xr_even, xr_odd, ys_even, ys_odd, *, which):
-    size_x, size_y = tile.shape[0], tile.shape[1]
+def ypack_kernel(place, *refs):
+    count = (len(refs) - 2) // 3
+    tiles, (xr_even, xr_odd), outs = refs[:count], refs[count : count + 2], refs[count + 2 :]
+    size_x, size_y = tiles[0].shape[0], tiles[0].shape[1]
     x_even, x_odd = sides(place[0], size_x)
-    for out, edge in ((ys_even, (1 - place[1]) * (size_y - 1)), (ys_odd, place[1] * (size_y - 1))):
-        out[x_even] = xr_even[which, edge]
-        out[x_odd] = xr_odd[which, edge]
-        for i in range(size_x):
-            out[i + 1] = tile[i, edge]
+    edges = (1 - place[1]) * (size_y - 1), place[1] * (size_y - 1)
+    for k, tile in enumerate(tiles):
+        for out, edge in zip(outs[2 * k : 2 * k + 2], edges):
+            out[x_even] = xr_even[k, edge]
+            out[x_odd] = xr_odd[k, edge]
+            for i in range(size_x):
+                out[i + 1] = tile[i, edge]
 
 
 def conv_padded(padded, weights, first, count, emit):
@@ -243,7 +246,11 @@
             for b in range(3):
                 for j in range(3):
                     grad_one[a, b, 2 - j] = block(one, a, b, j) * scale
-                    grad_two[2 - a, 2 - b, j] = block(two, a, b, j).T * scale
+                start = (3 * a + b) * chans
+                pair = two[start : start + chans, :].T * scale
+                grad_two[2 - a, 2 - b, 0] = pair[0:chans]
+                grad_two[2 - a, 2 - b, 1] = pair[chans : 2 * chans]
+                grad_two[2 - a, 2 - b, 2] = block(two, a, b, 2).T * scale
 
     @pl.when(place[0] == 0)
     def _():
@@ -301,12 +308,12 @@
     pad_b = jax.ShapeDtypeStruct((tile_x + 2, tile_y + 2, chans, tile_z), BF16)
     flops = 2 * 27 * chans * chans * tile_x * tile_y * tile_z
 
-    def y_sends(tile, halo_x, which):
-        kernel = functools.partial(ypack_kernel, which=which)
-        return call(kernel, [column_b] * 2, scalars=1)(place, tile, *halo_x)
-
-    in_sends = y_sends(masked_in, xr, 0)
-    grad_sends = y_sends(masked_grad, xr, 1)
+    def y_sends(tiles, halo_x):
+        outs = [column_b] * (2 * len(tiles))
+        return call(ypack_kernel, outs, scalars=1)(place, *tiles, *halo_x)
+
+    sends = y_sends((masked_in, masked_grad), xr)
+    in_sends, grad_sends = sends[:2], sends[2:]
     matrix = jax.ShapeDtypeStruct((3 * chans, 9 * chans), BF16)
     even, odd = swap_perms(lax.axis_size("gy"))
     in_even = lax.ppermute(in_sends[0], "gy", even)
@@ -330,8 +337,10 @@
     half = jax.ShapeDtypeStruct((packed, 2 * chans), F32)
     pre_xr = swap(xs_even, xs_odd, "gx")
     (packed_two,) = call(grad_two_kernel, [half], [tile_s, grad_s], flops=flops)(grad_pad, activ)
-    pre_sends = y_sends(pre_grad, pre_xr, 0)
-    pre_yr = swap(*pre_sends, "gy")
+    pre_sends = y_sends((pre_grad,), pre_xr)
+    pre_even = lax.ppermute(pre_sends[0], "gy", even)
+    pre_odd = lax.ppermute(pre_sends[1], "gy", odd)
+    pre_yr = (pre_even, pre_odd)
     keep, send = call(grad_one_kernel, [half, half], [tile_s, grad_s], scalars=1, flops=flops)(
         place, in_pad, pre_grad, packed_two
     )

time: 115 us -> 116 us (level)
  the two profiles are of different devices: /device:TPU:8 before, /device:TPU:15 now
where the time goes in v5:
time: 116 us
  starting transfers between devices  41.6 us (36%)
  Pallas kernels  34.8 us (30%)
  waiting for transfers between devices  28.8 us (25%)
  other arithmetic  5.83 us (5%)
  local copies, waits for them, and re-layouts  3.8 us (3%)
    pallas_call x12, Pallas kernels, run(): pl.pallas_call(kernel, out_shape=tuple(outs), in_specs=specs, out_specs=t...  34.8 us
    ppermute x14, starting transfers between devices, xor_permute(): return lax.ppermute(value, AXES, [(i, i ^ mask) for i in range(total)])  16.3 us
    ppermute x14, waiting for transfers between devices, xor_permute(): return lax.ppermute(value, AXES, [(i, i ^ mask) for i in range(total)])  11.8 us
    ppermute x3, starting transfers between devices, swap(): lax.ppermute(value_odd, axis, odd)  9.04 us
    ppermute x3, waiting for transfers between devices, swap(): lax.ppermute(value_odd, axis, odd)  6.54 us
    ppermute x1, starting transfers between devices, body(): in_odd = lax.ppermute(in_next, 'gy', odd)  5.38 us
    ppermute x3, starting transfers between devices, swap(): lax.ppermute(value_even, axis, even)  5.35 us
    ppermute x1, waiting for transfers between devices, body(): in_even = lax.ppermute(in_sends[0], 'gy', even)  5.2 us
  transfers between devices with their start and end apart: 24, of which 12 were waited for; matrix products, arithmetic and copies ran while one was open for 5% of the time, Pallas kernels for 13%

profile of v5, /device:TPU:15, one launch (start us, length us, event | category | flops | bytes accessed | tf_op | source)
XLA Modules:
  0.0 115.8 jit_solution(13190223839620114594)
XLA Ops:
  0.7 0.8 convert_bitcast_fusion
  1.4 0.1 broadcast_in_dim.8
  1.5 0.1 convert_element_type.32
  1.6 1.2 constant_dynamic-slice_fusion
  2.7 0.1 fusion.3
  2.8 0.7 pad_maximum_fusion
  3.6 0.7 collective-permute-start
  4.2 0.7 pad_maximum_fusion.1
  5.0 3.3 %collective-permute-start.1 = (bf16[2,8,64,128]{3,2,1,0:T(8,128)(2,1)}, bf16[2,8,64,128]{3,2,1,0:T(8,128)(2,1)S(1)}, u32[]{:S(2)}, u32[]{:S(2)}) collective-permute-start(bf16[2,8,64,128]{3,2,1,0:T(8,128)(2,1)} %pad_maximum_fusion.1), channel_id=1, source_target_pairs={{8,16},{16,8},{24,32},{32,24},{40,48},{48,40},{56,64},{64,56},{72,... | collective-permute-start | bytes 786440 | tf_op jit(solution)/shard_map/ppermute | solution.py:29
  8.3 0.3 shard_map.76
  8.6 0.1 pad_add_fusion.place.place_ref
  8.7 3.3 %fusion = (bf16[8,8,64,128]{3,2,1,0:T(8,128)(2,1)S(1)}, bf16[8,8,64,128]{3,2,1,0:T(8,128)(2,1)S(1)}) fusion(bf16[64,8,8,128]{3,2,1,0:T(8,128)(2,1)} %param.5, bf16[128]{0:T(256)(128)(2,1)S(1)} %convert_element_type.32, bf16[64,8,8,128]{3,2,1,0:T(8,128)(2,1)} %param.6), kind=kLoop, calls=%fused_computation.2 | loop fusion | flops 1048576 | bytes 4194560 | tf_op jit(solution)/shard_map/transpose | solution.py:301
  12.0 0.0 collective-permute-done.refs_2_.xr_even
  12.0 3.0 %collective-permute-done.1.refs_3_.xr_odd = bf16[2,8,64,128]{3,2,1,0:T(8,128)(2,1)S(1)} collective-permute-done((bf16[2,8,64,128]{3,2,1,0:T(8,128)(2,1)}, bf16[2,8,64,128]{3,2,1,0:T(8,128)(2,1)S(1)}, u32[]{:S(2)}, u32[]{:S(2)}) %collective-permute-start.1) | collective-permute-done | bytes 262176 | tf_op jit(solution)/shard_map/ppermute | solution.py:29
  15.0 1.3 %shard_map.77 = (bf16[10,64,128]{2,1,0:T(8,128)(2,1)}, bf16[10,64,128]{2,1,0:T(8,128)(2,1)}, bf16[10,64,128]{2,1,0:T(8,128)(2,1)S(1)}, bf16[10,64,128]{2,1,0:T(8,128)(2,1)S(1)}) custom-call(s32[3]{0:T(128)S(1)} %pad_add_fusion.place.place_ref, bf16[8,8,64,128]{3,2,1,0:T(8,128)(2,1)S(1)} %get-tuple-element.73.refs_0_.tile, ...), custom_call_target="tpu_custom_call" | custom-call | bytes 3276812 | tf_op jit(solution)/shard_map/pallas_call | solution.py:270
  16.3 0.7 copy-done.2
  16.9 5.4 %collective-permute-start.3 = (bf16[10,64,128]{2,1,0:T(8,128)(2,1)}, bf16[10,64,128]{2,1,0:T(8,128)(2,1)}, u32[]{:S(2)}, u32[]{:S(2)}) collective-permute-start(bf16[10,64,128]{2,1,0:T(8,128)(2,1)} %get-tuple-element.37), channel_id=1, source_target_pairs={{1,2},{2,1},{3,4},{4,3},{5,6},{6,5},{9,10},{10,9},{11,12},{12,11},... | collective-permute-start | bytes 491528 | tf_op jit(solution)/shard_map/ppermute | solution.py:322
  22.3 0.6 collective-permute-start.2
  22.9 0.1 broadcast_in_dim.7
  23.0 0.1 convert_element_type.29.mask
  23.1 2.5 %collective-permute-start.4 = (bf16[10,64,128]{2,1,0:T(8,128)(2,1)}, bf16[10,64,128]{2,1,0:T(8,128)(2,1)S(1)}, u32[]{:S(2)}, u32[]{:S(2)}) collective-permute-start(bf16[10,64,128]{2,1,0:T(8,128)(2,1)} %copy-done.2), channel_id=1, source_target_pairs={{0,1},{1,0},{2,3},{3,2},{4,5},{5,4},{6,7},{7,6},{8,9},{9,8},{10,11... | collective-permute-start | bytes 491528 | tf_op jit(solution)/shard_map/ppermute | solution.py:29
  25.6 2.3 %collective-permute-start.5 = (bf16[10,64,128]{2,1,0:T(8,128)(2,1)S(1)}, bf16[10,64,128]{2,1,0:T(8,128)(2,1)S(1)}, u32[]{:S(2)}, u32[]{:S(2)}) collective-permute-start(bf16[10,64,128]{2,1,0:T(8,128)(2,1)S(1)} %get-tuple-element.40), channel_id=1, source_target_pairs={{1,2},{2,1},{3,4},{4,3},{5,6},{6,5},{9,10},{10,9},{11,12},{12,11},... | collective-permute-start | bytes 491528 | tf_op jit(solution)/shard_map/ppermute | solution.py:29
  27.9 0.0 collective-permute-done.3.yr_odd
  27.9 5.2 %collective-permute-done.2.yr_even = bf16[10,64,128]{2,1,0:T(8,128)(2,1)} collective-permute-done((bf16[10,64,128]{2,1,0:T(8,128)(2,1)}, bf16[10,64,128]{2,1,0:T(8,128)(2,1)}, u32[]{:S(2)}, u32[]{:S(2)}) %collective-permute-start.2) | collective-permute-done | bytes 163872 | tf_op jit(solution)/shard_map/ppermute | solution.py:319
  33.1 5.9 %shard_map.78 = (bf16[8,8,64,128]{3,2,1,0:T(8,128)(2,1)S(1)}, f32[8,8,64,128]{3,2,1,0:T(8,128)S(1)}, bf16[10,10,64,128]{3,2,1,0:T(8,128)(2,1)S(1)}) custom-call(s32[3]{0:T(128)S(1)} %pad_add_fusion.place.place_ref, f32[1,128]{1,0:T(1,128)S(1)} %convert_element_type.29.mask, bf16[192,576]{1,0:T(8,128)(2,1)S(1)} %get-tuple-element.35.weights, ...), custom_call_target="tpu_custom_call" | custom-call | flops 1811939328 | bytes 6906380 | tf_op jit(solution)/shard_map/pallas_call | solution.py:270
  39.0 0.0 collective-permute-done.4.yr_even
  39.0 5.2 %shard_map.79 = (bf16[8,8,64,128]{3,2,1,0:T(8,128)(2,1)S(1)}, bf16[1,8,64,128]{3,2,1,0:T(8,128)(2,1)S(1)}, bf16[1,8,64,128]{3,2,1,0:T(8,128)(2,1)S(1)}, bf16[10,10,64,128]{3,2,1,0:T(8,128)(2,1)S(1)}) custom-call(s32[3]{0:T(128)S(1)} %pad_add_fusion.place.place_ref, bf16[192,576]{1,0:T(8,128)(2,1)S(1)} %get-tuple-element.32.weights, ...), custom_call_target="tpu_custom_call" | custom-call | flops 1811939328 | bytes 7168012 | tf_op jit(solution)/shard_map/pallas_call | solution.py:270
  44.3 5.1 %shard_map.83.packed_two = f32[864,128]{1,0:T(8,128)S(1)} custom-call(bf16[10,10,64,128]{3,2,1,0:T(8,128)(2,1)S(1)} %get-tuple-element.49.grad_pad, bf16[8,8,64,128]{3,2,1,0:T(8,128)(2,1)S(1)} %get-tuple-element.50.activ), custom_call_target="tpu_custom_call" | custom-call | flops 1811939328 | bytes 3129344 | tf_op jit(solution)/shard_map/pallas_call | solution.py:270
  49.4 5.7 %shard_map.84 = (f32[864,128]{1,0:T(8,128)S(1)}, f32[864,128]{1,0:T(8,128)S(1)}) custom-call(s32[3]{0:T(128)S(1)} %pad_add_fusion.place.place_ref, bf16[10,10,64,128]{3,2,1,0:T(8,128)(2,1)S(1)} %get-tuple-element.48.in_pad, bf16[8,8,64,128]{3,2,1,0:T(8,128)(2,1)S(1)} %get-tuple-element.41.refs_0_.tile.pre_grad, f32[864,128]{1,0:T(8,128)S(1)} %shard_map.83.packed_two), custom_call_target="tpu_custom_call" | custom-call | flops 1811939328 | bytes 4014092 | tf_op jit(solution)/shard_map/pallas_call | solution.py:270
  55.1 0.1 collective-permute-start.10
  55.2 1.8 %collective-permute-done.10.recv = f32[864,128]{1,0:T(8,128)S(1)} collective-permute-done((f32[864,128]{1,0:T(8,128)S(1)}, f32[864,128]{1,0:T(8,128)S(1)}, u32[]{:S(2)}, u32[]{:S(2)}) %collective-permute-start.10) | collective-permute-done | bytes 442400 | tf_op jit(solution)/shard_map/ppermute | solution.py:24
  57.0 0.6 shard_map.85
  57.6 0.2 collective-permute-start.11
  57.8 0.7 collective-permute-start.12
  58.4 3.1 %collective-permute-start.13 = (f32[216,128]{1,0:T(8,128)S(1)}, f32[216,128]{1,0:T(8,128)S(1)}, u32[]{:S(2)}, u32[]{:S(2)}) collective-permute-start(f32[216,128]{1,0:T(8,128)S(1)} %get-tuple-element.56), channel_id=1, source_target_pairs={{0,48},{1,49},{2,50},{3,51},{4,52},{5,53},{6,54},{7,55},{8,56},{9,... | collective-permute-start | bytes 331784 | tf_op jit(solution)/shard_map/ppermute | solution.py:24
  61.5 0.6 collective-permute-done.11
  62.1 1.1 collective-permute-done.12
  63.2 3.4 %collective-permute-done.13 = f32[216,128]{1,0:T(8,128)S(1)} collective-permute-done((f32[216,128]{1,0:T(8,128)S(1)}, f32[216,128]{1,0:T(8,128)S(1)}, u32[]{:S(2)}, u32[]{:S(2)}) %collective-permute-start.13) | collective-permute-done | bytes 110624 | tf_op jit(solution)/shard_map/ppermute | solution.py:24
  66.7 1.4 %collective-permute-start.16 = (f32[216,128]{1,0:T(8,128)S(1)}, f32[216,128]{1,0:T(8,128)S(1)}, u32[]{:S(2)}, u32[]{:S(2)}) collective-permute-start(f32[216,128]{1,0:T(8,128)S(1)} %add_add_fusion.2), channel_id=1, source_target_pairs={{0,6},{1,7},{2,4},{3,5},{4,2},{5,3},{6,0},{7,1},{8,14},{9,15},{10,... | collective-permute-start | bytes 331784 | tf_op jit(solution)/shard_map/ppermute | solution.py:24
  68.0 0.7 collective-permute-start.15
  68.7 1.3 %collective-permute-start.14 = (f32[216,128]{1,0:T(8,128)S(1)}, f32[216,128]{1,0:T(8,128)S(1)}, u32[]{:S(2)}, u32[]{:S(2)}) collective-permute-start(f32[216,128]{1,0:T(8,128)S(1)} %add_add_fusion.2), channel_id=1, source_target_pairs={{0,2},{1,3},{2,0},{3,1},{4,6},{5,7},{6,4},{7,5},{8,10},{9,11},{10,... | collective-permute-start | bytes 331784 | tf_op jit(solution)/shard_map/ppermute | solution.py:24
  70.0 0.9 collective-permute-done.16
  70.9 2.2 %collective-permute-done.15 = f32[216,128]{1,0:T(8,128)S(1)} collective-permute-done((f32[216,128]{1,0:T(8,128)S(1)}, f32[216,128]{1,0:T(8,128)S(1)}, u32[]{:S(2)}, u32[]{:S(2)}) %collective-permute-start.15) | collective-permute-done | bytes 110624 | tf_op jit(solution)/shard_map/ppermute | solution.py:24
  73.1 1.7 %collective-permute-done.14 = f32[216,128]{1,0:T(8,128)S(1)} collective-permute-done((f32[216,128]{1,0:T(8,128)S(1)}, f32[216,128]{1,0:T(8,128)S(1)}, u32[]{:S(2)}, u32[]{:S(2)}) %collective-permute-start.14) | collective-permute-done | bytes 110624 | tf_op jit(solution)/shard_map/ppermute | solution.py:24
  74.9 4.3 %collective-permute-start.19 = (f32[216,128]{1,0:T(8,128)S(1)}, f32[216,128]{1,0:T(8,128)S(1)}, u32[]{:S(2)}, u32[]{:S(2)}) collective-permute-start(f32[216,128]{1,0:T(8,128)S(1)} %add_add_fusion.1), channel_id=1, source_target_pairs={{0,65},{1,64},{2,67},{3,66},{4,69},{5,68},{6,71},{7,70},{8,73},{9,... | collective-permute-start | bytes 331784 | tf_op jit(solution)/shard_map/ppermute | solution.py:24
  79.2 1.3 %collective-permute-start.17 = (f32[216,128]{1,0:T(8,128)S(1)}, f32[216,128]{1,0:T(8,128)S(1)}, u32[]{:S(2)}, u32[]{:S(2)}) collective-permute-start(f32[216,128]{1,0:T(8,128)S(1)} %add_add_fusion.1), channel_id=1, source_target_pairs={{0,1},{1,0},{2,3},{3,2},{4,5},{5,4},{6,7},{7,6},{8,9},{9,8},{10,11... | collective-permute-start | bytes 331784 | tf_op jit(solution)/shard_map/ppermute | solution.py:24
  80.4 2.1 %collective-permute-start.6 = (bf16[1,8,64,128]{3,2,1,0:T(8,128)(2,1)S(1)}, bf16[1,8,64,128]{3,2,1,0:T(8,128)(2,1)S(1)}, u32[]{:S(2)}, u32[]{:S(2)}) collective-permute-start(bf16[1,8,64,128]{3,2,1,0:T(8,128)(2,1)S(1)} %get-tuple-element.42), channel_id=1, source_target_pairs={{0,8},{8,0},{16,24},{24,16},{32,40},{40,32},{48,56},{56,48},{64,72... | collective-permute-start | bytes 393224 | tf_op jit(solution)/shard_map/ppermute | solution.py:29
  82.6 3.4 %collective-permute-start.7 = (bf16[1,8,64,128]{3,2,1,0:T(8,128)(2,1)S(1)}, bf16[1,8,64,128]{3,2,1,0:T(8,128)(2,1)S(1)}, u32[]{:S(2)}, u32[]{:S(2)}) collective-permute-start(bf16[1,8,64,128]{3,2,1,0:T(8,128)(2,1)S(1)} %get-tuple-element.43), channel_id=1, source_target_pairs={{8,16},{16,8},{24,32},{32,24},{40,48},{48,40},{56,64},{64,56},{72,... | collective-permute-start | bytes 393224 | tf_op jit(solution)/shard_map/ppermute | solution.py:29
  86.1 1.2 %collective-permute-start.22 = (f32[216,128]{1,0:T(8,128)S(1)}, f32[216,128]{1,0:T(8,128)S(1)}, u32[]{:S(2)}, u32[]{:S(2)}) collective-permute-start(f32[216,128]{1,0:T(8,128)S(1)} %add_add_fusion.refs_0_), channel_id=1, source_target_pairs={{0,48},{1,49},{2,50},{3,51},{4,52},{5,53},{6,54},{7,55},{8,56},{9,... | collective-permute-start | bytes 331784 | tf_op jit(solution)/shard_map/ppermute | solution.py:24
  87.3 0.5 collective-permute-start.21
  87.8 1.6 %collective-permute-start.20 = (f32[216,128]{1,0:T(8,128)S(1)}, f32[216,128]{1,0:T(8,128)S(1)}, u32[]{:S(2)}, u32[]{:S(2)}) collective-permute-start(f32[216,128]{1,0:T(8,128)S(1)} %add_add_fusion.refs_0_), channel_id=1, source_target_pairs={{0,16},{1,17},{2,18},{3,19},{4,20},{5,21},{6,22},{7,23},{8,24},{9,... | collective-permute-start | bytes 331784 | tf_op jit(solution)/shard_map/ppermute | solution.py:24
  89.4 3.6 %collective-permute-done.7.refs_2_.xr_odd = bf16[1,8,64,128]{3,2,1,0:T(8,128)(2,1)S(1)} collective-permute-done((bf16[1,8,64,128]{3,2,1,0:T(8,128)(2,1)S(1)}, bf16[1,8,64,128]{3,2,1,0:T(8,128)(2,1)S(1)}, u32[]{:S(2)}, u32[]{:S(2)}) %collective-permute-start.7) | collective-permute-done | bytes 131104 | tf_op jit(solution)/shard_map/ppermute | solution.py:29
  93.0 0.6 shard_map.80
  93.6 2.1 %collective-permute-start.8 = (bf16[10,64,128]{2,1,0:T(8,128)(2,1)S(1)}, bf16[10,64,128]{2,1,0:T(8,128)(2,1)S(1)}, u32[]{:S(2)}, u32[]{:S(2)}) collective-permute-start(bf16[10,64,128]{2,1,0:T(8,128)(2,1)S(1)} %get-tuple-element.44), channel_id=1, source_target_pairs={{0,1},{1,0},{2,3},{3,2},{4,5},{5,4},{6,7},{7,6},{8,9},{9,8},{10,11... | collective-permute-start | bytes 491528 | tf_op jit(solution)/shard_map/ppermute | solution.py:341
  95.7 2.8 %collective-permute-start.9 = (bf16[10,64,128]{2,1,0:T(8,128)(2,1)S(1)}, bf16[10,64,128]{2,1,0:T(8,128)(2,1)S(1)}, u32[]{:S(2)}, u32[]{:S(2)}) collective-permute-start(bf16[10,64,128]{2,1,0:T(8,128)(2,1)S(1)} %get-tuple-element.45), channel_id=1, source_target_pairs={{1,2},{2,1},{3,4},{4,3},{5,6},{6,5},{9,10},{10,9},{11,12},{12,11},... | collective-permute-start | bytes 491528 | tf_op jit(solution)/shard_map/ppermute | solution.py:342
  98.5 0.6 shard_map.86.own_ref
  99.1 0.1 collective-permute-start.23
  99.2 0.9 collective-permute-done.8.yr_even
  100.1 4.3 %collective-permute-done.9.yr_odd = bf16[10,64,128]{2,1,0:T(8,128)(2,1)S(1)} collective-permute-done((bf16[10,64,128]{2,1,0:T(8,128)(2,1)S(1)}, bf16[10,64,128]{2,1,0:T(8,128)(2,1)S(1)}, u32[]{:S(2)}, u32[]{:S(2)}) %collective-permute-start.9) | collective-permute-done | bytes 163872 | tf_op jit(solution)/shard_map/ppermute | solution.py:342
  104.4 4.0 %shard_map.81 = (bf16[8,4,64,128]{3,2,1,0:T(8,128)(2,1)S(1)}, bf16[10,10,64,128]{3,2,1,0:T(8,128)(2,1)S(1)}) custom-call(s32[3]{0:T(128)S(1)} %pad_add_fusion.place.place_ref, f32[1,128]{1,0:T(1,128)S(1)} %convert_element_type.29.mask, bf16[192,576]{1,0:T(8,128)(2,1)S(1)} %get-tuple-element.31.weights, ...), custom_call_target="tpu_custom_call" | custom-call | flops 905969664 | bytes 5071372 | tf_op jit(solution)/shard_map/pallas_call | solution.py:270
  108.4 3.3 %shard_map.82 = bf16[8,4,64,128]{3,2,1,0:T(8,128)(2,1)S(1)} custom-call(f32[1,128]{1,0:T(1,128)S(1)} %convert_element_type.29.mask, bf16[192,576]{1,0:T(8,128)(2,1)S(1)} %get-tuple-element.31.weights, bf16[8,8,64,128]{3,2,1,0:T(8,128)(2,1)S(1)} %get-tuple-element.74.refs_1_.tile.base, bf16[10,10,64,128]{3,2,1,0:T(8,128)(2,1)S(1)} %get-tuple-element.47.padded), custom_call_target="tpu_custom_call" | custom-call | flops 905969664 | bytes 3432960 | tf_op jit(solution)/shard_map/pallas_call | solution.py:270
  111.8 0.1 maximum_bitcast_fusion
  111.9 1.6 %copy.21 = bf16[64,8,8,128]{3,2,1,0:T(8,128)(2,1)} copy(bf16[64,8,8,128]{3,0,2,1:T(8,128)(2,1)S(1)} %maximum_bitcast_fusion) | data formatting | bytes 2097152
  113.5 2.2 %shard_map.87 = (f32[3,3,3,64,64]{4,3,2,1,0:T(8,128)}, f32[3,3,3,64,64]{4,3,2,1,0:T(8,128)}) custom-call(s32[3]{0:T(128)S(1)} %pad_add_fusion.place.place_ref, f32[864,128]{1,0:T(8,128)S(1)} %shard_map.86.own_ref, f32[864,128]{1,0:T(8,128)S(1)} %collective-permute-done.23.other_ref), custom_call_target="tpu_custom_call" | custom-call | bytes 1769484 | tf_op jit(solution)/shard_map/pallas_call | solution.py:270
  (18 shorter events, 0.1 us)
Async XLA Ops:
  0.6 7.7 %copy-start.1 = (bf16[3,3,3,64,64]{4,3,2,1,0:T(8,128)(2,1)S(1)}, bf16[3,3,3,64,64]{4,3,2,1,0:T(8,128)(2,1)}, u32[]{:S(2)}) copy-start(bf16[3,3,3,64,64]{4,3,2,1,0:T(8,128)(2,1)} %two.1) | copy-start | bytes 663556
  0.6 7.7 %copy-start = (bf16[3,3,3,64,64]{4,3,2,1,0:T(8,128)(2,1)S(1)}, bf16[3,3,3,64,64]{4,3,2,1,0:T(8,128)(2,1)}, u32[]{:S(2)}) copy-start(bf16[3,3,3,64,64]{4,3,2,1,0:T(8,128)(2,1)} %one.1) | copy-start | bytes 663556
  3.6 8.4 %collective-permute-start = (bf16[2,8,64,128]{3,2,1,0:T(8,128)(2,1)}, bf16[2,8,64,128]{3,2,1,0:T(8,128)(2,1)S(1)}, u32[]{:S(2)}, u32[]{:S(2)}) collective-permute-start(bf16[2,8,64,128]{3,2,1,0:T(8,128)(2,1)} %pad_maximum_fusion), channel_id=1, source_target_pairs={{0,8},{8,0},{16,24},{24,16},{32,40},{40,32},{48,56},{56,48},{64,72... | collective-permute-start | bytes 786440 | tf_op jit(solution)/shard_map/ppermute | solution.py:29
  5.0 10.0 %collective-permute-start.1 = (bf16[2,8,64,128]{3,2,1,0:T(8,128)(2,1)}, bf16[2,8,64,128]{3,2,1,0:T(8,128)(2,1)S(1)}, u32[]{:S(2)}, u32[]{:S(2)}) collective-permute-start(bf16[2,8,64,128]{3,2,1,0:T(8,128)(2,1)} %pad_maximum_fusion.1), channel_id=1, source_target_pairs={{8,16},{16,8},{24,32},{32,24},{40,48},{48,40},{56,64},{64,56},{72,... | collective-permute-start | bytes 786440 | tf_op jit(solution)/shard_map/ppermute | solution.py:29
  16.3 0.7 copy-start.2
  16.9 11.0 %collective-permute-start.3 = (bf16[10,64,128]{2,1,0:T(8,128)(2,1)}, bf16[10,64,128]{2,1,0:T(8,128)(2,1)}, u32[]{:S(2)}, u32[]{:S(2)}) collective-permute-start(bf16[10,64,128]{2,1,0:T(8,128)(2,1)} %get-tuple-element.37), channel_id=1, source_target_pairs={{1,2},{2,1},{3,4},{4,3},{5,6},{6,5},{9,10},{10,9},{11,12},{12,11},... | collective-permute-start | bytes 491528 | tf_op jit(solution)/shard_map/ppermute | solution.py:322
  22.3 10.8 %collective-permute-start.2 = (bf16[10,64,128]{2,1,0:T(8,128)(2,1)}, bf16[10,64,128]{2,1,0:T(8,128)(2,1)}, u32[]{:S(2)}, u32[]{:S(2)}) collective-permute-start(bf16[10,64,128]{2,1,0:T(8,128)(2,1)} %get-tuple-element.36), channel_id=1, source_target_pairs={{0,1},{1,0},{2,3},{3,2},{4,5},{5,4},{6,7},{7,6},{8,9},{9,8},{10,11... | collective-permute-start | bytes 491528 | tf_op jit(solution)/shard_map/ppermute | solution.py:319
  23.1 15.9 %collective-permute-start.4 = (bf16[10,64,128]{2,1,0:T(8,128)(2,1)}, bf16[10,64,128]{2,1,0:T(8,128)(2,1)S(1)}, u32[]{:S(2)}, u32[]{:S(2)}) collective-permute-start(bf16[10,64,128]{2,1,0:T(8,128)(2,1)} %copy-done.2), channel_id=1, source_target_pairs={{0,1},{1,0},{2,3},{3,2},{4,5},{5,4},{6,7},{7,6},{8,9},{9,8},{10,11... | collective-permute-start | bytes 491528 | tf_op jit(solution)/shard_map/ppermute | solution.py:29
  25.6 13.4 %collective-permute-start.5 = (bf16[10,64,128]{2,1,0:T(8,128)(2,1)S(1)}, bf16[10,64,128]{2,1,0:T(8,128)(2,1)S(1)}, u32[]{:S(2)}, u32[]{:S(2)}) collective-permute-start(bf16[10,64,128]{2,1,0:T(8,128)(2,1)S(1)} %get-tuple-element.40), channel_id=1, source_target_pairs={{1,2},{2,1},{3,4},{4,3},{5,6},{6,5},{9,10},{10,9},{11,12},{12,11},... | collective-permute-start | bytes 491528 | tf_op jit(solution)/shard_map/ppermute | solution.py:29
  55.1 1.9 %collective-permute-start.10 = (f32[864,128]{1,0:T(8,128)S(1)}, f32[864,128]{1,0:T(8,128)S(1)}, u32[]{:S(2)}, u32[]{:S(2)}) collective-permute-start(f32[864,128]{1,0:T(8,128)S(1)} %get-tuple-element.52), channel_id=1, source_target_pairs={{0,8},{1,9},{2,10},{3,11},{4,12},{5,13},{6,14},{7,15},{8,0},{9,1},... | collective-permute-start | bytes 1327112 | tf_op jit(solution)/shard_map/ppermute | solution.py:24
  57.6 4.6 %collective-permute-start.11 = (f32[216,128]{1,0:T(8,128)S(1)}, f32[216,128]{1,0:T(8,128)S(1)}, u32[]{:S(2)}, u32[]{:S(2)}) collective-permute-start(f32[216,128]{1,0:T(8,128)S(1)} %get-tuple-element.54), channel_id=1, source_target_pairs={{0,16},{1,17},{2,18},{3,19},{4,20},{5,21},{6,22},{7,23},{8,24},{9,... | collective-permute-start | bytes 331784 | tf_op jit(solution)/shard_map/ppermute | solution.py:24
  57.8 5.5 %collective-permute-start.12 = (f32[216,128]{1,0:T(8,128)S(1)}, f32[216,128]{1,0:T(8,128)S(1)}, u32[]{:S(2)}, u32[]{:S(2)}) collective-permute-start(f32[216,128]{1,0:T(8,128)S(1)} %get-tuple-element.55), channel_id=1, source_target_pairs={{0,32},{1,33},{2,34},{3,35},{4,36},{5,37},{6,38},{7,39},{8,40},{9,... | collective-permute-start | bytes 331784 | tf_op jit(solution)/shard_map/ppermute | solution.py:24
  58.4 8.2 %collective-permute-start.13 = (f32[216,128]{1,0:T(8,128)S(1)}, f32[216,128]{1,0:T(8,128)S(1)}, u32[]{:S(2)}, u32[]{:S(2)}) collective-permute-start(f32[216,128]{1,0:T(8,128)S(1)} %get-tuple-element.56), channel_id=1, source_target_pairs={{0,48},{1,49},{2,50},{3,51},{4,52},{5,53},{6,54},{7,55},{8,56},{9,... | collective-permute-start | bytes 331784 | tf_op jit(solution)/shard_map/ppermute | solution.py:24
  66.7 4.2 %collective-permute-start.16 = (f32[216,128]{1,0:T(8,128)S(1)}, f32[216,128]{1,0:T(8,128)S(1)}, u32[]{:S(2)}, u32[]{:S(2)}) collective-permute-start(f32[216,128]{1,0:T(8,128)S(1)} %add_add_fusion.2), channel_id=1, source_target_pairs={{0,6},{1,7},{2,4},{3,5},{4,2},{5,3},{6,0},{7,1},{8,14},{9,15},{10,... | collective-permute-start | bytes 331784 | tf_op jit(solution)/shard_map/ppermute | solution.py:24
  68.0 5.1 %collective-permute-start.15 = (f32[216,128]{1,0:T(8,128)S(1)}, f32[216,128]{1,0:T(8,128)S(1)}, u32[]{:S(2)}, u32[]{:S(2)}) collective-permute-start(f32[216,128]{1,0:T(8,128)S(1)} %add_add_fusion.2), channel_id=1, source_target_pairs={{0,4},{1,5},{2,6},{3,7},{4,0},{5,1},{6,2},{7,3},{8,12},{9,13},{10,... | collective-permute-start | bytes 331784 | tf_op jit(solution)/shard_map/ppermute | solution.py:24
  68.7 6.2 %collective-permute-start.14 = (f32[216,128]{1,0:T(8,128)S(1)}, f32[216,128]{1,0:T(8,128)S(1)}, u32[]{:S(2)}, u32[]{:S(2)}) collective-permute-start(f32[216,128]{1,0:T(8,128)S(1)} %add_add_fusion.2), channel_id=1, source_target_pairs={{0,2},{1,3},{2,0},{3,1},{4,6},{5,7},{6,4},{7,5},{8,10},{9,11},{10,... | collective-permute-start | bytes 331784 | tf_op jit(solution)/shard_map/ppermute | solution.py:24
  74.9 11.1 %collective-permute-start.19 = (f32[216,128]{1,0:T(8,128)S(1)}, f32[216,128]{1,0:T(8,128)S(1)}, u32[]{:S(2)}, u32[]{:S(2)}) collective-permute-start(f32[216,128]{1,0:T(8,128)S(1)} %add_add_fusion.1), channel_id=1, source_target_pairs={{0,65},{1,64},{2,67},{3,66},{4,69},{5,68},{6,71},{7,70},{8,73},{9,... | collective-permute-start | bytes 331784 | tf_op jit(solution)/shard_map/ppermute | solution.py:24
  79.2 6.9 %collective-permute-start.18 = (f32[216,128]{1,0:T(8,128)S(1)}, f32[216,128]{1,0:T(8,128)S(1)}, u32[]{:S(2)}, u32[]{:S(2)}) collective-permute-start(f32[216,128]{1,0:T(8,128)S(1)} %add_add_fusion.1), channel_id=1, source_target_pairs={{0,64},{1,65},{2,66},{3,67},{4,68},{5,69},{6,70},{7,71},{8,72},{9,... | collective-permute-start | bytes 331784 | tf_op jit(solution)/shard_map/ppermute | solution.py:24
  79.2 6.9 %collective-permute-start.17 = (f32[216,128]{1,0:T(8,128)S(1)}, f32[216,128]{1,0:T(8,128)S(1)}, u32[]{:S(2)}, u32[]{:S(2)}) collective-permute-start(f32[216,128]{1,0:T(8,128)S(1)} %add_add_fusion.1), channel_id=1, source_target_pairs={{0,1},{1,0},{2,3},{3,2},{4,5},{5,4},{6,7},{7,6},{8,9},{9,8},{10,11... | collective-permute-start | bytes 331784 | tf_op jit(solution)/shard_map/ppermute | solution.py:24
  80.4 9.0 %collective-permute-start.6 = (bf16[1,8,64,128]{3,2,1,0:T(8,128)(2,1)S(1)}, bf16[1,8,64,128]{3,2,1,0:T(8,128)(2,1)S(1)}, u32[]{:S(2)}, u32[]{:S(2)}) collective-permute-start(bf16[1,8,64,128]{3,2,1,0:T(8,128)(2,1)S(1)} %get-tuple-element.42), channel_id=1, source_target_pairs={{0,8},{8,0},{16,24},{24,16},{32,40},{40,32},{48,56},{56,48},{64,72... | collective-permute-start | bytes 393224 | tf_op jit(solution)/shard_map/ppermute | solution.py:29
  82.6 10.4 %collective-permute-start.7 = (bf16[1,8,64,128]{3,2,1,0:T(8,128)(2,1)S(1)}, bf16[1,8,64,128]{3,2,1,0:T(8,128)(2,1)S(1)}, u32[]{:S(2)}, u32[]{:S(2)}) collective-permute-start(bf16[1,8,64,128]{3,2,1,0:T(8,128)(2,1)S(1)} %get-tuple-element.43), channel_id=1, source_target_pairs={{8,16},{16,8},{24,32},{32,24},{40,48},{48,40},{56,64},{64,56},{72,... | collective-permute-start | bytes 393224 | tf_op jit(solution)/shard_map/ppermute | solution.py:29
  86.1 12.4 %collective-permute-start.22 = (f32[216,128]{1,0:T(8,128)S(1)}, f32[216,128]{1,0:T(8,128)S(1)}, u32[]{:S(2)}, u32[]{:S(2)}) collective-permute-start(f32[216,128]{1,0:T(8,128)S(1)} %add_add_fusion.refs_0_), channel_id=1, source_target_pairs={{0,48},{1,49},{2,50},{3,51},{4,52},{5,53},{6,54},{7,55},{8,56},{9,... | collective-permute-start | bytes 331784 | tf_op jit(solution)/shard_map/ppermute | solution.py:24
  87.3 11.2 %collective-permute-start.21 = (f32[216,128]{1,0:T(8,128)S(1)}, f32[216,128]{1,0:T(8,128)S(1)}, u32[]{:S(2)}, u32[]{:S(2)}) collective-permute-start(f32[216,128]{1,0:T(8,128)S(1)} %add_add_fusion.refs_0_), channel_id=1, source_target_pairs={{0,32},{1,33},{2,34},{3,35},{4,36},{5,37},{6,38},{7,39},{8,40},{9,... | collective-permute-start | bytes 331784 | tf_op jit(solution)/shard_map/ppermute | solution.py:24
  87.8 10.7 %collective-permute-start.20 = (f32[216,128]{1,0:T(8,128)S(1)}, f32[216,128]{1,0:T(8,128)S(1)}, u32[]{:S(2)}, u32[]{:S(2)}) collective-permute-start(f32[216,128]{1,0:T(8,128)S(1)} %add_add_fusion.refs_0_), channel_id=1, source_target_pairs={{0,16},{1,17},{2,18},{3,19},{4,20},{5,21},{6,22},{7,23},{8,24},{9,... | collective-permute-start | bytes 331784 | tf_op jit(solution)/shard_map/ppermute | solution.py:24
  93.6 6.5 %collective-permute-start.8 = (bf16[10,64,128]{2,1,0:T(8,128)(2,1)S(1)}, bf16[10,64,128]{2,1,0:T(8,128)(2,1)S(1)}, u32[]{:S(2)}, u32[]{:S(2)}) collective-permute-start(bf16[10,64,128]{2,1,0:T(8,128)(2,1)S(1)} %get-tuple-element.44), channel_id=1, source_target_pairs={{0,1},{1,0},{2,3},{3,2},{4,5},{5,4},{6,7},{7,6},{8,9},{9,8},{10,11... | collective-permute-start | bytes 491528 | tf_op jit(solution)/shard_map/ppermute | solution.py:341
  95.7 8.8 %collective-permute-start.9 = (bf16[10,64,128]{2,1,0:T(8,128)(2,1)S(1)}, bf16[10,64,128]{2,1,0:T(8,128)(2,1)S(1)}, u32[]{:S(2)}, u32[]{:S(2)}) collective-permute-start(bf16[10,64,128]{2,1,0:T(8,128)(2,1)S(1)} %get-tuple-element.45), channel_id=1, source_target_pairs={{1,2},{2,1},{3,4},{4,3},{5,6},{6,5},{9,10},{10,9},{11,12},{12,11},... | collective-permute-start | bytes 491528 | tf_op jit(solution)/shard_map/ppermute | solution.py:342
  99.1 14.4 %collective-permute-start.23 = (f32[864,128]{1,0:T(8,128)S(1)}, f32[864,128]{1,0:T(8,128)S(1)}, u32[]{:S(2)}, u32[]{:S(2)}) collective-permute-start(f32[864,128]{1,0:T(8,128)S(1)} %shard_map.86.own_ref), channel_id=1, source_target_pairs={{0,8},{1,9},{2,10},{3,11},{4,12},{5,13},{6,14},{7,15},{8,0},{9,1},... | collective-permute-start | bytes 1327112 | tf_op jit(solution)/shard_map/ppermute | solution.py:24

commit v6 on v5

--- a/solution.py
+++ b/solution.py
@@ -1,3 +1,4 @@
+import functools
 import math
 
 import jax
@@ -125,7 +126,7 @@
 def backward_kernel(
     place, weights, slope, tile, xr_even, xr_odd, yr_even, yr_odd, pre_grad, xs_even, xs_odd, padded
 ):
-    pad_tile(padded, place, tile, xr_even, xr_odd, yr_even, yr_odd, 1)
+    pad_tile(padded, place, tile, xr_even, xr_odd, yr_even, yr_odd, 0)
     size_x = tile.shape[0]
 
     def emit(x, y, value):
@@ -223,55 +224,78 @@
         out[pl.ds(start, rows)] = part[...]
 
 
-def unpack_kernel(place, scale, own, other, grad_one, grad_two):
-    chans = grad_one.shape[-1]
+def unpack(scale, source, dest, second):
+    chans = dest.shape[-1]
     rows = 9 * chans
-    half = rows // 2
-
-    def block(source, a, b, j):
-        start = (3 * a + b) * chans
-        if j < 2:
-            return source[start : start + chans, j * chans : (j + 1) * chans]
-        pieces = []
-        step = chans // 2
-        for first in (start, start + step):
-            if first < half:
-                pieces.append(source[rows + first : rows + first + step, 0:chans])
+    half, step = rows // 2, chans // 2
+    for a in range(3):
+        for b in range(3):
+            start = (3 * a + b) * chans
+            both = source[start : start + chans, :] * scale
+            pieces = []
+            for first in (start, start + step):
+                if first < half:
+                    pieces.append(source[rows + first : rows + first + step, 0:chans])
+                else:
+                    pieces.append(source[rows + first - half : rows + first - half + step, chans : 2 * chans])
+            tail = jnp.concatenate(pieces, axis=0) * scale
+            if second:
+                both = both.T
+                dest[2 - a, 2 - b, 0] = both[0:chans]
+                dest[2 - a, 2 - b, 1] = both[chans : 2 * chans]
+                dest[2 - a, 2 - b, 2] = tail.T
             else:
-                pieces.append(source[rows + first - half : rows + first - half + step, chans : 2 * chans])
-        return jnp.concatenate(pieces, axis=0)
-
-    def write(one, two):
-        for a in range(3):
-            for b in range(3):
-                for j in range(3):
-                    grad_one[a, b, 2 - j] = block(one, a, b, j) * scale
-                start = (3 * a + b) * chans
-                pair = two[start : start + chans, :].T * scale
-                grad_two[2 - a, 2 - b, 0] = pair[0:chans]
-                grad_two[2 - a, 2 - b, 1] = pair[chans : 2 * chans]
-                grad_two[2 - a, 2 - b, 2] = block(two, a, b, 2).T * scale
-
+                dest[a, b, 2] = both[:, 0:chans]
+                dest[a, b, 1] = both[:, chans : 2 * chans]
+                dest[a, b, 0] = tail
+
+
+def unpack_own_kernel(place, own, dest, *, scale):
     @pl.when(place[0] == 0)
     def _():
-        write(own, other)
+        unpack(scale, own, dest, False)
 
     @pl.when(place[0] != 0)
     def _():
-        write(other, own)
-
-
-def call(kernel, outs, scratch=(), scalars=0, flops=0):
+        unpack(scale, own, dest, True)
+
+
+def unpack_other_kernel(place, mine, other, grad_one, grad_two, held, sems, *, scale):
+    def finish(own_dest, other_dest, second):
+        first = pltpu.make_async_copy(mine, own_dest, sems.at[0])
+        first.start()
+        unpack(scale, other, held, second)
+        last = pltpu.make_async_copy(held, other_dest, sems.at[1])
+        last.start()
+        first.wait()
+        last.wait()
+
+    @pl.when(place[0] == 0)
+    def _():
+        finish(grad_one, grad_two, True)
+
+    @pl.when(place[0] != 0)
+    def _():
+        finish(grad_two, grad_one, False)
+
+
+def call(kernel, outs, scratch=(), scalars=0, flops=0, inside=True):
+    def wrapped(*refs):
+        if scalars:
+            kernel([ref[0] for ref in refs[:scalars]], *refs[scalars:])
+        else:
+            kernel(*refs)
+
     def run(*operands):
         specs = [pl.BlockSpec(memory_space=pltpu.SMEM)] * scalars
         specs += [pl.BlockSpec(memory_space=pltpu.VMEM)] * (len(operands) - scalars)
         moved = sum(o.size * o.dtype.itemsize for o in operands)
         moved += sum(math.prod(o.shape) * o.dtype.itemsize for o in outs)
         return pl.pallas_call(
-            kernel,
+            wrapped,
             out_shape=tuple(outs),
             in_specs=specs,
-            out_specs=tuple(pl.BlockSpec(memory_space=pltpu.VMEM) for _ in outs),
+            out_specs=tuple(pl.BlockSpec(memory_space=pltpu.VMEM if inside else pl.ANY) for _ in outs),
             scratch_shapes=list(scratch),
             cost_estimate=pl.CostEstimate(flops=flops, bytes_accessed=moved, transcendentals=0),
             compiler_params=pltpu.CompilerParams(vmem_limit_bytes=40 * 1024 * 1024),
@@ -287,19 +311,21 @@
     scale = 1.0 / math.sqrt(cells_all)
     place_x, place_y = lax.axis_index("gx"), lax.axis_index("gy")
     x_odd, y_odd = place_x & 1, place_y & 1
-    place = jnp.stack([x_odd, y_odd, (place_x >> 1) & 3]).astype(jnp.int32)
+    place = [v.astype(jnp.int32).reshape(1) for v in (x_odd, y_odd, (place_x >> 1) & 3)]
 
     mask = jnp.broadcast_to(block_mask.reshape(blocks, 1), (blocks, tile_z // blocks)).reshape(1, tile_z)
     mask_f = mask.astype(F32)
     mask_b = mask.astype(BF16).reshape(1, 1, tile_z)
 
-    def x_edges(at):
-        both = [lax.dynamic_index_in_dim(a, at, 1, keepdims=False) * mask_b for a in (features, cotangent)]
-        return jnp.stack([jnp.transpose(a, (1, 0, 2)) for a in both])
-
-    xr = swap(x_edges((1 - x_odd) * (tile_x - 1)), x_edges(x_odd * (tile_x - 1)), "gx")
+    def x_swap(array):
+        def edge(at):
+            plane = lax.dynamic_index_in_dim(array, at, 1, keepdims=False) * mask_b
+            return jnp.transpose(plane, (1, 0, 2))[None]
+
+        return swap(edge((1 - x_odd) * (tile_x - 1)), edge(x_odd * (tile_x - 1)), "gx")
+
+    in_xr = x_swap(features)
     masked_in = jnp.transpose(features * mask_b[:, None], (1, 2, 0, 3))
-    masked_grad = jnp.transpose(cotangent * mask_b[:, None], (1, 2, 0, 3))
 
     tile_shape = (tile_x, tile_y, chans, tile_z)
     tile_b = jax.ShapeDtypeStruct(tile_shape, BF16)
@@ -310,28 +336,34 @@
 
     def y_sends(tiles, halo_x):
         outs = [column_b] * (2 * len(tiles))
-        return call(ypack_kernel, outs, scalars=1)(place, *tiles, *halo_x)
-
-    sends = y_sends((masked_in, masked_grad), xr)
-    in_sends, grad_sends = sends[:2], sends[2:]
+        return call(ypack_kernel, outs, scalars=3)(*place, *tiles, *halo_x)
+
+    in_sends = y_sends((masked_in,), in_xr)
     matrix = jax.ShapeDtypeStruct((3 * chans, 9 * chans), BF16)
     even, odd = swap_perms(lax.axis_size("gy"))
-    in_even = lax.ppermute(in_sends[0], "gy", even)
+    in_send, cotangent = lax.optimization_barrier((in_sends[0], cotangent))
+    in_even = lax.ppermute(in_send, "gy", even)
+    grad_xr = x_swap(cotangent)
+    masked_grad = jnp.transpose(cotangent * mask_b[:, None], (1, 2, 0, 3))
+    in_send, masked_grad = lax.optimization_barrier((in_sends[1], masked_grad))
+    in_odd = lax.ppermute(in_send, "gy", odd)
+    in_y = (in_even, in_odd)
+    grad_sends = y_sends((masked_grad,), grad_xr)
+    grad_even = lax.ppermute(grad_sends[0], "gy", even)
     w_pre, w_act, w_branch = call(weights_kernel, [matrix] * 3)(kernel_one, kernel_two)
-    in_next, w_pre = lax.optimization_barrier((in_sends[1], w_pre))
-    in_odd = lax.ppermute(in_next, "gy", odd)
-    in_y = (in_even, in_odd)
-    grad_y = swap(*grad_sends, "gy")
+    grad_send, w_pre = lax.optimization_barrier((grad_sends[1], w_pre))
+    grad_odd = lax.ppermute(grad_send, "gy", odd)
+    grad_y = (grad_even, grad_odd)
 
     tile_s = pltpu.VMEM((tile_x, tile_y, 3 * chans, tile_z), BF16)
     grad_s = pltpu.VMEM((9 * chans, 3 * chans), F32)
 
     activ, slope, in_pad = call(
-        forward_kernel, [tile_b, jax.ShapeDtypeStruct(tile_shape, F32), pad_b], scalars=1, flops=flops
-    )(place, mask_f, w_pre, masked_in, *xr, *in_y)
+        forward_kernel, [tile_b, jax.ShapeDtypeStruct(tile_shape, F32), pad_b], scalars=3, flops=flops
+    )(*place, mask_f, w_pre, masked_in, *in_xr, *in_y)
     pre_grad, xs_even, xs_odd, grad_pad = call(
-        backward_kernel, [tile_b, edge_b, edge_b, pad_b], scalars=1, flops=flops
-    )(place, w_act, slope, masked_grad, *xr, *grad_y)
+        backward_kernel, [tile_b, edge_b, edge_b, pad_b], scalars=3, flops=flops
+    )(*place, w_act, slope, masked_grad, *grad_xr, *grad_y)
 
     packed = 27 * chans * chans // (2 * chans)
     half = jax.ShapeDtypeStruct((packed, 2 * chans), F32)
@@ -341,32 +373,36 @@
     pre_even = lax.ppermute(pre_sends[0], "gy", even)
     pre_odd = lax.ppermute(pre_sends[1], "gy", odd)
     pre_yr = (pre_even, pre_odd)
-    keep, send = call(grad_one_kernel, [half, half], [tile_s, grad_s], scalars=1, flops=flops)(
-        place, in_pad, pre_grad, packed_two
+    keep, send = call(grad_one_kernel, [half, half], [tile_s, grad_s], scalars=3, flops=flops)(
+        *place, in_pad, pre_grad, packed_two
     )
 
     recv = xor_permute(send, 8)
     chunk = jax.ShapeDtypeStruct((packed // 4, 2 * chans), F32)
-    parts = call(split_kernel, [chunk] * 4, scalars=1)(place, keep, recv)
+    parts = call(split_kernel, [chunk] * 4, scalars=3)(*place, keep, recv)
     parts = [parts[0]] + [xor_permute(parts[d], 16 * d) for d in range(1, 4)]
     part = (parts[0] + parts[1]) + (parts[2] + parts[3])
     for masks in ((2, 4, 6), (1, 64, 65)):
         near, mid, far = [xor_permute(part, m) for m in masks]
         part = (part + near) + (mid + far)
     pieces = [part] + [xor_permute(part, 16 * d) for d in range(1, 4)]
-    (own,) = call(join_kernel, [half], scalars=1)(place, *pieces)
+    (own,) = call(join_kernel, [half], scalars=3)(*place, *pieces)
     other = xor_permute(own, 8)
     grad_shape = jax.ShapeDtypeStruct((3, 3, 3, chans, chans), F32)
 
-    def unpack(place_ref, own_ref, other_ref, one_ref, two_ref):
-        unpack_kernel(place_ref, scale, own_ref, other_ref, one_ref, two_ref)
-
-    grad_one, grad_two = call(unpack, [grad_shape, grad_shape], scalars=1)(place, own, other)
+    (mine,) = call(functools.partial(unpack_own_kernel, scale=scale), [grad_shape], scalars=3)(*place, own)
+    grad_one, grad_two = call(
+        functools.partial(unpack_other_kernel, scale=scale),
+        [grad_shape, grad_shape],
+        [pltpu.VMEM(grad_shape.shape, F32), pltpu.SemaphoreType.DMA((2,))],
+        scalars=3,
+        inside=False,
+    )(*place, mine, other)
 
     half_b = jax.ShapeDtypeStruct((tile_x, tile_y // 2, chans, tile_z), BF16)
     low, pre_pad = call(
-        branch_low_kernel, [half_b, pad_b], scalars=1, flops=flops // 2
-    )(place, mask_f, w_branch, masked_grad, pre_grad, *pre_xr, *pre_yr)
+        branch_low_kernel, [half_b, pad_b], scalars=3, flops=flops // 2
+    )(*place, mask_f, w_branch, masked_grad, pre_grad, *pre_xr, *pre_yr)
     (high,) = call(branch_high_kernel, [half_b], flops=flops // 2)(mask_f, w_branch, masked_grad, pre_pad)
     grad_features = jnp.transpose(jnp.concatenate([low, high], axis=1), (2, 0, 1, 3))
     return grad_features, grad_one, grad_two

time: 116 us -> 117 us (level)
  the two profiles are of different devices: /device:TPU:15 before, /device:TPU:31 now
where the time goes in v6:
time: 117 us
  starting transfers between devices  46.6 us (40%)
  Pallas kernels  30.5 us (26%)
  waiting for transfers between devices  30.3 us (26%)
  other arithmetic  4.27 us (4%)
  local copies, waits for them, and re-layouts  4.06 us (3%)
    pallas_call x14, Pallas kernels, run(): pl.pallas_call(wrapped, out_shape=tuple(outs), in_specs=specs, out_specs=...  30.5 us
    ppermute x14, starting transfers between devices, xor_permute(): return lax.ppermute(value, AXES, [(i, i ^ mask) for i in range(total)])  16.6 us
    ppermute x14, waiting for transfers between devices, xor_permute(): return lax.ppermute(value, AXES, [(i, i ^ mask) for i in range(total)])  12.3 us
    ppermute x3, waiting for transfers between devices, swap(): lax.ppermute(value_odd, axis, odd)  12.1 us
    ppermute x3, starting transfers between devices, swap(): lax.ppermute(value_odd, axis, odd)  10.3 us
    ppermute x1, starting transfers between devices, body(): grad_odd = lax.ppermute(grad_send, 'gy', odd)  6.78 us
    ppermute x1, waiting for transfers between devices, body(): pre_odd = lax.ppermute(pre_sends[1], 'gy', odd)  4.33 us
    ppermute x1, starting transfers between devices, body(): in_even = lax.ppermute(in_send, 'gy', even)  3.68 us
  transfers between devices with their start and end apart: 26, of which 12 were waited for; matrix products, arithmetic and copies ran while one was open for 3% of the time, Pallas kernels for 12%

profile of v6, /device:TPU:31, one launch (start us, length us, event | category | flops | bytes accessed | tf_op | source)
XLA Modules:
  0.0 116.7 jit_solution(3471338937276139012)
XLA Ops:
  0.6 0.0 copy-start.2
  0.7 0.8 convert_bitcast_fusion
  1.4 0.1 broadcast_in_dim.20
  1.5 0.1 convert_element_type.32
  1.6 1.0 constant_dynamic-slice_fusion.2
  2.6 4.0 %collective-permute-start.1 = (bf16[1,8,64,128]{3,2,1,0:T(8,128)(2,1)S(1)}, bf16[1,8,64,128]{3,2,1,0:T(8,128)(2,1)S(1)}, u32[]{:S(2)}, u32[]{:S(2)}) collective-permute-start(bf16[1,8,64,128]{3,2,1,0:T(8,128)(2,1)S(1)} %get-tuple-element.79), channel_id=1, source_target_pairs={{8,16},{16,8},{24,32},{32,24},{40,48},{48,40},{56,64},{64,56},{72,... | collective-permute-start | bytes 393224 | tf_op jit(solution)/shard_map/ppermute | solution.py:30
  6.7 0.1 collective-permute-start
  6.8 0.7 fusion.1.refs_3_.refs_5_
  7.5 3.6 %collective-permute-done.1.refs_5_.refs_7_ = bf16[1,8,64,128]{3,2,1,0:T(8,128)(2,1)S(1)} collective-permute-done((bf16[1,8,64,128]{3,2,1,0:T(8,128)(2,1)S(1)}, bf16[1,8,64,128]{3,2,1,0:T(8,128)(2,1)S(1)}, u32[]{:S(2)}, u32[]{:S(2)}) %collective-permute-start.1) | collective-permute-done | bytes 131104 | tf_op jit(solution)/shard_map/ppermute | solution.py:30
  11.0 0.7 shard_map.77
  11.8 1.1 constant_dynamic-slice_fusion
  12.9 1.9 %fusion.refs_3_.refs_5_.refs_2_ = bf16[8,8,64,128]{3,2,1,0:T(8,128)(2,1)S(1)} fusion(bf16[64,8,8,128]{3,2,1,0:T(8,128)(2,1)} %param.6, bf16[128]{0:T(256)(128)(2,1)S(1)} %convert_element_type.32), kind=kLoop, calls=%fused_computation.2 | loop fusion | flops 524288 | bytes 2097408 | tf_op jit(solution)/shard_map/transpose | solution.py:347
  14.8 3.7 %collective-permute-start.4 = (bf16[10,64,128]{2,1,0:T(8,128)(2,1)}, bf16[10,64,128]{2,1,0:T(8,128)(2,1)}, u32[]{:S(2)}, u32[]{:S(2)}) collective-permute-start(bf16[10,64,128]{2,1,0:T(8,128)(2,1)} %get-tuple-element.44), channel_id=1, source_target_pairs={{0,1},{1,0},{2,3},{3,2},{4,5},{5,4},{6,7},{7,6},{8,9},{9,8},{10,11... | collective-permute-start | bytes 491528 | tf_op jit(solution)/shard_map/ppermute | solution.py:345
  18.4 2.1 %collective-permute-start.5 = (bf16[10,64,128]{2,1,0:T(8,128)(2,1)}, bf16[10,64,128]{2,1,0:T(8,128)(2,1)}, u32[]{:S(2)}, u32[]{:S(2)}) collective-permute-start(bf16[10,64,128]{2,1,0:T(8,128)(2,1)} %get-tuple-element.45), channel_id=1, source_target_pairs={{1,2},{2,1},{3,4},{4,3},{5,6},{6,5},{9,10},{10,9},{11,12},{12,11},... | collective-permute-start | bytes 491528 | tf_op jit(solution)/shard_map/ppermute | solution.py:349
  20.5 0.7 fusion.2
  21.3 3.9 %collective-permute-start.3 = (bf16[1,8,64,128]{3,2,1,0:T(8,128)(2,1)}, bf16[1,8,64,128]{3,2,1,0:T(8,128)(2,1)S(1)}, u32[]{:S(2)}, u32[]{:S(2)}) collective-permute-start(bf16[1,8,64,128]{3,2,1,0:T(8,128)(2,1)} %get-tuple-element.77), channel_id=1, source_target_pairs={{8,16},{16,8},{24,32},{32,24},{40,48},{48,40},{56,64},{64,56},{72,... | collective-permute-start | bytes 393224 | tf_op jit(solution)/shard_map/ppermute | solution.py:30
  25.2 0.1 collective-permute-start.2
  25.3 0.1 broadcast_in_dim.19
  25.4 0.1 convert_element_type.29.refs_3_.refs_0_
  25.5 0.3 shard_map.76
  25.8 4.1 %collective-permute-done.3.refs_5_.refs_7_ = bf16[1,8,64,128]{3,2,1,0:T(8,128)(2,1)S(1)} collective-permute-done((bf16[1,8,64,128]{3,2,1,0:T(8,128)(2,1)}, bf16[1,8,64,128]{3,2,1,0:T(8,128)(2,1)S(1)}, u32[]{:S(2)}, u32[]{:S(2)}) %collective-permute-start.3) | collective-permute-done | bytes 131104 | tf_op jit(solution)/shard_map/ppermute | solution.py:30
  29.9 6.8 %collective-permute-start.7 = (bf16[10,64,128]{2,1,0:T(8,128)(2,1)S(1)}, bf16[10,64,128]{2,1,0:T(8,128)(2,1)S(1)}, u32[]{:S(2)}, u32[]{:S(2)}) collective-permute-start(bf16[10,64,128]{2,1,0:T(8,128)(2,1)S(1)} %get-tuple-element.48), channel_id=1, source_target_pairs={{1,2},{2,1},{3,4},{4,3},{5,6},{6,5},{9,10},{10,9},{11,12},{12,11},... | collective-permute-start | bytes 491528 | tf_op jit(solution)/shard_map/ppermute | solution.py:355
  36.7 0.1 collective-permute-start.6
  36.8 0.0 collective-permute-done.4.refs_8_
  36.8 0.0 collective-permute-done.5.refs_9_
  36.8 5.9 %shard_map.79 = (bf16[8,8,64,128]{3,2,1,0:T(8,128)(2,1)S(1)}, f32[8,8,64,128]{3,2,1,0:T(8,128)S(1)}, bf16[10,10,64,128]{3,2,1,0:T(8,128)(2,1)S(1)}) custom-call(s32[1]{0:T(128)} %bitcast.refs_0_, s32[1]{0:T(128)} %bitcast.1.refs_1_, s32[1]{0:T(128)} %bitcast.2.refs_2_, f32[1,128]{1,0:T(1,128)S(1)} %convert_element_type.29.refs_3_.refs_0_, ...), custom_call_target="tpu_custom_call" | custom-call | flops 1811939328 | bytes 6644236 | tf_op jit(solution)/shard_map/pallas_call | solution.py:294
  42.7 0.2 collective-permute-done.6.refs_8_
  42.9 4.7 %shard_map.80 = (bf16[8,8,64,128]{3,2,1,0:T(8,128)(2,1)S(1)}, bf16[1,8,64,128]{3,2,1,0:T(8,128)(2,1)S(1)}, bf16[1,8,64,128]{3,2,1,0:T(8,128)(2,1)S(1)}, bf16[10,10,64,128]{3,2,1,0:T(8,128)(2,1)S(1)}) custom-call(s32[1]{0:T(128)} %bitcast.refs_0_, s32[1]{0:T(128)} %bitcast.1.refs_1_, s32[1]{0:T(128)} %bitcast.2.refs_2_, ...), custom_call_target="tpu_custom_call" | custom-call | flops 1811939328 | bytes 6905868 | tf_op jit(solution)/shard_map/pallas_call | solution.py:294
  47.6 5.1 %shard_map.84.refs_5_ = f32[864,128]{1,0:T(8,128)S(1)} custom-call(bf16[10,10,64,128]{3,2,1,0:T(8,128)(2,1)S(1)} %get-tuple-element.57.refs_0_, bf16[8,8,64,128]{3,2,1,0:T(8,128)(2,1)S(1)} %get-tuple-element.58.refs_1_), custom_call_target="tpu_custom_call" | custom-call | flops 1811939328 | bytes 3129344 | tf_op jit(solution)/shard_map/pallas_call | solution.py:294
  52.7 5.2 %shard_map.85 = (f32[864,128]{1,0:T(8,128)S(1)}, f32[864,128]{1,0:T(8,128)S(1)}) custom-call(s32[1]{0:T(128)} %bitcast.refs_0_, s32[1]{0:T(128)} %bitcast.1.refs_1_, s32[1]{0:T(128)} %bitcast.2.refs_2_, bf16[10,10,64,128]{3,2,1,0:T(8,128)(2,1)S(1)} %get-tuple-element.56.refs_3_, bf16[8,8,64,128]{3,2,1,0:T(8,128)(2,1)S(1)} %get-tuple-element.49.refs_3_.refs_6_.refs_4_, ...), custom_call_target="tpu_custom_call" | custom-call | flops 1811939328 | bytes 4014092 | tf_op jit(solution)/shard_map/pallas_call | solution.py:294
  57.9 0.1 collective-permute-start.12
  58.0 1.8 %collective-permute-done.12.refs_4_ = f32[864,128]{1,0:T(8,128)S(1)} collective-permute-done((f32[864,128]{1,0:T(8,128)S(1)}, f32[864,128]{1,0:T(8,128)S(1)}, u32[]{:S(2)}, u32[]{:S(2)}) %collective-permute-start.12) | collective-permute-done | bytes 442400 | tf_op jit(solution)/shard_map/ppermute | solution.py:25
  59.9 0.1 collective-permute-start.13
  59.9 0.1 collective-permute-start.14
  60.0 3.8 %collective-permute-start.15 = (f32[216,128]{1,0:T(8,128)S(1)}, f32[216,128]{1,0:T(8,128)S(1)}, u32[]{:S(2)}, u32[]{:S(2)}) collective-permute-start(f32[216,128]{1,0:T(8,128)S(1)} %get-tuple-element.64), channel_id=1, source_target_pairs={{0,48},{1,49},{2,50},{3,51},{4,52},{5,53},{6,54},{7,55},{8,56},{9,... | collective-permute-start | bytes 331784 | tf_op jit(solution)/shard_map/ppermute | solution.py:25
  63.8 0.6 collective-permute-done.13
  64.4 1.6 %collective-permute-done.14 = f32[216,128]{1,0:T(8,128)S(1)} collective-permute-done((f32[216,128]{1,0:T(8,128)S(1)}, f32[216,128]{1,0:T(8,128)S(1)}, u32[]{:S(2)}, u32[]{:S(2)}) %collective-permute-start.14) | collective-permute-done | bytes 110624 | tf_op jit(solution)/shard_map/ppermute | solution.py:25
  66.0 2.9 %collective-permute-done.15 = f32[216,128]{1,0:T(8,128)S(1)} collective-permute-done((f32[216,128]{1,0:T(8,128)S(1)}, f32[216,128]{1,0:T(8,128)S(1)}, u32[]{:S(2)}, u32[]{:S(2)}) %collective-permute-start.15) | collective-permute-done | bytes 110624 | tf_op jit(solution)/shard_map/ppermute | solution.py:25
  68.9 0.1 collective-permute-start.18
  69.0 2.2 %collective-permute-start.17 = (f32[216,128]{1,0:T(8,128)S(1)}, f32[216,128]{1,0:T(8,128)S(1)}, u32[]{:S(2)}, u32[]{:S(2)}) collective-permute-start(f32[216,128]{1,0:T(8,128)S(1)} %add_add_fusion.2), channel_id=1, source_target_pairs={{0,4},{1,5},{2,6},{3,7},{4,0},{5,1},{6,2},{7,3},{8,12},{9,13},{10,... | collective-permute-start | bytes 331784 | tf_op jit(solution)/shard_map/ppermute | solution.py:25
  71.2 1.0 collective-permute-start.16
  72.3 4.9 %collective-permute-done.18 = f32[216,128]{1,0:T(8,128)S(1)} collective-permute-done((f32[216,128]{1,0:T(8,128)S(1)}, f32[216,128]{1,0:T(8,128)S(1)}, u32[]{:S(2)}, u32[]{:S(2)}) %collective-permute-start.18) | collective-permute-done | bytes 110624 | tf_op jit(solution)/shard_map/ppermute | solution.py:25
  77.2 0.0 collective-permute-done.17
  77.2 0.0 collective-permute-done.16
  77.2 4.6 %collective-permute-start.21 = (f32[216,128]{1,0:T(8,128)S(1)}, f32[216,128]{1,0:T(8,128)S(1)}, u32[]{:S(2)}, u32[]{:S(2)}) collective-permute-start(f32[216,128]{1,0:T(8,128)S(1)} %add_add_fusion.1), channel_id=1, source_target_pairs={{0,65},{1,64},{2,67},{3,66},{4,69},{5,68},{6,71},{7,70},{8,73},{9,... | collective-permute-start | bytes 331784 | tf_op jit(solution)/shard_map/ppermute | solution.py:25
  81.8 1.3 %collective-permute-start.19 = (f32[216,128]{1,0:T(8,128)S(1)}, f32[216,128]{1,0:T(8,128)S(1)}, u32[]{:S(2)}, u32[]{:S(2)}) collective-permute-start(f32[216,128]{1,0:T(8,128)S(1)} %add_add_fusion.1), channel_id=1, source_target_pairs={{0,1},{1,0},{2,3},{3,2},{4,5},{5,4},{6,7},{7,6},{8,9},{9,8},{10,11... | collective-permute-start | bytes 331784 | tf_op jit(solution)/shard_map/ppermute | solution.py:25
  83.0 2.0 %collective-permute-start.8 = (bf16[1,8,64,128]{3,2,1,0:T(8,128)(2,1)S(1)}, bf16[1,8,64,128]{3,2,1,0:T(8,128)(2,1)S(1)}, u32[]{:S(2)}, u32[]{:S(2)}) collective-permute-start(bf16[1,8,64,128]{3,2,1,0:T(8,128)(2,1)S(1)} %get-tuple-element.50), channel_id=1, source_target_pairs={{0,8},{8,0},{16,24},{24,16},{32,40},{40,32},{48,56},{56,48},{64,72... | collective-permute-start | bytes 393224 | tf_op jit(solution)/shard_map/ppermute | solution.py:30
  85.1 2.3 %collective-permute-start.9 = (bf16[1,8,64,128]{3,2,1,0:T(8,128)(2,1)S(1)}, bf16[1,8,64,128]{3,2,1,0:T(8,128)(2,1)S(1)}, u32[]{:S(2)}, u32[]{:S(2)}) collective-permute-start(bf16[1,8,64,128]{3,2,1,0:T(8,128)(2,1)S(1)} %get-tuple-element.51), channel_id=1, source_target_pairs={{8,16},{16,8},{24,32},{32,24},{40,48},{48,40},{56,64},{64,56},{72,... | collective-permute-start | bytes 393224 | tf_op jit(solution)/shard_map/ppermute | solution.py:30
  87.4 0.4 collective-permute-done.19
  87.9 0.5 collective-permute-start.24
  88.4 1.9 %collective-permute-start.23 = (f32[216,128]{1,0:T(8,128)S(1)}, f32[216,128]{1,0:T(8,128)S(1)}, u32[]{:S(2)}, u32[]{:S(2)}) collective-permute-start(f32[216,128]{1,0:T(8,128)S(1)} %add_add_fusion.refs_3_), channel_id=1, source_target_pairs={{0,32},{1,33},{2,34},{3,35},{4,36},{5,37},{6,38},{7,39},{8,40},{9,... | collective-permute-start | bytes 331784 | tf_op jit(solution)/shard_map/ppermute | solution.py:25
  90.3 1.0 collective-permute-start.22
  91.2 4.5 %collective-permute-done.9.refs_5_.refs_8_ = bf16[1,8,64,128]{3,2,1,0:T(8,128)(2,1)S(1)} collective-permute-done((bf16[1,8,64,128]{3,2,1,0:T(8,128)(2,1)S(1)}, bf16[1,8,64,128]{3,2,1,0:T(8,128)(2,1)S(1)}, u32[]{:S(2)}, u32[]{:S(2)}) %collective-permute-start.9) | collective-permute-done | bytes 131104 | tf_op jit(solution)/shard_map/ppermute | solution.py:30
  95.7 2.2 %collective-permute-start.10 = (bf16[10,64,128]{2,1,0:T(8,128)(2,1)S(1)}, bf16[10,64,128]{2,1,0:T(8,128)(2,1)S(1)}, u32[]{:S(2)}, u32[]{:S(2)}) collective-permute-start(bf16[10,64,128]{2,1,0:T(8,128)(2,1)S(1)} %get-tuple-element.52), channel_id=1, source_target_pairs={{0,1},{1,0},{2,3},{3,2},{4,5},{5,4},{6,7},{7,6},{8,9},{9,8},{10,11... | collective-permute-start | bytes 491528 | tf_op jit(solution)/shard_map/ppermute | solution.py:373
  97.9 2.7 %collective-permute-start.11 = (bf16[10,64,128]{2,1,0:T(8,128)(2,1)S(1)}, bf16[10,64,128]{2,1,0:T(8,128)(2,1)S(1)}, u32[]{:S(2)}, u32[]{:S(2)}) collective-permute-start(bf16[10,64,128]{2,1,0:T(8,128)(2,1)S(1)} %get-tuple-element.53), channel_id=1, source_target_pairs={{1,2},{2,1},{3,4},{4,3},{5,6},{6,5},{9,10},{10,9},{11,12},{12,11},... | collective-permute-start | bytes 491528 | tf_op jit(solution)/shard_map/ppermute | solution.py:374
  100.7 0.1 collective-permute-start.25
  100.8 1.3 %collective-permute-done.10.refs_9_ = bf16[10,64,128]{2,1,0:T(8,128)(2,1)S(1)} collective-permute-done((bf16[10,64,128]{2,1,0:T(8,128)(2,1)S(1)}, bf16[10,64,128]{2,1,0:T(8,128)(2,1)S(1)}, u32[]{:S(2)}, u32[]{:S(2)}) %collective-permute-start.10) | collective-permute-done | bytes 163872 | tf_op jit(solution)/shard_map/ppermute | solution.py:373
  102.1 4.3 %collective-permute-done.11.refs_10_ = bf16[10,64,128]{2,1,0:T(8,128)(2,1)S(1)} collective-permute-done((bf16[10,64,128]{2,1,0:T(8,128)(2,1)S(1)}, bf16[10,64,128]{2,1,0:T(8,128)(2,1)S(1)}, u32[]{:S(2)}, u32[]{:S(2)}) %collective-permute-start.11) | collective-permute-done | bytes 163872 | tf_op jit(solution)/shard_map/ppermute | solution.py:374
  106.5 3.5 %shard_map.82 = (bf16[8,4,64,128]{3,2,1,0:T(8,128)(2,1)S(1)}, bf16[10,10,64,128]{3,2,1,0:T(8,128)(2,1)S(1)}) custom-call(s32[1]{0:T(128)} %bitcast.refs_0_, s32[1]{0:T(128)} %bitcast.1.refs_1_, s32[1]{0:T(128)} %bitcast.2.refs_2_, f32[1,128]{1,0:T(1,128)S(1)} %convert_element_type.29.refs_3_.refs_0_, bf16[192,576]{1,0:T(8,128)(2,1)S(1)} %get-tuple-element.35.refs_4_.refs_1_, ...), custom_call_target="tpu_custom_call" | custom-call | flops 905969664 | bytes 5071372 | tf_op jit(solution)/shard_map/pallas_call | solution.py:294
  110.0 3.3 %shard_map.83 = bf16[8,4,64,128]{3,2,1,0:T(8,128)(2,1)S(1)} custom-call(f32[1,128]{1,0:T(1,128)S(1)} %convert_element_type.29.refs_3_.refs_0_, bf16[192,576]{1,0:T(8,128)(2,1)S(1)} %get-tuple-element.35.refs_4_.refs_1_, bf16[8,8,64,128]{3,2,1,0:T(8,128)(2,1)S(1)} %fusion.refs_3_.refs_5_.refs_2_, bf16[10,10,64,128]{3,2,1,0:T(8,128)(2,1)S(1)} %get-tuple-element.55.refs_3_), custom_call_target="tpu_custom_call" | custom-call | flops 905969664 | bytes 3432960 | tf_op jit(solution)/shard_map/pallas_call | solution.py:294
  113.3 0.1 maximum_bitcast_fusion
  113.4 1.6 %copy.21 = bf16[64,8,8,128]{3,2,1,0:T(8,128)(2,1)} copy(bf16[64,8,8,128]{3,0,2,1:T(8,128)(2,1)S(1)} %maximum_bitcast_fusion) | data formatting | bytes 2097152
  115.1 0.4 shard_map.88.refs_3_
  115.5 1.2 %shard_map.89 = (f32[3,3,3,64,64]{4,3,2,1,0:T(8,128)}, f32[3,3,3,64,64]{4,3,2,1,0:T(8,128)}) custom-call(s32[1]{0:T(128)} %bitcast.refs_0_, s32[1]{0:T(128)} %bitcast.1.refs_1_, s32[1]{0:T(128)} %bitcast.2.refs_2_, f32[3,3,3,64,64]{4,3,2,1,0:T(8,128)S(1)} %shard_map.88.refs_3_, f32[864,128]{1,0:T(8,128)S(1)} %collective-permute-done.25.refs_4_), custom_call_target="tpu_custom_call" | custom-call | bytes 1769484 | tf_op jit(solution)/shard_map/pallas_call | solution.py:294
  (24 shorter events, 0.3 us)
Async XLA Ops:
  0.6 6.1 %copy-start.2 = (bf16[64,8,8,128]{3,2,1,0:T(8,128)(2,1)S(1)}, bf16[64,8,8,128]{3,2,1,0:T(8,128)(2,1)}, u32[]{:S(2)}) copy-start(bf16[64,8,8,128]{3,2,1,0:T(8,128)(2,1)} %param.5) | copy-start | bytes 3145732
  2.6 8.4 %collective-permute-start.1 = (bf16[1,8,64,128]{3,2,1,0:T(8,128)(2,1)S(1)}, bf16[1,8,64,128]{3,2,1,0:T(8,128)(2,1)S(1)}, u32[]{:S(2)}, u32[]{:S(2)}) collective-permute-start(bf16[1,8,64,128]{3,2,1,0:T(8,128)(2,1)S(1)} %get-tuple-element.79), channel_id=1, source_target_pairs={{8,16},{16,8},{24,32},{32,24},{40,48},{48,40},{56,64},{64,56},{72,... | collective-permute-start | bytes 393224 | tf_op jit(solution)/shard_map/ppermute | solution.py:30
  6.7 4.4 %collective-permute-start = (bf16[1,8,64,128]{3,2,1,0:T(8,128)(2,1)S(1)}, bf16[1,8,64,128]{3,2,1,0:T(8,128)(2,1)S(1)}, u32[]{:S(2)}, u32[]{:S(2)}) collective-permute-start(bf16[1,8,64,128]{3,2,1,0:T(8,128)(2,1)S(1)} %get-tuple-element.80), channel_id=1, source_target_pairs={{0,8},{8,0},{16,24},{24,16},{32,40},{40,32},{48,56},{56,48},{64,72... | collective-permute-start | bytes 393224 | tf_op jit(solution)/shard_map/ppermute | solution.py:30
  11.8 13.7 %copy-start = (bf16[3,3,3,64,64]{4,3,2,1,0:T(8,128)(2,1)S(1)}, bf16[3,3,3,64,64]{4,3,2,1,0:T(8,128)(2,1)}, u32[]{:S(2)}) copy-start(bf16[3,3,3,64,64]{4,3,2,1,0:T(8,128)(2,1)} %refs_0_.1) | copy-start | bytes 663556
  11.8 13.7 %copy-start.1 = (bf16[3,3,3,64,64]{4,3,2,1,0:T(8,128)(2,1)S(1)}, bf16[3,3,3,64,64]{4,3,2,1,0:T(8,128)(2,1)}, u32[]{:S(2)}) copy-start(bf16[3,3,3,64,64]{4,3,2,1,0:T(8,128)(2,1)} %refs_1_.1) | copy-start | bytes 663556
  14.8 22.0 %collective-permute-start.4 = (bf16[10,64,128]{2,1,0:T(8,128)(2,1)}, bf16[10,64,128]{2,1,0:T(8,128)(2,1)}, u32[]{:S(2)}, u32[]{:S(2)}) collective-permute-start(bf16[10,64,128]{2,1,0:T(8,128)(2,1)} %get-tuple-element.44), channel_id=1, source_target_pairs={{0,1},{1,0},{2,3},{3,2},{4,5},{5,4},{6,7},{7,6},{8,9},{9,8},{10,11... | collective-permute-start | bytes 491528 | tf_op jit(solution)/shard_map/ppermute | solution.py:345
  18.4 18.4 %collective-permute-start.5 = (bf16[10,64,128]{2,1,0:T(8,128)(2,1)}, bf16[10,64,128]{2,1,0:T(8,128)(2,1)}, u32[]{:S(2)}, u32[]{:S(2)}) collective-permute-start(bf16[10,64,128]{2,1,0:T(8,128)(2,1)} %get-tuple-element.45), channel_id=1, source_target_pairs={{1,2},{2,1},{3,4},{4,3},{5,6},{6,5},{9,10},{10,9},{11,12},{12,11},... | collective-permute-start | bytes 491528 | tf_op jit(solution)/shard_map/ppermute | solution.py:349
  21.3 8.6 %collective-permute-start.3 = (bf16[1,8,64,128]{3,2,1,0:T(8,128)(2,1)}, bf16[1,8,64,128]{3,2,1,0:T(8,128)(2,1)S(1)}, u32[]{:S(2)}, u32[]{:S(2)}) collective-permute-start(bf16[1,8,64,128]{3,2,1,0:T(8,128)(2,1)} %get-tuple-element.77), channel_id=1, source_target_pairs={{8,16},{16,8},{24,32},{32,24},{40,48},{48,40},{56,64},{64,56},{72,... | collective-permute-start | bytes 393224 | tf_op jit(solution)/shard_map/ppermute | solution.py:30
  25.2 4.7 %collective-permute-start.2 = (bf16[1,8,64,128]{3,2,1,0:T(8,128)(2,1)}, bf16[1,8,64,128]{3,2,1,0:T(8,128)(2,1)S(1)}, u32[]{:S(2)}, u32[]{:S(2)}) collective-permute-start(bf16[1,8,64,128]{3,2,1,0:T(8,128)(2,1)} %get-tuple-element.78), channel_id=1, source_target_pairs={{0,8},{8,0},{16,24},{24,16},{32,40},{40,32},{48,56},{56,48},{64,72... | collective-permute-start | bytes 393224 | tf_op jit(solution)/shard_map/ppermute | solution.py:30
  29.9 12.8 %collective-permute-start.7 = (bf16[10,64,128]{2,1,0:T(8,128)(2,1)S(1)}, bf16[10,64,128]{2,1,0:T(8,128)(2,1)S(1)}, u32[]{:S(2)}, u32[]{:S(2)}) collective-permute-start(bf16[10,64,128]{2,1,0:T(8,128)(2,1)S(1)} %get-tuple-element.48), channel_id=1, source_target_pairs={{1,2},{2,1},{3,4},{4,3},{5,6},{6,5},{9,10},{10,9},{11,12},{12,11},... | collective-permute-start | bytes 491528 | tf_op jit(solution)/shard_map/ppermute | solution.py:355
  36.7 6.2 %collective-permute-start.6 = (bf16[10,64,128]{2,1,0:T(8,128)(2,1)S(1)}, bf16[10,64,128]{2,1,0:T(8,128)(2,1)S(1)}, u32[]{:S(2)}, u32[]{:S(2)}) collective-permute-start(bf16[10,64,128]{2,1,0:T(8,128)(2,1)S(1)} %get-tuple-element.47), channel_id=1, source_target_pairs={{0,1},{1,0},{2,3},{3,2},{4,5},{5,4},{6,7},{7,6},{8,9},{9,8},{10,11... | collective-permute-start | bytes 491528 | tf_op jit(solution)/shard_map/ppermute | solution.py:352
  57.9 1.9 %collective-permute-start.12 = (f32[864,128]{1,0:T(8,128)S(1)}, f32[864,128]{1,0:T(8,128)S(1)}, u32[]{:S(2)}, u32[]{:S(2)}) collective-permute-start(f32[864,128]{1,0:T(8,128)S(1)} %get-tuple-element.60), channel_id=1, source_target_pairs={{0,8},{1,9},{2,10},{3,11},{4,12},{5,13},{6,14},{7,15},{8,0},{9,1},... | collective-permute-start | bytes 1327112 | tf_op jit(solution)/shard_map/ppermute | solution.py:25
  59.9 4.6 %collective-permute-start.13 = (f32[216,128]{1,0:T(8,128)S(1)}, f32[216,128]{1,0:T(8,128)S(1)}, u32[]{:S(2)}, u32[]{:S(2)}) collective-permute-start(f32[216,128]{1,0:T(8,128)S(1)} %get-tuple-element.62), channel_id=1, source_target_pairs={{0,16},{1,17},{2,18},{3,19},{4,20},{5,21},{6,22},{7,23},{8,24},{9,... | collective-permute-start | bytes 331784 | tf_op jit(solution)/shard_map/ppermute | solution.py:25
  59.9 6.1 %collective-permute-start.14 = (f32[216,128]{1,0:T(8,128)S(1)}, f32[216,128]{1,0:T(8,128)S(1)}, u32[]{:S(2)}, u32[]{:S(2)}) collective-permute-start(f32[216,128]{1,0:T(8,128)S(1)} %get-tuple-element.63), channel_id=1, source_target_pairs={{0,32},{1,33},{2,34},{3,35},{4,36},{5,37},{6,38},{7,39},{8,40},{9,... | collective-permute-start | bytes 331784 | tf_op jit(solution)/shard_map/ppermute | solution.py:25
  60.0 8.9 %collective-permute-start.15 = (f32[216,128]{1,0:T(8,128)S(1)}, f32[216,128]{1,0:T(8,128)S(1)}, u32[]{:S(2)}, u32[]{:S(2)}) collective-permute-start(f32[216,128]{1,0:T(8,128)S(1)} %get-tuple-element.64), channel_id=1, source_target_pairs={{0,48},{1,49},{2,50},{3,51},{4,52},{5,53},{6,54},{7,55},{8,56},{9,... | collective-permute-start | bytes 331784 | tf_op jit(solution)/shard_map/ppermute | solution.py:25
  68.9 8.3 %collective-permute-start.18 = (f32[216,128]{1,0:T(8,128)S(1)}, f32[216,128]{1,0:T(8,128)S(1)}, u32[]{:S(2)}, u32[]{:S(2)}) collective-permute-start(f32[216,128]{1,0:T(8,128)S(1)} %add_add_fusion.2), channel_id=1, source_target_pairs={{0,6},{1,7},{2,4},{3,5},{4,2},{5,3},{6,0},{7,1},{8,14},{9,15},{10,... | collective-permute-start | bytes 331784 | tf_op jit(solution)/shard_map/ppermute | solution.py:25
  69.0 8.2 %collective-permute-start.17 = (f32[216,128]{1,0:T(8,128)S(1)}, f32[216,128]{1,0:T(8,128)S(1)}, u32[]{:S(2)}, u32[]{:S(2)}) collective-permute-start(f32[216,128]{1,0:T(8,128)S(1)} %add_add_fusion.2), channel_id=1, source_target_pairs={{0,4},{1,5},{2,6},{3,7},{4,0},{5,1},{6,2},{7,3},{8,12},{9,13},{10,... | collective-permute-start | bytes 331784 | tf_op jit(solution)/shard_map/ppermute | solution.py:25
  71.2 6.0 %collective-permute-start.16 = (f32[216,128]{1,0:T(8,128)S(1)}, f32[216,128]{1,0:T(8,128)S(1)}, u32[]{:S(2)}, u32[]{:S(2)}) collective-permute-start(f32[216,128]{1,0:T(8,128)S(1)} %add_add_fusion.2), channel_id=1, source_target_pairs={{0,2},{1,3},{2,0},{3,1},{4,6},{5,7},{6,4},{7,5},{8,10},{9,11},{10,... | collective-permute-start | bytes 331784 | tf_op jit(solution)/shard_map/ppermute | solution.py:25
  77.2 10.2 %collective-permute-start.21 = (f32[216,128]{1,0:T(8,128)S(1)}, f32[216,128]{1,0:T(8,128)S(1)}, u32[]{:S(2)}, u32[]{:S(2)}) collective-permute-start(f32[216,128]{1,0:T(8,128)S(1)} %add_add_fusion.1), channel_id=1, source_target_pairs={{0,65},{1,64},{2,67},{3,66},{4,69},{5,68},{6,71},{7,70},{8,73},{9,... | collective-permute-start | bytes 331784 | tf_op jit(solution)/shard_map/ppermute | solution.py:25
  81.8 5.6 %collective-permute-start.20 = (f32[216,128]{1,0:T(8,128)S(1)}, f32[216,128]{1,0:T(8,128)S(1)}, u32[]{:S(2)}, u32[]{:S(2)}) collective-permute-start(f32[216,128]{1,0:T(8,128)S(1)} %add_add_fusion.1), channel_id=1, source_target_pairs={{0,64},{1,65},{2,66},{3,67},{4,68},{5,69},{6,70},{7,71},{8,72},{9,... | collective-permute-start | bytes 331784 | tf_op jit(solution)/shard_map/ppermute | solution.py:25
  81.8 6.1 %collective-permute-start.19 = (f32[216,128]{1,0:T(8,128)S(1)}, f32[216,128]{1,0:T(8,128)S(1)}, u32[]{:S(2)}, u32[]{:S(2)}) collective-permute-start(f32[216,128]{1,0:T(8,128)S(1)} %add_add_fusion.1), channel_id=1, source_target_pairs={{0,1},{1,0},{2,3},{3,2},{4,5},{5,4},{6,7},{7,6},{8,9},{9,8},{10,11... | collective-permute-start | bytes 331784 | tf_op jit(solution)/shard_map/ppermute | solution.py:25
  83.0 8.2 %collective-permute-start.8 = (bf16[1,8,64,128]{3,2,1,0:T(8,128)(2,1)S(1)}, bf16[1,8,64,128]{3,2,1,0:T(8,128)(2,1)S(1)}, u32[]{:S(2)}, u32[]{:S(2)}) collective-permute-start(bf16[1,8,64,128]{3,2,1,0:T(8,128)(2,1)S(1)} %get-tuple-element.50), channel_id=1, source_target_pairs={{0,8},{8,0},{16,24},{24,16},{32,40},{40,32},{48,56},{56,48},{64,72... | collective-permute-start | bytes 393224 | tf_op jit(solution)/shard_map/ppermute | solution.py:30
  85.1 10.6 %collective-permute-start.9 = (bf16[1,8,64,128]{3,2,1,0:T(8,128)(2,1)S(1)}, bf16[1,8,64,128]{3,2,1,0:T(8,128)(2,1)S(1)}, u32[]{:S(2)}, u32[]{:S(2)}) collective-permute-start(bf16[1,8,64,128]{3,2,1,0:T(8,128)(2,1)S(1)} %get-tuple-element.51), channel_id=1, source_target_pairs={{8,16},{16,8},{24,32},{32,24},{40,48},{48,40},{56,64},{64,56},{72,... | collective-permute-start | bytes 393224 | tf_op jit(solution)/shard_map/ppermute | solution.py:30
  87.9 12.8 %collective-permute-start.24 = (f32[216,128]{1,0:T(8,128)S(1)}, f32[216,128]{1,0:T(8,128)S(1)}, u32[]{:S(2)}, u32[]{:S(2)}) collective-permute-start(f32[216,128]{1,0:T(8,128)S(1)} %add_add_fusion.refs_3_), channel_id=1, source_target_pairs={{0,48},{1,49},{2,50},{3,51},{4,52},{5,53},{6,54},{7,55},{8,56},{9,... | collective-permute-start | bytes 331784 | tf_op jit(solution)/shard_map/ppermute | solution.py:25
  88.4 12.3 %collective-permute-start.23 = (f32[216,128]{1,0:T(8,128)S(1)}, f32[216,128]{1,0:T(8,128)S(1)}, u32[]{:S(2)}, u32[]{:S(2)}) collective-permute-start(f32[216,128]{1,0:T(8,128)S(1)} %add_add_fusion.refs_3_), channel_id=1, source_target_pairs={{0,32},{1,33},{2,34},{3,35},{4,36},{5,37},{6,38},{7,39},{8,40},{9,... | collective-permute-start | bytes 331784 | tf_op jit(solution)/shard_map/ppermute | solution.py:25
  90.3 10.4 %collective-permute-start.22 = (f32[216,128]{1,0:T(8,128)S(1)}, f32[216,128]{1,0:T(8,128)S(1)}, u32[]{:S(2)}, u32[]{:S(2)}) collective-permute-start(f32[216,128]{1,0:T(8,128)S(1)} %add_add_fusion.refs_3_), channel_id=1, source_target_pairs={{0,16},{1,17},{2,18},{3,19},{4,20},{5,21},{6,22},{7,23},{8,24},{9,... | collective-permute-start | bytes 331784 | tf_op jit(solution)/shard_map/ppermute | solution.py:25
  95.7 6.5 %collective-permute-start.10 = (bf16[10,64,128]{2,1,0:T(8,128)(2,1)S(1)}, bf16[10,64,128]{2,1,0:T(8,128)(2,1)S(1)}, u32[]{:S(2)}, u32[]{:S(2)}) collective-permute-start(bf16[10,64,128]{2,1,0:T(8,128)(2,1)S(1)} %get-tuple-element.52), channel_id=1, source_target_pairs={{0,1},{1,0},{2,3},{3,2},{4,5},{5,4},{6,7},{7,6},{8,9},{9,8},{10,11... | collective-permute-start | bytes 491528 | tf_op jit(solution)/shard_map/ppermute | solution.py:373
  97.9 8.6 %collective-permute-start.11 = (bf16[10,64,128]{2,1,0:T(8,128)(2,1)S(1)}, bf16[10,64,128]{2,1,0:T(8,128)(2,1)S(1)}, u32[]{:S(2)}, u32[]{:S(2)}) collective-permute-start(bf16[10,64,128]{2,1,0:T(8,128)(2,1)S(1)} %get-tuple-element.53), channel_id=1, source_target_pairs={{1,2},{2,1},{3,4},{4,3},{5,6},{6,5},{9,10},{10,9},{11,12},{12,11},... | collective-permute-start | bytes 491528 | tf_op jit(solution)/shard_map/ppermute | solution.py:374
  100.7 14.7 %collective-permute-start.25 = (f32[864,128]{1,0:T(8,128)S(1)}, f32[864,128]{1,0:T(8,128)S(1)}, u32[]{:S(2)}, u32[]{:S(2)}) collective-permute-start(f32[864,128]{1,0:T(8,128)S(1)} %shard_map.87.refs_3_), channel_id=1, source_target_pairs={{0,8},{1,9},{2,10},{3,11},{4,12},{5,13},{6,14},{7,15},{8,0},{9,1},... | collective-permute-start | bytes 1327112 | tf_op jit(solution)/shard_map/ppermute | solution.py:25

commit v7 on v6

--- a/solution.py
+++ b/solution.py
@@ -126,7 +126,7 @@
 def backward_kernel(
     place, weights, slope, tile, xr_even, xr_odd, yr_even, yr_odd, pre_grad, xs_even, xs_odd, padded
 ):
-    pad_tile(padded, place, tile, xr_even, xr_odd, yr_even, yr_odd, 0)
+    pad_tile(padded, place, tile, xr_even, xr_odd, yr_even, yr_odd, 1)
     size_x = tile.shape[0]
 
     def emit(x, y, value):
@@ -317,15 +317,13 @@
     mask_f = mask.astype(F32)
     mask_b = mask.astype(BF16).reshape(1, 1, tile_z)
 
-    def x_swap(array):
-        def edge(at):
-            plane = lax.dynamic_index_in_dim(array, at, 1, keepdims=False) * mask_b
-            return jnp.transpose(plane, (1, 0, 2))[None]
-
-        return swap(edge((1 - x_odd) * (tile_x - 1)), edge(x_odd * (tile_x - 1)), "gx")
-
-    in_xr = x_swap(features)
+    def x_edges(at):
+        both = [lax.dynamic_index_in_dim(a, at, 1, keepdims=False) * mask_b for a in (features, cotangent)]
+        return jnp.stack([jnp.transpose(a, (1, 0, 2)) for a in both])
+
+    xr = swap(x_edges((1 - x_odd) * (tile_x - 1)), x_edges(x_odd * (tile_x - 1)), "gx")
     masked_in = jnp.transpose(features * mask_b[:, None], (1, 2, 0, 3))
+    masked_grad = jnp.transpose(cotangent * mask_b[:, None], (1, 2, 0, 3))
 
     tile_shape = (tile_x, tile_y, chans, tile_z)
     tile_b = jax.ShapeDtypeStruct(tile_shape, BF16)
@@ -338,32 +336,25 @@
         outs = [column_b] * (2 * len(tiles))
         return call(ypack_kernel, outs, scalars=3)(*place, *tiles, *halo_x)
 
-    in_sends = y_sends((masked_in,), in_xr)
+    sends = y_sends((masked_in, masked_grad), xr)
     matrix = jax.ShapeDtypeStruct((3 * chans, 9 * chans), BF16)
     even, odd = swap_perms(lax.axis_size("gy"))
-    in_send, cotangent = lax.optimization_barrier((in_sends[0], cotangent))
-    in_even = lax.ppermute(in_send, "gy", even)
-    grad_xr = x_swap(cotangent)
-    masked_grad = jnp.transpose(cotangent * mask_b[:, None], (1, 2, 0, 3))
-    in_send, masked_grad = lax.optimization_barrier((in_sends[1], masked_grad))
-    in_odd = lax.ppermute(in_send, "gy", odd)
+    in_even = lax.ppermute(sends[0], "gy", even)
+    w_pre, w_act, w_branch = call(weights_kernel, [matrix] * 3)(kernel_one, kernel_two)
+    in_next, w_pre = lax.optimization_barrier((sends[1], w_pre))
+    in_odd = lax.ppermute(in_next, "gy", odd)
     in_y = (in_even, in_odd)
-    grad_sends = y_sends((masked_grad,), grad_xr)
-    grad_even = lax.ppermute(grad_sends[0], "gy", even)
-    w_pre, w_act, w_branch = call(weights_kernel, [matrix] * 3)(kernel_one, kernel_two)
-    grad_send, w_pre = lax.optimization_barrier((grad_sends[1], w_pre))
-    grad_odd = lax.ppermute(grad_send, "gy", odd)
-    grad_y = (grad_even, grad_odd)
+    grad_y = swap(*sends[2:], "gy")
 
     tile_s = pltpu.VMEM((tile_x, tile_y, 3 * chans, tile_z), BF16)
     grad_s = pltpu.VMEM((9 * chans, 3 * chans), F32)
 
     activ, slope, in_pad = call(
         forward_kernel, [tile_b, jax.ShapeDtypeStruct(tile_shape, F32), pad_b], scalars=3, flops=flops
-    )(*place, mask_f, w_pre, masked_in, *in_xr, *in_y)
+    )(*place, mask_f, w_pre, masked_in, *xr, *in_y)
     pre_grad, xs_even, xs_odd, grad_pad = call(
         backward_kernel, [tile_b, edge_b, edge_b, pad_b], scalars=3, flops=flops
-    )(*place, w_act, slope, masked_grad, *grad_xr, *grad_y)
+    )(*place, w_act, slope, masked_grad, *xr, *grad_y)
 
     packed = 27 * chans * chans // (2 * chans)
     half = jax.ShapeDtypeStruct((packed, 2 * chans), F32)

time: 117 us -> 112 us (0.957)
  the two profiles are of different devices: /device:TPU:31 before, /device:TPU:15 now
where the time goes in v7:
time: 112 us
  starting transfers between devices  41.5 us (37%)
  Pallas kernels  30.4 us (27%)
  waiting for transfers between devices  29.5 us (26%)
  other arithmetic  5.75 us (5%)
  local copies, waits for them, and re-layouts  3.8 us (3%)
    pallas_call x13, Pallas kernels, run(): pl.pallas_call(wrapped, out_shape=tuple(outs), in_specs=specs, out_specs=...  30.4 us
    ppermute x14, starting transfers between devices, xor_permute(): return lax.ppermute(value, AXES, [(i, i ^ mask) for i in range(total)])  16.3 us
    ppermute x14, waiting for transfers between devices, xor_permute(): return lax.ppermute(value, AXES, [(i, i ^ mask) for i in range(total)])  11.8 us
    ppermute x3, starting transfers between devices, swap(): lax.ppermute(value_odd, axis, odd)  9.05 us
    ppermute x3, waiting for transfers between devices, swap(): lax.ppermute(value_odd, axis, odd)  6.7 us
    ppermute x1, starting transfers between devices, body(): in_odd = lax.ppermute(in_next, 'gy', odd)  5.38 us
    ppermute x3, starting transfers between devices, swap(): lax.ppermute(value_even, axis, even)  5.35 us
    ppermute x1, waiting for transfers between devices, body(): in_even = lax.ppermute(sends[0], 'gy', even)  5.2 us
  transfers between devices with their start and end apart: 24, of which 12 were waited for; matrix products, arithmetic and copies ran while one was open for 5% of the time, Pallas kernels for 12%

profile of v7, /device:TPU:15, one launch (start us, length us, event | category | flops | bytes accessed | tf_op | source)
XLA Modules:
  0.0 111.9 jit_solution(12926843147134831175)
XLA Ops:
  0.7 0.8 convert_bitcast_fusion
  1.4 0.1 broadcast_in_dim.8
  1.5 0.1 convert_element_type.32
  1.6 1.2 %constant_dynamic-slice_fusion = (bf16[64,1,8,128]{3,2,1,0:T(8,128)(2,1)S(1)}, bf16[64,1,8,128]{3,2,1,0:T(8,128)(2,1)S(1)}, bf16[64,1,8,128]{3,2,1,0:T(8,128)(2,1)S(1)}, bf16[64,1,8,128]{3,2,1,0:T(8,128)(2,1)S(1)}) fusion(bf16[64,8,8,128]{3,2,1,0:T(8,128)(2,1)} %param.6, s32[]{:T(128)S(6)} %select_n.10, s32[]{:T(128)S(6)} %select_n.9, ...), kind=kLoop, calls=%fused_computation.18 | loop fusion | bytes 1048584 | tf_op jit(solution)/shard_map/jit(dynamic_index_in_dim)/dynamic_slice | solution.py:321
  2.7 0.1 fusion.3
  2.8 0.7 pad_maximum_fusion
  3.6 0.7 collective-permute-start
  4.2 0.7 pad_maximum_fusion.1
  5.0 3.3 %collective-permute-start.1 = (bf16[2,8,64,128]{3,2,1,0:T(8,128)(2,1)}, bf16[2,8,64,128]{3,2,1,0:T(8,128)(2,1)S(1)}, u32[]{:S(2)}, u32[]{:S(2)}) collective-permute-start(bf16[2,8,64,128]{3,2,1,0:T(8,128)(2,1)} %pad_maximum_fusion.1), channel_id=1, source_target_pairs={{8,16},{16,8},{24,32},{32,24},{40,48},{48,40},{56,64},{64,56},{72,... | collective-permute-start | bytes 786440 | tf_op jit(solution)/shard_map/ppermute | solution.py:30
  8.3 0.3 shard_map.76
  8.6 3.3 %fusion = (bf16[8,8,64,128]{3,2,1,0:T(8,128)(2,1)S(1)}, bf16[8,8,64,128]{3,2,1,0:T(8,128)(2,1)S(1)}) fusion(bf16[64,8,8,128]{3,2,1,0:T(8,128)(2,1)} %param.5, bf16[128]{0:T(256)(128)(2,1)S(1)} %convert_element_type.32, bf16[64,8,8,128]{3,2,1,0:T(8,128)(2,1)} %param.6), kind=kLoop, calls=%fused_computation.2 | loop fusion | flops 1048576 | bytes 4194560 | tf_op jit(solution)/shard_map/transpose | solution.py:325
  11.9 3.0 %collective-permute-done.1.refs_6_.refs_7_ = bf16[2,8,64,128]{3,2,1,0:T(8,128)(2,1)S(1)} collective-permute-done((bf16[2,8,64,128]{3,2,1,0:T(8,128)(2,1)}, bf16[2,8,64,128]{3,2,1,0:T(8,128)(2,1)S(1)}, u32[]{:S(2)}, u32[]{:S(2)}) %collective-permute-start.1) | collective-permute-done | bytes 262176 | tf_op jit(solution)/shard_map/ppermute | solution.py:30
  15.0 0.8 shard_map.77
  15.7 0.7 copy-done.2
  16.4 5.4 %collective-permute-start.3 = (bf16[10,64,128]{2,1,0:T(8,128)(2,1)}, bf16[10,64,128]{2,1,0:T(8,128)(2,1)}, u32[]{:S(2)}, u32[]{:S(2)}) collective-permute-start(bf16[10,64,128]{2,1,0:T(8,128)(2,1)} %get-tuple-element.37), channel_id=1, source_target_pairs={{1,2},{2,1},{3,4},{4,3},{5,6},{6,5},{9,10},{10,9},{11,12},{12,11},... | collective-permute-start | bytes 491528 | tf_op jit(solution)/shard_map/ppermute | solution.py:345
  21.8 0.6 collective-permute-start.2
  22.4 0.1 broadcast_in_dim.7
  22.4 0.1 convert_element_type.29.refs_3_.refs_0_
  22.5 2.5 %collective-permute-start.4 = (bf16[10,64,128]{2,1,0:T(8,128)(2,1)}, bf16[10,64,128]{2,1,0:T(8,128)(2,1)S(1)}, u32[]{:S(2)}, u32[]{:S(2)}) collective-permute-start(bf16[10,64,128]{2,1,0:T(8,128)(2,1)} %copy-done.2), channel_id=1, source_target_pairs={{0,1},{1,0},{2,3},{3,2},{4,5},{5,4},{6,7},{7,6},{8,9},{9,8},{10,11... | collective-permute-start | bytes 491528 | tf_op jit(solution)/shard_map/ppermute | solution.py:30
  25.1 2.3 %collective-permute-start.5 = (bf16[10,64,128]{2,1,0:T(8,128)(2,1)S(1)}, bf16[10,64,128]{2,1,0:T(8,128)(2,1)S(1)}, u32[]{:S(2)}, u32[]{:S(2)}) collective-permute-start(bf16[10,64,128]{2,1,0:T(8,128)(2,1)S(1)} %get-tuple-element.40), channel_id=1, source_target_pairs={{1,2},{2,1},{3,4},{4,3},{5,6},{6,5},{9,10},{10,9},{11,12},{12,11},... | collective-permute-start | bytes 491528 | tf_op jit(solution)/shard_map/ppermute | solution.py:30
  27.4 5.2 %collective-permute-done.2.refs_8_ = bf16[10,64,128]{2,1,0:T(8,128)(2,1)} collective-permute-done((bf16[10,64,128]{2,1,0:T(8,128)(2,1)}, bf16[10,64,128]{2,1,0:T(8,128)(2,1)}, u32[]{:S(2)}, u32[]{:S(2)}) %collective-permute-start.2) | collective-permute-done | bytes 163872 | tf_op jit(solution)/shard_map/ppermute | solution.py:342
  32.6 5.9 %shard_map.78 = (bf16[8,8,64,128]{3,2,1,0:T(8,128)(2,1)S(1)}, f32[8,8,64,128]{3,2,1,0:T(8,128)S(1)}, bf16[10,10,64,128]{3,2,1,0:T(8,128)(2,1)S(1)}) custom-call(s32[1]{0:T(128)} %bitcast.refs_0_, s32[1]{0:T(128)} %bitcast.1.refs_1_, s32[1]{0:T(128)} %bitcast.2.refs_2_, f32[1,128]{1,0:T(1,128)S(1)} %convert_element_type.29.refs_3_.refs_0_, ...), custom_call_target="tpu_custom_call" | custom-call | flops 1811939328 | bytes 6906380 | tf_op jit(solution)/shard_map/pallas_call | solution.py:294
  38.4 0.0 collective-permute-done.4.refs_8_
  38.5 4.7 %shard_map.79 = (bf16[8,8,64,128]{3,2,1,0:T(8,128)(2,1)S(1)}, bf16[1,8,64,128]{3,2,1,0:T(8,128)(2,1)S(1)}, bf16[1,8,64,128]{3,2,1,0:T(8,128)(2,1)S(1)}, bf16[10,10,64,128]{3,2,1,0:T(8,128)(2,1)S(1)}) custom-call(s32[1]{0:T(128)} %bitcast.refs_0_, s32[1]{0:T(128)} %bitcast.1.refs_1_, s32[1]{0:T(128)} %bitcast.2.refs_2_, ...), custom_call_target="tpu_custom_call" | custom-call | flops 1811939328 | bytes 7168012 | tf_op jit(solution)/shard_map/pallas_call | solution.py:294
  43.2 5.1 %shard_map.83.refs_5_ = f32[864,128]{1,0:T(8,128)S(1)} custom-call(bf16[10,10,64,128]{3,2,1,0:T(8,128)(2,1)S(1)} %get-tuple-element.49.refs_0_, bf16[8,8,64,128]{3,2,1,0:T(8,128)(2,1)S(1)} %get-tuple-element.50.refs_1_), custom_call_target="tpu_custom_call" | custom-call | flops 1811939328 | bytes 3129344 | tf_op jit(solution)/shard_map/pallas_call | solution.py:294
  48.3 5.1 %shard_map.84 = (f32[864,128]{1,0:T(8,128)S(1)}, f32[864,128]{1,0:T(8,128)S(1)}) custom-call(s32[1]{0:T(128)} %bitcast.refs_0_, s32[1]{0:T(128)} %bitcast.1.refs_1_, s32[1]{0:T(128)} %bitcast.2.refs_2_, bf16[10,10,64,128]{3,2,1,0:T(8,128)(2,1)S(1)} %get-tuple-element.48.refs_3_, bf16[8,8,64,128]{3,2,1,0:T(8,128)(2,1)S(1)} %get-tuple-element.41.refs_3_.refs_6_.refs_4_, ...), custom_call_target="tpu_custom_call" | custom-call | flops 1811939328 | bytes 4014092 | tf_op jit(solution)/shard_map/pallas_call | solution.py:294
  53.5 0.1 collective-permute-start.10
  53.6 1.8 %collective-permute-done.10.refs_4_ = f32[864,128]{1,0:T(8,128)S(1)} collective-permute-done((f32[864,128]{1,0:T(8,128)S(1)}, f32[864,128]{1,0:T(8,128)S(1)}, u32[]{:S(2)}, u32[]{:S(2)}) %collective-permute-start.10) | collective-permute-done | bytes 442400 | tf_op jit(solution)/shard_map/ppermute | solution.py:25
  55.4 0.2 collective-permute-start.11
  55.6 0.7 collective-permute-start.12
  56.2 3.1 %collective-permute-start.13 = (f32[216,128]{1,0:T(8,128)S(1)}, f32[216,128]{1,0:T(8,128)S(1)}, u32[]{:S(2)}, u32[]{:S(2)}) collective-permute-start(f32[216,128]{1,0:T(8,128)S(1)} %get-tuple-element.56), channel_id=1, source_target_pairs={{0,48},{1,49},{2,50},{3,51},{4,52},{5,53},{6,54},{7,55},{8,56},{9,... | collective-permute-start | bytes 331784 | tf_op jit(solution)/shard_map/ppermute | solution.py:25
  59.3 0.6 collective-permute-done.11
  59.9 1.1 collective-permute-done.12
  61.0 3.4 %collective-permute-done.13 = f32[216,128]{1,0:T(8,128)S(1)} collective-permute-done((f32[216,128]{1,0:T(8,128)S(1)}, f32[216,128]{1,0:T(8,128)S(1)}, u32[]{:S(2)}, u32[]{:S(2)}) %collective-permute-start.13) | collective-permute-done | bytes 110624 | tf_op jit(solution)/shard_map/ppermute | solution.py:25
  64.5 1.4 %collective-permute-start.16 = (f32[216,128]{1,0:T(8,128)S(1)}, f32[216,128]{1,0:T(8,128)S(1)}, u32[]{:S(2)}, u32[]{:S(2)}) collective-permute-start(f32[216,128]{1,0:T(8,128)S(1)} %add_add_fusion.2), channel_id=1, source_target_pairs={{0,6},{1,7},{2,4},{3,5},{4,2},{5,3},{6,0},{7,1},{8,14},{9,15},{10,... | collective-permute-start | bytes 331784 | tf_op jit(solution)/shard_map/ppermute | solution.py:25
  65.8 0.7 collective-permute-start.15
  66.5 1.3 %collective-permute-start.14 = (f32[216,128]{1,0:T(8,128)S(1)}, f32[216,128]{1,0:T(8,128)S(1)}, u32[]{:S(2)}, u32[]{:S(2)}) collective-permute-start(f32[216,128]{1,0:T(8,128)S(1)} %add_add_fusion.2), channel_id=1, source_target_pairs={{0,2},{1,3},{2,0},{3,1},{4,6},{5,7},{6,4},{7,5},{8,10},{9,11},{10,... | collective-permute-start | bytes 331784 | tf_op jit(solution)/shard_map/ppermute | solution.py:25
  67.8 0.9 collective-permute-done.16
  68.7 2.2 %collective-permute-done.15 = f32[216,128]{1,0:T(8,128)S(1)} collective-permute-done((f32[216,128]{1,0:T(8,128)S(1)}, f32[216,128]{1,0:T(8,128)S(1)}, u32[]{:S(2)}, u32[]{:S(2)}) %collective-permute-start.15) | collective-permute-done | bytes 110624 | tf_op jit(solution)/shard_map/ppermute | solution.py:25
  70.9 1.7 %collective-permute-done.14 = f32[216,128]{1,0:T(8,128)S(1)} collective-permute-done((f32[216,128]{1,0:T(8,128)S(1)}, f32[216,128]{1,0:T(8,128)S(1)}, u32[]{:S(2)}, u32[]{:S(2)}) %collective-permute-start.14) | collective-permute-done | bytes 110624 | tf_op jit(solution)/shard_map/ppermute | solution.py:25
  72.7 4.3 %collective-permute-start.19 = (f32[216,128]{1,0:T(8,128)S(1)}, f32[216,128]{1,0:T(8,128)S(1)}, u32[]{:S(2)}, u32[]{:S(2)}) collective-permute-start(f32[216,128]{1,0:T(8,128)S(1)} %add_add_fusion.1), channel_id=1, source_target_pairs={{0,65},{1,64},{2,67},{3,66},{4,69},{5,68},{6,71},{7,70},{8,73},{9,... | collective-permute-start | bytes 331784 | tf_op jit(solution)/shard_map/ppermute | solution.py:25
  77.0 0.0 collective-permute-start.18
  77.0 1.3 %collective-permute-start.17 = (f32[216,128]{1,0:T(8,128)S(1)}, f32[216,128]{1,0:T(8,128)S(1)}, u32[]{:S(2)}, u32[]{:S(2)}) collective-permute-start(f32[216,128]{1,0:T(8,128)S(1)} %add_add_fusion.1), channel_id=1, source_target_pairs={{0,1},{1,0},{2,3},{3,2},{4,5},{5,4},{6,7},{7,6},{8,9},{9,8},{10,11... | collective-permute-start | bytes 331784 | tf_op jit(solution)/shard_map/ppermute | solution.py:25
  78.2 2.1 %collective-permute-start.6 = (bf16[1,8,64,128]{3,2,1,0:T(8,128)(2,1)S(1)}, bf16[1,8,64,128]{3,2,1,0:T(8,128)(2,1)S(1)}, u32[]{:S(2)}, u32[]{:S(2)}) collective-permute-start(bf16[1,8,64,128]{3,2,1,0:T(8,128)(2,1)S(1)} %get-tuple-element.42), channel_id=1, source_target_pairs={{0,8},{8,0},{16,24},{24,16},{32,40},{40,32},{48,56},{56,48},{64,72... | collective-permute-start | bytes 393224 | tf_op jit(solution)/shard_map/ppermute | solution.py:30
  80.4 3.4 %collective-permute-start.7 = (bf16[1,8,64,128]{3,2,1,0:T(8,128)(2,1)S(1)}, bf16[1,8,64,128]{3,2,1,0:T(8,128)(2,1)S(1)}, u32[]{:S(2)}, u32[]{:S(2)}) collective-permute-start(bf16[1,8,64,128]{3,2,1,0:T(8,128)(2,1)S(1)} %get-tuple-element.43), channel_id=1, source_target_pairs={{8,16},{16,8},{24,32},{32,24},{40,48},{48,40},{56,64},{64,56},{72,... | collective-permute-start | bytes 393224 | tf_op jit(solution)/shard_map/ppermute | solution.py:30
  83.8 0.0 collective-permute-done.18
  83.8 0.0 collective-permute-done.17
  83.9 1.2 %collective-permute-start.22 = (f32[216,128]{1,0:T(8,128)S(1)}, f32[216,128]{1,0:T(8,128)S(1)}, u32[]{:S(2)}, u32[]{:S(2)}) collective-permute-start(f32[216,128]{1,0:T(8,128)S(1)} %add_add_fusion.refs_3_), channel_id=1, source_target_pairs={{0,48},{1,49},{2,50},{3,51},{4,52},{5,53},{6,54},{7,55},{8,56},{9,... | collective-permute-start | bytes 331784 | tf_op jit(solution)/shard_map/ppermute | solution.py:25
  85.1 0.5 collective-permute-start.21
  85.6 1.6 %collective-permute-start.20 = (f32[216,128]{1,0:T(8,128)S(1)}, f32[216,128]{1,0:T(8,128)S(1)}, u32[]{:S(2)}, u32[]{:S(2)}) collective-permute-start(f32[216,128]{1,0:T(8,128)S(1)} %add_add_fusion.refs_3_), channel_id=1, source_target_pairs={{0,16},{1,17},{2,18},{3,19},{4,20},{5,21},{6,22},{7,23},{8,24},{9,... | collective-permute-start | bytes 331784 | tf_op jit(solution)/shard_map/ppermute | solution.py:25
  87.2 3.7 %collective-permute-done.7.refs_5_.refs_8_ = bf16[1,8,64,128]{3,2,1,0:T(8,128)(2,1)S(1)} collective-permute-done((bf16[1,8,64,128]{3,2,1,0:T(8,128)(2,1)S(1)}, bf16[1,8,64,128]{3,2,1,0:T(8,128)(2,1)S(1)}, u32[]{:S(2)}, u32[]{:S(2)}) %collective-permute-start.7) | collective-permute-done | bytes 131104 | tf_op jit(solution)/shard_map/ppermute | solution.py:30
  90.9 2.0 %collective-permute-start.8 = (bf16[10,64,128]{2,1,0:T(8,128)(2,1)S(1)}, bf16[10,64,128]{2,1,0:T(8,128)(2,1)S(1)}, u32[]{:S(2)}, u32[]{:S(2)}) collective-permute-start(bf16[10,64,128]{2,1,0:T(8,128)(2,1)S(1)} %get-tuple-element.44), channel_id=1, source_target_pairs={{0,1},{1,0},{2,3},{3,2},{4,5},{5,4},{6,7},{7,6},{8,9},{9,8},{10,11... | collective-permute-start | bytes 491528 | tf_op jit(solution)/shard_map/ppermute | solution.py:364
  92.9 2.8 %collective-permute-start.9 = (bf16[10,64,128]{2,1,0:T(8,128)(2,1)S(1)}, bf16[10,64,128]{2,1,0:T(8,128)(2,1)S(1)}, u32[]{:S(2)}, u32[]{:S(2)}) collective-permute-start(bf16[10,64,128]{2,1,0:T(8,128)(2,1)S(1)} %get-tuple-element.45), channel_id=1, source_target_pairs={{1,2},{2,1},{3,4},{4,3},{5,6},{6,5},{9,10},{10,9},{11,12},{12,11},... | collective-permute-start | bytes 491528 | tf_op jit(solution)/shard_map/ppermute | solution.py:365
  95.7 0.0 collective-permute-done.22.refs_6_
  95.7 0.0 collective-permute-done.20.refs_4_
  95.8 0.1 collective-permute-start.23
  95.9 1.4 %collective-permute-done.8.refs_9_ = bf16[10,64,128]{2,1,0:T(8,128)(2,1)S(1)} collective-permute-done((bf16[10,64,128]{2,1,0:T(8,128)(2,1)S(1)}, bf16[10,64,128]{2,1,0:T(8,128)(2,1)S(1)}, u32[]{:S(2)}, u32[]{:S(2)}) %collective-permute-start.8) | collective-permute-done | bytes 163872 | tf_op jit(solution)/shard_map/ppermute | solution.py:364
  97.3 4.3 %collective-permute-done.9.refs_10_ = bf16[10,64,128]{2,1,0:T(8,128)(2,1)S(1)} collective-permute-done((bf16[10,64,128]{2,1,0:T(8,128)(2,1)S(1)}, bf16[10,64,128]{2,1,0:T(8,128)(2,1)S(1)}, u32[]{:S(2)}, u32[]{:S(2)}) %collective-permute-start.9) | collective-permute-done | bytes 163872 | tf_op jit(solution)/shard_map/ppermute | solution.py:365
  101.7 3.5 %shard_map.81 = (bf16[8,4,64,128]{3,2,1,0:T(8,128)(2,1)S(1)}, bf16[10,10,64,128]{3,2,1,0:T(8,128)(2,1)S(1)}) custom-call(s32[1]{0:T(128)} %bitcast.refs_0_, s32[1]{0:T(128)} %bitcast.1.refs_1_, s32[1]{0:T(128)} %bitcast.2.refs_2_, f32[1,128]{1,0:T(1,128)S(1)} %convert_element_type.29.refs_3_.refs_0_, bf16[192,576]{1,0:T(8,128)(2,1)S(1)} %get-tuple-element.31.refs_4_.refs_1_, ...), custom_call_target="tpu_custom_call" | custom-call | flops 905969664 | bytes 5071372 | tf_op jit(solution)/shard_map/pallas_call | solution.py:294
  105.1 3.3 %shard_map.82 = bf16[8,4,64,128]{3,2,1,0:T(8,128)(2,1)S(1)} custom-call(f32[1,128]{1,0:T(1,128)S(1)} %convert_element_type.29.refs_3_.refs_0_, bf16[192,576]{1,0:T(8,128)(2,1)S(1)} %get-tuple-element.31.refs_4_.refs_1_, bf16[8,8,64,128]{3,2,1,0:T(8,128)(2,1)S(1)} %get-tuple-element.74.refs_4_.refs_5_.refs_2_, ...), custom_call_target="tpu_custom_call" | custom-call | flops 905969664 | bytes 3432960 | tf_op jit(solution)/shard_map/pallas_call | solution.py:294
  108.5 0.1 maximum_bitcast_fusion
  108.6 1.6 %copy.21 = bf16[64,8,8,128]{3,2,1,0:T(8,128)(2,1)} copy(bf16[64,8,8,128]{3,0,2,1:T(8,128)(2,1)S(1)} %maximum_bitcast_fusion) | data formatting | bytes 2097152
  110.2 0.4 shard_map.87.refs_3_
  110.6 1.2 %shard_map.88 = (f32[3,3,3,64,64]{4,3,2,1,0:T(8,128)}, f32[3,3,3,64,64]{4,3,2,1,0:T(8,128)}) custom-call(s32[1]{0:T(128)} %bitcast.refs_0_, s32[1]{0:T(128)} %bitcast.1.refs_1_, s32[1]{0:T(128)} %bitcast.2.refs_2_, f32[3,3,3,64,64]{4,3,2,1,0:T(8,128)S(1)} %shard_map.87.refs_3_, f32[864,128]{1,0:T(8,128)S(1)} %collective-permute-done.23.refs_4_), custom_call_target="tpu_custom_call" | custom-call | bytes 1769484 | tf_op jit(solution)/shard_map/pallas_call | solution.py:294
  (18 shorter events, 0.2 us)
Async XLA Ops:
  0.6 7.7 %copy-start.1 = (bf16[3,3,3,64,64]{4,3,2,1,0:T(8,128)(2,1)S(1)}, bf16[3,3,3,64,64]{4,3,2,1,0:T(8,128)(2,1)}, u32[]{:S(2)}) copy-start(bf16[3,3,3,64,64]{4,3,2,1,0:T(8,128)(2,1)} %refs_1_.1) | copy-start | bytes 663556
  0.6 7.7 %copy-start = (bf16[3,3,3,64,64]{4,3,2,1,0:T(8,128)(2,1)S(1)}, bf16[3,3,3,64,64]{4,3,2,1,0:T(8,128)(2,1)}, u32[]{:S(2)}) copy-start(bf16[3,3,3,64,64]{4,3,2,1,0:T(8,128)(2,1)} %refs_0_.1) | copy-start | bytes 663556
  3.6 8.3 %collective-permute-start = (bf16[2,8,64,128]{3,2,1,0:T(8,128)(2,1)}, bf16[2,8,64,128]{3,2,1,0:T(8,128)(2,1)S(1)}, u32[]{:S(2)}, u32[]{:S(2)}) collective-permute-start(bf16[2,8,64,128]{3,2,1,0:T(8,128)(2,1)} %pad_maximum_fusion), channel_id=1, source_target_pairs={{0,8},{8,0},{16,24},{24,16},{32,40},{40,32},{48,56},{56,48},{64,72... | collective-permute-start | bytes 786440 | tf_op jit(solution)/shard_map/ppermute | solution.py:30
  5.0 10.0 %collective-permute-start.1 = (bf16[2,8,64,128]{3,2,1,0:T(8,128)(2,1)}, bf16[2,8,64,128]{3,2,1,0:T(8,128)(2,1)S(1)}, u32[]{:S(2)}, u32[]{:S(2)}) collective-permute-start(bf16[2,8,64,128]{3,2,1,0:T(8,128)(2,1)} %pad_maximum_fusion.1), channel_id=1, source_target_pairs={{8,16},{16,8},{24,32},{32,24},{40,48},{48,40},{56,64},{64,56},{72,... | collective-permute-start | bytes 786440 | tf_op jit(solution)/shard_map/ppermute | solution.py:30
  15.7 0.7 copy-start.2
  16.4 11.0 %collective-permute-start.3 = (bf16[10,64,128]{2,1,0:T(8,128)(2,1)}, bf16[10,64,128]{2,1,0:T(8,128)(2,1)}, u32[]{:S(2)}, u32[]{:S(2)}) collective-permute-start(bf16[10,64,128]{2,1,0:T(8,128)(2,1)} %get-tuple-element.37), channel_id=1, source_target_pairs={{1,2},{2,1},{3,4},{4,3},{5,6},{6,5},{9,10},{10,9},{11,12},{12,11},... | collective-permute-start | bytes 491528 | tf_op jit(solution)/shard_map/ppermute | solution.py:345
  21.8 10.8 %collective-permute-start.2 = (bf16[10,64,128]{2,1,0:T(8,128)(2,1)}, bf16[10,64,128]{2,1,0:T(8,128)(2,1)}, u32[]{:S(2)}, u32[]{:S(2)}) collective-permute-start(bf16[10,64,128]{2,1,0:T(8,128)(2,1)} %get-tuple-element.36), channel_id=1, source_target_pairs={{0,1},{1,0},{2,3},{3,2},{4,5},{5,4},{6,7},{7,6},{8,9},{9,8},{10,11... | collective-permute-start | bytes 491528 | tf_op jit(solution)/shard_map/ppermute | solution.py:342
  22.5 15.9 %collective-permute-start.4 = (bf16[10,64,128]{2,1,0:T(8,128)(2,1)}, bf16[10,64,128]{2,1,0:T(8,128)(2,1)S(1)}, u32[]{:S(2)}, u32[]{:S(2)}) collective-permute-start(bf16[10,64,128]{2,1,0:T(8,128)(2,1)} %copy-done.2), channel_id=1, source_target_pairs={{0,1},{1,0},{2,3},{3,2},{4,5},{5,4},{6,7},{7,6},{8,9},{9,8},{10,11... | collective-permute-start | bytes 491528 | tf_op jit(solution)/shard_map/ppermute | solution.py:30
  25.1 13.4 %collective-permute-start.5 = (bf16[10,64,128]{2,1,0:T(8,128)(2,1)S(1)}, bf16[10,64,128]{2,1,0:T(8,128)(2,1)S(1)}, u32[]{:S(2)}, u32[]{:S(2)}) collective-permute-start(bf16[10,64,128]{2,1,0:T(8,128)(2,1)S(1)} %get-tuple-element.40), channel_id=1, source_target_pairs={{1,2},{2,1},{3,4},{4,3},{5,6},{6,5},{9,10},{10,9},{11,12},{12,11},... | collective-permute-start | bytes 491528 | tf_op jit(solution)/shard_map/ppermute | solution.py:30
  53.5 1.9 %collective-permute-start.10 = (f32[864,128]{1,0:T(8,128)S(1)}, f32[864,128]{1,0:T(8,128)S(1)}, u32[]{:S(2)}, u32[]{:S(2)}) collective-permute-start(f32[864,128]{1,0:T(8,128)S(1)} %get-tuple-element.52), channel_id=1, source_target_pairs={{0,8},{1,9},{2,10},{3,11},{4,12},{5,13},{6,14},{7,15},{8,0},{9,1},... | collective-permute-start | bytes 1327112 | tf_op jit(solution)/shard_map/ppermute | solution.py:25
  55.4 4.6 %collective-permute-start.11 = (f32[216,128]{1,0:T(8,128)S(1)}, f32[216,128]{1,0:T(8,128)S(1)}, u32[]{:S(2)}, u32[]{:S(2)}) collective-permute-start(f32[216,128]{1,0:T(8,128)S(1)} %get-tuple-element.54), channel_id=1, source_target_pairs={{0,16},{1,17},{2,18},{3,19},{4,20},{5,21},{6,22},{7,23},{8,24},{9,... | collective-permute-start | bytes 331784 | tf_op jit(solution)/shard_map/ppermute | solution.py:25
  55.6 5.5 %collective-permute-start.12 = (f32[216,128]{1,0:T(8,128)S(1)}, f32[216,128]{1,0:T(8,128)S(1)}, u32[]{:S(2)}, u32[]{:S(2)}) collective-permute-start(f32[216,128]{1,0:T(8,128)S(1)} %get-tuple-element.55), channel_id=1, source_target_pairs={{0,32},{1,33},{2,34},{3,35},{4,36},{5,37},{6,38},{7,39},{8,40},{9,... | collective-permute-start | bytes 331784 | tf_op jit(solution)/shard_map/ppermute | solution.py:25
  56.2 8.2 %collective-permute-start.13 = (f32[216,128]{1,0:T(8,128)S(1)}, f32[216,128]{1,0:T(8,128)S(1)}, u32[]{:S(2)}, u32[]{:S(2)}) collective-permute-start(f32[216,128]{1,0:T(8,128)S(1)} %get-tuple-element.56), channel_id=1, source_target_pairs={{0,48},{1,49},{2,50},{3,51},{4,52},{5,53},{6,54},{7,55},{8,56},{9,... | collective-permute-start | bytes 331784 | tf_op jit(solution)/shard_map/ppermute | solution.py:25
  64.5 4.2 %collective-permute-start.16 = (f32[216,128]{1,0:T(8,128)S(1)}, f32[216,128]{1,0:T(8,128)S(1)}, u32[]{:S(2)}, u32[]{:S(2)}) collective-permute-start(f32[216,128]{1,0:T(8,128)S(1)} %add_add_fusion.2), channel_id=1, source_target_pairs={{0,6},{1,7},{2,4},{3,5},{4,2},{5,3},{6,0},{7,1},{8,14},{9,15},{10,... | collective-permute-start | bytes 331784 | tf_op jit(solution)/shard_map/ppermute | solution.py:25
  65.8 5.1 %collective-permute-start.15 = (f32[216,128]{1,0:T(8,128)S(1)}, f32[216,128]{1,0:T(8,128)S(1)}, u32[]{:S(2)}, u32[]{:S(2)}) collective-permute-start(f32[216,128]{1,0:T(8,128)S(1)} %add_add_fusion.2), channel_id=1, source_target_pairs={{0,4},{1,5},{2,6},{3,7},{4,0},{5,1},{6,2},{7,3},{8,12},{9,13},{10,... | collective-permute-start | bytes 331784 | tf_op jit(solution)/shard_map/ppermute | solution.py:25
  66.5 6.2 %collective-permute-start.14 = (f32[216,128]{1,0:T(8,128)S(1)}, f32[216,128]{1,0:T(8,128)S(1)}, u32[]{:S(2)}, u32[]{:S(2)}) collective-permute-start(f32[216,128]{1,0:T(8,128)S(1)} %add_add_fusion.2), channel_id=1, source_target_pairs={{0,2},{1,3},{2,0},{3,1},{4,6},{5,7},{6,4},{7,5},{8,10},{9,11},{10,... | collective-permute-start | bytes 331784 | tf_op jit(solution)/shard_map/ppermute | solution.py:25
  72.7 11.1 %collective-permute-start.19 = (f32[216,128]{1,0:T(8,128)S(1)}, f32[216,128]{1,0:T(8,128)S(1)}, u32[]{:S(2)}, u32[]{:S(2)}) collective-permute-start(f32[216,128]{1,0:T(8,128)S(1)} %add_add_fusion.1), channel_id=1, source_target_pairs={{0,65},{1,64},{2,67},{3,66},{4,69},{5,68},{6,71},{7,70},{8,73},{9,... | collective-permute-start | bytes 331784 | tf_op jit(solution)/shard_map/ppermute | solution.py:25
  77.0 6.9 %collective-permute-start.18 = (f32[216,128]{1,0:T(8,128)S(1)}, f32[216,128]{1,0:T(8,128)S(1)}, u32[]{:S(2)}, u32[]{:S(2)}) collective-permute-start(f32[216,128]{1,0:T(8,128)S(1)} %add_add_fusion.1), channel_id=1, source_target_pairs={{0,64},{1,65},{2,66},{3,67},{4,68},{5,69},{6,70},{7,71},{8,72},{9,... | collective-permute-start | bytes 331784 | tf_op jit(solution)/shard_map/ppermute | solution.py:25
  77.0 6.9 %collective-permute-start.17 = (f32[216,128]{1,0:T(8,128)S(1)}, f32[216,128]{1,0:T(8,128)S(1)}, u32[]{:S(2)}, u32[]{:S(2)}) collective-permute-start(f32[216,128]{1,0:T(8,128)S(1)} %add_add_fusion.1), channel_id=1, source_target_pairs={{0,1},{1,0},{2,3},{3,2},{4,5},{5,4},{6,7},{7,6},{8,9},{9,8},{10,11... | collective-permute-start | bytes 331784 | tf_op jit(solution)/shard_map/ppermute | solution.py:25
  78.2 9.0 %collective-permute-start.6 = (bf16[1,8,64,128]{3,2,1,0:T(8,128)(2,1)S(1)}, bf16[1,8,64,128]{3,2,1,0:T(8,128)(2,1)S(1)}, u32[]{:S(2)}, u32[]{:S(2)}) collective-permute-start(bf16[1,8,64,128]{3,2,1,0:T(8,128)(2,1)S(1)} %get-tuple-element.42), channel_id=1, source_target_pairs={{0,8},{8,0},{16,24},{24,16},{32,40},{40,32},{48,56},{56,48},{64,72... | collective-permute-start | bytes 393224 | tf_op jit(solution)/shard_map/ppermute | solution.py:30
  80.4 10.5 %collective-permute-start.7 = (bf16[1,8,64,128]{3,2,1,0:T(8,128)(2,1)S(1)}, bf16[1,8,64,128]{3,2,1,0:T(8,128)(2,1)S(1)}, u32[]{:S(2)}, u32[]{:S(2)}) collective-permute-start(bf16[1,8,64,128]{3,2,1,0:T(8,128)(2,1)S(1)} %get-tuple-element.43), channel_id=1, source_target_pairs={{8,16},{16,8},{24,32},{32,24},{40,48},{48,40},{56,64},{64,56},{72,... | collective-permute-start | bytes 393224 | tf_op jit(solution)/shard_map/ppermute | solution.py:30
  83.9 11.9 %collective-permute-start.22 = (f32[216,128]{1,0:T(8,128)S(1)}, f32[216,128]{1,0:T(8,128)S(1)}, u32[]{:S(2)}, u32[]{:S(2)}) collective-permute-start(f32[216,128]{1,0:T(8,128)S(1)} %add_add_fusion.refs_3_), channel_id=1, source_target_pairs={{0,48},{1,49},{2,50},{3,51},{4,52},{5,53},{6,54},{7,55},{8,56},{9,... | collective-permute-start | bytes 331784 | tf_op jit(solution)/shard_map/ppermute | solution.py:25
  85.1 10.7 %collective-permute-start.21 = (f32[216,128]{1,0:T(8,128)S(1)}, f32[216,128]{1,0:T(8,128)S(1)}, u32[]{:S(2)}, u32[]{:S(2)}) collective-permute-start(f32[216,128]{1,0:T(8,128)S(1)} %add_add_fusion.refs_3_), channel_id=1, source_target_pairs={{0,32},{1,33},{2,34},{3,35},{4,36},{5,37},{6,38},{7,39},{8,40},{9,... | collective-permute-start | bytes 331784 | tf_op jit(solution)/shard_map/ppermute | solution.py:25
  85.6 10.2 %collective-permute-start.20 = (f32[216,128]{1,0:T(8,128)S(1)}, f32[216,128]{1,0:T(8,128)S(1)}, u32[]{:S(2)}, u32[]{:S(2)}) collective-permute-start(f32[216,128]{1,0:T(8,128)S(1)} %add_add_fusion.refs_3_), channel_id=1, source_target_pairs={{0,16},{1,17},{2,18},{3,19},{4,20},{5,21},{6,22},{7,23},{8,24},{9,... | collective-permute-start | bytes 331784 | tf_op jit(solution)/shard_map/ppermute | solution.py:25
  90.9 6.4 %collective-permute-start.8 = (bf16[10,64,128]{2,1,0:T(8,128)(2,1)S(1)}, bf16[10,64,128]{2,1,0:T(8,128)(2,1)S(1)}, u32[]{:S(2)}, u32[]{:S(2)}) collective-permute-start(bf16[10,64,128]{2,1,0:T(8,128)(2,1)S(1)} %get-tuple-element.44), channel_id=1, source_target_pairs={{0,1},{1,0},{2,3},{3,2},{4,5},{5,4},{6,7},{7,6},{8,9},{9,8},{10,11... | collective-permute-start | bytes 491528 | tf_op jit(solution)/shard_map/ppermute | solution.py:364
  92.9 8.8 %collective-permute-start.9 = (bf16[10,64,128]{2,1,0:T(8,128)(2,1)S(1)}, bf16[10,64,128]{2,1,0:T(8,128)(2,1)S(1)}, u32[]{:S(2)}, u32[]{:S(2)}) collective-permute-start(bf16[10,64,128]{2,1,0:T(8,128)(2,1)S(1)} %get-tuple-element.45), channel_id=1, source_target_pairs={{1,2},{2,1},{3,4},{4,3},{5,6},{6,5},{9,10},{10,9},{11,12},{12,11},... | collective-permute-start | bytes 491528 | tf_op jit(solution)/shard_map/ppermute | solution.py:365
  95.8 14.8 %collective-permute-start.23 = (f32[864,128]{1,0:T(8,128)S(1)}, f32[864,128]{1,0:T(8,128)S(1)}, u32[]{:S(2)}, u32[]{:S(2)}) collective-permute-start(f32[864,128]{1,0:T(8,128)S(1)} %shard_map.86.refs_3_), channel_id=1, source_target_pairs={{0,8},{1,9},{2,10},{3,11},{4,12},{5,13},{6,14},{7,15},{8,0},{9,1},... | collective-permute-start | bytes 1327112 | tf_op jit(solution)/shard_map/ppermute | solution.py:25

commit v8 on v7

--- a/solution.py
+++ b/solution.py
@@ -40,6 +40,16 @@
     stack[at_x, ys, 0:chans, :] = below
     stack[at_x, ys, chans : 2 * chans, :] = row
     stack[at_x, ys, 2 * chans : 3 * chans, :] = above
+
+
+def store_shifted(stack, x, y, value):
+    chans, depth = value.shape
+    lane = lax.broadcasted_iota(jnp.int32, value.shape, 1)
+    below = jnp.where(lane == 0, 0.0, pltpu.roll(value, 1, 1))
+    above = jnp.where(lane == depth - 1, 0.0, pltpu.roll(value, depth - 1, 1))
+    stack[x, y, 0:chans] = below.astype(BF16)
+    stack[x, y, chans : 2 * chans] = value.astype(BF16)
+    stack[x, y, 2 * chans : 3 * chans] = above.astype(BF16)
 
 
 def sides(parity, size):
@@ -117,7 +127,7 @@
 
     def emit(x, y, value):
         sig = jax.nn.sigmoid(value)
-        activ[x, y] = (mask[...] * (value * sig)).astype(BF16)
+        store_shifted(activ, x, y, mask[...] * (value * sig))
         slope[x, y] = mask[...] * (sig * (1.0 + value * (1.0 - sig)))
 
     conv_padded(padded, weights, 0, tile.shape[1], emit)
@@ -144,13 +154,13 @@
     conv_padded(padded, weights, first, result.shape[1], emit)
 
 
-def branch_low_kernel(place, mask, weights, base, tile, xr_even, xr_odd, yr_even, yr_odd, result, padded):
+def branch_first_kernel(place, mask, weights, base, tile, xr_even, xr_odd, yr_even, yr_odd, result, padded):
     pad_tile(padded, place, tile, xr_even, xr_odd, yr_even, yr_odd, 0)
     branch_part(mask, weights, base, padded, result, 0)
 
 
-def branch_high_kernel(mask, weights, base, padded, result):
-    branch_part(mask, weights, base, padded, result, base.shape[1] // 2)
+def branch_next_kernel(mask, weights, base, padded, result, *, first):
+    branch_part(mask, weights, base, padded, result, first)
 
 
 def grad_accumulate(padded, stack, acc):
@@ -188,10 +198,9 @@
     lax.fori_loop(0, source.shape[0], body, 0)
 
 
-def grad_two_kernel(grad_pad, activ, packed, stack, acc):
-    stack_tile(stack, activ)
-    grad_accumulate(grad_pad, stack, acc)
-    pack_grad(packed, acc, activ.shape[2])
+def grad_two_kernel(grad_pad, activ, packed, acc):
+    grad_accumulate(grad_pad, activ, acc)
+    pack_grad(packed, acc, grad_pad.shape[2])
 
 
 def grad_one_kernel(place, in_pad, pre_grad, packed_two, keep, send, stack, acc):
@@ -347,10 +356,11 @@
     grad_y = swap(*sends[2:], "gy")
 
     tile_s = pltpu.VMEM((tile_x, tile_y, 3 * chans, tile_z), BF16)
+    shifted_b = jax.ShapeDtypeStruct((tile_x, tile_y, 3 * chans, tile_z), BF16)
     grad_s = pltpu.VMEM((9 * chans, 3 * chans), F32)
 
     activ, slope, in_pad = call(
-        forward_kernel, [tile_b, jax.ShapeDtypeStruct(tile_shape, F32), pad_b], scalars=3, flops=flops
+        forward_kernel, [shifted_b, jax.ShapeDtypeStruct(tile_shape, F32), pad_b], scalars=3, flops=flops
     )(*place, mask_f, w_pre, masked_in, *xr, *in_y)
     pre_grad, xs_even, xs_odd, grad_pad = call(
         backward_kernel, [tile_b, edge_b, edge_b, pad_b], scalars=3, flops=flops
@@ -359,7 +369,7 @@
     packed = 27 * chans * chans // (2 * chans)
     half = jax.ShapeDtypeStruct((packed, 2 * chans), F32)
     pre_xr = swap(xs_even, xs_odd, "gx")
-    (packed_two,) = call(grad_two_kernel, [half], [tile_s, grad_s], flops=flops)(grad_pad, activ)
+    (packed_two,) = call(grad_two_kernel, [half], [grad_s], flops=flops)(grad_pad, activ)
     pre_sends = y_sends((pre_grad,), pre_xr)
     pre_even = lax.ppermute(pre_sends[0], "gy", even)
     pre_odd = lax.ppermute(pre_sends[1], "gy", odd)
@@ -390,12 +400,19 @@
         inside=False,
     )(*place, mine, other)
 
-    half_b = jax.ShapeDtypeStruct((tile_x, tile_y // 2, chans, tile_z), BF16)
-    low, pre_pad = call(
-        branch_low_kernel, [half_b, pad_b], scalars=3, flops=flops // 2
+    cuts = (0, tile_y // 4, tile_y // 2, tile_y)
+
+    def rows_b(k):
+        return [jax.ShapeDtypeStruct((tile_x, cuts[k + 1] - cuts[k], chans, tile_z), BF16)]
+
+    piece, pre_pad = call(
+        branch_first_kernel, rows_b(0) + [pad_b], scalars=3, flops=flops // 4
     )(*place, mask_f, w_branch, masked_grad, pre_grad, *pre_xr, *pre_yr)
-    (high,) = call(branch_high_kernel, [half_b], flops=flops // 2)(mask_f, w_branch, masked_grad, pre_pad)
-    grad_features = jnp.transpose(jnp.concatenate([low, high], axis=1), (2, 0, 1, 3))
+    pieces = [piece]
+    for k in (1, 2):
+        kernel = functools.partial(branch_next_kernel, first=cuts[k])
+        pieces += call(kernel, rows_b(k), flops=flops // 4 * k)(mask_f, w_branch, masked_grad, pre_pad)
+    grad_features = jnp.transpose(jnp.concatenate(pieces, axis=1), (2, 0, 1, 3))
     return grad_features, grad_one, grad_two
 
 

time: 112 us -> 114 us (1.018)
  Pallas kernels: 30.4 us -> 31.9 us
    pallas_call x13 -> x14, Pallas kernels: 30.4 us -> 31.9 us  [run(): pl.pallas_call(wrapped, out_shape=tuple(outs), in_specs=specs, out_specs=...]
  transfers between devices with their start and end apart: 24 -> 24, of which waited for: 12 -> 12; matrix products, arithmetic and copies ran while one was open for 5% -> 5% of each run, Pallas kernels for 12% -> 14%
where the time goes in v8:
time: 114 us; the launch traced here: 113 us
  starting transfers between devices  41.5 us (36%)
  Pallas kernels  31.9 us (28%)
  waiting for transfers between devices  29.5 us (26%)
  other arithmetic  5.75 us (5%)
  local copies, waits for them, and re-layouts  3.8 us (3%)
    pallas_call x14, Pallas kernels, run(): pl.pallas_call(wrapped, out_shape=tuple(outs), in_specs=specs, out_specs=...  31.9 us
    ppermute x14, starting transfers between devices, xor_permute(): return lax.ppermute(value, AXES, [(i, i ^ mask) for i in range(total)])  16.3 us
    ppermute x14, waiting for transfers between devices, xor_permute(): return lax.ppermute(value, AXES, [(i, i ^ mask) for i in range(total)])  11.8 us
    ppermute x3, starting transfers between devices, swap(): lax.ppermute(value_odd, axis, odd)  9.05 us
    ppermute x3, waiting for transfers between devices, swap(): lax.ppermute(value_odd, axis, odd)  6.7 us
    ppermute x1, starting transfers between devices, body(): in_odd = lax.ppermute(in_next, 'gy', odd)  5.38 us
    ppermute x3, starting transfers between devices, swap(): lax.ppermute(value_even, axis, even)  5.35 us
    ppermute x1, waiting for transfers between devices, body(): in_even = lax.ppermute(sends[0], 'gy', even)  5.2 us
  transfers between devices with their start and end apart: 24, of which 12 were waited for; matrix products, arithmetic and copies ran while one was open for 5% of the time, Pallas kernels for 14%

profile of v8, /device:TPU:15, one launch (start us, length us, event | category | flops | bytes accessed | tf_op | source)
XLA Modules:
  0.0 113.4 jit_solution(8827243379607436929)
XLA Ops:
  0.7 0.8 convert_bitcast_fusion
  1.4 0.1 broadcast_in_dim.8
  1.5 0.1 convert_element_type.32
  1.6 1.2 %constant_dynamic-slice_fusion = (bf16[64,1,8,128]{3,2,1,0:T(8,128)(2,1)S(1)}, bf16[64,1,8,128]{3,2,1,0:T(8,128)(2,1)S(1)}, bf16[64,1,8,128]{3,2,1,0:T(8,128)(2,1)S(1)}, bf16[64,1,8,128]{3,2,1,0:T(8,128)(2,1)S(1)}) fusion(bf16[64,8,8,128]{3,2,1,0:T(8,128)(2,1)} %param.6, s32[]{:T(128)S(6)} %select_n.10, s32[]{:T(128)S(6)} %select_n.9, ...), kind=kLoop, calls=%fused_computation.18 | loop fusion | bytes 1048584 | tf_op jit(solution)/shard_map/jit(dynamic_index_in_dim)/dynamic_slice | solution.py:330
  2.7 0.1 fusion.3
  2.8 0.7 pad_maximum_fusion
  3.6 0.7 collective-permute-start
  4.2 0.7 pad_maximum_fusion.1
  5.0 3.3 %collective-permute-start.1 = (bf16[2,8,64,128]{3,2,1,0:T(8,128)(2,1)}, bf16[2,8,64,128]{3,2,1,0:T(8,128)(2,1)S(1)}, u32[]{:S(2)}, u32[]{:S(2)}) collective-permute-start(bf16[2,8,64,128]{3,2,1,0:T(8,128)(2,1)} %pad_maximum_fusion.1), channel_id=1, source_target_pairs={{8,16},{16,8},{24,32},{32,24},{40,48},{48,40},{56,64},{64,56},{72,... | collective-permute-start | bytes 786440 | tf_op jit(solution)/shard_map/ppermute | solution.py:30
  8.3 0.3 shard_map.76
  8.6 3.3 %fusion = (bf16[8,8,64,128]{3,2,1,0:T(8,128)(2,1)S(1)}, bf16[8,8,64,128]{3,2,1,0:T(8,128)(2,1)S(1)}) fusion(bf16[64,8,8,128]{3,2,1,0:T(8,128)(2,1)} %param.5, bf16[128]{0:T(256)(128)(2,1)S(1)} %convert_element_type.32, bf16[64,8,8,128]{3,2,1,0:T(8,128)(2,1)} %param.6), kind=kLoop, calls=%fused_computation.2 | loop fusion | flops 1048576 | bytes 4194560 | tf_op jit(solution)/shard_map/transpose | solution.py:334
  11.9 3.0 %collective-permute-done.1.refs_6_.refs_7_ = bf16[2,8,64,128]{3,2,1,0:T(8,128)(2,1)S(1)} collective-permute-done((bf16[2,8,64,128]{3,2,1,0:T(8,128)(2,1)}, bf16[2,8,64,128]{3,2,1,0:T(8,128)(2,1)S(1)}, u32[]{:S(2)}, u32[]{:S(2)}) %collective-permute-start.1) | collective-permute-done | bytes 262176 | tf_op jit(solution)/shard_map/ppermute | solution.py:30
  15.0 0.8 shard_map.77
  15.7 0.7 copy-done.2
  16.4 5.4 %collective-permute-start.3 = (bf16[10,64,128]{2,1,0:T(8,128)(2,1)}, bf16[10,64,128]{2,1,0:T(8,128)(2,1)}, u32[]{:S(2)}, u32[]{:S(2)}) collective-permute-start(bf16[10,64,128]{2,1,0:T(8,128)(2,1)} %get-tuple-element.37), channel_id=1, source_target_pairs={{1,2},{2,1},{3,4},{4,3},{5,6},{6,5},{9,10},{10,9},{11,12},{12,11},... | collective-permute-start | bytes 491528 | tf_op jit(solution)/shard_map/ppermute | solution.py:354
  21.8 0.6 collective-permute-start.2
  22.4 0.1 broadcast_in_dim.7
  22.4 0.1 convert_element_type.29.refs_3_.refs_0_
  22.5 2.5 %collective-permute-start.4 = (bf16[10,64,128]{2,1,0:T(8,128)(2,1)}, bf16[10,64,128]{2,1,0:T(8,128)(2,1)S(1)}, u32[]{:S(2)}, u32[]{:S(2)}) collective-permute-start(bf16[10,64,128]{2,1,0:T(8,128)(2,1)} %copy-done.2), channel_id=1, source_target_pairs={{0,1},{1,0},{2,3},{3,2},{4,5},{5,4},{6,7},{7,6},{8,9},{9,8},{10,11... | collective-permute-start | bytes 491528 | tf_op jit(solution)/shard_map/ppermute | solution.py:30
  25.1 2.3 %collective-permute-start.5 = (bf16[10,64,128]{2,1,0:T(8,128)(2,1)S(1)}, bf16[10,64,128]{2,1,0:T(8,128)(2,1)S(1)}, u32[]{:S(2)}, u32[]{:S(2)}) collective-permute-start(bf16[10,64,128]{2,1,0:T(8,128)(2,1)S(1)} %get-tuple-element.40), channel_id=1, source_target_pairs={{1,2},{2,1},{3,4},{4,3},{5,6},{6,5},{9,10},{10,9},{11,12},{12,11},... | collective-permute-start | bytes 491528 | tf_op jit(solution)/shard_map/ppermute | solution.py:30
  27.4 5.2 %collective-permute-done.2.refs_8_ = bf16[10,64,128]{2,1,0:T(8,128)(2,1)} collective-permute-done((bf16[10,64,128]{2,1,0:T(8,128)(2,1)}, bf16[10,64,128]{2,1,0:T(8,128)(2,1)}, u32[]{:S(2)}, u32[]{:S(2)}) %collective-permute-start.2) | collective-permute-done | bytes 163872 | tf_op jit(solution)/shard_map/ppermute | solution.py:351
  32.6 6.6 %shard_map.78 = (bf16[8,8,192,128]{3,2,1,0:T(8,128)(2,1)S(1)}, f32[8,8,64,128]{3,2,1,0:T(8,128)S(1)}, bf16[10,10,64,128]{3,2,1,0:T(8,128)(2,1)S(1)}) custom-call(s32[1]{0:T(128)} %bitcast.refs_0_, s32[1]{0:T(128)} %bitcast.1.refs_1_, s32[1]{0:T(128)} %bitcast.2.refs_2_, f32[1,128]{1,0:T(1,128)S(1)} %convert_element_type.29.refs_3_.refs_0_, ...), custom_call_target="tpu_custom_call" | custom-call | flops 1811939328 | bytes 9003532 | tf_op jit(solution)/shard_map/pallas_call | solution.py:303
  39.2 0.0 collective-permute-done.4.refs_8_
  39.2 0.0 collective-permute-done.5.refs_9_
  39.2 4.7 %shard_map.79 = (bf16[8,8,64,128]{3,2,1,0:T(8,128)(2,1)S(1)}, bf16[1,8,64,128]{3,2,1,0:T(8,128)(2,1)S(1)}, bf16[1,8,64,128]{3,2,1,0:T(8,128)(2,1)S(1)}, bf16[10,10,64,128]{3,2,1,0:T(8,128)(2,1)S(1)}) custom-call(s32[1]{0:T(128)} %bitcast.refs_0_, s32[1]{0:T(128)} %bitcast.1.refs_1_, s32[1]{0:T(128)} %bitcast.2.refs_2_, ...), custom_call_target="tpu_custom_call" | custom-call | flops 1811939328 | bytes 7168012 | tf_op jit(solution)/shard_map/pallas_call | solution.py:303
  43.9 4.0 %shard_map.84.refs_5_ = f32[864,128]{1,0:T(8,128)S(1)} custom-call(bf16[10,10,64,128]{3,2,1,0:T(8,128)(2,1)S(1)} %get-tuple-element.49.refs_0_, bf16[8,8,192,128]{3,2,1,0:T(8,128)(2,1)S(1)} %get-tuple-element.50.refs_1_), custom_call_target="tpu_custom_call" | custom-call | flops 1811939328 | bytes 5226496 | tf_op jit(solution)/shard_map/pallas_call | solution.py:303
  48.0 5.1 %shard_map.85 = (f32[864,128]{1,0:T(8,128)S(1)}, f32[864,128]{1,0:T(8,128)S(1)}) custom-call(s32[1]{0:T(128)} %bitcast.refs_0_, s32[1]{0:T(128)} %bitcast.1.refs_1_, s32[1]{0:T(128)} %bitcast.2.refs_2_, bf16[10,10,64,128]{3,2,1,0:T(8,128)(2,1)S(1)} %get-tuple-element.48.refs_3_, bf16[8,8,64,128]{3,2,1,0:T(8,128)(2,1)S(1)} %get-tuple-element.41.refs_3_.refs_6_.refs_4_, ...), custom_call_target="tpu_custom_call" | custom-call | flops 1811939328 | bytes 4014092 | tf_op jit(solution)/shard_map/pallas_call | solution.py:303
  53.1 0.1 collective-permute-start.10
  53.2 1.8 %collective-permute-done.10.refs_4_ = f32[864,128]{1,0:T(8,128)S(1)} collective-permute-done((f32[864,128]{1,0:T(8,128)S(1)}, f32[864,128]{1,0:T(8,128)S(1)}, u32[]{:S(2)}, u32[]{:S(2)}) %collective-permute-start.10) | collective-permute-done | bytes 442400 | tf_op jit(solution)/shard_map/ppermute | solution.py:25
  55.1 0.2 collective-permute-start.11
  55.2 0.7 collective-permute-start.12
  55.9 3.1 %collective-permute-start.13 = (f32[216,128]{1,0:T(8,128)S(1)}, f32[216,128]{1,0:T(8,128)S(1)}, u32[]{:S(2)}, u32[]{:S(2)}) collective-permute-start(f32[216,128]{1,0:T(8,128)S(1)} %get-tuple-element.56), channel_id=1, source_target_pairs={{0,48},{1,49},{2,50},{3,51},{4,52},{5,53},{6,54},{7,55},{8,56},{9,... | collective-permute-start | bytes 331784 | tf_op jit(solution)/shard_map/ppermute | solution.py:25
  59.0 0.6 collective-permute-done.11
  59.6 1.1 collective-permute-done.12
  60.7 3.4 %collective-permute-done.13 = f32[216,128]{1,0:T(8,128)S(1)} collective-permute-done((f32[216,128]{1,0:T(8,128)S(1)}, f32[216,128]{1,0:T(8,128)S(1)}, u32[]{:S(2)}, u32[]{:S(2)}) %collective-permute-start.13) | collective-permute-done | bytes 110624 | tf_op jit(solution)/shard_map/ppermute | solution.py:25
  64.2 1.4 %collective-permute-start.16 = (f32[216,128]{1,0:T(8,128)S(1)}, f32[216,128]{1,0:T(8,128)S(1)}, u32[]{:S(2)}, u32[]{:S(2)}) collective-permute-start(f32[216,128]{1,0:T(8,128)S(1)} %add_add_fusion.2), channel_id=1, source_target_pairs={{0,6},{1,7},{2,4},{3,5},{4,2},{5,3},{6,0},{7,1},{8,14},{9,15},{10,... | collective-permute-start | bytes 331784 | tf_op jit(solution)/shard_map/ppermute | solution.py:25
  65.5 0.7 collective-permute-start.15
  66.2 1.3 %collective-permute-start.14 = (f32[216,128]{1,0:T(8,128)S(1)}, f32[216,128]{1,0:T(8,128)S(1)}, u32[]{:S(2)}, u32[]{:S(2)}) collective-permute-start(f32[216,128]{1,0:T(8,128)S(1)} %add_add_fusion.2), channel_id=1, source_target_pairs={{0,2},{1,3},{2,0},{3,1},{4,6},{5,7},{6,4},{7,5},{8,10},{9,11},{10,... | collective-permute-start | bytes 331784 | tf_op jit(solution)/shard_map/ppermute | solution.py:25
  67.5 0.9 collective-permute-done.16
  68.4 2.2 %collective-permute-done.15 = f32[216,128]{1,0:T(8,128)S(1)} collective-permute-done((f32[216,128]{1,0:T(8,128)S(1)}, f32[216,128]{1,0:T(8,128)S(1)}, u32[]{:S(2)}, u32[]{:S(2)}) %collective-permute-start.15) | collective-permute-done | bytes 110624 | tf_op jit(solution)/shard_map/ppermute | solution.py:25
  70.6 1.7 %collective-permute-done.14 = f32[216,128]{1,0:T(8,128)S(1)} collective-permute-done((f32[216,128]{1,0:T(8,128)S(1)}, f32[216,128]{1,0:T(8,128)S(1)}, u32[]{:S(2)}, u32[]{:S(2)}) %collective-permute-start.14) | collective-permute-done | bytes 110624 | tf_op jit(solution)/shard_map/ppermute | solution.py:25
  72.4 4.3 %collective-permute-start.19 = (f32[216,128]{1,0:T(8,128)S(1)}, f32[216,128]{1,0:T(8,128)S(1)}, u32[]{:S(2)}, u32[]{:S(2)}) collective-permute-start(f32[216,128]{1,0:T(8,128)S(1)} %add_add_fusion.1), channel_id=1, source_target_pairs={{0,65},{1,64},{2,67},{3,66},{4,69},{5,68},{6,71},{7,70},{8,73},{9,... | collective-permute-start | bytes 331784 | tf_op jit(solution)/shard_map/ppermute | solution.py:25
  76.7 1.3 %collective-permute-start.17 = (f32[216,128]{1,0:T(8,128)S(1)}, f32[216,128]{1,0:T(8,128)S(1)}, u32[]{:S(2)}, u32[]{:S(2)}) collective-permute-start(f32[216,128]{1,0:T(8,128)S(1)} %add_add_fusion.1), channel_id=1, source_target_pairs={{0,1},{1,0},{2,3},{3,2},{4,5},{5,4},{6,7},{7,6},{8,9},{9,8},{10,11... | collective-permute-start | bytes 331784 | tf_op jit(solution)/shard_map/ppermute | solution.py:25
  77.9 2.1 %collective-permute-start.6 = (bf16[1,8,64,128]{3,2,1,0:T(8,128)(2,1)S(1)}, bf16[1,8,64,128]{3,2,1,0:T(8,128)(2,1)S(1)}, u32[]{:S(2)}, u32[]{:S(2)}) collective-permute-start(bf16[1,8,64,128]{3,2,1,0:T(8,128)(2,1)S(1)} %get-tuple-element.42), channel_id=1, source_target_pairs={{0,8},{8,0},{16,24},{24,16},{32,40},{40,32},{48,56},{56,48},{64,72... | collective-permute-start | bytes 393224 | tf_op jit(solution)/shard_map/ppermute | solution.py:30
  80.1 3.4 %collective-permute-start.7 = (bf16[1,8,64,128]{3,2,1,0:T(8,128)(2,1)S(1)}, bf16[1,8,64,128]{3,2,1,0:T(8,128)(2,1)S(1)}, u32[]{:S(2)}, u32[]{:S(2)}) collective-permute-start(bf16[1,8,64,128]{3,2,1,0:T(8,128)(2,1)S(1)} %get-tuple-element.43), channel_id=1, source_target_pairs={{8,16},{16,8},{24,32},{32,24},{40,48},{48,40},{56,64},{64,56},{72,... | collective-permute-start | bytes 393224 | tf_op jit(solution)/shard_map/ppermute | solution.py:30
  83.5 0.0 collective-permute-done.19
  83.5 0.0 collective-permute-done.17
  83.6 1.2 %collective-permute-start.22 = (f32[216,128]{1,0:T(8,128)S(1)}, f32[216,128]{1,0:T(8,128)S(1)}, u32[]{:S(2)}, u32[]{:S(2)}) collective-permute-start(f32[216,128]{1,0:T(8,128)S(1)} %add_add_fusion.refs_3_), channel_id=1, source_target_pairs={{0,48},{1,49},{2,50},{3,51},{4,52},{5,53},{6,54},{7,55},{8,56},{9,... | collective-permute-start | bytes 331784 | tf_op jit(solution)/shard_map/ppermute | solution.py:25
  84.7 0.5 collective-permute-start.21
  85.2 1.7 %collective-permute-start.20 = (f32[216,128]{1,0:T(8,128)S(1)}, f32[216,128]{1,0:T(8,128)S(1)}, u32[]{:S(2)}, u32[]{:S(2)}) collective-permute-start(f32[216,128]{1,0:T(8,128)S(1)} %add_add_fusion.refs_3_), channel_id=1, source_target_pairs={{0,16},{1,17},{2,18},{3,19},{4,20},{5,21},{6,22},{7,23},{8,24},{9,... | collective-permute-start | bytes 331784 | tf_op jit(solution)/shard_map/ppermute | solution.py:25
  86.9 0.0 collective-permute-done.6.refs_4_.refs_7_
  86.9 3.6 %collective-permute-done.7.refs_5_.refs_8_ = bf16[1,8,64,128]{3,2,1,0:T(8,128)(2,1)S(1)} collective-permute-done((bf16[1,8,64,128]{3,2,1,0:T(8,128)(2,1)S(1)}, bf16[1,8,64,128]{3,2,1,0:T(8,128)(2,1)S(1)}, u32[]{:S(2)}, u32[]{:S(2)}) %collective-permute-start.7) | collective-permute-done | bytes 131104 | tf_op jit(solution)/shard_map/ppermute | solution.py:30
  90.6 2.0 %collective-permute-start.8 = (bf16[10,64,128]{2,1,0:T(8,128)(2,1)S(1)}, bf16[10,64,128]{2,1,0:T(8,128)(2,1)S(1)}, u32[]{:S(2)}, u32[]{:S(2)}) collective-permute-start(bf16[10,64,128]{2,1,0:T(8,128)(2,1)S(1)} %get-tuple-element.44), channel_id=1, source_target_pairs={{0,1},{1,0},{2,3},{3,2},{4,5},{5,4},{6,7},{7,6},{8,9},{9,8},{10,11... | collective-permute-start | bytes 491528 | tf_op jit(solution)/shard_map/ppermute | solution.py:374
  92.6 2.8 %collective-permute-start.9 = (bf16[10,64,128]{2,1,0:T(8,128)(2,1)S(1)}, bf16[10,64,128]{2,1,0:T(8,128)(2,1)S(1)}, u32[]{:S(2)}, u32[]{:S(2)}) collective-permute-start(bf16[10,64,128]{2,1,0:T(8,128)(2,1)S(1)} %get-tuple-element.45), channel_id=1, source_target_pairs={{1,2},{2,1},{3,4},{4,3},{5,6},{6,5},{9,10},{10,9},{11,12},{12,11},... | collective-permute-start | bytes 491528 | tf_op jit(solution)/shard_map/ppermute | solution.py:375
  95.5 0.1 collective-permute-start.23
  95.6 1.4 %collective-permute-done.8.refs_9_ = bf16[10,64,128]{2,1,0:T(8,128)(2,1)S(1)} collective-permute-done((bf16[10,64,128]{2,1,0:T(8,128)(2,1)S(1)}, bf16[10,64,128]{2,1,0:T(8,128)(2,1)S(1)}, u32[]{:S(2)}, u32[]{:S(2)}) %collective-permute-start.8) | collective-permute-done | bytes 163872 | tf_op jit(solution)/shard_map/ppermute | solution.py:374
  97.0 4.3 %collective-permute-done.9.refs_10_ = bf16[10,64,128]{2,1,0:T(8,128)(2,1)S(1)} collective-permute-done((bf16[10,64,128]{2,1,0:T(8,128)(2,1)S(1)}, bf16[10,64,128]{2,1,0:T(8,128)(2,1)S(1)}, u32[]{:S(2)}, u32[]{:S(2)}) %collective-permute-start.9) | collective-permute-done | bytes 163872 | tf_op jit(solution)/shard_map/ppermute | solution.py:375
  101.4 2.7 %shard_map.81 = (bf16[8,2,64,128]{3,2,1,0:T(8,128)(2,1)S(1)}, bf16[10,10,64,128]{3,2,1,0:T(8,128)(2,1)S(1)}) custom-call(s32[1]{0:T(128)} %bitcast.refs_0_, s32[1]{0:T(128)} %bitcast.1.refs_1_, s32[1]{0:T(128)} %bitcast.2.refs_2_, f32[1,128]{1,0:T(1,128)S(1)} %convert_element_type.29.refs_3_.refs_0_, bf16[192,576]{1,0:T(8,128)(2,1)S(1)} %get-tuple-element.31.refs_4_.refs_1_, ...), custom_call_target="tpu_custom_call" | custom-call | flops 452984832 | bytes 4809228 | tf_op jit(solution)/shard_map/pallas_call | solution.py:303
  104.1 2.6 %shard_map.82 = bf16[8,2,64,128]{3,2,1,0:T(8,128)(2,1)S(1)} custom-call(f32[1,128]{1,0:T(1,128)S(1)} %convert_element_type.29.refs_3_.refs_0_, bf16[192,576]{1,0:T(8,128)(2,1)S(1)} %get-tuple-element.31.refs_4_.refs_1_, bf16[8,8,64,128]{3,2,1,0:T(8,128)(2,1)S(1)} %get-tuple-element.74.refs_4_.refs_5_.refs_2_, ...), custom_call_target="tpu_custom_call" | custom-call | flops 452984832 | bytes 3170816 | tf_op jit(solution)/shard_map/pallas_call | solution.py:303
  106.6 3.3 %shard_map.83 = bf16[8,4,64,128]{3,2,1,0:T(8,128)(2,1)S(1)} custom-call(f32[1,128]{1,0:T(1,128)S(1)} %convert_element_type.29.refs_3_.refs_0_, bf16[192,576]{1,0:T(8,128)(2,1)S(1)} %get-tuple-element.31.refs_4_.refs_1_, bf16[8,8,64,128]{3,2,1,0:T(8,128)(2,1)S(1)} %get-tuple-element.74.refs_4_.refs_5_.refs_2_, ...), custom_call_target="tpu_custom_call" | custom-call | flops 905969664 | bytes 3432960 | tf_op jit(solution)/shard_map/pallas_call | solution.py:303
  110.0 0.1 maximum_bitcast_fusion
  110.1 1.6 %copy.21 = bf16[64,8,8,128]{3,2,1,0:T(8,128)(2,1)} copy(bf16[64,8,8,128]{3,0,2,1:T(8,128)(2,1)S(1)} %maximum_bitcast_fusion) | data formatting | bytes 2097152
  111.7 0.4 shard_map.88.refs_3_
  112.1 1.2 %shard_map.89 = (f32[3,3,3,64,64]{4,3,2,1,0:T(8,128)}, f32[3,3,3,64,64]{4,3,2,1,0:T(8,128)}) custom-call(s32[1]{0:T(128)} %bitcast.refs_0_, s32[1]{0:T(128)} %bitcast.1.refs_1_, s32[1]{0:T(128)} %bitcast.2.refs_2_, f32[3,3,3,64,64]{4,3,2,1,0:T(8,128)S(1)} %shard_map.88.refs_3_, f32[864,128]{1,0:T(8,128)S(1)} %collective-permute-done.23.refs_4_), custom_call_target="tpu_custom_call" | custom-call | bytes 1769484 | tf_op jit(solution)/shard_map/pallas_call | solution.py:303
  (19 shorter events, 0.2 us)
Async XLA Ops:
  0.6 7.7 %copy-start.1 = (bf16[3,3,3,64,64]{4,3,2,1,0:T(8,128)(2,1)S(1)}, bf16[3,3,3,64,64]{4,3,2,1,0:T(8,128)(2,1)}, u32[]{:S(2)}) copy-start(bf16[3,3,3,64,64]{4,3,2,1,0:T(8,128)(2,1)} %refs_1_.1) | copy-start | bytes 663556
  0.6 7.7 %copy-start = (bf16[3,3,3,64,64]{4,3,2,1,0:T(8,128)(2,1)S(1)}, bf16[3,3,3,64,64]{4,3,2,1,0:T(8,128)(2,1)}, u32[]{:S(2)}) copy-start(bf16[3,3,3,64,64]{4,3,2,1,0:T(8,128)(2,1)} %refs_0_.1) | copy-start | bytes 663556
  3.6 8.3 %collective-permute-start = (bf16[2,8,64,128]{3,2,1,0:T(8,128)(2,1)}, bf16[2,8,64,128]{3,2,1,0:T(8,128)(2,1)S(1)}, u32[]{:S(2)}, u32[]{:S(2)}) collective-permute-start(bf16[2,8,64,128]{3,2,1,0:T(8,128)(2,1)} %pad_maximum_fusion), channel_id=1, source_target_pairs={{0,8},{8,0},{16,24},{24,16},{32,40},{40,32},{48,56},{56,48},{64,72... | collective-permute-start | bytes 786440 | tf_op jit(solution)/shard_map/ppermute | solution.py:30
  5.0 10.0 %collective-permute-start.1 = (bf16[2,8,64,128]{3,2,1,0:T(8,128)(2,1)}, bf16[2,8,64,128]{3,2,1,0:T(8,128)(2,1)S(1)}, u32[]{:S(2)}, u32[]{:S(2)}) collective-permute-start(bf16[2,8,64,128]{3,2,1,0:T(8,128)(2,1)} %pad_maximum_fusion.1), channel_id=1, source_target_pairs={{8,16},{16,8},{24,32},{32,24},{40,48},{48,40},{56,64},{64,56},{72,... | collective-permute-start | bytes 786440 | tf_op jit(solution)/shard_map/ppermute | solution.py:30
  15.7 0.7 copy-start.2
  16.4 11.0 %collective-permute-start.3 = (bf16[10,64,128]{2,1,0:T(8,128)(2,1)}, bf16[10,64,128]{2,1,0:T(8,128)(2,1)}, u32[]{:S(2)}, u32[]{:S(2)}) collective-permute-start(bf16[10,64,128]{2,1,0:T(8,128)(2,1)} %get-tuple-element.37), channel_id=1, source_target_pairs={{1,2},{2,1},{3,4},{4,3},{5,6},{6,5},{9,10},{10,9},{11,12},{12,11},... | collective-permute-start | bytes 491528 | tf_op jit(solution)/shard_map/ppermute | solution.py:354
  21.8 10.8 %collective-permute-start.2 = (bf16[10,64,128]{2,1,0:T(8,128)(2,1)}, bf16[10,64,128]{2,1,0:T(8,128)(2,1)}, u32[]{:S(2)}, u32[]{:S(2)}) collective-permute-start(bf16[10,64,128]{2,1,0:T(8,128)(2,1)} %get-tuple-element.36), channel_id=1, source_target_pairs={{0,1},{1,0},{2,3},{3,2},{4,5},{5,4},{6,7},{7,6},{8,9},{9,8},{10,11... | collective-permute-start | bytes 491528 | tf_op jit(solution)/shard_map/ppermute | solution.py:351
  22.5 16.7 %collective-permute-start.4 = (bf16[10,64,128]{2,1,0:T(8,128)(2,1)}, bf16[10,64,128]{2,1,0:T(8,128)(2,1)S(1)}, u32[]{:S(2)}, u32[]{:S(2)}) collective-permute-start(bf16[10,64,128]{2,1,0:T(8,128)(2,1)} %copy-done.2), channel_id=1, source_target_pairs={{0,1},{1,0},{2,3},{3,2},{4,5},{5,4},{6,7},{7,6},{8,9},{9,8},{10,11... | collective-permute-start | bytes 491528 | tf_op jit(solution)/shard_map/ppermute | solution.py:30
  25.1 14.2 %collective-permute-start.5 = (bf16[10,64,128]{2,1,0:T(8,128)(2,1)S(1)}, bf16[10,64,128]{2,1,0:T(8,128)(2,1)S(1)}, u32[]{:S(2)}, u32[]{:S(2)}) collective-permute-start(bf16[10,64,128]{2,1,0:T(8,128)(2,1)S(1)} %get-tuple-element.40), channel_id=1, source_target_pairs={{1,2},{2,1},{3,4},{4,3},{5,6},{6,5},{9,10},{10,9},{11,12},{12,11},... | collective-permute-start | bytes 491528 | tf_op jit(solution)/shard_map/ppermute | solution.py:30
  53.1 1.9 %collective-permute-start.10 = (f32[864,128]{1,0:T(8,128)S(1)}, f32[864,128]{1,0:T(8,128)S(1)}, u32[]{:S(2)}, u32[]{:S(2)}) collective-permute-start(f32[864,128]{1,0:T(8,128)S(1)} %get-tuple-element.52), channel_id=1, source_target_pairs={{0,8},{1,9},{2,10},{3,11},{4,12},{5,13},{6,14},{7,15},{8,0},{9,1},... | collective-permute-start | bytes 1327112 | tf_op jit(solution)/shard_map/ppermute | solution.py:25
  55.1 4.6 %collective-permute-start.11 = (f32[216,128]{1,0:T(8,128)S(1)}, f32[216,128]{1,0:T(8,128)S(1)}, u32[]{:S(2)}, u32[]{:S(2)}) collective-permute-start(f32[216,128]{1,0:T(8,128)S(1)} %get-tuple-element.54), channel_id=1, source_target_pairs={{0,16},{1,17},{2,18},{3,19},{4,20},{5,21},{6,22},{7,23},{8,24},{9,... | collective-permute-start | bytes 331784 | tf_op jit(solution)/shard_map/ppermute | solution.py:25
  55.2 5.5 %collective-permute-start.12 = (f32[216,128]{1,0:T(8,128)S(1)}, f32[216,128]{1,0:T(8,128)S(1)}, u32[]{:S(2)}, u32[]{:S(2)}) collective-permute-start(f32[216,128]{1,0:T(8,128)S(1)} %get-tuple-element.55), channel_id=1, source_target_pairs={{0,32},{1,33},{2,34},{3,35},{4,36},{5,37},{6,38},{7,39},{8,40},{9,... | collective-permute-start | bytes 331784 | tf_op jit(solution)/shard_map/ppermute | solution.py:25
  55.9 8.2 %collective-permute-start.13 = (f32[216,128]{1,0:T(8,128)S(1)}, f32[216,128]{1,0:T(8,128)S(1)}, u32[]{:S(2)}, u32[]{:S(2)}) collective-permute-start(f32[216,128]{1,0:T(8,128)S(1)} %get-tuple-element.56), channel_id=1, source_target_pairs={{0,48},{1,49},{2,50},{3,51},{4,52},{5,53},{6,54},{7,55},{8,56},{9,... | collective-permute-start | bytes 331784 | tf_op jit(solution)/shard_map/ppermute | solution.py:25
  64.2 4.2 %collective-permute-start.16 = (f32[216,128]{1,0:T(8,128)S(1)}, f32[216,128]{1,0:T(8,128)S(1)}, u32[]{:S(2)}, u32[]{:S(2)}) collective-permute-start(f32[216,128]{1,0:T(8,128)S(1)} %add_add_fusion.2), channel_id=1, source_target_pairs={{0,6},{1,7},{2,4},{3,5},{4,2},{5,3},{6,0},{7,1},{8,14},{9,15},{10,... | collective-permute-start | bytes 331784 | tf_op jit(solution)/shard_map/ppermute | solution.py:25
  65.5 5.1 %collective-permute-start.15 = (f32[216,128]{1,0:T(8,128)S(1)}, f32[216,128]{1,0:T(8,128)S(1)}, u32[]{:S(2)}, u32[]{:S(2)}) collective-permute-start(f32[216,128]{1,0:T(8,128)S(1)} %add_add_fusion.2), channel_id=1, source_target_pairs={{0,4},{1,5},{2,6},{3,7},{4,0},{5,1},{6,2},{7,3},{8,12},{9,13},{10,... | collective-permute-start | bytes 331784 | tf_op jit(solution)/shard_map/ppermute | solution.py:25
  66.2 6.2 %collective-permute-start.14 = (f32[216,128]{1,0:T(8,128)S(1)}, f32[216,128]{1,0:T(8,128)S(1)}, u32[]{:S(2)}, u32[]{:S(2)}) collective-permute-start(f32[216,128]{1,0:T(8,128)S(1)} %add_add_fusion.2), channel_id=1, source_target_pairs={{0,2},{1,3},{2,0},{3,1},{4,6},{5,7},{6,4},{7,5},{8,10},{9,11},{10,... | collective-permute-start | bytes 331784 | tf_op jit(solution)/shard_map/ppermute | solution.py:25
  72.4 11.1 %collective-permute-start.19 = (f32[216,128]{1,0:T(8,128)S(1)}, f32[216,128]{1,0:T(8,128)S(1)}, u32[]{:S(2)}, u32[]{:S(2)}) collective-permute-start(f32[216,128]{1,0:T(8,128)S(1)} %add_add_fusion.1), channel_id=1, source_target_pairs={{0,65},{1,64},{2,67},{3,66},{4,69},{5,68},{6,71},{7,70},{8,73},{9,... | collective-permute-start | bytes 331784 | tf_op jit(solution)/shard_map/ppermute | solution.py:25
  76.6 6.9 %collective-permute-start.18 = (f32[216,128]{1,0:T(8,128)S(1)}, f32[216,128]{1,0:T(8,128)S(1)}, u32[]{:S(2)}, u32[]{:S(2)}) collective-permute-start(f32[216,128]{1,0:T(8,128)S(1)} %add_add_fusion.1), channel_id=1, source_target_pairs={{0,64},{1,65},{2,66},{3,67},{4,68},{5,69},{6,70},{7,71},{8,72},{9,... | collective-permute-start | bytes 331784 | tf_op jit(solution)/shard_map/ppermute | solution.py:25
  76.7 6.9 %collective-permute-start.17 = (f32[216,128]{1,0:T(8,128)S(1)}, f32[216,128]{1,0:T(8,128)S(1)}, u32[]{:S(2)}, u32[]{:S(2)}) collective-permute-start(f32[216,128]{1,0:T(8,128)S(1)} %add_add_fusion.1), channel_id=1, source_target_pairs={{0,1},{1,0},{2,3},{3,2},{4,5},{5,4},{6,7},{7,6},{8,9},{9,8},{10,11... | collective-permute-start | bytes 331784 | tf_op jit(solution)/shard_map/ppermute | solution.py:25
  77.9 9.0 %collective-permute-start.6 = (bf16[1,8,64,128]{3,2,1,0:T(8,128)(2,1)S(1)}, bf16[1,8,64,128]{3,2,1,0:T(8,128)(2,1)S(1)}, u32[]{:S(2)}, u32[]{:S(2)}) collective-permute-start(bf16[1,8,64,128]{3,2,1,0:T(8,128)(2,1)S(1)} %get-tuple-element.42), channel_id=1, source_target_pairs={{0,8},{8,0},{16,24},{24,16},{32,40},{40,32},{48,56},{56,48},{64,72... | collective-permute-start | bytes 393224 | tf_op jit(solution)/shard_map/ppermute | solution.py:30
  80.1 10.5 %collective-permute-start.7 = (bf16[1,8,64,128]{3,2,1,0:T(8,128)(2,1)S(1)}, bf16[1,8,64,128]{3,2,1,0:T(8,128)(2,1)S(1)}, u32[]{:S(2)}, u32[]{:S(2)}) collective-permute-start(bf16[1,8,64,128]{3,2,1,0:T(8,128)(2,1)S(1)} %get-tuple-element.43), channel_id=1, source_target_pairs={{8,16},{16,8},{24,32},{32,24},{40,48},{48,40},{56,64},{64,56},{72,... | collective-permute-start | bytes 393224 | tf_op jit(solution)/shard_map/ppermute | solution.py:30
  83.6 11.8 %collective-permute-start.22 = (f32[216,128]{1,0:T(8,128)S(1)}, f32[216,128]{1,0:T(8,128)S(1)}, u32[]{:S(2)}, u32[]{:S(2)}) collective-permute-start(f32[216,128]{1,0:T(8,128)S(1)} %add_add_fusion.refs_3_), channel_id=1, source_target_pairs={{0,48},{1,49},{2,50},{3,51},{4,52},{5,53},{6,54},{7,55},{8,56},{9,... | collective-permute-start | bytes 331784 | tf_op jit(solution)/shard_map/ppermute | solution.py:25
  84.7 10.7 %collective-permute-start.21 = (f32[216,128]{1,0:T(8,128)S(1)}, f32[216,128]{1,0:T(8,128)S(1)}, u32[]{:S(2)}, u32[]{:S(2)}) collective-permute-start(f32[216,128]{1,0:T(8,128)S(1)} %add_add_fusion.refs_3_), channel_id=1, source_target_pairs={{0,32},{1,33},{2,34},{3,35},{4,36},{5,37},{6,38},{7,39},{8,40},{9,... | collective-permute-start | bytes 331784 | tf_op jit(solution)/shard_map/ppermute | solution.py:25
  85.2 10.2 %collective-permute-start.20 = (f32[216,128]{1,0:T(8,128)S(1)}, f32[216,128]{1,0:T(8,128)S(1)}, u32[]{:S(2)}, u32[]{:S(2)}) collective-permute-start(f32[216,128]{1,0:T(8,128)S(1)} %add_add_fusion.refs_3_), channel_id=1, source_target_pairs={{0,16},{1,17},{2,18},{3,19},{4,20},{5,21},{6,22},{7,23},{8,24},{9,... | collective-permute-start | bytes 331784 | tf_op jit(solution)/shard_map/ppermute | solution.py:25
  90.6 6.4 %collective-permute-start.8 = (bf16[10,64,128]{2,1,0:T(8,128)(2,1)S(1)}, bf16[10,64,128]{2,1,0:T(8,128)(2,1)S(1)}, u32[]{:S(2)}, u32[]{:S(2)}) collective-permute-start(bf16[10,64,128]{2,1,0:T(8,128)(2,1)S(1)} %get-tuple-element.44), channel_id=1, source_target_pairs={{0,1},{1,0},{2,3},{3,2},{4,5},{5,4},{6,7},{7,6},{8,9},{9,8},{10,11... | collective-permute-start | bytes 491528 | tf_op jit(solution)/shard_map/ppermute | solution.py:374
  92.6 8.8 %collective-permute-start.9 = (bf16[10,64,128]{2,1,0:T(8,128)(2,1)S(1)}, bf16[10,64,128]{2,1,0:T(8,128)(2,1)S(1)}, u32[]{:S(2)}, u32[]{:S(2)}) collective-permute-start(bf16[10,64,128]{2,1,0:T(8,128)(2,1)S(1)} %get-tuple-element.45), channel_id=1, source_target_pairs={{1,2},{2,1},{3,4},{4,3},{5,6},{6,5},{9,10},{10,9},{11,12},{12,11},... | collective-permute-start | bytes 491528 | tf_op jit(solution)/shard_map/ppermute | solution.py:375
  95.5 16.6 %collective-permute-start.23 = (f32[864,128]{1,0:T(8,128)S(1)}, f32[864,128]{1,0:T(8,128)S(1)}, u32[]{:S(2)}, u32[]{:S(2)}) collective-permute-start(f32[864,128]{1,0:T(8,128)S(1)} %shard_map.87.refs_3_), channel_id=1, source_target_pairs={{0,8},{1,9},{2,10},{3,11},{4,12},{5,13},{6,14},{7,15},{8,0},{9,1},... | collective-permute-start | bytes 1327112 | tf_op jit(solution)/shard_map/ppermute | solution.py:25

commit v9 on v8

--- a/solution.py
+++ b/solution.py
@@ -107,7 +107,7 @@
                 emit(x, y + side, below + part[chans : 2 * chans] + above)
         return carry
 
-    lax.fori_loop(0, wide - 2, body, 0)
+    lax.fori_loop(0, wide - 2, body, 0, unroll=4)
 
 
 def weights_kernel(one, two, w_pre, w_act, w_branch):
@@ -178,7 +178,7 @@
         acc[...] += lax.dot_general(left, right, (((1,), (1,)), ((), ())), preferred_element_type=F32)
         return carry
 
-    lax.fori_loop(0, size_x, body, 0)
+    lax.fori_loop(0, size_x, body, 0, unroll=4)
 
 
 def pack_grad(dest, acc, chans):
@@ -195,7 +195,7 @@
         stack_row(stack, i, 0, source[i])
         return carry
 
-    lax.fori_loop(0, source.shape[0], body, 0)
+    lax.fori_loop(0, source.shape[0], body, 0, unroll=4)
 
 
 def grad_two_kernel(grad_pad, activ, packed, acc):

time: 114 us -> 104 us (0.912)
  Pallas kernels: 31.9 us -> 21.9 us
    pallas_call x14, Pallas kernels: 31.9 us -> 21.9 us  [run(): pl.pallas_call(wrapped, out_shape=tuple(outs), in_specs=specs, out_specs=...]
  transfers between devices with their start and end apart: 24 -> 24, of which waited for: 12 -> 12; matrix products, arithmetic and copies ran while one was open for 5% -> 6% of each run, Pallas kernels for 14% -> 9%
where the time goes in v9:
time: 104 us
  starting transfers between devices  41.5 us (40%)
  waiting for transfers between devices  29.5 us (28%)
  Pallas kernels  21.9 us (21%)
  other arithmetic  5.75 us (6%)
  local copies, waits for them, and re-layouts  3.8 us (4%)
  between operations  1.11 us (1%)
    pallas_call x14, Pallas kernels, run(): pl.pallas_call(wrapped, out_shape=tuple(outs), in_specs=specs, out_specs=...  21.9 us
    ppermute x14, starting transfers between devices, xor_permute(): return lax.ppermute(value, AXES, [(i, i ^ mask) for i in range(total)])  16.3 us
    ppermute x14, waiting for transfers between devices, xor_permute(): return lax.ppermute(value, AXES, [(i, i ^ mask) for i in range(total)])  11.8 us
    ppermute x3, starting transfers between devices, swap(): lax.ppermute(value_odd, axis, odd)  9.04 us
    ppermute x3, waiting for transfers between devices, swap(): lax.ppermute(value_odd, axis, odd)  6.71 us
    ppermute x1, starting transfers between devices, body(): in_odd = lax.ppermute(in_next, 'gy', odd)  5.38 us
    ppermute x3, starting transfers between devices, swap(): lax.ppermute(value_even, axis, even)  5.35 us
    ppermute x1, waiting for transfers between devices, body(): in_even = lax.ppermute(sends[0], 'gy', even)  5.2 us
  transfers between devices with their start and end apart: 24, of which 12 were waited for; matrix products, arithmetic and copies ran while one was open for 6% of the time, Pallas kernels for 9%

profile of v9, /device:TPU:15, one launch (start us, length us, event | category | flops | bytes accessed | tf_op | source)
XLA Modules:
  0.0 103.5 jit_solution(10374569251831710190)
XLA Ops:
  0.7 0.8 convert_bitcast_fusion
  1.4 0.1 broadcast_in_dim.8
  1.5 0.1 convert_element_type.32
  1.6 1.2 %constant_dynamic-slice_fusion = (bf16[64,1,8,128]{3,2,1,0:T(8,128)(2,1)S(1)}, bf16[64,1,8,128]{3,2,1,0:T(8,128)(2,1)S(1)}, bf16[64,1,8,128]{3,2,1,0:T(8,128)(2,1)S(1)}, bf16[64,1,8,128]{3,2,1,0:T(8,128)(2,1)S(1)}) fusion(bf16[64,8,8,128]{3,2,1,0:T(8,128)(2,1)} %param.6, s32[]{:T(128)S(6)} %select_n.10, s32[]{:T(128)S(6)} %select_n.9, ...), kind=kLoop, calls=%fused_computation.18 | loop fusion | bytes 1048584 | tf_op jit(solution)/shard_map/jit(dynamic_index_in_dim)/dynamic_slice | solution.py:330
  2.7 0.1 fusion.3
  2.8 0.7 pad_maximum_fusion
  3.6 0.7 collective-permute-start
  4.2 0.7 pad_maximum_fusion.1
  5.0 3.3 %collective-permute-start.1 = (bf16[2,8,64,128]{3,2,1,0:T(8,128)(2,1)}, bf16[2,8,64,128]{3,2,1,0:T(8,128)(2,1)S(1)}, u32[]{:S(2)}, u32[]{:S(2)}) collective-permute-start(bf16[2,8,64,128]{3,2,1,0:T(8,128)(2,1)} %pad_maximum_fusion.1), channel_id=1, source_target_pairs={{8,16},{16,8},{24,32},{32,24},{40,48},{48,40},{56,64},{64,56},{72,... | collective-permute-start | bytes 786440 | tf_op jit(solution)/shard_map/ppermute | solution.py:30
  8.3 0.3 shard_map.76
  8.6 3.3 %fusion = (bf16[8,8,64,128]{3,2,1,0:T(8,128)(2,1)S(1)}, bf16[8,8,64,128]{3,2,1,0:T(8,128)(2,1)S(1)}) fusion(bf16[64,8,8,128]{3,2,1,0:T(8,128)(2,1)} %param.5, bf16[128]{0:T(256)(128)(2,1)S(1)} %convert_element_type.32, bf16[64,8,8,128]{3,2,1,0:T(8,128)(2,1)} %param.6), kind=kLoop, calls=%fused_computation.2 | loop fusion | flops 1048576 | bytes 4194560 | tf_op jit(solution)/shard_map/transpose | solution.py:334
  11.9 3.0 %collective-permute-done.1.refs_6_.refs_7_ = bf16[2,8,64,128]{3,2,1,0:T(8,128)(2,1)S(1)} collective-permute-done((bf16[2,8,64,128]{3,2,1,0:T(8,128)(2,1)}, bf16[2,8,64,128]{3,2,1,0:T(8,128)(2,1)S(1)}, u32[]{:S(2)}, u32[]{:S(2)}) %collective-permute-start.1) | collective-permute-done | bytes 262176 | tf_op jit(solution)/shard_map/ppermute | solution.py:30
  15.0 0.8 shard_map.77
  15.7 0.7 copy-done.2
  16.4 5.4 %collective-permute-start.3 = (bf16[10,64,128]{2,1,0:T(8,128)(2,1)}, bf16[10,64,128]{2,1,0:T(8,128)(2,1)}, u32[]{:S(2)}, u32[]{:S(2)}) collective-permute-start(bf16[10,64,128]{2,1,0:T(8,128)(2,1)} %get-tuple-element.37), channel_id=1, source_target_pairs={{1,2},{2,1},{3,4},{4,3},{5,6},{6,5},{9,10},{10,9},{11,12},{12,11},... | collective-permute-start | bytes 491528 | tf_op jit(solution)/shard_map/ppermute | solution.py:354
  21.8 0.6 collective-permute-start.2
  22.4 0.1 broadcast_in_dim.7
  22.4 0.1 convert_element_type.29.refs_3_.refs_0_
  22.5 2.5 %collective-permute-start.4 = (bf16[10,64,128]{2,1,0:T(8,128)(2,1)}, bf16[10,64,128]{2,1,0:T(8,128)(2,1)S(1)}, u32[]{:S(2)}, u32[]{:S(2)}) collective-permute-start(bf16[10,64,128]{2,1,0:T(8,128)(2,1)} %copy-done.2), channel_id=1, source_target_pairs={{0,1},{1,0},{2,3},{3,2},{4,5},{5,4},{6,7},{7,6},{8,9},{9,8},{10,11... | collective-permute-start | bytes 491528 | tf_op jit(solution)/shard_map/ppermute | solution.py:30
  25.1 2.3 %collective-permute-start.5 = (bf16[10,64,128]{2,1,0:T(8,128)(2,1)S(1)}, bf16[10,64,128]{2,1,0:T(8,128)(2,1)S(1)}, u32[]{:S(2)}, u32[]{:S(2)}) collective-permute-start(bf16[10,64,128]{2,1,0:T(8,128)(2,1)S(1)} %get-tuple-element.40), channel_id=1, source_target_pairs={{1,2},{2,1},{3,4},{4,3},{5,6},{6,5},{9,10},{10,9},{11,12},{12,11},... | collective-permute-start | bytes 491528 | tf_op jit(solution)/shard_map/ppermute | solution.py:30
  27.4 5.2 %collective-permute-done.2.refs_8_ = bf16[10,64,128]{2,1,0:T(8,128)(2,1)} collective-permute-done((bf16[10,64,128]{2,1,0:T(8,128)(2,1)}, bf16[10,64,128]{2,1,0:T(8,128)(2,1)}, u32[]{:S(2)}, u32[]{:S(2)}) %collective-permute-start.2) | collective-permute-done | bytes 163872 | tf_op jit(solution)/shard_map/ppermute | solution.py:351
  32.6 4.7 %shard_map.78 = (bf16[8,8,192,128]{3,2,1,0:T(8,128)(2,1)S(1)}, f32[8,8,64,128]{3,2,1,0:T(8,128)S(1)}, bf16[10,10,64,128]{3,2,1,0:T(8,128)(2,1)S(1)}) custom-call(s32[1]{0:T(128)} %bitcast.refs_0_, s32[1]{0:T(128)} %bitcast.1.refs_1_, s32[1]{0:T(128)} %bitcast.2.refs_2_, f32[1,128]{1,0:T(1,128)S(1)} %convert_element_type.29.refs_3_.refs_0_, ...), custom_call_target="tpu_custom_call" | custom-call | flops 1811939328 | bytes 9003532 | tf_op jit(solution)/shard_map/pallas_call | solution.py:303
  37.3 0.0 collective-permute-done.5.refs_9_
  37.3 3.1 %shard_map.79 = (bf16[8,8,64,128]{3,2,1,0:T(8,128)(2,1)S(1)}, bf16[1,8,64,128]{3,2,1,0:T(8,128)(2,1)S(1)}, bf16[1,8,64,128]{3,2,1,0:T(8,128)(2,1)S(1)}, bf16[10,10,64,128]{3,2,1,0:T(8,128)(2,1)S(1)}) custom-call(s32[1]{0:T(128)} %bitcast.refs_0_, s32[1]{0:T(128)} %bitcast.1.refs_1_, s32[1]{0:T(128)} %bitcast.2.refs_2_, ...), custom_call_target="tpu_custom_call" | custom-call | flops 1811939328 | bytes 7168012 | tf_op jit(solution)/shard_map/pallas_call | solution.py:303
  40.5 3.2 %shard_map.84.refs_5_ = f32[864,128]{1,0:T(8,128)S(1)} custom-call(bf16[10,10,64,128]{3,2,1,0:T(8,128)(2,1)S(1)} %get-tuple-element.49.refs_0_, bf16[8,8,192,128]{3,2,1,0:T(8,128)(2,1)S(1)} %get-tuple-element.50.refs_1_), custom_call_target="tpu_custom_call" | custom-call | flops 1811939328 | bytes 5226496 | tf_op jit(solution)/shard_map/pallas_call | solution.py:303
  43.7 3.9 %shard_map.85 = (f32[864,128]{1,0:T(8,128)S(1)}, f32[864,128]{1,0:T(8,128)S(1)}) custom-call(s32[1]{0:T(128)} %bitcast.refs_0_, s32[1]{0:T(128)} %bitcast.1.refs_1_, s32[1]{0:T(128)} %bitcast.2.refs_2_, bf16[10,10,64,128]{3,2,1,0:T(8,128)(2,1)S(1)} %get-tuple-element.48.refs_3_, bf16[8,8,64,128]{3,2,1,0:T(8,128)(2,1)S(1)} %get-tuple-element.41.refs_3_.refs_6_.refs_4_, ...), custom_call_target="tpu_custom_call" | custom-call | flops 1811939328 | bytes 4014092 | tf_op jit(solution)/shard_map/pallas_call | solution.py:303
  47.6 0.1 collective-permute-start.10
  47.7 1.8 %collective-permute-done.10.refs_4_ = f32[864,128]{1,0:T(8,128)S(1)} collective-permute-done((f32[864,128]{1,0:T(8,128)S(1)}, f32[864,128]{1,0:T(8,128)S(1)}, u32[]{:S(2)}, u32[]{:S(2)}) %collective-permute-start.10) | collective-permute-done | bytes 442400 | tf_op jit(solution)/shard_map/ppermute | solution.py:25
  49.5 0.2 collective-permute-start.11
  49.7 0.7 collective-permute-start.12
  50.3 3.1 %collective-permute-start.13 = (f32[216,128]{1,0:T(8,128)S(1)}, f32[216,128]{1,0:T(8,128)S(1)}, u32[]{:S(2)}, u32[]{:S(2)}) collective-permute-start(f32[216,128]{1,0:T(8,128)S(1)} %get-tuple-element.56), channel_id=1, source_target_pairs={{0,48},{1,49},{2,50},{3,51},{4,52},{5,53},{6,54},{7,55},{8,56},{9,... | collective-permute-start | bytes 331784 | tf_op jit(solution)/shard_map/ppermute | solution.py:25
  53.4 0.6 collective-permute-done.11
  54.0 1.1 %collective-permute-done.12 = f32[216,128]{1,0:T(8,128)S(1)} collective-permute-done((f32[216,128]{1,0:T(8,128)S(1)}, f32[216,128]{1,0:T(8,128)S(1)}, u32[]{:S(2)}, u32[]{:S(2)}) %collective-permute-start.12) | collective-permute-done | bytes 110624 | tf_op jit(solution)/shard_map/ppermute | solution.py:25
  55.1 3.4 %collective-permute-done.13 = f32[216,128]{1,0:T(8,128)S(1)} collective-permute-done((f32[216,128]{1,0:T(8,128)S(1)}, f32[216,128]{1,0:T(8,128)S(1)}, u32[]{:S(2)}, u32[]{:S(2)}) %collective-permute-start.13) | collective-permute-done | bytes 110624 | tf_op jit(solution)/shard_map/ppermute | solution.py:25
  58.6 1.4 %collective-permute-start.16 = (f32[216,128]{1,0:T(8,128)S(1)}, f32[216,128]{1,0:T(8,128)S(1)}, u32[]{:S(2)}, u32[]{:S(2)}) collective-permute-start(f32[216,128]{1,0:T(8,128)S(1)} %add_add_fusion.2), channel_id=1, source_target_pairs={{0,6},{1,7},{2,4},{3,5},{4,2},{5,3},{6,0},{7,1},{8,14},{9,15},{10,... | collective-permute-start | bytes 331784 | tf_op jit(solution)/shard_map/ppermute | solution.py:25
  59.9 0.7 collective-permute-start.15
  60.6 1.3 %collective-permute-start.14 = (f32[216,128]{1,0:T(8,128)S(1)}, f32[216,128]{1,0:T(8,128)S(1)}, u32[]{:S(2)}, u32[]{:S(2)}) collective-permute-start(f32[216,128]{1,0:T(8,128)S(1)} %add_add_fusion.2), channel_id=1, source_target_pairs={{0,2},{1,3},{2,0},{3,1},{4,6},{5,7},{6,4},{7,5},{8,10},{9,11},{10,... | collective-permute-start | bytes 331784 | tf_op jit(solution)/shard_map/ppermute | solution.py:25
  61.9 0.9 collective-permute-done.16
  62.8 2.2 %collective-permute-done.15 = f32[216,128]{1,0:T(8,128)S(1)} collective-permute-done((f32[216,128]{1,0:T(8,128)S(1)}, f32[216,128]{1,0:T(8,128)S(1)}, u32[]{:S(2)}, u32[]{:S(2)}) %collective-permute-start.15) | collective-permute-done | bytes 110624 | tf_op jit(solution)/shard_map/ppermute | solution.py:25
  65.0 1.7 %collective-permute-done.14 = f32[216,128]{1,0:T(8,128)S(1)} collective-permute-done((f32[216,128]{1,0:T(8,128)S(1)}, f32[216,128]{1,0:T(8,128)S(1)}, u32[]{:S(2)}, u32[]{:S(2)}) %collective-permute-start.14) | collective-permute-done | bytes 110624 | tf_op jit(solution)/shard_map/ppermute | solution.py:25
  66.8 4.3 %collective-permute-start.19 = (f32[216,128]{1,0:T(8,128)S(1)}, f32[216,128]{1,0:T(8,128)S(1)}, u32[]{:S(2)}, u32[]{:S(2)}) collective-permute-start(f32[216,128]{1,0:T(8,128)S(1)} %add_add_fusion.1), channel_id=1, source_target_pairs={{0,65},{1,64},{2,67},{3,66},{4,69},{5,68},{6,71},{7,70},{8,73},{9,... | collective-permute-start | bytes 331784 | tf_op jit(solution)/shard_map/ppermute | solution.py:25
  71.1 0.0 collective-permute-start.18
  71.1 1.3 %collective-permute-start.17 = (f32[216,128]{1,0:T(8,128)S(1)}, f32[216,128]{1,0:T(8,128)S(1)}, u32[]{:S(2)}, u32[]{:S(2)}) collective-permute-start(f32[216,128]{1,0:T(8,128)S(1)} %add_add_fusion.1), channel_id=1, source_target_pairs={{0,1},{1,0},{2,3},{3,2},{4,5},{5,4},{6,7},{7,6},{8,9},{9,8},{10,11... | collective-permute-start | bytes 331784 | tf_op jit(solution)/shard_map/ppermute | solution.py:25
  72.4 2.1 %collective-permute-start.6 = (bf16[1,8,64,128]{3,2,1,0:T(8,128)(2,1)S(1)}, bf16[1,8,64,128]{3,2,1,0:T(8,128)(2,1)S(1)}, u32[]{:S(2)}, u32[]{:S(2)}) collective-permute-start(bf16[1,8,64,128]{3,2,1,0:T(8,128)(2,1)S(1)} %get-tuple-element.42), channel_id=1, source_target_pairs={{0,8},{8,0},{16,24},{24,16},{32,40},{40,32},{48,56},{56,48},{64,72... | collective-permute-start | bytes 393224 | tf_op jit(solution)/shard_map/ppermute | solution.py:30
  74.5 3.4 %collective-permute-start.7 = (bf16[1,8,64,128]{3,2,1,0:T(8,128)(2,1)S(1)}, bf16[1,8,64,128]{3,2,1,0:T(8,128)(2,1)S(1)}, u32[]{:S(2)}, u32[]{:S(2)}) collective-permute-start(bf16[1,8,64,128]{3,2,1,0:T(8,128)(2,1)S(1)} %get-tuple-element.43), channel_id=1, source_target_pairs={{8,16},{16,8},{24,32},{32,24},{40,48},{48,40},{56,64},{64,56},{72,... | collective-permute-start | bytes 393224 | tf_op jit(solution)/shard_map/ppermute | solution.py:30
  77.9 0.0 collective-permute-done.19
  77.9 0.0 collective-permute-done.17
  78.0 1.2 %collective-permute-start.22 = (f32[216,128]{1,0:T(8,128)S(1)}, f32[216,128]{1,0:T(8,128)S(1)}, u32[]{:S(2)}, u32[]{:S(2)}) collective-permute-start(f32[216,128]{1,0:T(8,128)S(1)} %add_add_fusion.refs_3_), channel_id=1, source_target_pairs={{0,48},{1,49},{2,50},{3,51},{4,52},{5,53},{6,54},{7,55},{8,56},{9,... | collective-permute-start | bytes 331784 | tf_op jit(solution)/shard_map/ppermute | solution.py:25
  79.2 0.5 collective-permute-start.21
  79.7 1.6 %collective-permute-start.20 = (f32[216,128]{1,0:T(8,128)S(1)}, f32[216,128]{1,0:T(8,128)S(1)}, u32[]{:S(2)}, u32[]{:S(2)}) collective-permute-start(f32[216,128]{1,0:T(8,128)S(1)} %add_add_fusion.refs_3_), channel_id=1, source_target_pairs={{0,16},{1,17},{2,18},{3,19},{4,20},{5,21},{6,22},{7,23},{8,24},{9,... | collective-permute-start | bytes 331784 | tf_op jit(solution)/shard_map/ppermute | solution.py:25
  81.3 0.0 collective-permute-done.6.refs_4_.refs_7_
  81.3 3.7 %collective-permute-done.7.refs_5_.refs_8_ = bf16[1,8,64,128]{3,2,1,0:T(8,128)(2,1)S(1)} collective-permute-done((bf16[1,8,64,128]{3,2,1,0:T(8,128)(2,1)S(1)}, bf16[1,8,64,128]{3,2,1,0:T(8,128)(2,1)S(1)}, u32[]{:S(2)}, u32[]{:S(2)}) %collective-permute-start.7) | collective-permute-done | bytes 131104 | tf_op jit(solution)/shard_map/ppermute | solution.py:30
  85.0 2.0 %collective-permute-start.8 = (bf16[10,64,128]{2,1,0:T(8,128)(2,1)S(1)}, bf16[10,64,128]{2,1,0:T(8,128)(2,1)S(1)}, u32[]{:S(2)}, u32[]{:S(2)}) collective-permute-start(bf16[10,64,128]{2,1,0:T(8,128)(2,1)S(1)} %get-tuple-element.44), channel_id=1, source_target_pairs={{0,1},{1,0},{2,3},{3,2},{4,5},{5,4},{6,7},{7,6},{8,9},{9,8},{10,11... | collective-permute-start | bytes 491528 | tf_op jit(solution)/shard_map/ppermute | solution.py:374
  87.0 2.8 %collective-permute-start.9 = (bf16[10,64,128]{2,1,0:T(8,128)(2,1)S(1)}, bf16[10,64,128]{2,1,0:T(8,128)(2,1)S(1)}, u32[]{:S(2)}, u32[]{:S(2)}) collective-permute-start(bf16[10,64,128]{2,1,0:T(8,128)(2,1)S(1)} %get-tuple-element.45), channel_id=1, source_target_pairs={{1,2},{2,1},{3,4},{4,3},{5,6},{6,5},{9,10},{10,9},{11,12},{12,11},... | collective-permute-start | bytes 491528 | tf_op jit(solution)/shard_map/ppermute | solution.py:375
  89.9 0.1 collective-permute-start.23
  90.0 1.5 %collective-permute-done.8.refs_9_ = bf16[10,64,128]{2,1,0:T(8,128)(2,1)S(1)} collective-permute-done((bf16[10,64,128]{2,1,0:T(8,128)(2,1)S(1)}, bf16[10,64,128]{2,1,0:T(8,128)(2,1)S(1)}, u32[]{:S(2)}, u32[]{:S(2)}) %collective-permute-start.8) | collective-permute-done | bytes 163872 | tf_op jit(solution)/shard_map/ppermute | solution.py:374
  91.5 4.3 %collective-permute-done.9.refs_10_ = bf16[10,64,128]{2,1,0:T(8,128)(2,1)S(1)} collective-permute-done((bf16[10,64,128]{2,1,0:T(8,128)(2,1)S(1)}, bf16[10,64,128]{2,1,0:T(8,128)(2,1)S(1)}, u32[]{:S(2)}, u32[]{:S(2)}) %collective-permute-start.9) | collective-permute-done | bytes 163872 | tf_op jit(solution)/shard_map/ppermute | solution.py:375
  95.8 1.3 %shard_map.81 = (bf16[8,2,64,128]{3,2,1,0:T(8,128)(2,1)S(1)}, bf16[10,10,64,128]{3,2,1,0:T(8,128)(2,1)S(1)}) custom-call(s32[1]{0:T(128)} %bitcast.refs_0_, s32[1]{0:T(128)} %bitcast.1.refs_1_, s32[1]{0:T(128)} %bitcast.2.refs_2_, f32[1,128]{1,0:T(1,128)S(1)} %convert_element_type.29.refs_3_.refs_0_, bf16[192,576]{1,0:T(8,128)(2,1)S(1)} %get-tuple-element.31.refs_4_.refs_1_, ...), custom_call_target="tpu_custom_call" | custom-call | flops 452984832 | bytes 4809228 | tf_op jit(solution)/shard_map/pallas_call | solution.py:303
  97.1 1.1 %shard_map.82 = bf16[8,2,64,128]{3,2,1,0:T(8,128)(2,1)S(1)} custom-call(f32[1,128]{1,0:T(1,128)S(1)} %convert_element_type.29.refs_3_.refs_0_, bf16[192,576]{1,0:T(8,128)(2,1)S(1)} %get-tuple-element.31.refs_4_.refs_1_, bf16[8,8,64,128]{3,2,1,0:T(8,128)(2,1)S(1)} %get-tuple-element.74.refs_4_.refs_5_.refs_2_, ...), custom_call_target="tpu_custom_call" | custom-call | flops 452984832 | bytes 3170816 | tf_op jit(solution)/shard_map/pallas_call | solution.py:303
  98.2 1.8 %shard_map.83 = bf16[8,4,64,128]{3,2,1,0:T(8,128)(2,1)S(1)} custom-call(f32[1,128]{1,0:T(1,128)S(1)} %convert_element_type.29.refs_3_.refs_0_, bf16[192,576]{1,0:T(8,128)(2,1)S(1)} %get-tuple-element.31.refs_4_.refs_1_, bf16[8,8,64,128]{3,2,1,0:T(8,128)(2,1)S(1)} %get-tuple-element.74.refs_4_.refs_5_.refs_2_, ...), custom_call_target="tpu_custom_call" | custom-call | flops 905969664 | bytes 3432960 | tf_op jit(solution)/shard_map/pallas_call | solution.py:303
  100.0 0.1 maximum_bitcast_fusion
  100.1 1.6 %copy.21 = bf16[64,8,8,128]{3,2,1,0:T(8,128)(2,1)} copy(bf16[64,8,8,128]{3,0,2,1:T(8,128)(2,1)S(1)} %maximum_bitcast_fusion) | data formatting | bytes 2097152
  101.7 0.4 shard_map.88.refs_3_
  102.1 1.2 %shard_map.89 = (f32[3,3,3,64,64]{4,3,2,1,0:T(8,128)}, f32[3,3,3,64,64]{4,3,2,1,0:T(8,128)}) custom-call(s32[1]{0:T(128)} %bitcast.refs_0_, s32[1]{0:T(128)} %bitcast.1.refs_1_, s32[1]{0:T(128)} %bitcast.2.refs_2_, f32[3,3,3,64,64]{4,3,2,1,0:T(8,128)S(1)} %shard_map.88.refs_3_, f32[864,128]{1,0:T(8,128)S(1)} %collective-permute-done.23.refs_4_), custom_call_target="tpu_custom_call" | custom-call | bytes 1769484 | tf_op jit(solution)/shard_map/pallas_call | solution.py:303
  (19 shorter events, 0.2 us)
Async XLA Ops:
  0.6 7.7 %copy-start.1 = (bf16[3,3,3,64,64]{4,3,2,1,0:T(8,128)(2,1)S(1)}, bf16[3,3,3,64,64]{4,3,2,1,0:T(8,128)(2,1)}, u32[]{:S(2)}) copy-start(bf16[3,3,3,64,64]{4,3,2,1,0:T(8,128)(2,1)} %refs_1_.1) | copy-start | bytes 663556
  0.6 7.7 %copy-start = (bf16[3,3,3,64,64]{4,3,2,1,0:T(8,128)(2,1)S(1)}, bf16[3,3,3,64,64]{4,3,2,1,0:T(8,128)(2,1)}, u32[]{:S(2)}) copy-start(bf16[3,3,3,64,64]{4,3,2,1,0:T(8,128)(2,1)} %refs_0_.1) | copy-start | bytes 663556
  3.6 8.3 %collective-permute-start = (bf16[2,8,64,128]{3,2,1,0:T(8,128)(2,1)}, bf16[2,8,64,128]{3,2,1,0:T(8,128)(2,1)S(1)}, u32[]{:S(2)}, u32[]{:S(2)}) collective-permute-start(bf16[2,8,64,128]{3,2,1,0:T(8,128)(2,1)} %pad_maximum_fusion), channel_id=1, source_target_pairs={{0,8},{8,0},{16,24},{24,16},{32,40},{40,32},{48,56},{56,48},{64,72... | collective-permute-start | bytes 786440 | tf_op jit(solution)/shard_map/ppermute | solution.py:30
  5.0 10.0 %collective-permute-start.1 = (bf16[2,8,64,128]{3,2,1,0:T(8,128)(2,1)}, bf16[2,8,64,128]{3,2,1,0:T(8,128)(2,1)S(1)}, u32[]{:S(2)}, u32[]{:S(2)}) collective-permute-start(bf16[2,8,64,128]{3,2,1,0:T(8,128)(2,1)} %pad_maximum_fusion.1), channel_id=1, source_target_pairs={{8,16},{16,8},{24,32},{32,24},{40,48},{48,40},{56,64},{64,56},{72,... | collective-permute-start | bytes 786440 | tf_op jit(solution)/shard_map/ppermute | solution.py:30
  15.7 0.7 copy-start.2
  16.4 11.0 %collective-permute-start.3 = (bf16[10,64,128]{2,1,0:T(8,128)(2,1)}, bf16[10,64,128]{2,1,0:T(8,128)(2,1)}, u32[]{:S(2)}, u32[]{:S(2)}) collective-permute-start(bf16[10,64,128]{2,1,0:T(8,128)(2,1)} %get-tuple-element.37), channel_id=1, source_target_pairs={{1,2},{2,1},{3,4},{4,3},{5,6},{6,5},{9,10},{10,9},{11,12},{12,11},... | collective-permute-start | bytes 491528 | tf_op jit(solution)/shard_map/ppermute | solution.py:354
  21.8 10.8 %collective-permute-start.2 = (bf16[10,64,128]{2,1,0:T(8,128)(2,1)}, bf16[10,64,128]{2,1,0:T(8,128)(2,1)}, u32[]{:S(2)}, u32[]{:S(2)}) collective-permute-start(bf16[10,64,128]{2,1,0:T(8,128)(2,1)} %get-tuple-element.36), channel_id=1, source_target_pairs={{0,1},{1,0},{2,3},{3,2},{4,5},{5,4},{6,7},{7,6},{8,9},{9,8},{10,11... | collective-permute-start | bytes 491528 | tf_op jit(solution)/shard_map/ppermute | solution.py:351
  22.5 14.8 %collective-permute-start.4 = (bf16[10,64,128]{2,1,0:T(8,128)(2,1)}, bf16[10,64,128]{2,1,0:T(8,128)(2,1)S(1)}, u32[]{:S(2)}, u32[]{:S(2)}) collective-permute-start(bf16[10,64,128]{2,1,0:T(8,128)(2,1)} %copy-done.2), channel_id=1, source_target_pairs={{0,1},{1,0},{2,3},{3,2},{4,5},{5,4},{6,7},{7,6},{8,9},{9,8},{10,11... | collective-permute-start | bytes 491528 | tf_op jit(solution)/shard_map/ppermute | solution.py:30
  25.1 12.3 %collective-permute-start.5 = (bf16[10,64,128]{2,1,0:T(8,128)(2,1)S(1)}, bf16[10,64,128]{2,1,0:T(8,128)(2,1)S(1)}, u32[]{:S(2)}, u32[]{:S(2)}) collective-permute-start(bf16[10,64,128]{2,1,0:T(8,128)(2,1)S(1)} %get-tuple-element.40), channel_id=1, source_target_pairs={{1,2},{2,1},{3,4},{4,3},{5,6},{6,5},{9,10},{10,9},{11,12},{12,11},... | collective-permute-start | bytes 491528 | tf_op jit(solution)/shard_map/ppermute | solution.py:30
  47.6 1.9 %collective-permute-start.10 = (f32[864,128]{1,0:T(8,128)S(1)}, f32[864,128]{1,0:T(8,128)S(1)}, u32[]{:S(2)}, u32[]{:S(2)}) collective-permute-start(f32[864,128]{1,0:T(8,128)S(1)} %get-tuple-element.52), channel_id=1, source_target_pairs={{0,8},{1,9},{2,10},{3,11},{4,12},{5,13},{6,14},{7,15},{8,0},{9,1},... | collective-permute-start | bytes 1327112 | tf_op jit(solution)/shard_map/ppermute | solution.py:25
  49.5 4.6 %collective-permute-start.11 = (f32[216,128]{1,0:T(8,128)S(1)}, f32[216,128]{1,0:T(8,128)S(1)}, u32[]{:S(2)}, u32[]{:S(2)}) collective-permute-start(f32[216,128]{1,0:T(8,128)S(1)} %get-tuple-element.54), channel_id=1, source_target_pairs={{0,16},{1,17},{2,18},{3,19},{4,20},{5,21},{6,22},{7,23},{8,24},{9,... | collective-permute-start | bytes 331784 | tf_op jit(solution)/shard_map/ppermute | solution.py:25
  49.7 5.5 %collective-permute-start.12 = (f32[216,128]{1,0:T(8,128)S(1)}, f32[216,128]{1,0:T(8,128)S(1)}, u32[]{:S(2)}, u32[]{:S(2)}) collective-permute-start(f32[216,128]{1,0:T(8,128)S(1)} %get-tuple-element.55), channel_id=1, source_target_pairs={{0,32},{1,33},{2,34},{3,35},{4,36},{5,37},{6,38},{7,39},{8,40},{9,... | collective-permute-start | bytes 331784 | tf_op jit(solution)/shard_map/ppermute | solution.py:25
  50.3 8.2 %collective-permute-start.13 = (f32[216,128]{1,0:T(8,128)S(1)}, f32[216,128]{1,0:T(8,128)S(1)}, u32[]{:S(2)}, u32[]{:S(2)}) collective-permute-start(f32[216,128]{1,0:T(8,128)S(1)} %get-tuple-element.56), channel_id=1, source_target_pairs={{0,48},{1,49},{2,50},{3,51},{4,52},{5,53},{6,54},{7,55},{8,56},{9,... | collective-permute-start | bytes 331784 | tf_op jit(solution)/shard_map/ppermute | solution.py:25
  58.6 4.2 %collective-permute-start.16 = (f32[216,128]{1,0:T(8,128)S(1)}, f32[216,128]{1,0:T(8,128)S(1)}, u32[]{:S(2)}, u32[]{:S(2)}) collective-permute-start(f32[216,128]{1,0:T(8,128)S(1)} %add_add_fusion.2), channel_id=1, source_target_pairs={{0,6},{1,7},{2,4},{3,5},{4,2},{5,3},{6,0},{7,1},{8,14},{9,15},{10,... | collective-permute-start | bytes 331784 | tf_op jit(solution)/shard_map/ppermute | solution.py:25
  59.9 5.1 %collective-permute-start.15 = (f32[216,128]{1,0:T(8,128)S(1)}, f32[216,128]{1,0:T(8,128)S(1)}, u32[]{:S(2)}, u32[]{:S(2)}) collective-permute-start(f32[216,128]{1,0:T(8,128)S(1)} %add_add_fusion.2), channel_id=1, source_target_pairs={{0,4},{1,5},{2,6},{3,7},{4,0},{5,1},{6,2},{7,3},{8,12},{9,13},{10,... | collective-permute-start | bytes 331784 | tf_op jit(solution)/shard_map/ppermute | solution.py:25
  60.6 6.2 %collective-permute-start.14 = (f32[216,128]{1,0:T(8,128)S(1)}, f32[216,128]{1,0:T(8,128)S(1)}, u32[]{:S(2)}, u32[]{:S(2)}) collective-permute-start(f32[216,128]{1,0:T(8,128)S(1)} %add_add_fusion.2), channel_id=1, source_target_pairs={{0,2},{1,3},{2,0},{3,1},{4,6},{5,7},{6,4},{7,5},{8,10},{9,11},{10,... | collective-permute-start | bytes 331784 | tf_op jit(solution)/shard_map/ppermute | solution.py:25
  66.8 11.1 %collective-permute-start.19 = (f32[216,128]{1,0:T(8,128)S(1)}, f32[216,128]{1,0:T(8,128)S(1)}, u32[]{:S(2)}, u32[]{:S(2)}) collective-permute-start(f32[216,128]{1,0:T(8,128)S(1)} %add_add_fusion.1), channel_id=1, source_target_pairs={{0,65},{1,64},{2,67},{3,66},{4,69},{5,68},{6,71},{7,70},{8,73},{9,... | collective-permute-start | bytes 331784 | tf_op jit(solution)/shard_map/ppermute | solution.py:25
  71.1 6.8 %collective-permute-start.18 = (f32[216,128]{1,0:T(8,128)S(1)}, f32[216,128]{1,0:T(8,128)S(1)}, u32[]{:S(2)}, u32[]{:S(2)}) collective-permute-start(f32[216,128]{1,0:T(8,128)S(1)} %add_add_fusion.1), channel_id=1, source_target_pairs={{0,64},{1,65},{2,66},{3,67},{4,68},{5,69},{6,70},{7,71},{8,72},{9,... | collective-permute-start | bytes 331784 | tf_op jit(solution)/shard_map/ppermute | solution.py:25
  71.1 6.9 %collective-permute-start.17 = (f32[216,128]{1,0:T(8,128)S(1)}, f32[216,128]{1,0:T(8,128)S(1)}, u32[]{:S(2)}, u32[]{:S(2)}) collective-permute-start(f32[216,128]{1,0:T(8,128)S(1)} %add_add_fusion.1), channel_id=1, source_target_pairs={{0,1},{1,0},{2,3},{3,2},{4,5},{5,4},{6,7},{7,6},{8,9},{9,8},{10,11... | collective-permute-start | bytes 331784 | tf_op jit(solution)/shard_map/ppermute | solution.py:25
  72.4 9.0 %collective-permute-start.6 = (bf16[1,8,64,128]{3,2,1,0:T(8,128)(2,1)S(1)}, bf16[1,8,64,128]{3,2,1,0:T(8,128)(2,1)S(1)}, u32[]{:S(2)}, u32[]{:S(2)}) collective-permute-start(bf16[1,8,64,128]{3,2,1,0:T(8,128)(2,1)S(1)} %get-tuple-element.42), channel_id=1, source_target_pairs={{0,8},{8,0},{16,24},{24,16},{32,40},{40,32},{48,56},{56,48},{64,72... | collective-permute-start | bytes 393224 | tf_op jit(solution)/shard_map/ppermute | solution.py:30
  74.5 10.5 %collective-permute-start.7 = (bf16[1,8,64,128]{3,2,1,0:T(8,128)(2,1)S(1)}, bf16[1,8,64,128]{3,2,1,0:T(8,128)(2,1)S(1)}, u32[]{:S(2)}, u32[]{:S(2)}) collective-permute-start(bf16[1,8,64,128]{3,2,1,0:T(8,128)(2,1)S(1)} %get-tuple-element.43), channel_id=1, source_target_pairs={{8,16},{16,8},{24,32},{32,24},{40,48},{48,40},{56,64},{64,56},{72,... | collective-permute-start | bytes 393224 | tf_op jit(solution)/shard_map/ppermute | solution.py:30
  78.0 11.9 %collective-permute-start.22 = (f32[216,128]{1,0:T(8,128)S(1)}, f32[216,128]{1,0:T(8,128)S(1)}, u32[]{:S(2)}, u32[]{:S(2)}) collective-permute-start(f32[216,128]{1,0:T(8,128)S(1)} %add_add_fusion.refs_3_), channel_id=1, source_target_pairs={{0,48},{1,49},{2,50},{3,51},{4,52},{5,53},{6,54},{7,55},{8,56},{9,... | collective-permute-start | bytes 331784 | tf_op jit(solution)/shard_map/ppermute | solution.py:25
  79.2 10.7 %collective-permute-start.21 = (f32[216,128]{1,0:T(8,128)S(1)}, f32[216,128]{1,0:T(8,128)S(1)}, u32[]{:S(2)}, u32[]{:S(2)}) collective-permute-start(f32[216,128]{1,0:T(8,128)S(1)} %add_add_fusion.refs_3_), channel_id=1, source_target_pairs={{0,32},{1,33},{2,34},{3,35},{4,36},{5,37},{6,38},{7,39},{8,40},{9,... | collective-permute-start | bytes 331784 | tf_op jit(solution)/shard_map/ppermute | solution.py:25
  79.7 10.2 %collective-permute-start.20 = (f32[216,128]{1,0:T(8,128)S(1)}, f32[216,128]{1,0:T(8,128)S(1)}, u32[]{:S(2)}, u32[]{:S(2)}) collective-permute-start(f32[216,128]{1,0:T(8,128)S(1)} %add_add_fusion.refs_3_), channel_id=1, source_target_pairs={{0,16},{1,17},{2,18},{3,19},{4,20},{5,21},{6,22},{7,23},{8,24},{9,... | collective-permute-start | bytes 331784 | tf_op jit(solution)/shard_map/ppermute | solution.py:25
  85.0 6.4 %collective-permute-start.8 = (bf16[10,64,128]{2,1,0:T(8,128)(2,1)S(1)}, bf16[10,64,128]{2,1,0:T(8,128)(2,1)S(1)}, u32[]{:S(2)}, u32[]{:S(2)}) collective-permute-start(bf16[10,64,128]{2,1,0:T(8,128)(2,1)S(1)} %get-tuple-element.44), channel_id=1, source_target_pairs={{0,1},{1,0},{2,3},{3,2},{4,5},{5,4},{6,7},{7,6},{8,9},{9,8},{10,11... | collective-permute-start | bytes 491528 | tf_op jit(solution)/shard_map/ppermute | solution.py:374
  87.0 8.8 %collective-permute-start.9 = (bf16[10,64,128]{2,1,0:T(8,128)(2,1)S(1)}, bf16[10,64,128]{2,1,0:T(8,128)(2,1)S(1)}, u32[]{:S(2)}, u32[]{:S(2)}) collective-permute-start(bf16[10,64,128]{2,1,0:T(8,128)(2,1)S(1)} %get-tuple-element.45), channel_id=1, source_target_pairs={{1,2},{2,1},{3,4},{4,3},{5,6},{6,5},{9,10},{10,9},{11,12},{12,11},... | collective-permute-start | bytes 491528 | tf_op jit(solution)/shard_map/ppermute | solution.py:375
  89.9 12.2 %collective-permute-start.23 = (f32[864,128]{1,0:T(8,128)S(1)}, f32[864,128]{1,0:T(8,128)S(1)}, u32[]{:S(2)}, u32[]{:S(2)}) collective-permute-start(f32[864,128]{1,0:T(8,128)S(1)} %shard_map.87.refs_3_), channel_id=1, source_target_pairs={{0,8},{1,9},{2,10},{3,11},{4,12},{5,13},{6,14},{7,15},{8,0},{9,1},... | collective-permute-start | bytes 1327112 | tf_op jit(solution)/shard_map/ppermute | solution.py:25

commit v10 on v9

--- a/solution.py
+++ b/solution.py
@@ -288,8 +288,9 @@
         finish(grad_two, grad_one, False)
 
 
-def call(kernel, outs, scratch=(), scalars=0, flops=0, inside=True):
+def call(kernel, outs, scratch=(), scalars=0, flops=0, inside=True, after=0):
     def wrapped(*refs):
+        refs = refs[: len(refs) - len(outs) - len(scratch) - after] + refs[len(refs) - len(outs) - len(scratch) :]
         if scalars:
             kernel([ref[0] for ref in refs[:scalars]], *refs[scalars:])
         else:
@@ -297,7 +298,8 @@
 
     def run(*operands):
         specs = [pl.BlockSpec(memory_space=pltpu.SMEM)] * scalars
-        specs += [pl.BlockSpec(memory_space=pltpu.VMEM)] * (len(operands) - scalars)
+        specs += [pl.BlockSpec(memory_space=pltpu.VMEM)] * (len(operands) - scalars - after)
+        specs += [pl.BlockSpec(memory_space=pl.ANY)] * after
         moved = sum(o.size * o.dtype.itemsize for o in operands)
         moved += sum(math.prod(o.shape) * o.dtype.itemsize for o in outs)
         return pl.pallas_call(
@@ -387,7 +389,22 @@
         near, mid, far = [xor_permute(part, m) for m in masks]
         part = (part + near) + (mid + far)
     pieces = [part] + [xor_permute(part, 16 * d) for d in range(1, 4)]
-    (own,) = call(join_kernel, [half], scalars=3)(*place, *pieces)
+    cuts = (0, tile_y // 4, 3 * tile_y // 4, tile_y)
+
+    def rows_b(k):
+        return [jax.ShapeDtypeStruct((tile_x, cuts[k + 1] - cuts[k], chans, tile_z), BF16)]
+
+    piece, pre_pad = call(
+        branch_first_kernel, rows_b(0) + [pad_b], scalars=3, flops=flops // 4
+    )(*place, mask_f, w_branch, masked_grad, pre_grad, *pre_xr, *pre_yr)
+    parts_y = [piece]
+    for k in (1, 2):
+        kernel = functools.partial(branch_next_kernel, first=cuts[k])
+        parts_y += call(kernel, rows_b(k), flops=flops // 4)(mask_f, w_branch, masked_grad, pre_pad)
+    grad_features = jnp.transpose(jnp.concatenate(parts_y, axis=1), (2, 0, 1, 3))
+    (own,) = call(join_kernel, [half], scalars=3, after=1)(
+        *place, *pieces, grad_features
+    )
     other = xor_permute(own, 8)
     grad_shape = jax.ShapeDtypeStruct((3, 3, 3, chans, chans), F32)
 
@@ -400,19 +417,6 @@
         inside=False,
     )(*place, mine, other)
 
-    cuts = (0, tile_y // 4, tile_y // 2, tile_y)
-
-    def rows_b(k):
-        return [jax.ShapeDtypeStruct((tile_x, cuts[k + 1] - cuts[k], chans, tile_z), BF16)]
-
-    piece, pre_pad = call(
-        branch_first_kernel, rows_b(0) + [pad_b], scalars=3, flops=flops // 4
-    )(*place, mask_f, w_branch, masked_grad, pre_grad, *pre_xr, *pre_yr)
-    pieces = [piece]
-    for k in (1, 2):
-        kernel = functools.partial(branch_next_kernel, first=cuts[k])
-        pieces += call(kernel, rows_b(k), flops=flops // 4 * k)(mask_f, w_branch, masked_grad, pre_pad)
-    grad_features = jnp.transpose(jnp.concatenate(pieces, axis=1), (2, 0, 1, 3))
     return grad_features, grad_one, grad_two
 
 

time: 104 us -> 96.5 us (0.928)
  the two profiles are of different devices: /device:TPU:15 before, /device:TPU:1 now
where the time goes in v10:
time: 96.5 us; the launch traced here: 95.1 us
  starting transfers between devices  41.8 us (43%)
  Pallas kernels  21.8 us (23%)
  waiting for transfers between devices  20.7 us (21%)
  other arithmetic  6.53 us (7%)
  local copies, waits for them, and re-layouts  3.11 us (3%)
  between operations  1.12 us (1%)
    ppermute x14, starting transfers between devices, xor_permute(): return lax.ppermute(value, AXES, [(i, i ^ mask) for i in range(total)])  23.2 us
    pallas_call x14, Pallas kernels, run(): pl.pallas_call(wrapped, out_shape=tuple(outs), in_specs=specs, out_specs=...  21.8 us
    ppermute x14, waiting for transfers between devices, xor_permute(): return lax.ppermute(value, AXES, [(i, i ^ mask) for i in range(total)])  10.9 us
    ppermute x1, waiting for transfers between devices, body(): in_even = lax.ppermute(sends[0], 'gy', even)  8.66 us
    ppermute x3, starting transfers between devices, swap(): lax.ppermute(value_odd, axis, odd)  5.83 us
    ppermute x1, starting transfers between devices, body(): in_even = lax.ppermute(sends[0], 'gy', even)  4.76 us
    ppermute x1, starting transfers between devices, body(): pre_even = lax.ppermute(pre_sends[0], 'gy', even)  3.68 us
    transpose x1, other arithmetic, body(): masked_in = jnp.transpose(features * mask_b[:, None], (1, 2, 0, 3))  3.27 us
  transfers between devices with their start and end apart: 24, of which 10 were waited for; matrix products, arithmetic and copies ran while one was open for 6% of the time, Pallas kernels for 10%

profile of v10, /device:TPU:1, one launch (start us, length us, event | category | flops | bytes accessed | tf_op | source)
XLA Modules:
  0.0 95.1 jit_solution(40421425072003957)
XLA Ops:
  0.7 0.8 convert_bitcast_fusion
  1.4 0.1 broadcast_in_dim.8
  1.5 0.1 convert_element_type.32
  1.6 1.2 %constant_dynamic-slice_fusion = (bf16[64,1,8,128]{3,2,1,0:T(8,128)(2,1)S(1)}, bf16[64,1,8,128]{3,2,1,0:T(8,128)(2,1)S(1)}, bf16[64,1,8,128]{3,2,1,0:T(8,128)(2,1)S(1)}, bf16[64,1,8,128]{3,2,1,0:T(8,128)(2,1)S(1)}) fusion(bf16[64,8,8,128]{3,2,1,0:T(8,128)(2,1)} %param.6, s32[]{:T(128)S(6)} %select_n.10, s32[]{:T(128)S(6)} %select_n.9, ...), kind=kLoop, calls=%fused_computation.18 | loop fusion | bytes 1048584 | tf_op jit(solution)/shard_map/jit(dynamic_index_in_dim)/dynamic_slice | solution.py:332
  2.7 0.1 fusion.3
  2.8 0.7 pad_maximum_fusion
  3.6 1.4 %collective-permute-start = (bf16[2,8,64,128]{3,2,1,0:T(8,128)(2,1)}, bf16[2,8,64,128]{3,2,1,0:T(8,128)(2,1)S(1)}, u32[]{:S(2)}, u32[]{:S(2)}) collective-permute-start(bf16[2,8,64,128]{3,2,1,0:T(8,128)(2,1)} %pad_maximum_fusion), channel_id=1, source_target_pairs={{0,8},{8,0},{16,24},{24,16},{32,40},{40,32},{48,56},{56,48},{64,72... | collective-permute-start | bytes 786440 | tf_op jit(solution)/shard_map/ppermute | solution.py:30
  4.9 0.7 pad_maximum_fusion.1
  5.7 3.1 %collective-permute-start.1 = (bf16[2,8,64,128]{3,2,1,0:T(8,128)(2,1)}, bf16[2,8,64,128]{3,2,1,0:T(8,128)(2,1)S(1)}, u32[]{:S(2)}, u32[]{:S(2)}) collective-permute-start(bf16[2,8,64,128]{3,2,1,0:T(8,128)(2,1)} %pad_maximum_fusion.1), channel_id=1, source_target_pairs={{8,16},{16,8},{24,32},{32,24},{40,48},{48,40},{56,64},{64,56},{72,... | collective-permute-start | bytes 786440 | tf_op jit(solution)/shard_map/ppermute | solution.py:30
  8.8 0.3 shard_map.76
  9.1 3.3 %fusion = (bf16[8,8,64,128]{3,2,1,0:T(8,128)(2,1)S(1)}, bf16[8,8,64,128]{3,2,1,0:T(8,128)(2,1)S(1)}) fusion(bf16[64,8,8,128]{3,2,1,0:T(8,128)(2,1)} %param.5, bf16[128]{0:T(256)(128)(2,1)S(1)} %convert_element_type.32, bf16[64,8,8,128]{3,2,1,0:T(8,128)(2,1)} %param.6), kind=kLoop, calls=%fused_computation.2 | loop fusion | flops 1048576 | bytes 4194560 | tf_op jit(solution)/shard_map/transpose | solution.py:336
  12.4 1.2 %collective-permute-done.1.refs_6_.refs_7_ = bf16[2,8,64,128]{3,2,1,0:T(8,128)(2,1)S(1)} collective-permute-done((bf16[2,8,64,128]{3,2,1,0:T(8,128)(2,1)}, bf16[2,8,64,128]{3,2,1,0:T(8,128)(2,1)S(1)}, u32[]{:S(2)}, u32[]{:S(2)}) %collective-permute-start.1) | collective-permute-done | bytes 262176 | tf_op jit(solution)/shard_map/ppermute | solution.py:30
  13.6 0.8 shard_map.77
  14.3 0.7 copy-done.3
  15.0 1.3 %collective-permute-start.3 = (bf16[10,64,128]{2,1,0:T(8,128)(2,1)}, bf16[10,64,128]{2,1,0:T(8,128)(2,1)}, u32[]{:S(2)}, u32[]{:S(2)}) collective-permute-start(bf16[10,64,128]{2,1,0:T(8,128)(2,1)} %get-tuple-element.37), channel_id=1, source_target_pairs={{1,2},{2,1},{3,4},{4,3},{5,6},{6,5},{9,10},{10,9},{11,12},{12,11},... | collective-permute-start | bytes 491528 | tf_op jit(solution)/shard_map/ppermute | solution.py:356
  16.3 4.8 %collective-permute-start.2 = (bf16[10,64,128]{2,1,0:T(8,128)(2,1)}, bf16[10,64,128]{2,1,0:T(8,128)(2,1)}, u32[]{:S(2)}, u32[]{:S(2)}) collective-permute-start(bf16[10,64,128]{2,1,0:T(8,128)(2,1)} %get-tuple-element.36), channel_id=1, source_target_pairs={{0,1},{1,0},{2,3},{3,2},{4,5},{5,4},{6,7},{7,6},{8,9},{9,8},{10,11... | collective-permute-start | bytes 491528 | tf_op jit(solution)/shard_map/ppermute | solution.py:353
  21.1 0.1 broadcast_in_dim.7
  21.1 0.1 convert_element_type.29.refs_3_.refs_0_
  21.2 0.1 collective-permute-start.4
  21.3 0.7 collective-permute-start.5
  22.0 0.0 collective-permute-done.3.refs_9_
  22.0 8.7 %collective-permute-done.2.refs_8_ = bf16[10,64,128]{2,1,0:T(8,128)(2,1)} collective-permute-done((bf16[10,64,128]{2,1,0:T(8,128)(2,1)}, bf16[10,64,128]{2,1,0:T(8,128)(2,1)}, u32[]{:S(2)}, u32[]{:S(2)}) %collective-permute-start.2) | collective-permute-done | bytes 163872 | tf_op jit(solution)/shard_map/ppermute | solution.py:353
  30.7 4.7 %shard_map.78 = (bf16[8,8,192,128]{3,2,1,0:T(8,128)(2,1)S(1)}, f32[8,8,64,128]{3,2,1,0:T(8,128)S(1)}, bf16[10,10,64,128]{3,2,1,0:T(8,128)(2,1)S(1)}) custom-call(s32[1]{0:T(128)} %bitcast.refs_0_, s32[1]{0:T(128)} %bitcast.1.refs_1_, s32[1]{0:T(128)} %bitcast.2.refs_2_, f32[1,128]{1,0:T(1,128)S(1)} %convert_element_type.29.refs_3_.refs_0_, ...), custom_call_target="tpu_custom_call" | custom-call | flops 1811939328 | bytes 9003532 | tf_op jit(solution)/shard_map/pallas_call | solution.py:305
  35.4 0.0 collective-permute-done.4.refs_8_
  35.4 0.0 collective-permute-done.5.refs_9_
  35.4 3.2 %shard_map.79 = (bf16[8,8,64,128]{3,2,1,0:T(8,128)(2,1)S(1)}, bf16[1,8,64,128]{3,2,1,0:T(8,128)(2,1)S(1)}, bf16[1,8,64,128]{3,2,1,0:T(8,128)(2,1)S(1)}, bf16[10,10,64,128]{3,2,1,0:T(8,128)(2,1)S(1)}) custom-call(s32[1]{0:T(128)} %bitcast.refs_0_, s32[1]{0:T(128)} %bitcast.1.refs_1_, s32[1]{0:T(128)} %bitcast.2.refs_2_, ...), custom_call_target="tpu_custom_call" | custom-call | flops 1811939328 | bytes 7168012 | tf_op jit(solution)/shard_map/pallas_call | solution.py:305
  38.6 3.2 %shard_map.84.refs_5_ = f32[864,128]{1,0:T(8,128)S(1)} custom-call(bf16[10,10,64,128]{3,2,1,0:T(8,128)(2,1)S(1)} %get-tuple-element.49.refs_0_, bf16[8,8,192,128]{3,2,1,0:T(8,128)(2,1)S(1)} %get-tuple-element.50.refs_1_), custom_call_target="tpu_custom_call" | custom-call | flops 1811939328 | bytes 5226496 | tf_op jit(solution)/shard_map/pallas_call | solution.py:305
  41.8 3.9 %shard_map.85 = (f32[864,128]{1,0:T(8,128)S(1)}, f32[864,128]{1,0:T(8,128)S(1)}) custom-call(s32[1]{0:T(128)} %bitcast.refs_0_, s32[1]{0:T(128)} %bitcast.1.refs_1_, s32[1]{0:T(128)} %bitcast.2.refs_2_, bf16[10,10,64,128]{3,2,1,0:T(8,128)(2,1)S(1)} %get-tuple-element.48.refs_3_, bf16[8,8,64,128]{3,2,1,0:T(8,128)(2,1)S(1)} %get-tuple-element.41.refs_3_.refs_6_.refs_4_, ...), custom_call_target="tpu_custom_call" | custom-call | flops 1811939328 | bytes 4014092 | tf_op jit(solution)/shard_map/pallas_call | solution.py:305
  45.7 0.1 collective-permute-start.10
  45.7 1.8 %collective-permute-done.10.refs_4_ = f32[864,128]{1,0:T(8,128)S(1)} collective-permute-done((f32[864,128]{1,0:T(8,128)S(1)}, f32[864,128]{1,0:T(8,128)S(1)}, u32[]{:S(2)}, u32[]{:S(2)}) %collective-permute-start.10) | collective-permute-done | bytes 442400 | tf_op jit(solution)/shard_map/ppermute | solution.py:25
  47.6 3.6 %collective-permute-start.11 = (f32[216,128]{1,0:T(8,128)S(1)}, f32[216,128]{1,0:T(8,128)S(1)}, u32[]{:S(2)}, u32[]{:S(2)}) collective-permute-start(f32[216,128]{1,0:T(8,128)S(1)} %get-tuple-element.54), channel_id=1, source_target_pairs={{0,16},{1,17},{2,18},{3,19},{4,20},{5,21},{6,22},{7,23},{8,24},{9,... | collective-permute-start | bytes 331784 | tf_op jit(solution)/shard_map/ppermute | solution.py:25
  51.2 2.9 %collective-permute-start.12 = (f32[216,128]{1,0:T(8,128)S(1)}, f32[216,128]{1,0:T(8,128)S(1)}, u32[]{:S(2)}, u32[]{:S(2)}) collective-permute-start(f32[216,128]{1,0:T(8,128)S(1)} %get-tuple-element.55), channel_id=1, source_target_pairs={{0,32},{1,33},{2,34},{3,35},{4,36},{5,37},{6,38},{7,39},{8,40},{9,... | collective-permute-start | bytes 331784 | tf_op jit(solution)/shard_map/ppermute | solution.py:25
  54.0 0.0 collective-permute-start.13
  54.1 0.7 collective-permute-start.6
  54.7 2.1 %collective-permute-start.7 = (bf16[1,8,64,128]{3,2,1,0:T(8,128)(2,1)S(1)}, bf16[1,8,64,128]{3,2,1,0:T(8,128)(2,1)S(1)}, u32[]{:S(2)}, u32[]{:S(2)}) collective-permute-start(bf16[1,8,64,128]{3,2,1,0:T(8,128)(2,1)S(1)} %get-tuple-element.43), channel_id=1, source_target_pairs={{8,16},{16,8},{24,32},{32,24},{40,48},{48,40},{56,64},{64,56},{72,... | collective-permute-start | bytes 393224 | tf_op jit(solution)/shard_map/ppermute | solution.py:30
  56.8 2.6 %collective-permute-done.12 = f32[216,128]{1,0:T(8,128)S(1)} collective-permute-done((f32[216,128]{1,0:T(8,128)S(1)}, f32[216,128]{1,0:T(8,128)S(1)}, u32[]{:S(2)}, u32[]{:S(2)}) %collective-permute-start.12) | collective-permute-done | bytes 110624 | tf_op jit(solution)/shard_map/ppermute | solution.py:25
  59.5 2.5 %collective-permute-done.13 = f32[216,128]{1,0:T(8,128)S(1)} collective-permute-done((f32[216,128]{1,0:T(8,128)S(1)}, f32[216,128]{1,0:T(8,128)S(1)}, u32[]{:S(2)}, u32[]{:S(2)}) %collective-permute-start.13) | collective-permute-done | bytes 110624 | tf_op jit(solution)/shard_map/ppermute | solution.py:25
  62.0 1.2 %collective-permute-start.16 = (f32[216,128]{1,0:T(8,128)S(1)}, f32[216,128]{1,0:T(8,128)S(1)}, u32[]{:S(2)}, u32[]{:S(2)}) collective-permute-start(f32[216,128]{1,0:T(8,128)S(1)} %add_add_fusion.2), channel_id=1, source_target_pairs={{0,6},{1,7},{2,4},{3,5},{4,2},{5,3},{6,0},{7,1},{8,14},{9,15},{10,... | collective-permute-start | bytes 331784 | tf_op jit(solution)/shard_map/ppermute | solution.py:25
  63.2 2.0 %collective-permute-start.15 = (f32[216,128]{1,0:T(8,128)S(1)}, f32[216,128]{1,0:T(8,128)S(1)}, u32[]{:S(2)}, u32[]{:S(2)}) collective-permute-start(f32[216,128]{1,0:T(8,128)S(1)} %add_add_fusion.2), channel_id=1, source_target_pairs={{0,4},{1,5},{2,6},{3,7},{4,0},{5,1},{6,2},{7,3},{8,12},{9,13},{10,... | collective-permute-start | bytes 331784 | tf_op jit(solution)/shard_map/ppermute | solution.py:25
  65.2 0.2 collective-permute-start.14
  65.4 3.7 %collective-permute-start.8 = (bf16[10,64,128]{2,1,0:T(8,128)(2,1)S(1)}, bf16[10,64,128]{2,1,0:T(8,128)(2,1)S(1)}, u32[]{:S(2)}, u32[]{:S(2)}) collective-permute-start(bf16[10,64,128]{2,1,0:T(8,128)(2,1)S(1)} %get-tuple-element.44), channel_id=1, source_target_pairs={{0,1},{1,0},{2,3},{3,2},{4,5},{5,4},{6,7},{7,6},{8,9},{9,8},{10,11... | collective-permute-start | bytes 491528 | tf_op jit(solution)/shard_map/ppermute | solution.py:376
  69.1 0.8 collective-permute-start.9
  70.0 0.0 collective-permute-done.14
  70.0 4.3 %collective-permute-start.19 = (f32[216,128]{1,0:T(8,128)S(1)}, f32[216,128]{1,0:T(8,128)S(1)}, u32[]{:S(2)}, u32[]{:S(2)}) collective-permute-start(f32[216,128]{1,0:T(8,128)S(1)} %add_add_fusion.1), channel_id=1, source_target_pairs={{0,65},{1,64},{2,67},{3,66},{4,69},{5,68},{6,71},{7,70},{8,73},{9,... | collective-permute-start | bytes 331784 | tf_op jit(solution)/shard_map/ppermute | solution.py:25
  74.3 0.7 collective-permute-start.18
  75.0 0.6 collective-permute-start.17
  75.6 1.3 %shard_map.81 = (bf16[8,2,64,128]{3,2,1,0:T(8,128)(2,1)S(1)}, bf16[10,10,64,128]{3,2,1,0:T(8,128)(2,1)S(1)}) custom-call(s32[1]{0:T(128)} %bitcast.refs_0_, s32[1]{0:T(128)} %bitcast.1.refs_1_, s32[1]{0:T(128)} %bitcast.2.refs_2_, f32[1,128]{1,0:T(1,128)S(1)} %convert_element_type.29.refs_3_.refs_0_, bf16[192,576]{1,0:T(8,128)(2,1)S(1)} %get-tuple-element.31.refs_4_.refs_1_, ...), custom_call_target="tpu_custom_call" | custom-call | flops 452984832 | bytes 4809228 | tf_op jit(solution)/shard_map/pallas_call | solution.py:305
  76.9 0.3 copy.23
  77.2 1.8 %shard_map.82 = bf16[8,4,64,128]{3,2,1,0:T(8,128)(2,1)S(1)} custom-call(f32[1,128]{1,0:T(1,128)S(1)} %convert_element_type.29.refs_3_.refs_0_, bf16[192,576]{1,0:T(8,128)(2,1)S(1)} %get-tuple-element.31.refs_4_.refs_1_, bf16[8,8,64,128]{3,2,1,0:T(8,128)(2,1)S(1)} %get-tuple-element.68.refs_4_.refs_5_.refs_2_, ...), custom_call_target="tpu_custom_call" | custom-call | flops 452984832 | bytes 3432960 | tf_op jit(solution)/shard_map/pallas_call | solution.py:305
  78.9 0.4 copy.24
  79.3 1.1 %shard_map.83 = bf16[8,2,64,128]{3,2,1,0:T(8,128)(2,1)S(1)} custom-call(f32[1,128]{1,0:T(1,128)S(1)} %convert_element_type.29.refs_3_.refs_0_, bf16[192,576]{1,0:T(8,128)(2,1)S(1)} %get-tuple-element.31.refs_4_.refs_1_, bf16[8,8,64,128]{3,2,1,0:T(8,128)(2,1)S(1)} %get-tuple-element.68.refs_4_.refs_5_.refs_2_, ...), custom_call_target="tpu_custom_call" | custom-call | flops 452984832 | bytes 3170816 | tf_op jit(solution)/shard_map/pallas_call | solution.py:305
  80.5 0.3 copy.25
  80.8 0.4 collective-permute-done.17
  81.2 1.1 %collective-permute-start.22 = (f32[216,128]{1,0:T(8,128)S(1)}, f32[216,128]{1,0:T(8,128)S(1)}, u32[]{:S(2)}, u32[]{:S(2)}) collective-permute-start(f32[216,128]{1,0:T(8,128)S(1)} %add_add_fusion.refs_3_), channel_id=1, source_target_pairs={{0,48},{1,49},{2,50},{3,51},{4,52},{5,53},{6,54},{7,55},{8,56},{9,... | collective-permute-start | bytes 331784 | tf_op jit(solution)/shard_map/ppermute | solution.py:25
  82.3 2.3 %collective-permute-start.20 = (f32[216,128]{1,0:T(8,128)S(1)}, f32[216,128]{1,0:T(8,128)S(1)}, u32[]{:S(2)}, u32[]{:S(2)}) collective-permute-start(f32[216,128]{1,0:T(8,128)S(1)} %add_add_fusion.refs_3_), channel_id=1, source_target_pairs={{0,16},{1,17},{2,18},{3,19},{4,20},{5,21},{6,22},{7,23},{8,24},{9,... | collective-permute-start | bytes 331784 | tf_op jit(solution)/shard_map/ppermute | solution.py:25
  84.6 0.9 maximum_bitcast_fusion.refs_7_
  85.5 0.0 copy-start
  85.5 0.7 collective-permute-done.22.refs_6_
  86.1 1.3 %collective-permute-done.21.refs_5_ = f32[216,128]{1,0:T(8,128)S(1)} collective-permute-done((f32[216,128]{1,0:T(8,128)S(1)}, f32[216,128]{1,0:T(8,128)S(1)}, u32[]{:S(2)}, u32[]{:S(2)}) %collective-permute-start.21) | collective-permute-done | bytes 110624 | tf_op jit(solution)/shard_map/ppermute | solution.py:25
  87.4 0.5 collective-permute-done.20.refs_4_
  87.9 4.4 %collective-permute-start.23 = (f32[864,128]{1,0:T(8,128)S(1)}, f32[864,128]{1,0:T(8,128)S(1)}, u32[]{:S(2)}, u32[]{:S(2)}) collective-permute-start(f32[864,128]{1,0:T(8,128)S(1)} %shard_map.87.refs_3_), channel_id=1, source_target_pairs={{0,8},{1,9},{2,10},{3,11},{4,12},{5,13},{6,14},{7,15},{8,0},{9,1},... | collective-permute-start | bytes 1327112 | tf_op jit(solution)/shard_map/ppermute | solution.py:25
  92.3 0.4 shard_map.88.refs_3_
  92.7 1.0 %collective-permute-done.23.refs_4_ = f32[864,128]{1,0:T(8,128)S(1)} collective-permute-done((f32[864,128]{1,0:T(8,128)S(1)}, f32[864,128]{1,0:T(8,128)S(1)}, u32[]{:S(2)}, u32[]{:S(2)}) %collective-permute-start.23) | collective-permute-done | bytes 442400 | tf_op jit(solution)/shard_map/ppermute | solution.py:25
  93.7 1.2 %shard_map.89 = (f32[3,3,3,64,64]{4,3,2,1,0:T(8,128)}, f32[3,3,3,64,64]{4,3,2,1,0:T(8,128)}) custom-call(s32[1]{0:T(128)} %bitcast.refs_0_, s32[1]{0:T(128)} %bitcast.1.refs_1_, s32[1]{0:T(128)} %bitcast.2.refs_2_, f32[3,3,3,64,64]{4,3,2,1,0:T(8,128)S(1)} %shard_map.88.refs_3_, f32[864,128]{1,0:T(8,128)S(1)} %collective-permute-done.23.refs_4_), custom_call_target="tpu_custom_call" | custom-call | bytes 1769484 | tf_op jit(solution)/shard_map/pallas_call | solution.py:305
  (23 shorter events, 0.2 us)
Async XLA Ops:
  0.6 8.2 %copy-start.2 = (bf16[3,3,3,64,64]{4,3,2,1,0:T(8,128)(2,1)S(1)}, bf16[3,3,3,64,64]{4,3,2,1,0:T(8,128)(2,1)}, u32[]{:S(2)}) copy-start(bf16[3,3,3,64,64]{4,3,2,1,0:T(8,128)(2,1)} %refs_1_.1) | copy-start | bytes 663556
  0.6 8.2 %copy-start.1 = (bf16[3,3,3,64,64]{4,3,2,1,0:T(8,128)(2,1)S(1)}, bf16[3,3,3,64,64]{4,3,2,1,0:T(8,128)(2,1)}, u32[]{:S(2)}) copy-start(bf16[3,3,3,64,64]{4,3,2,1,0:T(8,128)(2,1)} %refs_0_.1) | copy-start | bytes 663556
  3.6 8.8 %collective-permute-start = (bf16[2,8,64,128]{3,2,1,0:T(8,128)(2,1)}, bf16[2,8,64,128]{3,2,1,0:T(8,128)(2,1)S(1)}, u32[]{:S(2)}, u32[]{:S(2)}) collective-permute-start(bf16[2,8,64,128]{3,2,1,0:T(8,128)(2,1)} %pad_maximum_fusion), channel_id=1, source_target_pairs={{0,8},{8,0},{16,24},{24,16},{32,40},{40,32},{48,56},{56,48},{64,72... | collective-permute-start | bytes 786440 | tf_op jit(solution)/shard_map/ppermute | solution.py:30
  5.7 7.9 %collective-permute-start.1 = (bf16[2,8,64,128]{3,2,1,0:T(8,128)(2,1)}, bf16[2,8,64,128]{3,2,1,0:T(8,128)(2,1)S(1)}, u32[]{:S(2)}, u32[]{:S(2)}) collective-permute-start(bf16[2,8,64,128]{3,2,1,0:T(8,128)(2,1)} %pad_maximum_fusion.1), channel_id=1, source_target_pairs={{8,16},{16,8},{24,32},{32,24},{40,48},{48,40},{56,64},{64,56},{72,... | collective-permute-start | bytes 786440 | tf_op jit(solution)/shard_map/ppermute | solution.py:30
  14.3 0.7 copy-start.3
  15.0 7.0 %collective-permute-start.3 = (bf16[10,64,128]{2,1,0:T(8,128)(2,1)}, bf16[10,64,128]{2,1,0:T(8,128)(2,1)}, u32[]{:S(2)}, u32[]{:S(2)}) collective-permute-start(bf16[10,64,128]{2,1,0:T(8,128)(2,1)} %get-tuple-element.37), channel_id=1, source_target_pairs={{1,2},{2,1},{3,4},{4,3},{5,6},{6,5},{9,10},{10,9},{11,12},{12,11},... | collective-permute-start | bytes 491528 | tf_op jit(solution)/shard_map/ppermute | solution.py:356
  16.3 14.4 %collective-permute-start.2 = (bf16[10,64,128]{2,1,0:T(8,128)(2,1)}, bf16[10,64,128]{2,1,0:T(8,128)(2,1)}, u32[]{:S(2)}, u32[]{:S(2)}) collective-permute-start(bf16[10,64,128]{2,1,0:T(8,128)(2,1)} %get-tuple-element.36), channel_id=1, source_target_pairs={{0,1},{1,0},{2,3},{3,2},{4,5},{5,4},{6,7},{7,6},{8,9},{9,8},{10,11... | collective-permute-start | bytes 491528 | tf_op jit(solution)/shard_map/ppermute | solution.py:353
  21.2 14.2 %collective-permute-start.4 = (bf16[10,64,128]{2,1,0:T(8,128)(2,1)}, bf16[10,64,128]{2,1,0:T(8,128)(2,1)S(1)}, u32[]{:S(2)}, u32[]{:S(2)}) collective-permute-start(bf16[10,64,128]{2,1,0:T(8,128)(2,1)} %copy-done.3), channel_id=1, source_target_pairs={{0,1},{1,0},{2,3},{3,2},{4,5},{5,4},{6,7},{7,6},{8,9},{9,8},{10,11... | collective-permute-start | bytes 491528 | tf_op jit(solution)/shard_map/ppermute | solution.py:30
  21.3 14.1 %collective-permute-start.5 = (bf16[10,64,128]{2,1,0:T(8,128)(2,1)S(1)}, bf16[10,64,128]{2,1,0:T(8,128)(2,1)S(1)}, u32[]{:S(2)}, u32[]{:S(2)}) collective-permute-start(bf16[10,64,128]{2,1,0:T(8,128)(2,1)S(1)} %get-tuple-element.40), channel_id=1, source_target_pairs={{1,2},{2,1},{3,4},{4,3},{5,6},{6,5},{9,10},{10,9},{11,12},{12,11},... | collective-permute-start | bytes 491528 | tf_op jit(solution)/shard_map/ppermute | solution.py:30
  45.7 1.9 %collective-permute-start.10 = (f32[864,128]{1,0:T(8,128)S(1)}, f32[864,128]{1,0:T(8,128)S(1)}, u32[]{:S(2)}, u32[]{:S(2)}) collective-permute-start(f32[864,128]{1,0:T(8,128)S(1)} %get-tuple-element.52), channel_id=1, source_target_pairs={{0,8},{1,9},{2,10},{3,11},{4,12},{5,13},{6,14},{7,15},{8,0},{9,1},... | collective-permute-start | bytes 1327112 | tf_op jit(solution)/shard_map/ppermute | solution.py:25
  47.6 9.2 %collective-permute-start.11 = (f32[216,128]{1,0:T(8,128)S(1)}, f32[216,128]{1,0:T(8,128)S(1)}, u32[]{:S(2)}, u32[]{:S(2)}) collective-permute-start(f32[216,128]{1,0:T(8,128)S(1)} %get-tuple-element.54), channel_id=1, source_target_pairs={{0,16},{1,17},{2,18},{3,19},{4,20},{5,21},{6,22},{7,23},{8,24},{9,... | collective-permute-start | bytes 331784 | tf_op jit(solution)/shard_map/ppermute | solution.py:25
  51.2 8.3 %collective-permute-start.12 = (f32[216,128]{1,0:T(8,128)S(1)}, f32[216,128]{1,0:T(8,128)S(1)}, u32[]{:S(2)}, u32[]{:S(2)}) collective-permute-start(f32[216,128]{1,0:T(8,128)S(1)} %get-tuple-element.55), channel_id=1, source_target_pairs={{0,32},{1,33},{2,34},{3,35},{4,36},{5,37},{6,38},{7,39},{8,40},{9,... | collective-permute-start | bytes 331784 | tf_op jit(solution)/shard_map/ppermute | solution.py:25
  54.0 8.0 %collective-permute-start.13 = (f32[216,128]{1,0:T(8,128)S(1)}, f32[216,128]{1,0:T(8,128)S(1)}, u32[]{:S(2)}, u32[]{:S(2)}) collective-permute-start(f32[216,128]{1,0:T(8,128)S(1)} %get-tuple-element.56), channel_id=1, source_target_pairs={{0,48},{1,49},{2,50},{3,51},{4,52},{5,53},{6,54},{7,55},{8,56},{9,... | collective-permute-start | bytes 331784 | tf_op jit(solution)/shard_map/ppermute | solution.py:25
  54.1 11.3 %collective-permute-start.6 = (bf16[1,8,64,128]{3,2,1,0:T(8,128)(2,1)S(1)}, bf16[1,8,64,128]{3,2,1,0:T(8,128)(2,1)S(1)}, u32[]{:S(2)}, u32[]{:S(2)}) collective-permute-start(bf16[1,8,64,128]{3,2,1,0:T(8,128)(2,1)S(1)} %get-tuple-element.42), channel_id=1, source_target_pairs={{0,8},{8,0},{16,24},{24,16},{32,40},{40,32},{48,56},{56,48},{64,72... | collective-permute-start | bytes 393224 | tf_op jit(solution)/shard_map/ppermute | solution.py:30
  54.7 10.6 %collective-permute-start.7 = (bf16[1,8,64,128]{3,2,1,0:T(8,128)(2,1)S(1)}, bf16[1,8,64,128]{3,2,1,0:T(8,128)(2,1)S(1)}, u32[]{:S(2)}, u32[]{:S(2)}) collective-permute-start(bf16[1,8,64,128]{3,2,1,0:T(8,128)(2,1)S(1)} %get-tuple-element.43), channel_id=1, source_target_pairs={{8,16},{16,8},{24,32},{32,24},{40,48},{48,40},{56,64},{64,56},{72,... | collective-permute-start | bytes 393224 | tf_op jit(solution)/shard_map/ppermute | solution.py:30
  62.0 7.9 %collective-permute-start.16 = (f32[216,128]{1,0:T(8,128)S(1)}, f32[216,128]{1,0:T(8,128)S(1)}, u32[]{:S(2)}, u32[]{:S(2)}) collective-permute-start(f32[216,128]{1,0:T(8,128)S(1)} %add_add_fusion.2), channel_id=1, source_target_pairs={{0,6},{1,7},{2,4},{3,5},{4,2},{5,3},{6,0},{7,1},{8,14},{9,15},{10,... | collective-permute-start | bytes 331784 | tf_op jit(solution)/shard_map/ppermute | solution.py:25
  63.2 6.7 %collective-permute-start.15 = (f32[216,128]{1,0:T(8,128)S(1)}, f32[216,128]{1,0:T(8,128)S(1)}, u32[]{:S(2)}, u32[]{:S(2)}) collective-permute-start(f32[216,128]{1,0:T(8,128)S(1)} %add_add_fusion.2), channel_id=1, source_target_pairs={{0,4},{1,5},{2,6},{3,7},{4,0},{5,1},{6,2},{7,3},{8,12},{9,13},{10,... | collective-permute-start | bytes 331784 | tf_op jit(solution)/shard_map/ppermute | solution.py:25
  65.2 4.8 %collective-permute-start.14 = (f32[216,128]{1,0:T(8,128)S(1)}, f32[216,128]{1,0:T(8,128)S(1)}, u32[]{:S(2)}, u32[]{:S(2)}) collective-permute-start(f32[216,128]{1,0:T(8,128)S(1)} %add_add_fusion.2), channel_id=1, source_target_pairs={{0,2},{1,3},{2,0},{3,1},{4,6},{5,7},{6,4},{7,5},{8,10},{9,11},{10,... | collective-permute-start | bytes 331784 | tf_op jit(solution)/shard_map/ppermute | solution.py:25
  65.4 10.2 %collective-permute-start.8 = (bf16[10,64,128]{2,1,0:T(8,128)(2,1)S(1)}, bf16[10,64,128]{2,1,0:T(8,128)(2,1)S(1)}, u32[]{:S(2)}, u32[]{:S(2)}) collective-permute-start(bf16[10,64,128]{2,1,0:T(8,128)(2,1)S(1)} %get-tuple-element.44), channel_id=1, source_target_pairs={{0,1},{1,0},{2,3},{3,2},{4,5},{5,4},{6,7},{7,6},{8,9},{9,8},{10,11... | collective-permute-start | bytes 491528 | tf_op jit(solution)/shard_map/ppermute | solution.py:376
  69.1 6.5 %collective-permute-start.9 = (bf16[10,64,128]{2,1,0:T(8,128)(2,1)S(1)}, bf16[10,64,128]{2,1,0:T(8,128)(2,1)S(1)}, u32[]{:S(2)}, u32[]{:S(2)}) collective-permute-start(bf16[10,64,128]{2,1,0:T(8,128)(2,1)S(1)} %get-tuple-element.45), channel_id=1, source_target_pairs={{1,2},{2,1},{3,4},{4,3},{5,6},{6,5},{9,10},{10,9},{11,12},{12,11},... | collective-permute-start | bytes 491528 | tf_op jit(solution)/shard_map/ppermute | solution.py:377
  70.0 10.7 %collective-permute-start.19 = (f32[216,128]{1,0:T(8,128)S(1)}, f32[216,128]{1,0:T(8,128)S(1)}, u32[]{:S(2)}, u32[]{:S(2)}) collective-permute-start(f32[216,128]{1,0:T(8,128)S(1)} %add_add_fusion.1), channel_id=1, source_target_pairs={{0,65},{1,64},{2,67},{3,66},{4,69},{5,68},{6,71},{7,70},{8,73},{9,... | collective-permute-start | bytes 331784 | tf_op jit(solution)/shard_map/ppermute | solution.py:25
  74.3 6.4 %collective-permute-start.18 = (f32[216,128]{1,0:T(8,128)S(1)}, f32[216,128]{1,0:T(8,128)S(1)}, u32[]{:S(2)}, u32[]{:S(2)}) collective-permute-start(f32[216,128]{1,0:T(8,128)S(1)} %add_add_fusion.1), channel_id=1, source_target_pairs={{0,64},{1,65},{2,66},{3,67},{4,68},{5,69},{6,70},{7,71},{8,72},{9,... | collective-permute-start | bytes 331784 | tf_op jit(solution)/shard_map/ppermute | solution.py:25
  75.0 6.2 %collective-permute-start.17 = (f32[216,128]{1,0:T(8,128)S(1)}, f32[216,128]{1,0:T(8,128)S(1)}, u32[]{:S(2)}, u32[]{:S(2)}) collective-permute-start(f32[216,128]{1,0:T(8,128)S(1)} %add_add_fusion.1), channel_id=1, source_target_pairs={{0,1},{1,0},{2,3},{3,2},{4,5},{5,4},{6,7},{7,6},{8,9},{9,8},{10,11... | collective-permute-start | bytes 331784 | tf_op jit(solution)/shard_map/ppermute | solution.py:25
  81.2 4.9 %collective-permute-start.22 = (f32[216,128]{1,0:T(8,128)S(1)}, f32[216,128]{1,0:T(8,128)S(1)}, u32[]{:S(2)}, u32[]{:S(2)}) collective-permute-start(f32[216,128]{1,0:T(8,128)S(1)} %add_add_fusion.refs_3_), channel_id=1, source_target_pairs={{0,48},{1,49},{2,50},{3,51},{4,52},{5,53},{6,54},{7,55},{8,56},{9,... | collective-permute-start | bytes 331784 | tf_op jit(solution)/shard_map/ppermute | solution.py:25
  82.3 5.1 %collective-permute-start.21 = (f32[216,128]{1,0:T(8,128)S(1)}, f32[216,128]{1,0:T(8,128)S(1)}, u32[]{:S(2)}, u32[]{:S(2)}) collective-permute-start(f32[216,128]{1,0:T(8,128)S(1)} %add_add_fusion.refs_3_), channel_id=1, source_target_pairs={{0,32},{1,33},{2,34},{3,35},{4,36},{5,37},{6,38},{7,39},{8,40},{9,... | collective-permute-start | bytes 331784 | tf_op jit(solution)/shard_map/ppermute | solution.py:25
  82.3 5.6 %collective-permute-start.20 = (f32[216,128]{1,0:T(8,128)S(1)}, f32[216,128]{1,0:T(8,128)S(1)}, u32[]{:S(2)}, u32[]{:S(2)}) collective-permute-start(f32[216,128]{1,0:T(8,128)S(1)} %add_add_fusion.refs_3_), channel_id=1, source_target_pairs={{0,16},{1,17},{2,18},{3,19},{4,20},{5,21},{6,22},{7,23},{8,24},{9,... | collective-permute-start | bytes 331784 | tf_op jit(solution)/shard_map/ppermute | solution.py:25
  85.5 9.5 %copy-start = (bf16[64,8,8,128]{3,2,1,0:T(8,128)(2,1)}, bf16[64,8,8,128]{3,2,1,0:T(8,128)(2,1)S(1)}, u32[]{:S(2)}) copy-start(bf16[64,8,8,128]{3,2,1,0:T(8,128)(2,1)S(1)} %maximum_bitcast_fusion.refs_7_) | copy-start | bytes 3145732
  87.9 5.8 %collective-permute-start.23 = (f32[864,128]{1,0:T(8,128)S(1)}, f32[864,128]{1,0:T(8,128)S(1)}, u32[]{:S(2)}, u32[]{:S(2)}) collective-permute-start(f32[864,128]{1,0:T(8,128)S(1)} %shard_map.87.refs_3_), channel_id=1, source_target_pairs={{0,8},{1,9},{2,10},{3,11},{4,12},{5,13},{6,14},{7,15},{8,0},{9,1},... | collective-permute-start | bytes 1327112 | tf_op jit(solution)/shard_map/ppermute | solution.py:25

commit v11 on v10

--- a/solution.py
+++ b/solution.py
@@ -107,7 +107,7 @@
                 emit(x, y + side, below + part[chans : 2 * chans] + above)
         return carry
 
-    lax.fori_loop(0, wide - 2, body, 0, unroll=4)
+    lax.fori_loop(0, wide - 2, body, 0, unroll=8)
 
 
 def weights_kernel(one, two, w_pre, w_act, w_branch):
@@ -178,7 +178,7 @@
         acc[...] += lax.dot_general(left, right, (((1,), (1,)), ((), ())), preferred_element_type=F32)
         return carry
 
-    lax.fori_loop(0, size_x, body, 0, unroll=4)
+    lax.fori_loop(0, size_x, body, 0, unroll=8)
 
 
 def pack_grad(dest, acc, chans):
@@ -195,7 +195,7 @@
         stack_row(stack, i, 0, source[i])
         return carry
 
-    lax.fori_loop(0, source.shape[0], body, 0, unroll=4)
+    lax.fori_loop(0, source.shape[0], body, 0, unroll=8)
 
 
 def grad_two_kernel(grad_pad, activ, packed, acc):

time: 96.5 us -> 94.8 us (0.982)
  Pallas kernels: 21.8 us -> 19.7 us
    pallas_call x14, Pallas kernels: 21.8 us -> 19.7 us  [run(): pl.pallas_call(wrapped, out_shape=tuple(outs), in_specs=specs, out_specs=...]
    ppermute x14, waiting for transfers between devices: 10.9 us -> 11.9 us  [xor_permute(): return lax.ppermute(value, AXES, [(i, i ^ mask) for i in range(total)])]
  transfers between devices with their start and end apart: 24 -> 24, of which waited for: 10 -> 10; matrix products, arithmetic and copies ran while one was open for 6% -> 6% of each run, Pallas kernels for 10% -> 9%
where the time goes in v11:
time: 94.8 us; the launch traced here: 93.6 us
  starting transfers between devices  41.6 us (44%)
  waiting for transfers between devices  21.5 us (23%)
  Pallas kernels  19.7 us (21%)
  other arithmetic  6.53 us (7%)
  local copies, waits for them, and re-layouts  3.11 us (3%)
  between operations  1.12 us (1%)
    ppermute x14, starting transfers between devices, xor_permute(): return lax.ppermute(value, AXES, [(i, i ^ mask) for i in range(total)])  23 us
    pallas_call x14, Pallas kernels, run(): pl.pallas_call(wrapped, out_shape=tuple(outs), in_specs=specs, out_specs=...  19.7 us
    ppermute x14, waiting for transfers between devices, xor_permute(): return lax.ppermute(value, AXES, [(i, i ^ mask) for i in range(total)])  11.9 us
    ppermute x1, waiting for transfers between devices, body(): in_even = lax.ppermute(sends[0], 'gy', even)  8.48 us
    ppermute x3, starting transfers between devices, swap(): lax.ppermute(value_odd, axis, odd)  6.01 us
    ppermute x1, starting transfers between devices, body(): in_even = lax.ppermute(sends[0], 'gy', even)  4.76 us
    ppermute x1, starting transfers between devices, body(): pre_even = lax.ppermute(pre_sends[0], 'gy', even)  3.69 us
    transpose x1, other arithmetic, body(): masked_in = jnp.transpose(features * mask_b[:, None], (1, 2, 0, 3))  3.27 us
  transfers between devices with their start and end apart: 24, of which 10 were waited for; matrix products, arithmetic and copies ran while one was open for 6% of the time, Pallas kernels for 9%

profile of v11, /device:TPU:1, one launch (start us, length us, event | category | flops | bytes accessed | tf_op | source)
XLA Modules:
  0.0 93.6 jit_solution(14080681247053474440)
XLA Ops:
  0.7 0.8 convert_bitcast_fusion
  1.4 0.1 broadcast_in_dim.8
  1.5 0.1 convert_element_type.32
  1.6 1.2 %constant_dynamic-slice_fusion = (bf16[64,1,8,128]{3,2,1,0:T(8,128)(2,1)S(1)}, bf16[64,1,8,128]{3,2,1,0:T(8,128)(2,1)S(1)}, bf16[64,1,8,128]{3,2,1,0:T(8,128)(2,1)S(1)}, bf16[64,1,8,128]{3,2,1,0:T(8,128)(2,1)S(1)}) fusion(bf16[64,8,8,128]{3,2,1,0:T(8,128)(2,1)} %param.6, s32[]{:T(128)S(6)} %select_n.10, s32[]{:T(128)S(6)} %select_n.9, ...), kind=kLoop, calls=%fused_computation.18 | loop fusion | bytes 1048584 | tf_op jit(solution)/shard_map/jit(dynamic_index_in_dim)/dynamic_slice | solution.py:332
  2.7 0.1 fusion.3
  2.8 0.7 pad_maximum_fusion
  3.6 1.4 %collective-permute-start = (bf16[2,8,64,128]{3,2,1,0:T(8,128)(2,1)}, bf16[2,8,64,128]{3,2,1,0:T(8,128)(2,1)S(1)}, u32[]{:S(2)}, u32[]{:S(2)}) collective-permute-start(bf16[2,8,64,128]{3,2,1,0:T(8,128)(2,1)} %pad_maximum_fusion), channel_id=1, source_target_pairs={{0,8},{8,0},{16,24},{24,16},{32,40},{40,32},{48,56},{56,48},{64,72... | collective-permute-start | bytes 786440 | tf_op jit(solution)/shard_map/ppermute | solution.py:30
  4.9 0.7 pad_maximum_fusion.1
  5.7 3.1 %collective-permute-start.1 = (bf16[2,8,64,128]{3,2,1,0:T(8,128)(2,1)}, bf16[2,8,64,128]{3,2,1,0:T(8,128)(2,1)S(1)}, u32[]{:S(2)}, u32[]{:S(2)}) collective-permute-start(bf16[2,8,64,128]{3,2,1,0:T(8,128)(2,1)} %pad_maximum_fusion.1), channel_id=1, source_target_pairs={{8,16},{16,8},{24,32},{32,24},{40,48},{48,40},{56,64},{64,56},{72,... | collective-permute-start | bytes 786440 | tf_op jit(solution)/shard_map/ppermute | solution.py:30
  8.8 0.3 shard_map.76
  9.1 3.3 %fusion = (bf16[8,8,64,128]{3,2,1,0:T(8,128)(2,1)S(1)}, bf16[8,8,64,128]{3,2,1,0:T(8,128)(2,1)S(1)}) fusion(bf16[64,8,8,128]{3,2,1,0:T(8,128)(2,1)} %param.5, bf16[128]{0:T(256)(128)(2,1)S(1)} %convert_element_type.32, bf16[64,8,8,128]{3,2,1,0:T(8,128)(2,1)} %param.6), kind=kLoop, calls=%fused_computation.2 | loop fusion | flops 1048576 | bytes 4194560 | tf_op jit(solution)/shard_map/transpose | solution.py:336
  12.4 1.2 %collective-permute-done.1.refs_6_.refs_7_ = bf16[2,8,64,128]{3,2,1,0:T(8,128)(2,1)S(1)} collective-permute-done((bf16[2,8,64,128]{3,2,1,0:T(8,128)(2,1)}, bf16[2,8,64,128]{3,2,1,0:T(8,128)(2,1)S(1)}, u32[]{:S(2)}, u32[]{:S(2)}) %collective-permute-start.1) | collective-permute-done | bytes 262176 | tf_op jit(solution)/shard_map/ppermute | solution.py:30
  13.6 0.8 shard_map.77
  14.3 0.7 copy-done.3
  15.0 1.3 %collective-permute-start.3 = (bf16[10,64,128]{2,1,0:T(8,128)(2,1)}, bf16[10,64,128]{2,1,0:T(8,128)(2,1)}, u32[]{:S(2)}, u32[]{:S(2)}) collective-permute-start(bf16[10,64,128]{2,1,0:T(8,128)(2,1)} %get-tuple-element.37), channel_id=1, source_target_pairs={{1,2},{2,1},{3,4},{4,3},{5,6},{6,5},{9,10},{10,9},{11,12},{12,11},... | collective-permute-start | bytes 491528 | tf_op jit(solution)/shard_map/ppermute | solution.py:356
  16.3 4.8 %collective-permute-start.2 = (bf16[10,64,128]{2,1,0:T(8,128)(2,1)}, bf16[10,64,128]{2,1,0:T(8,128)(2,1)}, u32[]{:S(2)}, u32[]{:S(2)}) collective-permute-start(bf16[10,64,128]{2,1,0:T(8,128)(2,1)} %get-tuple-element.36), channel_id=1, source_target_pairs={{0,1},{1,0},{2,3},{3,2},{4,5},{5,4},{6,7},{7,6},{8,9},{9,8},{10,11... | collective-permute-start | bytes 491528 | tf_op jit(solution)/shard_map/ppermute | solution.py:353
  21.1 0.1 broadcast_in_dim.7
  21.1 0.1 convert_element_type.29.refs_3_.refs_0_
  21.2 0.1 collective-permute-start.4
  21.3 0.8 collective-permute-start.5
  22.2 0.0 collective-permute-done.3.refs_9_
  22.2 8.5 %collective-permute-done.2.refs_8_ = bf16[10,64,128]{2,1,0:T(8,128)(2,1)} collective-permute-done((bf16[10,64,128]{2,1,0:T(8,128)(2,1)}, bf16[10,64,128]{2,1,0:T(8,128)(2,1)}, u32[]{:S(2)}, u32[]{:S(2)}) %collective-permute-start.2) | collective-permute-done | bytes 163872 | tf_op jit(solution)/shard_map/ppermute | solution.py:353
  30.7 4.5 %shard_map.78 = (bf16[8,8,192,128]{3,2,1,0:T(8,128)(2,1)S(1)}, f32[8,8,64,128]{3,2,1,0:T(8,128)S(1)}, bf16[10,10,64,128]{3,2,1,0:T(8,128)(2,1)S(1)}) custom-call(s32[1]{0:T(128)} %bitcast.refs_0_, s32[1]{0:T(128)} %bitcast.1.refs_1_, s32[1]{0:T(128)} %bitcast.2.refs_2_, f32[1,128]{1,0:T(1,128)S(1)} %convert_element_type.29.refs_3_.refs_0_, ...), custom_call_target="tpu_custom_call" | custom-call | flops 1811939328 | bytes 9003532 | tf_op jit(solution)/shard_map/pallas_call | solution.py:305
  35.2 0.0 collective-permute-done.4.refs_8_
  35.2 2.9 %shard_map.79 = (bf16[8,8,64,128]{3,2,1,0:T(8,128)(2,1)S(1)}, bf16[1,8,64,128]{3,2,1,0:T(8,128)(2,1)S(1)}, bf16[1,8,64,128]{3,2,1,0:T(8,128)(2,1)S(1)}, bf16[10,10,64,128]{3,2,1,0:T(8,128)(2,1)S(1)}) custom-call(s32[1]{0:T(128)} %bitcast.refs_0_, s32[1]{0:T(128)} %bitcast.1.refs_1_, s32[1]{0:T(128)} %bitcast.2.refs_2_, ...), custom_call_target="tpu_custom_call" | custom-call | flops 1811939328 | bytes 7168012 | tf_op jit(solution)/shard_map/pallas_call | solution.py:305
  38.2 2.9 %shard_map.84.refs_5_ = f32[864,128]{1,0:T(8,128)S(1)} custom-call(bf16[10,10,64,128]{3,2,1,0:T(8,128)(2,1)S(1)} %get-tuple-element.49.refs_0_, bf16[8,8,192,128]{3,2,1,0:T(8,128)(2,1)S(1)} %get-tuple-element.50.refs_1_), custom_call_target="tpu_custom_call" | custom-call | flops 1811939328 | bytes 5226496 | tf_op jit(solution)/shard_map/pallas_call | solution.py:305
  41.1 3.2 %shard_map.85 = (f32[864,128]{1,0:T(8,128)S(1)}, f32[864,128]{1,0:T(8,128)S(1)}) custom-call(s32[1]{0:T(128)} %bitcast.refs_0_, s32[1]{0:T(128)} %bitcast.1.refs_1_, s32[1]{0:T(128)} %bitcast.2.refs_2_, bf16[10,10,64,128]{3,2,1,0:T(8,128)(2,1)S(1)} %get-tuple-element.48.refs_3_, bf16[8,8,64,128]{3,2,1,0:T(8,128)(2,1)S(1)} %get-tuple-element.41.refs_3_.refs_6_.refs_4_, ...), custom_call_target="tpu_custom_call" | custom-call | flops 1811939328 | bytes 4014092 | tf_op jit(solution)/shard_map/pallas_call | solution.py:305
  44.3 0.1 collective-permute-start.10
  44.4 1.8 %collective-permute-done.10.refs_4_ = f32[864,128]{1,0:T(8,128)S(1)} collective-permute-done((f32[864,128]{1,0:T(8,128)S(1)}, f32[864,128]{1,0:T(8,128)S(1)}, u32[]{:S(2)}, u32[]{:S(2)}) %collective-permute-start.10) | collective-permute-done | bytes 442400 | tf_op jit(solution)/shard_map/ppermute | solution.py:25
  46.2 3.6 %collective-permute-start.11 = (f32[216,128]{1,0:T(8,128)S(1)}, f32[216,128]{1,0:T(8,128)S(1)}, u32[]{:S(2)}, u32[]{:S(2)}) collective-permute-start(f32[216,128]{1,0:T(8,128)S(1)} %get-tuple-element.54), channel_id=1, source_target_pairs={{0,16},{1,17},{2,18},{3,19},{4,20},{5,21},{6,22},{7,23},{8,24},{9,... | collective-permute-start | bytes 331784 | tf_op jit(solution)/shard_map/ppermute | solution.py:25
  49.8 2.9 %collective-permute-start.12 = (f32[216,128]{1,0:T(8,128)S(1)}, f32[216,128]{1,0:T(8,128)S(1)}, u32[]{:S(2)}, u32[]{:S(2)}) collective-permute-start(f32[216,128]{1,0:T(8,128)S(1)} %get-tuple-element.55), channel_id=1, source_target_pairs={{0,32},{1,33},{2,34},{3,35},{4,36},{5,37},{6,38},{7,39},{8,40},{9,... | collective-permute-start | bytes 331784 | tf_op jit(solution)/shard_map/ppermute | solution.py:25
  52.7 0.0 collective-permute-start.13
  52.7 0.7 collective-permute-start.6
  53.4 2.1 %collective-permute-start.7 = (bf16[1,8,64,128]{3,2,1,0:T(8,128)(2,1)S(1)}, bf16[1,8,64,128]{3,2,1,0:T(8,128)(2,1)S(1)}, u32[]{:S(2)}, u32[]{:S(2)}) collective-permute-start(bf16[1,8,64,128]{3,2,1,0:T(8,128)(2,1)S(1)} %get-tuple-element.43), channel_id=1, source_target_pairs={{8,16},{16,8},{24,32},{32,24},{40,48},{48,40},{56,64},{64,56},{72,... | collective-permute-start | bytes 393224 | tf_op jit(solution)/shard_map/ppermute | solution.py:30
  55.5 2.7 %collective-permute-done.12 = f32[216,128]{1,0:T(8,128)S(1)} collective-permute-done((f32[216,128]{1,0:T(8,128)S(1)}, f32[216,128]{1,0:T(8,128)S(1)}, u32[]{:S(2)}, u32[]{:S(2)}) %collective-permute-start.12) | collective-permute-done | bytes 110624 | tf_op jit(solution)/shard_map/ppermute | solution.py:25
  58.1 2.5 %collective-permute-done.13 = f32[216,128]{1,0:T(8,128)S(1)} collective-permute-done((f32[216,128]{1,0:T(8,128)S(1)}, f32[216,128]{1,0:T(8,128)S(1)}, u32[]{:S(2)}, u32[]{:S(2)}) %collective-permute-start.13) | collective-permute-done | bytes 110624 | tf_op jit(solution)/shard_map/ppermute | solution.py:25
  60.7 1.4 %collective-permute-start.16 = (f32[216,128]{1,0:T(8,128)S(1)}, f32[216,128]{1,0:T(8,128)S(1)}, u32[]{:S(2)}, u32[]{:S(2)}) collective-permute-start(f32[216,128]{1,0:T(8,128)S(1)} %add_add_fusion.2), channel_id=1, source_target_pairs={{0,6},{1,7},{2,4},{3,5},{4,2},{5,3},{6,0},{7,1},{8,14},{9,15},{10,... | collective-permute-start | bytes 331784 | tf_op jit(solution)/shard_map/ppermute | solution.py:25
  62.1 1.8 %collective-permute-start.15 = (f32[216,128]{1,0:T(8,128)S(1)}, f32[216,128]{1,0:T(8,128)S(1)}, u32[]{:S(2)}, u32[]{:S(2)}) collective-permute-start(f32[216,128]{1,0:T(8,128)S(1)} %add_add_fusion.2), channel_id=1, source_target_pairs={{0,4},{1,5},{2,6},{3,7},{4,0},{5,1},{6,2},{7,3},{8,12},{9,13},{10,... | collective-permute-start | bytes 331784 | tf_op jit(solution)/shard_map/ppermute | solution.py:25
  63.9 0.2 collective-permute-start.14
  64.1 3.7 %collective-permute-start.8 = (bf16[10,64,128]{2,1,0:T(8,128)(2,1)S(1)}, bf16[10,64,128]{2,1,0:T(8,128)(2,1)S(1)}, u32[]{:S(2)}, u32[]{:S(2)}) collective-permute-start(bf16[10,64,128]{2,1,0:T(8,128)(2,1)S(1)} %get-tuple-element.44), channel_id=1, source_target_pairs={{0,1},{1,0},{2,3},{3,2},{4,5},{5,4},{6,7},{7,6},{8,9},{9,8},{10,11... | collective-permute-start | bytes 491528 | tf_op jit(solution)/shard_map/ppermute | solution.py:376
  67.8 0.7 collective-permute-start.9
  68.4 0.0 collective-permute-done.16
  68.4 0.2 collective-permute-done.14
  68.7 4.1 %collective-permute-start.19 = (f32[216,128]{1,0:T(8,128)S(1)}, f32[216,128]{1,0:T(8,128)S(1)}, u32[]{:S(2)}, u32[]{:S(2)}) collective-permute-start(f32[216,128]{1,0:T(8,128)S(1)} %add_add_fusion.1), channel_id=1, source_target_pairs={{0,65},{1,64},{2,67},{3,66},{4,69},{5,68},{6,71},{7,70},{8,73},{9,... | collective-permute-start | bytes 331784 | tf_op jit(solution)/shard_map/ppermute | solution.py:25
  72.8 0.7 collective-permute-start.18
  73.5 0.6 collective-permute-start.17
  74.1 0.0 collective-permute-done.9.refs_10_
  74.1 1.0 %shard_map.81 = (bf16[8,2,64,128]{3,2,1,0:T(8,128)(2,1)S(1)}, bf16[10,10,64,128]{3,2,1,0:T(8,128)(2,1)S(1)}) custom-call(s32[1]{0:T(128)} %bitcast.refs_0_, s32[1]{0:T(128)} %bitcast.1.refs_1_, s32[1]{0:T(128)} %bitcast.2.refs_2_, f32[1,128]{1,0:T(1,128)S(1)} %convert_element_type.29.refs_3_.refs_0_, bf16[192,576]{1,0:T(8,128)(2,1)S(1)} %get-tuple-element.31.refs_4_.refs_1_, ...), custom_call_target="tpu_custom_call" | custom-call | flops 452984832 | bytes 4809228 | tf_op jit(solution)/shard_map/pallas_call | solution.py:305
  75.1 0.3 copy.23
  75.3 1.5 %shard_map.82 = bf16[8,4,64,128]{3,2,1,0:T(8,128)(2,1)S(1)} custom-call(f32[1,128]{1,0:T(1,128)S(1)} %convert_element_type.29.refs_3_.refs_0_, bf16[192,576]{1,0:T(8,128)(2,1)S(1)} %get-tuple-element.31.refs_4_.refs_1_, bf16[8,8,64,128]{3,2,1,0:T(8,128)(2,1)S(1)} %get-tuple-element.68.refs_4_.refs_5_.refs_2_, ...), custom_call_target="tpu_custom_call" | custom-call | flops 452984832 | bytes 3432960 | tf_op jit(solution)/shard_map/pallas_call | solution.py:305
  76.8 0.4 copy.24
  77.3 0.9 shard_map.83
  78.1 0.3 copy.25
  78.4 1.2 %collective-permute-done.17 = f32[216,128]{1,0:T(8,128)S(1)} collective-permute-done((f32[216,128]{1,0:T(8,128)S(1)}, f32[216,128]{1,0:T(8,128)S(1)}, u32[]{:S(2)}, u32[]{:S(2)}) %collective-permute-start.17) | collective-permute-done | bytes 110624 | tf_op jit(solution)/shard_map/ppermute | solution.py:25
  79.7 0.3 collective-permute-start.22
  80.0 3.1 %collective-permute-start.20 = (f32[216,128]{1,0:T(8,128)S(1)}, f32[216,128]{1,0:T(8,128)S(1)}, u32[]{:S(2)}, u32[]{:S(2)}) collective-permute-start(f32[216,128]{1,0:T(8,128)S(1)} %add_add_fusion.refs_3_), channel_id=1, source_target_pairs={{0,16},{1,17},{2,18},{3,19},{4,20},{5,21},{6,22},{7,23},{8,24},{9,... | collective-permute-start | bytes 331784 | tf_op jit(solution)/shard_map/ppermute | solution.py:25
  83.0 0.9 maximum_bitcast_fusion.refs_7_
  83.9 0.0 copy-start
  83.9 1.8 %collective-permute-done.22.refs_6_ = f32[216,128]{1,0:T(8,128)S(1)} collective-permute-done((f32[216,128]{1,0:T(8,128)S(1)}, f32[216,128]{1,0:T(8,128)S(1)}, u32[]{:S(2)}, u32[]{:S(2)}) %collective-permute-start.22) | collective-permute-done | bytes 110624 | tf_op jit(solution)/shard_map/ppermute | solution.py:25
  85.8 0.6 collective-permute-done.20.refs_4_
  86.4 4.4 %collective-permute-start.23 = (f32[864,128]{1,0:T(8,128)S(1)}, f32[864,128]{1,0:T(8,128)S(1)}, u32[]{:S(2)}, u32[]{:S(2)}) collective-permute-start(f32[864,128]{1,0:T(8,128)S(1)} %shard_map.87.refs_3_), channel_id=1, source_target_pairs={{0,8},{1,9},{2,10},{3,11},{4,12},{5,13},{6,14},{7,15},{8,0},{9,1},... | collective-permute-start | bytes 1327112 | tf_op jit(solution)/shard_map/ppermute | solution.py:25
  90.8 0.4 shard_map.88.refs_3_
  91.2 1.0 %collective-permute-done.23.refs_4_ = f32[864,128]{1,0:T(8,128)S(1)} collective-permute-done((f32[864,128]{1,0:T(8,128)S(1)}, f32[864,128]{1,0:T(8,128)S(1)}, u32[]{:S(2)}, u32[]{:S(2)}) %collective-permute-start.23) | collective-permute-done | bytes 442400 | tf_op jit(solution)/shard_map/ppermute | solution.py:25
  92.2 1.2 %shard_map.89 = (f32[3,3,3,64,64]{4,3,2,1,0:T(8,128)}, f32[3,3,3,64,64]{4,3,2,1,0:T(8,128)}) custom-call(s32[1]{0:T(128)} %bitcast.refs_0_, s32[1]{0:T(128)} %bitcast.1.refs_1_, s32[1]{0:T(128)} %bitcast.2.refs_2_, f32[3,3,3,64,64]{4,3,2,1,0:T(8,128)S(1)} %shard_map.88.refs_3_, f32[864,128]{1,0:T(8,128)S(1)} %collective-permute-done.23.refs_4_), custom_call_target="tpu_custom_call" | custom-call | bytes 1769484 | tf_op jit(solution)/shard_map/pallas_call | solution.py:305
  (23 shorter events, 0.2 us)
Async XLA Ops:
  0.6 8.2 %copy-start.2 = (bf16[3,3,3,64,64]{4,3,2,1,0:T(8,128)(2,1)S(1)}, bf16[3,3,3,64,64]{4,3,2,1,0:T(8,128)(2,1)}, u32[]{:S(2)}) copy-start(bf16[3,3,3,64,64]{4,3,2,1,0:T(8,128)(2,1)} %refs_1_.1) | copy-start | bytes 663556
  0.6 8.2 %copy-start.1 = (bf16[3,3,3,64,64]{4,3,2,1,0:T(8,128)(2,1)S(1)}, bf16[3,3,3,64,64]{4,3,2,1,0:T(8,128)(2,1)}, u32[]{:S(2)}) copy-start(bf16[3,3,3,64,64]{4,3,2,1,0:T(8,128)(2,1)} %refs_0_.1) | copy-start | bytes 663556
  3.6 8.8 %collective-permute-start = (bf16[2,8,64,128]{3,2,1,0:T(8,128)(2,1)}, bf16[2,8,64,128]{3,2,1,0:T(8,128)(2,1)S(1)}, u32[]{:S(2)}, u32[]{:S(2)}) collective-permute-start(bf16[2,8,64,128]{3,2,1,0:T(8,128)(2,1)} %pad_maximum_fusion), channel_id=1, source_target_pairs={{0,8},{8,0},{16,24},{24,16},{32,40},{40,32},{48,56},{56,48},{64,72... | collective-permute-start | bytes 786440 | tf_op jit(solution)/shard_map/ppermute | solution.py:30
  5.7 7.9 %collective-permute-start.1 = (bf16[2,8,64,128]{3,2,1,0:T(8,128)(2,1)}, bf16[2,8,64,128]{3,2,1,0:T(8,128)(2,1)S(1)}, u32[]{:S(2)}, u32[]{:S(2)}) collective-permute-start(bf16[2,8,64,128]{3,2,1,0:T(8,128)(2,1)} %pad_maximum_fusion.1), channel_id=1, source_target_pairs={{8,16},{16,8},{24,32},{32,24},{40,48},{48,40},{56,64},{64,56},{72,... | collective-permute-start | bytes 786440 | tf_op jit(solution)/shard_map/ppermute | solution.py:30
  14.3 0.7 copy-start.3
  15.0 7.2 %collective-permute-start.3 = (bf16[10,64,128]{2,1,0:T(8,128)(2,1)}, bf16[10,64,128]{2,1,0:T(8,128)(2,1)}, u32[]{:S(2)}, u32[]{:S(2)}) collective-permute-start(bf16[10,64,128]{2,1,0:T(8,128)(2,1)} %get-tuple-element.37), channel_id=1, source_target_pairs={{1,2},{2,1},{3,4},{4,3},{5,6},{6,5},{9,10},{10,9},{11,12},{12,11},... | collective-permute-start | bytes 491528 | tf_op jit(solution)/shard_map/ppermute | solution.py:356
  16.3 14.4 %collective-permute-start.2 = (bf16[10,64,128]{2,1,0:T(8,128)(2,1)}, bf16[10,64,128]{2,1,0:T(8,128)(2,1)}, u32[]{:S(2)}, u32[]{:S(2)}) collective-permute-start(bf16[10,64,128]{2,1,0:T(8,128)(2,1)} %get-tuple-element.36), channel_id=1, source_target_pairs={{0,1},{1,0},{2,3},{3,2},{4,5},{5,4},{6,7},{7,6},{8,9},{9,8},{10,11... | collective-permute-start | bytes 491528 | tf_op jit(solution)/shard_map/ppermute | solution.py:353
  21.2 14.0 %collective-permute-start.4 = (bf16[10,64,128]{2,1,0:T(8,128)(2,1)}, bf16[10,64,128]{2,1,0:T(8,128)(2,1)S(1)}, u32[]{:S(2)}, u32[]{:S(2)}) collective-permute-start(bf16[10,64,128]{2,1,0:T(8,128)(2,1)} %copy-done.3), channel_id=1, source_target_pairs={{0,1},{1,0},{2,3},{3,2},{4,5},{5,4},{6,7},{7,6},{8,9},{9,8},{10,11... | collective-permute-start | bytes 491528 | tf_op jit(solution)/shard_map/ppermute | solution.py:30
  21.3 13.9 %collective-permute-start.5 = (bf16[10,64,128]{2,1,0:T(8,128)(2,1)S(1)}, bf16[10,64,128]{2,1,0:T(8,128)(2,1)S(1)}, u32[]{:S(2)}, u32[]{:S(2)}) collective-permute-start(bf16[10,64,128]{2,1,0:T(8,128)(2,1)S(1)} %get-tuple-element.40), channel_id=1, source_target_pairs={{1,2},{2,1},{3,4},{4,3},{5,6},{6,5},{9,10},{10,9},{11,12},{12,11},... | collective-permute-start | bytes 491528 | tf_op jit(solution)/shard_map/ppermute | solution.py:30
  44.3 1.9 %collective-permute-start.10 = (f32[864,128]{1,0:T(8,128)S(1)}, f32[864,128]{1,0:T(8,128)S(1)}, u32[]{:S(2)}, u32[]{:S(2)}) collective-permute-start(f32[864,128]{1,0:T(8,128)S(1)} %get-tuple-element.52), channel_id=1, source_target_pairs={{0,8},{1,9},{2,10},{3,11},{4,12},{5,13},{6,14},{7,15},{8,0},{9,1},... | collective-permute-start | bytes 1327112 | tf_op jit(solution)/shard_map/ppermute | solution.py:25
  46.2 9.2 %collective-permute-start.11 = (f32[216,128]{1,0:T(8,128)S(1)}, f32[216,128]{1,0:T(8,128)S(1)}, u32[]{:S(2)}, u32[]{:S(2)}) collective-permute-start(f32[216,128]{1,0:T(8,128)S(1)} %get-tuple-element.54), channel_id=1, source_target_pairs={{0,16},{1,17},{2,18},{3,19},{4,20},{5,21},{6,22},{7,23},{8,24},{9,... | collective-permute-start | bytes 331784 | tf_op jit(solution)/shard_map/ppermute | solution.py:25
  49.8 8.3 %collective-permute-start.12 = (f32[216,128]{1,0:T(8,128)S(1)}, f32[216,128]{1,0:T(8,128)S(1)}, u32[]{:S(2)}, u32[]{:S(2)}) collective-permute-start(f32[216,128]{1,0:T(8,128)S(1)} %get-tuple-element.55), channel_id=1, source_target_pairs={{0,32},{1,33},{2,34},{3,35},{4,36},{5,37},{6,38},{7,39},{8,40},{9,... | collective-permute-start | bytes 331784 | tf_op jit(solution)/shard_map/ppermute | solution.py:25
  52.7 8.0 %collective-permute-start.13 = (f32[216,128]{1,0:T(8,128)S(1)}, f32[216,128]{1,0:T(8,128)S(1)}, u32[]{:S(2)}, u32[]{:S(2)}) collective-permute-start(f32[216,128]{1,0:T(8,128)S(1)} %get-tuple-element.56), channel_id=1, source_target_pairs={{0,48},{1,49},{2,50},{3,51},{4,52},{5,53},{6,54},{7,55},{8,56},{9,... | collective-permute-start | bytes 331784 | tf_op jit(solution)/shard_map/ppermute | solution.py:25
  52.7 11.3 %collective-permute-start.6 = (bf16[1,8,64,128]{3,2,1,0:T(8,128)(2,1)S(1)}, bf16[1,8,64,128]{3,2,1,0:T(8,128)(2,1)S(1)}, u32[]{:S(2)}, u32[]{:S(2)}) collective-permute-start(bf16[1,8,64,128]{3,2,1,0:T(8,128)(2,1)S(1)} %get-tuple-element.42), channel_id=1, source_target_pairs={{0,8},{8,0},{16,24},{24,16},{32,40},{40,32},{48,56},{56,48},{64,72... | collective-permute-start | bytes 393224 | tf_op jit(solution)/shard_map/ppermute | solution.py:30
  53.4 10.6 %collective-permute-start.7 = (bf16[1,8,64,128]{3,2,1,0:T(8,128)(2,1)S(1)}, bf16[1,8,64,128]{3,2,1,0:T(8,128)(2,1)S(1)}, u32[]{:S(2)}, u32[]{:S(2)}) collective-permute-start(bf16[1,8,64,128]{3,2,1,0:T(8,128)(2,1)S(1)} %get-tuple-element.43), channel_id=1, source_target_pairs={{8,16},{16,8},{24,32},{32,24},{40,48},{48,40},{56,64},{64,56},{72,... | collective-permute-start | bytes 393224 | tf_op jit(solution)/shard_map/ppermute | solution.py:30
  60.7 7.7 %collective-permute-start.16 = (f32[216,128]{1,0:T(8,128)S(1)}, f32[216,128]{1,0:T(8,128)S(1)}, u32[]{:S(2)}, u32[]{:S(2)}) collective-permute-start(f32[216,128]{1,0:T(8,128)S(1)} %add_add_fusion.2), channel_id=1, source_target_pairs={{0,6},{1,7},{2,4},{3,5},{4,2},{5,3},{6,0},{7,1},{8,14},{9,15},{10,... | collective-permute-start | bytes 331784 | tf_op jit(solution)/shard_map/ppermute | solution.py:25
  62.1 6.4 %collective-permute-start.15 = (f32[216,128]{1,0:T(8,128)S(1)}, f32[216,128]{1,0:T(8,128)S(1)}, u32[]{:S(2)}, u32[]{:S(2)}) collective-permute-start(f32[216,128]{1,0:T(8,128)S(1)} %add_add_fusion.2), channel_id=1, source_target_pairs={{0,4},{1,5},{2,6},{3,7},{4,0},{5,1},{6,2},{7,3},{8,12},{9,13},{10,... | collective-permute-start | bytes 331784 | tf_op jit(solution)/shard_map/ppermute | solution.py:25
  63.9 4.8 %collective-permute-start.14 = (f32[216,128]{1,0:T(8,128)S(1)}, f32[216,128]{1,0:T(8,128)S(1)}, u32[]{:S(2)}, u32[]{:S(2)}) collective-permute-start(f32[216,128]{1,0:T(8,128)S(1)} %add_add_fusion.2), channel_id=1, source_target_pairs={{0,2},{1,3},{2,0},{3,1},{4,6},{5,7},{6,4},{7,5},{8,10},{9,11},{10,... | collective-permute-start | bytes 331784 | tf_op jit(solution)/shard_map/ppermute | solution.py:25
  64.1 10.0 %collective-permute-start.8 = (bf16[10,64,128]{2,1,0:T(8,128)(2,1)S(1)}, bf16[10,64,128]{2,1,0:T(8,128)(2,1)S(1)}, u32[]{:S(2)}, u32[]{:S(2)}) collective-permute-start(bf16[10,64,128]{2,1,0:T(8,128)(2,1)S(1)} %get-tuple-element.44), channel_id=1, source_target_pairs={{0,1},{1,0},{2,3},{3,2},{4,5},{5,4},{6,7},{7,6},{8,9},{9,8},{10,11... | collective-permute-start | bytes 491528 | tf_op jit(solution)/shard_map/ppermute | solution.py:376
  67.8 6.3 %collective-permute-start.9 = (bf16[10,64,128]{2,1,0:T(8,128)(2,1)S(1)}, bf16[10,64,128]{2,1,0:T(8,128)(2,1)S(1)}, u32[]{:S(2)}, u32[]{:S(2)}) collective-permute-start(bf16[10,64,128]{2,1,0:T(8,128)(2,1)S(1)} %get-tuple-element.45), channel_id=1, source_target_pairs={{1,2},{2,1},{3,4},{4,3},{5,6},{6,5},{9,10},{10,9},{11,12},{12,11},... | collective-permute-start | bytes 491528 | tf_op jit(solution)/shard_map/ppermute | solution.py:377
  68.7 9.7 %collective-permute-start.19 = (f32[216,128]{1,0:T(8,128)S(1)}, f32[216,128]{1,0:T(8,128)S(1)}, u32[]{:S(2)}, u32[]{:S(2)}) collective-permute-start(f32[216,128]{1,0:T(8,128)S(1)} %add_add_fusion.1), channel_id=1, source_target_pairs={{0,65},{1,64},{2,67},{3,66},{4,69},{5,68},{6,71},{7,70},{8,73},{9,... | collective-permute-start | bytes 331784 | tf_op jit(solution)/shard_map/ppermute | solution.py:25
  72.8 5.6 %collective-permute-start.18 = (f32[216,128]{1,0:T(8,128)S(1)}, f32[216,128]{1,0:T(8,128)S(1)}, u32[]{:S(2)}, u32[]{:S(2)}) collective-permute-start(f32[216,128]{1,0:T(8,128)S(1)} %add_add_fusion.1), channel_id=1, source_target_pairs={{0,64},{1,65},{2,66},{3,67},{4,68},{5,69},{6,70},{7,71},{8,72},{9,... | collective-permute-start | bytes 331784 | tf_op jit(solution)/shard_map/ppermute | solution.py:25
  73.5 6.2 %collective-permute-start.17 = (f32[216,128]{1,0:T(8,128)S(1)}, f32[216,128]{1,0:T(8,128)S(1)}, u32[]{:S(2)}, u32[]{:S(2)}) collective-permute-start(f32[216,128]{1,0:T(8,128)S(1)} %add_add_fusion.1), channel_id=1, source_target_pairs={{0,1},{1,0},{2,3},{3,2},{4,5},{5,4},{6,7},{7,6},{8,9},{9,8},{10,11... | collective-permute-start | bytes 331784 | tf_op jit(solution)/shard_map/ppermute | solution.py:25
  79.7 6.1 %collective-permute-start.22 = (f32[216,128]{1,0:T(8,128)S(1)}, f32[216,128]{1,0:T(8,128)S(1)}, u32[]{:S(2)}, u32[]{:S(2)}) collective-permute-start(f32[216,128]{1,0:T(8,128)S(1)} %add_add_fusion.refs_3_), channel_id=1, source_target_pairs={{0,48},{1,49},{2,50},{3,51},{4,52},{5,53},{6,54},{7,55},{8,56},{9,... | collective-permute-start | bytes 331784 | tf_op jit(solution)/shard_map/ppermute | solution.py:25
  80.0 5.8 %collective-permute-start.21 = (f32[216,128]{1,0:T(8,128)S(1)}, f32[216,128]{1,0:T(8,128)S(1)}, u32[]{:S(2)}, u32[]{:S(2)}) collective-permute-start(f32[216,128]{1,0:T(8,128)S(1)} %add_add_fusion.refs_3_), channel_id=1, source_target_pairs={{0,32},{1,33},{2,34},{3,35},{4,36},{5,37},{6,38},{7,39},{8,40},{9,... | collective-permute-start | bytes 331784 | tf_op jit(solution)/shard_map/ppermute | solution.py:25
  80.0 6.4 %collective-permute-start.20 = (f32[216,128]{1,0:T(8,128)S(1)}, f32[216,128]{1,0:T(8,128)S(1)}, u32[]{:S(2)}, u32[]{:S(2)}) collective-permute-start(f32[216,128]{1,0:T(8,128)S(1)} %add_add_fusion.refs_3_), channel_id=1, source_target_pairs={{0,16},{1,17},{2,18},{3,19},{4,20},{5,21},{6,22},{7,23},{8,24},{9,... | collective-permute-start | bytes 331784 | tf_op jit(solution)/shard_map/ppermute | solution.py:25
  83.9 9.5 %copy-start = (bf16[64,8,8,128]{3,2,1,0:T(8,128)(2,1)}, bf16[64,8,8,128]{3,2,1,0:T(8,128)(2,1)S(1)}, u32[]{:S(2)}) copy-start(bf16[64,8,8,128]{3,2,1,0:T(8,128)(2,1)S(1)} %maximum_bitcast_fusion.refs_7_) | copy-start | bytes 3145732
  86.4 5.8 %collective-permute-start.23 = (f32[864,128]{1,0:T(8,128)S(1)}, f32[864,128]{1,0:T(8,128)S(1)}, u32[]{:S(2)}, u32[]{:S(2)}) collective-permute-start(f32[864,128]{1,0:T(8,128)S(1)} %shard_map.87.refs_3_), channel_id=1, source_target_pairs={{0,8},{1,9},{2,10},{3,11},{4,12},{5,13},{6,14},{7,15},{8,0},{9,1},... | collective-permute-start | bytes 1327112 | tf_op jit(solution)/shard_map/ppermute | solution.py:25
